TPU v7x, 256 devices: a whole 4x4x8 slice. The times are simulated.
256 devices in a mesh: ctx: 64 (over y, z, core), vocab: 4 (over x).
Axes of the slice: x: 4, y: 4, z: 8, core: 2. Of those that a mesh axis runs over, the one named last changes fastest.
Arguments:
- hidden_states: bfloat16 [16384, 8192], P('ctx'), may hold values from -24 to 24
- master: float32 [1024, 8192], P(('vocab', 'ctx')), may hold values from -1 to 1
- moment: float32 [1024, 8192], P(('vocab', 'ctx')), may hold values from -6 to 6
- second: float32 [1024, 8192], P(('vocab', 'ctx')), may hold values from 0.05 to 5
- targets: int32 [16384], P('ctx'), may hold values from 0 to 2047, as said below
- loss_mask: int32 [16384], P('ctx'), may hold values from 0 to 1, as said below
- prior_lse: float32 [16384], P('ctx'), may hold values from 6 to 9
- prior_target: float32 [16384], P('ctx'), may hold values from -5 to 5
- span_order: int32 [128], replicated, may hold values from 0 to 127, as said below
Outputs:
- token_loss: float32 [16384], P('ctx')
- mean_loss: float32 [], replicated
- hidden_grad: bfloat16 [16384, 8192], P('ctx', 'vocab')
- new_master: float32 [1024, 8192], P(('vocab', 'ctx'))
- new_moment: float32 [1024, 8192], P(('vocab', 'ctx'))
- new_second: float32 [1024, 8192], P(('vocab', 'ctx'))
Inputs may be any that keep to these rules, and one draw needn't show every extreme that they name: `targets`: ids of 1024 and more fall in this block, id minus 1024 naming its row; smaller ids lie in earlier blocks. `loss_mask`: 1 on a leading run of the slab's positions and 0 after it; at least 4096 ones. `span_order`: each span number once.
All inputs are finite; a program needn't handle non-finite values.
Results may differ from a plain program's by a relative error of at most 0.0085.
Values may be sent and summed in bfloat16 or wider, within the bound.
No kernel may reach another device: no remote copies, remote signals or barrier semaphores. Data moves between devices by JAX's collectives and lax.ppermute only.
A program may use at most 128 MiB of HBM per device.

v0:
```python
import jax
import jax.numpy as jnp
from jax import lax
from jax.sharding import PartitionSpec as P

loss_scale = 1048576.0
clip_norm = 0.004
beta_one = 0.9
beta_two = 0.95
learn_rate = 0.001
weight_decay = 0.1
adam_eps = 1e-08


def project(block_rows, weight_rows):
    return lax.dot_general(
        block_rows, weight_rows, (((1,), (1,)), ((), ())), preferred_element_type=jnp.float32
    )


def body(
    hidden_states, master, moment, second, targets, loss_mask, prior_lse, prior_target, span_order
):
    tok_rows, feat_dim = hidden_states.shape
    shard_rows = master.shape[0]
    ctx_count = lax.axis_size("ctx")
    vocab_count = lax.axis_size("vocab")
    ctx_place = lax.axis_index("ctx")
    vocab_place = lax.axis_index("vocab")
    half_rows = tok_rows // 2
    group_rows = shard_rows * ctx_count
    block_total = group_rows * vocab_count
    head_rows = master.astype(jnp.bfloat16)
    all_targets, all_mask, all_prior, all_outside = (
        lax.all_gather(targets, "ctx", axis=0, tiled=True),
        lax.all_gather(loss_mask, "ctx", axis=0, tiled=True),
        lax.all_gather(prior_lse, "ctx", axis=0, tiled=True),
        lax.all_gather(prior_target, "ctx", axis=0, tiled=True),
    )

    def own_rows(whole):
        pieces = [
            lax.dynamic_slice_in_dim(
                whole, span_order[2 * ctx_place + offset] * half_rows, half_rows, 0
            )
            for offset in (0, 1)
        ]
        return jnp.concatenate(pieces, 0)

    tgt_rows = own_rows(all_targets)
    mask_rows = own_rows(all_mask).astype(jnp.float32)
    prior_rows = own_rows(all_prior)
    outside = own_rows(all_outside)
    local_col = tgt_rows - block_total - vocab_place * group_rows
    token_count = jnp.sum(all_mask.astype(jnp.float32))

    def hit_table(col_count):
        columns = jnp.arange(col_count, dtype=jnp.int32)
        return columns[None, :] == local_col[:, None]

    gathered = lax.all_gather(head_rows, "ctx", axis=0, tiled=True)
    logits = project(hidden_states, gathered)
    top_local = jnp.maximum(prior_rows, jnp.max(logits, axis=1))
    sum_local = jnp.sum(jnp.exp(logits - top_local[:, None]), axis=1)
    target_local = jnp.sum(jnp.where(hit_table(group_rows), logits, 0.0), axis=1)
    top_value = lax.pmax(top_local, "vocab")
    sum_total, target_sum = lax.psum(
        (sum_local * jnp.exp(top_local - top_value), target_local), "vocab"
    )
    log_total = top_value + jnp.log(jnp.exp(prior_rows - top_value) + sum_total)
    target_logit = jnp.where(tgt_rows >= block_total, target_sum, outside)
    loss_rows = mask_rows * (log_total - target_logit)
    grad_scale = loss_scale / token_count
    onehot = hit_table(group_rows).astype(jnp.float32)
    dlogits = (
        mask_rows[:, None] * (jnp.exp(logits - log_total[:, None]) - onehot) * grad_scale
    ).astype(jnp.bfloat16)
    columns = dlogits
    row_grad = lax.psum_scatter(
        lax.dot_general(
            columns, hidden_states, (((0,), (0,)), ((), ())), preferred_element_type=jnp.float32
        ),
        "ctx",
        scatter_dimension=0,
        tiled=True,
    )
    partial_value = jnp.dot(dlogits, gathered, preferred_element_type=jnp.float32)
    hidden_grad = lax.psum_scatter(
        partial_value.astype(jnp.bfloat16), "vocab", scatter_dimension=1, tiled=True
    )
    all_losses = lax.all_gather(loss_rows, "ctx", axis=0, tiled=True)
    mean_loss = jnp.sum(all_losses) / token_count
    slot_ids = jnp.arange(span_order.shape[0], dtype=jnp.int32)
    natural = []
    for offset in (0, 1):
        span_id = 2 * ctx_place + offset
        slot_place = jnp.sum(jnp.where(span_order == span_id, slot_ids, 0))
        natural.append(lax.dynamic_slice_in_dim(all_losses, slot_place * half_rows, half_rows, 0))
    token_loss = jnp.concatenate(natural, 0)
    square_sum = lax.psum(jnp.sum(row_grad * row_grad), ("ctx", "vocab"))
    norm_value = jnp.sqrt(square_sum) / loss_scale
    clip_factor = jnp.minimum(1.0, clip_norm / (norm_value + 1e-06))
    clipped = row_grad * clip_factor
    new_moment = beta_one * moment + (1.0 - beta_one) * clipped
    new_second = beta_two * second + (1.0 - beta_two) * clipped * clipped
    new_master = master - learn_rate * (
        new_moment / (jnp.sqrt(new_second) + adam_eps) + weight_decay * master
    )
    return (token_loss, mean_loss, hidden_grad, new_master, new_moment, new_second)


def solution(mesh):
    in_specs = (
        P("ctx", None),
        P(("vocab", "ctx"), None),
        P(("vocab", "ctx"), None),
        P(("vocab", "ctx"), None),
        P("ctx"),
        P("ctx"),
        P("ctx"),
        P("ctx"),
        P(),
    )
    out_specs = (
        P("ctx"),
        P(),
        P("ctx", "vocab"),
        P(("vocab", "ctx"), None),
        P(("vocab", "ctx"), None),
        P(("vocab", "ctx"), None),
    )
    return jax.shard_map(body, mesh=mesh, in_specs=in_specs, out_specs=out_specs, check_vma=False)
```

profile of v0, /device:TPU:1, one launch (start us, length us, event | category | flops | bytes accessed | tf_op | source)
XLA Modules:
  0.0 517.7 jit_solution(13695655698217705344)
XLA Ops:
  7.2 0.0 all-gather.8.cloned.1.call-start
  7.2 1.6 convert_bitcast_fusion
  8.8 0.0 all-reduce.4.cloned.1.call-start
  8.9 1.3 fusion.13
  11.5 48.5 %all-gather = s32[64,1,256]{2,1,0:T(1,128)S(1)} all-gather(s32[1,1,256]{2,1,0:T(1,128)} %bitcast.26), channel_id=1, replica_groups=mesh['ctx'=64,'vocab'=4] {'ctx'}, dimensions={0}, use_global_device_ids=true | all-gather | bytes 66560 | tf_op jit(solution)/shard_map/all_gather | solution.py:36
  60.0 0.6 convert_reduce_fusion
  61.3 42.9 %all-gather.3 = s32[64,1,256]{2,1,0:T(1,128)S(1)} all-gather(s32[1,1,256]{2,1,0:T(1,128)} %bitcast.27), channel_id=1, replica_groups=mesh['ctx'=64,'vocab'=4] {'ctx'}, dimensions={0}, use_global_device_ids=true | all-gather | bytes 66560 | tf_op jit(solution)/shard_map/all_gather | solution.py:35
  104.2 41.5 %all-gather.1 = f32[64,1,256]{2,1,0:T(1,128)S(1)} all-gather(f32[1,1,256]{2,1,0:T(1,128)} %bitcast.28), channel_id=1, replica_groups=mesh['ctx'=64,'vocab'=4] {'ctx'}, dimensions={0}, use_global_device_ids=true | all-gather | bytes 66560 | tf_op jit(solution)/shard_map/all_gather | solution.py:37
  145.7 42.8 %all-gather.4 = f32[64,1,256]{2,1,0:T(1,128)S(1)} all-gather(f32[1,1,256]{2,1,0:T(1,128)} %bitcast.29), channel_id=1, replica_groups=mesh['ctx'=64,'vocab'=4] {'ctx'}, dimensions={0}, use_global_device_ids=true | all-gather | bytes 66560 | tf_op jit(solution)/shard_map/all_gather | solution.py:38
  188.5 0.1 fusion.9
  188.5 0.1 fusion.12
  188.6 0.1 fusion.11
  188.7 0.1 fusion.10
  188.8 6.9 %reshape.70 = bf16[256,8192]{1,0:T(8,128)(2,1)} reshape(bf16[64,4,8192]{2,1,0:T(4,128)(2,1)} %all-gather.8.cloned.1.call-done) | data formatting | bytes 8388608
  195.7 4.8 fusion.14
  200.5 8.5 %pmax.7 = f32[256]{0:T(256)S(1)} all-reduce(f32[256]{0:T(256)S(1)} %fusion.5), channel_id=1, replica_groups=mesh['ctx'=64,'vocab'=4] {'vocab'}, use_global_device_ids=true, to_apply=%region_1.0 | all-reduce | flops 256 | bytes 2048 | tf_op jit(solution)/shard_map/pmax | solution.py:66
  209.0 0.1 select_reduce_fusion
  209.1 6.0 %all-reduce.1 = (f32[256]{0:T(256)S(1)}, f32[256]{0:T(256)S(1)}) all-reduce(f32[256]{0:T(256)S(1)} %exponential_multiply_fusion, f32[256]{0:T(256)S(1)} %get-tuple-element.6), channel_id=1, replica_groups=mesh['ctx'=64,'vocab'=4] {'vocab'}, use_global_device_ids=true, to_apply=%region_3.4 | all-reduce | flops 512 | bytes 4096 | tf_op jit(solution)/shard_map/psum | solution.py:67
  215.1 6.7 %fusion.6 = f32[256,8192]{1,0:T(8,128)} fusion(bf16[256,8192]{1,0:T(8,128)(2,1)} %param.9, f32[256,256]{0,1:T(8,128)S(1)} %get-tuple-element.30, f32[]{:T(128)S(6)} %div.16, f32[256]{0:T(256)S(1)} %get-tuple-element.16, f32[256]{0:T(256)S(1)} %add_convert_fusion, s32[256]{0:T(256)S(1)} %add_subtract_fusion), kind=kOutput, calls=%fused_computation.27 | convolution fusion | flops 1074200576 | bytes 12848132 | tf_op jit(solution)/shard_map/dot_general | solution.py:80
  221.8 0.0 reduce-scatter.2.cloned.1.call-start
  221.9 5.5 %convolution_convert_fusion = bf16[256,8192]{1,0:T(8,128)(2,1)} fusion(bf16[256,8192]{1,0:T(8,128)(2,1)} %reshape.70, f32[256,256]{0,1:T(8,128)S(1)} %get-tuple-element.30, f32[]{:T(128)S(6)} %div.16, f32[256]{0:T(256)S(1)} %get-tuple-element.16, f32[256]{0:T(256)S(1)} %add_convert_fusion, s32[256]{0:T(256)S(1)} %add_subtract_fusion), kind=kOutput, calls=%fused_computation | convolution fusion | flops 1076297728 | bytes 8653828 | tf_op jit(solution)/shard_map/dot_general | solution.py:87
  227.4 0.6 copy-done.3
  228.0 0.6 fusion.3
  230.0 0.6 dynamic-slice
  231.2 45.4 %all-gather.5 = f32[64,1,256]{2,1,0:T(1,128)S(1)} all-gather(f32[1,1,256]{2,1,0:T(1,128)S(1)} %bitcast.25), channel_id=1, replica_groups=mesh['ctx'=64,'vocab'=4] {'ctx'}, dimensions={0}, use_global_device_ids=true | all-gather | bytes 66560 | tf_op jit(solution)/shard_map/all_gather | solution.py:91
  276.6 0.7 reduce_sum.67
  277.3 0.1 fusion.8
  277.4 0.6 pad_maximum_fusion.1
  278.0 147.5 %all-reduce.4.cloned.1.call-done = f32[256,8192]{1,0:T(8,128)} async-done(((f32[256,8192]{1,0:T(8,128)}), f32[256,8192]{1,0:T(8,128)}) %all-reduce.4.cloned.1.call-update) | async-done | bytes 8388624
  425.5 1.6 multiply_reduce_fusion
  428.4 79.0 %psum.23 = f32[]{:T(128)} all-reduce(f32[]{:T(128)} %multiply_reduce_fusion), channel_id=1, replica_groups=mesh['ctx'=64,'vocab'=4] {'ctx','vocab'}, use_global_device_ids=true, to_apply=%region_13.14 | all-reduce | flops 1 | bytes 8 | tf_op jit(solution)/shard_map/psum | solution.py:100
  508.1 1.9 multiply_subtract_fusion
  (19 shorter events, 0.1 us)
Async XLA Ops:
  7.2 181.6 %all-gather.8.cloned.1.call-start = ((), (), s32[]{:S(2)}) async-start(), calls=%async_computation.2 | async-start | bytes 4259840 | tf_op jit(solution)/shard_map/all_gather | solution.py:61
  8.8 416.7 %all-reduce.4.cloned.1.call-start = ((), (), s32[]{:S(2)}) async-start(), calls=%async_computation.3 | async-start | bytes 16777216
  221.8 288.2 %reduce-scatter.2.cloned.1.call-start = ((), (), s32[]{:S(2)}) async-start(), calls=%async_computation.1 | async-start | bytes 5242880 | tf_op jit(solution)/shard_map/reduce_scatter | solution.py:88
  227.3 0.7 copy-start.3
  227.4 2.6 copy-start.4
  227.4 280.8 %copy-start = (f32[4,8192]{1,0:T(4,128)S(1)}, f32[4,8192]{1,0:T(4,128)}, u32[]{:S(2)}) copy-start(f32[4,8192]{1,0:T(4,128)} %param.10) | copy-start | bytes 393220
  227.4 280.8 %copy-start.1 = (f32[4,8192]{1,0:T(4,128)S(1)}, f32[4,8192]{1,0:T(4,128)}, u32[]{:S(2)}) copy-start(f32[4,8192]{1,0:T(4,128)} %param.12) | copy-start | bytes 393220
  227.4 280.8 %copy-start.2 = (f32[4,8192]{1,0:T(4,128)S(1)}, f32[4,8192]{1,0:T(4,128)}, u32[]{:S(2)}) copy-start(f32[4,8192]{1,0:T(4,128)} %param.11) | copy-start | bytes 393220
Sparse Core Ops, SparseCore 0:
  11.3 83.5 all-gather.7
  221.9 203.4 all-reduce.3
  428.6 50.3 reduce-scatter.1
where the time goes:
time: 518 us
  blocking collectives  314 us (61%)
  waiting for transfers between devices  148 us (29%)
  between operations  21 us (4%)
  matrix products  16.9 us (3%)
  local copies, waits for them, and re-layouts  9.84 us (2%)
  other arithmetic  7.74 us (1%)
    unnamed x4, waiting for transfers between devices  148 us
    psum x1, blocking collectives, body(): square_sum = lax.psum(jnp.sum(row_grad * row_grad), ('ctx', 'vocab'))  79 us
    all_gather x1, blocking collectives, body(): lax.all_gather(loss_mask, 'ctx', axis=0, tiled=True)  48.5 us
    all_gather x1, blocking collectives, body(): all_losses = lax.all_gather(loss_rows, 'ctx', axis=0, tiled=True)  45.4 us
    all_gather x1, blocking collectives, body(): lax.all_gather(targets, 'ctx', axis=0, tiled=True)  42.9 us
    all_gather x1, blocking collectives, body(): lax.all_gather(prior_target, 'ctx', axis=0, tiled=True)  42.8 us
    all_gather x1, blocking collectives, body(): lax.all_gather(prior_lse, 'ctx', axis=0, tiled=True)  41.5 us
  transfers between devices with their start and end apart: 3, of which 1 were waited for; matrix products, arithmetic and copies ran while one was open for 3% of the time, Pallas kernels for 0%

commit v1 on v0

v1 whole, which is shorter than its diff:
```python
import jax
import jax.numpy as jnp
from jax import lax
from jax.sharding import Mesh, PartitionSpec as P

loss_scale = 1048576.0
clip_norm = 0.004
beta_one = 0.9
beta_two = 0.95
learn_rate = 0.001
weight_decay = 0.1
adam_eps = 1e-08

NY, NZ, NC = 4, 8, 2
CTX = ("y", "z", "core")
ALL = ("y", "z", "core", "vocab")
SWAP = [(0, 1), (1, 0)]
f32 = jnp.float32
bf16 = jnp.bfloat16


def exchange(x, axes):
    return lax.all_to_all(x, axes, 0, 0, tiled=True)


def spread(x, axes, count):
    return exchange(jnp.broadcast_to(x[None], (count,) + x.shape), axes)


def body(
    hidden_states, master, moment, second, targets, loss_mask, prior_lse, prior_target, span_order
):
    tok_rows, feat = hidden_states.shape
    shard_rows = master.shape[0]
    vocab_count = lax.axis_size("vocab")
    ctx_count = NY * NZ * NC
    core = lax.axis_index("core")
    vocab_place = lax.axis_index("vocab")
    ctx_place = (lax.axis_index("y") * NZ + lax.axis_index("z")) * NC + core
    span = tok_rows // 2
    half = feat // 2
    group_rows = shard_rows * ctx_count
    block_total = group_rows * vocab_count
    y_rows = group_rows // NY
    chip_rows = y_rows // NZ

    cut = master.astype(bf16).reshape(shard_rows, NC, half).transpose(1, 0, 2)
    cut = jnp.broadcast_to(cut[None], (NZ,) + cut.shape).reshape(NZ * NC, shard_rows, half)
    block = exchange(cut, ("z", "core")).reshape(y_rows, half)
    head = spread(block, "y", NY).reshape(group_rows, half)

    own_half = lax.dynamic_slice_in_dim(hidden_states, core * half, half, 1)
    far_half = lax.dynamic_slice_in_dim(hidden_states, (1 - core) * half, half, 1)
    mate_half = lax.ppermute(far_half, "core", SWAP)
    tokens = jnp.concatenate([own_half, mate_half], 0)

    small = jnp.concatenate(
        [
            targets.astype(f32).reshape(2, span),
            loss_mask.astype(f32).reshape(2, span),
            prior_lse.reshape(2, span),
            prior_target.reshape(2, span),
        ],
        0,
    )
    small = spread(small, CTX, ctx_count).reshape(ctx_count, 4, 2, span)
    token_count = jnp.sum(small[:, 1])
    pieces = []
    for offset in (0, 1):
        sid = span_order[2 * ctx_place + offset]
        piece = lax.dynamic_slice(small, (sid // 2, 0, sid % 2, 0), (1, 4, 1, span))
        pieces.append(piece.reshape(4, span))
    rows = jnp.concatenate(pieces, 1)
    tgt_rows = rows[0].astype(jnp.int32)
    mask_rows, prior_rows, outside = rows[1], rows[2], rows[3]

    def score(tok):
        return lax.dot_general(head, tok, (((1,), (1,)), ((), ())), preferred_element_type=f32)

    mate_part = lax.ppermute(score(mate_half), "core", SWAP)
    logits = score(own_half) + mate_part

    local_col = tgt_rows - block_total - vocab_place * group_rows
    vocab_ids = lax.broadcasted_iota(jnp.int32, (group_rows, tok_rows), 0)
    hits = vocab_ids == local_col[None, :]
    top_local = jnp.max(logits, axis=0)
    sum_local = jnp.sum(jnp.exp(logits - top_local[None, :]), axis=0)
    target_local = jnp.sum(jnp.where(hits, logits, 0.0), axis=0)
    stats = jnp.stack([top_local, sum_local, target_local], 0)
    stats = spread(stats, "vocab", vocab_count)
    top_value = jnp.maximum(prior_rows, jnp.max(stats[:, 0], axis=0))
    sum_total = jnp.sum(stats[:, 1] * jnp.exp(stats[:, 0] - top_value[None, :]), axis=0)
    target_sum = jnp.sum(stats[:, 2], axis=0)
    log_total = top_value + jnp.log(jnp.exp(prior_rows - top_value) + sum_total)
    target_logit = jnp.where(tgt_rows >= block_total, target_sum, outside)
    loss_rows = mask_rows * (log_total - target_logit)
    grad_scale = loss_scale / token_count
    dlogits = (
        mask_rows[None, :]
        * (jnp.exp(logits - log_total[None, :]) - hits.astype(f32))
        * grad_scale
    ).astype(bf16)
    mate_dlogits = lax.ppermute(dlogits, "core", SWAP)

    both = jnp.concatenate([dlogits, mate_dlogits], 1)
    partial_rows = jnp.dot(both, tokens, preferred_element_type=f32).astype(bf16)
    by_y = exchange(partial_rows.reshape(NY, y_rows, half), "y")
    by_y = jnp.sum(by_y.astype(f32), axis=0).astype(bf16)
    by_z = exchange(by_y.reshape(NZ, chip_rows, half), "z")
    chip_grad = jnp.sum(by_z.astype(f32), axis=0)
    square = jnp.sum(chip_grad * chip_grad)
    squares = spread(jnp.full((1, 128), square), ALL, ctx_count * vocab_count)
    square_sum = jnp.sum(squares) / 128.0
    near = lax.dynamic_slice_in_dim(chip_grad, core * shard_rows, shard_rows, 0)
    far = lax.dynamic_slice_in_dim(chip_grad, (1 - core) * shard_rows, shard_rows, 0)
    mate = lax.ppermute(far, "core", SWAP)
    row_grad = jnp.where(
        core == 0, jnp.concatenate([near, mate], 1), jnp.concatenate([mate, near], 1)
    )

    mate_head = lax.ppermute(head, "core", SWAP)
    low = jnp.where(core == 0, head, mate_head)
    high = jnp.where(core == 0, mate_head, head)
    width = feat // vocab_count
    parts = []
    for q in range(vocab_count):
        side = low if q < vocab_count // 2 else high
        at = (q % (vocab_count // 2)) * width
        parts.append(
            lax.dot_general(
                dlogits,
                side[:, at : at + width],
                (((0,), (0,)), ((), ())),
                preferred_element_type=f32,
            ).astype(bf16)
        )
    hidden_parts = exchange(jnp.stack(parts, 0), "vocab")
    hidden_grad = jnp.sum(hidden_parts.astype(f32), axis=0).astype(bf16)

    losses = spread(loss_rows.reshape(2, span), CTX, ctx_count).reshape(2 * ctx_count, span)
    mean_loss = jnp.sum(losses) / token_count
    slot_ids = jnp.arange(span_order.shape[0], dtype=jnp.int32)
    natural = []
    for offset in (0, 1):
        slot = jnp.sum(jnp.where(span_order == 2 * ctx_place + offset, slot_ids, 0))
        natural.append(lax.dynamic_slice_in_dim(losses, slot, 1, 0).reshape(span))
    token_loss = jnp.concatenate(natural, 0)

    norm_value = jnp.sqrt(square_sum) / loss_scale
    clip_factor = jnp.minimum(1.0, clip_norm / (norm_value + 1e-06))
    clipped = row_grad * clip_factor
    new_moment = beta_one * moment + (1.0 - beta_one) * clipped
    new_second = beta_two * second + (1.0 - beta_two) * clipped * clipped
    new_master = master - learn_rate * (
        new_moment / (jnp.sqrt(new_second) + adam_eps) + weight_decay * master
    )
    return (token_loss, mean_loss, hidden_grad, new_master, new_moment, new_second)


def solution(mesh):
    grid = Mesh(mesh.devices.reshape(NY, NZ, NC, mesh.devices.shape[1]), ALL)
    head_spec = P(("vocab",) + CTX, None)
    in_specs = (
        P(CTX, None),
        head_spec,
        head_spec,
        head_spec,
        P(CTX),
        P(CTX),
        P(CTX),
        P(CTX),
        P(),
    )
    out_specs = (P(CTX), P(), P(CTX, "vocab"), head_spec, head_spec, head_spec)
    return jax.shard_map(body, mesh=grid, in_specs=in_specs, out_specs=out_specs, check_vma=False)
```

time: 518 us -> 252 us (0.49)
  blocking collectives: 314 us -> 0 us
  starting transfers between devices: 0.12 us -> 54.2 us
  other arithmetic: 7.74 us -> 19.4 us
  waiting for transfers between devices: 148 us -> 141 us
  between operations: 21 us -> 14 us
  matrix products: 16.9 us -> 10.9 us
    all_gather x5 -> x0, blocking collectives: 221 us -> none  [the longest x1 48.5 us: body(): lax.all_gather(loss_mask, 'ctx', axis=0, tiled=True)]
    unnamed x4 -> x0, waiting for transfers between devices: 148 us -> none
    all_to_all x0 -> x9, waiting for transfers between devices: none -> 140 us  [exchange(): return lax.all_to_all(x, axes, 0, 0, tiled=True)]
    psum x2 -> x0, blocking collectives: 85 us -> none  [the longest x1 79 us: body(): square_sum = lax.psum(jnp.sum(row_grad * row_grad), ('ctx', 'vocab'))]
    all_to_all x0 -> x9, starting transfers between devices: none -> 48.7 us  [exchange(): return lax.all_to_all(x, axes, 0, 0, tiled=True)]
    pmax x1 -> x0, blocking collectives: 8.46 us -> none  [body(): top_value = lax.pmax(top_local, 'vocab')]
    unnamed x12 -> x18, local copies, waits for them, and re-layouts: 8.13 us -> 0.04 us
    reduce_sum x5 -> x10, other arithmetic: 3.7 us -> 11.5 us  [the longest x1 4.25 us: body(): hidden_grad = jnp.sum(hidden_parts.astype(f32), axis=0).astype(bf16)]
  transfers between devices with their start and end apart: 3 -> 14, of which waited for: 1 -> 11; matrix products, arithmetic and copies ran while one was open for 3% -> 12% of each run, Pallas kernels for 0% -> 0%
where the time goes in v1:
time: 252 us; the launch traced here: 251 us
  waiting for transfers between devices  141 us (56%)
  starting transfers between devices  54.2 us (22%)
  other arithmetic  19.4 us (8%)
  between operations  14 us (6%)
  local copies, waits for them, and re-layouts  11.6 us (5%)
  matrix products  10.9 us (4%)
    all_to_all x9, waiting for transfers between devices, exchange(): return lax.all_to_all(x, axes, 0, 0, tiled=True)  140 us
    all_to_all x9, starting transfers between devices, exchange(): return lax.all_to_all(x, axes, 0, 0, tiled=True)  48.7 us
  transfers between devices with their start and end apart: 14, of which 11 were waited for; matrix products, arithmetic and copies ran while one was open for 12% of the time, Pallas kernels for 0%

profile of v1, /device:TPU:1, one launch (start us, length us, event | category | flops | bytes accessed | tf_op | source)
XLA Modules:
  0.0 250.9 jit_solution(12622020149604917850)
XLA Ops:
  2.7 10.0 %all-to-all-start.1 = ((bf16[16,4,4096]{2,1,0:T(4,128)(2,1)}), bf16[16,4,4096]{2,1,0:T(4,128)(2,1)S(1)}, u32[]{:S(2)}, u32[]{:S(2)}) async-start(bf16[16,4,4096]{2,1,0:T(4,128)(2,1)} %bitcast.12), calls=%async_computation.1 | async-start | bytes 1048576 | tf_op jit(solution)/shard_map/all_to_all | solution.py:23
  12.7 4.7 %constant_dynamic-slice_fusion.4 = (bf16[256,4096]{1,0:T(8,128)(2,1)}, bf16[256,4096]{1,0:T(8,128)(2,1)}) fusion(bf16[256,8192]{1,0:T(8,128)(2,1)} %param.9, s32[]{:T(128)S(6)} %select_n.104, s32[]{:T(128)S(6)} %select_n.103), kind=kLoop, calls=%fused_computation.56 | loop fusion | bytes 8388616 | tf_op jit(solution)/shard_map/dynamic_slice | solution.py:53
  17.5 12.3 %all-to-all-done.1 = bf16[16,4,4096]{2,1,0:T(4,128)(2,1)S(1)} async-done(((bf16[16,4,4096]{2,1,0:T(4,128)(2,1)}), bf16[16,4,4096]{2,1,0:T(4,128)(2,1)S(1)}, u32[]{:S(2)}, u32[]{:S(2)}) %all-to-all-start.1) | async-done | bytes 524320 | tf_op jit(solution)/shard_map/all_to_all | solution.py:23
  30.6 6.2 %all-to-all-start = ((f32[64,8,128]{2,1,0:T(8,128)}), f32[64,8,128]{2,1,0:T(8,128)S(1)}, u32[]{:S(2)}, u32[]{:S(2)}) async-start(f32[64,8,128]{2,1,0:T(8,128)} %broadcast_in_dim.20), calls=%async_computation | async-start | bytes 524288 | tf_op jit(solution)/shard_map/all_to_all | solution.py:23
  36.9 11.8 %all-to-all-done = f32[64,8,128]{2,1,0:T(8,128)S(1)} async-done(((f32[64,8,128]{2,1,0:T(8,128)}), f32[64,8,128]{2,1,0:T(8,128)S(1)}, u32[]{:S(2)}, u32[]{:S(2)}) %all-to-all-start) | async-done | bytes 262176 | tf_op jit(solution)/shard_map/all_to_all | solution.py:23
  48.7 1.6 broadcast_in_dim.23
  50.3 3.9 %all-to-all-start.2 = ((bf16[4,64,4096]{2,1,0:T(8,128)(2,1)}), bf16[4,64,4096]{2,1,0:T(8,128)(2,1)S(1)}, u32[]{:S(2)}, u32[]{:S(2)}) async-start(bf16[4,64,4096]{2,1,0:T(8,128)(2,1)} %broadcast_in_dim.23), calls=%async_computation.2 | async-start | bytes 4194304 | tf_op jit(solution)/shard_map/all_to_all | solution.py:23
  60.2 19.8 %all-to-all-done.2 = bf16[4,64,4096]{2,1,0:T(8,128)(2,1)S(1)} async-done(((bf16[4,64,4096]{2,1,0:T(8,128)(2,1)}), bf16[4,64,4096]{2,1,0:T(8,128)(2,1)S(1)}, u32[]{:S(2)}, u32[]{:S(2)}) %all-to-all-start.2) | async-done | bytes 2097184 | tf_op jit(solution)/shard_map/all_to_all | solution.py:23
  80.0 2.5 convolution_bitcast_fusion
  82.5 1.6 collective-permute-start.1
  86.1 4.0 %all-to-all-start.3 = ((f32[4,3,256]{2,1,0:T(4,128)}), f32[4,3,256]{2,1,0:T(4,128)S(1)}, u32[]{:S(2)}, u32[]{:S(2)}) async-start(f32[4,3,256]{2,1,0:T(4,128)} %broadcast_in_dim.48), calls=%async_computation.3 | async-start | bytes 32768 | tf_op jit(solution)/shard_map/all_to_all | solution.py:23
  92.1 2.2 all-to-all-done.3
  94.5 1.9 collective-permute-start.3
  97.4 4.8 %convolution_convert_fusion = bf16[256,4096]{1,0:T(8,128)(2,1)} fusion(bf16[256,4096]{1,0:T(8,128)(2,1)} %collective-permute-done, bf16[256,4096]{1,0:T(8,128)(2,1)} %get-tuple-element.24, bf16[256,256]{1,0:T(8,128)(2,1)S(1)} %collective-permute-done.3, bf16[256,256]{1,0:T(8,128)(2,1)S(1)} %multiply_convert_fusion), kind=kOutput, calls=%fused_computation | convolution fusion | flops 1083703296 | bytes 6553600 | tf_op jit(solution)/shard_map/dot_general | solution.py:106
  102.2 4.4 %all-to-all-start.6 = ((bf16[4,64,4096]{2,1,0:T(8,128)(2,1)}), bf16[4,64,4096]{2,1,0:T(8,128)(2,1)}, u32[]{:S(2)}, u32[]{:S(2)}) async-start(bf16[4,64,4096]{2,1,0:T(8,128)(2,1)} %bitcast.91), calls=%async_computation.6 | async-start | bytes 4194304 | tf_op jit(solution)/shard_map/all_to_all | solution.py:23
  106.7 26.1 %all-to-all-done.6 = bf16[4,64,4096]{2,1,0:T(8,128)(2,1)} async-done(((bf16[4,64,4096]{2,1,0:T(8,128)(2,1)}), bf16[4,64,4096]{2,1,0:T(8,128)(2,1)}, u32[]{:S(2)}, u32[]{:S(2)}) %all-to-all-start.6) | async-done | bytes 2097184 | tf_op jit(solution)/shard_map/all_to_all | solution.py:23
  132.8 2.9 %reduce_sum.141 = bf16[64,4096]{1,0:T(8,128)(2,1)} reduce(bf16[4,64,4096]{2,1,0:T(8,128)(2,1)} %all-to-all-done.6, bf16[]{:T(256)} %constant.93.clone.1), dimensions={0}, to_apply=%region_11.12 | reduce | flops 786432 | bytes 2621442 | tf_op jit(solution)/shard_map/reduce_sum | solution.py:108
  135.7 4.1 %all-to-all-start.7 = ((bf16[8,8,4096]{2,1,0:T(8,128)(2,1)}), bf16[8,8,4096]{2,1,0:T(8,128)(2,1)}, u32[]{:S(2)}, u32[]{:S(2)}) async-start(bf16[8,8,4096]{2,1,0:T(8,128)(2,1)} %bitcast.38), calls=%async_computation.7 | async-start | bytes 1048576 | tf_op jit(solution)/shard_map/all_to_all | solution.py:23
  139.8 1.9 broadcast_select_fusion.1
  143.1 1.4 fusion.6
  144.5 12.3 %all-to-all-done.7 = bf16[8,8,4096]{2,1,0:T(8,128)(2,1)} async-done(((bf16[8,8,4096]{2,1,0:T(8,128)(2,1)}), bf16[8,8,4096]{2,1,0:T(8,128)(2,1)}, u32[]{:S(2)}, u32[]{:S(2)}) %all-to-all-start.7) | async-done | bytes 524320 | tf_op jit(solution)/shard_map/all_to_all | solution.py:23
  157.5 5.4 %all-to-all-start.4 = ((f32[64,2,128]{2,1,0:T(2,128)}), f32[64,2,128]{2,1,0:T(2,128)S(1)}, u32[]{:S(2)}, u32[]{:S(2)}) async-start(f32[64,2,128]{2,1,0:T(2,128)} %broadcast_in_dim.49), calls=%async_computation.4 | async-start | bytes 131072 | tf_op jit(solution)/shard_map/all_to_all | solution.py:23
  162.9 1.1 convert_reduce_fusion
  164.7 8.1 %all-to-all-done.4 = f32[64,2,128]{2,1,0:T(2,128)S(1)} async-done(((f32[64,2,128]{2,1,0:T(2,128)}), f32[64,2,128]{2,1,0:T(2,128)S(1)}, u32[]{:S(2)}, u32[]{:S(2)}) %all-to-all-start.4) | async-done | bytes 65568 | tf_op jit(solution)/shard_map/all_to_all | solution.py:23
  172.8 1.4 broadcast_in_dim_broadcast_in_dim_broadcast_in_dim.3
  174.2 5.8 %all-to-all-start.8 = ((f32[256,1,128]{2,1,0:T(1,128)}), f32[256,1,128]{2,1,0:T(1,128)S(1)}, u32[]{:S(2)}, u32[]{:S(2)}) async-start(f32[256,1,128]{2,1,0:T(1,128)} %broadcast_in_dim_broadcast_in_dim_broadcast_in_dim.3), calls=%async_computation.8 | async-start | bytes 262144 | tf_op jit(solution)/shard_map/all_to_all | solution.py:23
  180.0 3.3 %pad_maximum_fusion = bf16[4,256,2048]{2,1,0:T(8,128)(2,1)} fusion(bf16[1,256,2048]{2,1,0:T(8,128)(2,1)} %fusion.6, bf16[1,256,2048]{2,1,0:T(8,128)(2,1)S(1)} %fusion.5, bf16[1,256,2048]{2,1,0:T(8,128)(2,1)S(1)} %fusion.4, bf16[1,256,2048]{2,1,0:T(8,128)(2,1)S(1)} %fusion.3), kind=kLoop, calls=%fused_computation.1 | loop fusion | flops 6291456 | bytes 8388608 | tf_op jit(solution)/shard_map/stack | solution.py:137
  183.3 9.4 %all-to-all-done.8 = f32[256,1,128]{2,1,0:T(1,128)S(1)} async-done(((f32[256,1,128]{2,1,0:T(1,128)}), f32[256,1,128]{2,1,0:T(1,128)S(1)}, u32[]{:S(2)}, u32[]{:S(2)}) %all-to-all-start.8) | async-done | bytes 131104 | tf_op jit(solution)/shard_map/all_to_all | solution.py:23
  192.7 4.9 %all-to-all-start.5 = ((bf16[4,256,2048]{2,1,0:T(8,128)(2,1)}), bf16[4,256,2048]{2,1,0:T(8,128)(2,1)}, u32[]{:S(2)}, u32[]{:S(2)}) async-start(bf16[4,256,2048]{2,1,0:T(8,128)(2,1)} %pad_maximum_fusion), calls=%async_computation.5 | async-start | bytes 8388608 | tf_op jit(solution)/shard_map/all_to_all | solution.py:23
  204.1 1.1 collective-permute-start.4
  208.1 37.4 %all-to-all-done.5 = bf16[4,256,2048]{2,1,0:T(8,128)(2,1)} async-done(((bf16[4,256,2048]{2,1,0:T(8,128)(2,1)}), bf16[4,256,2048]{2,1,0:T(8,128)(2,1)}, u32[]{:S(2)}, u32[]{:S(2)}) %all-to-all-start.5) | async-done | bytes 4194336 | tf_op jit(solution)/shard_map/all_to_all | solution.py:23
  245.5 4.2 %reduce_sum.140 = bf16[256,2048]{1,0:T(8,128)(2,1)} reduce(bf16[4,256,2048]{2,1,0:T(8,128)(2,1)} %all-to-all-done.5, bf16[]{:T(256)} %constant.93.clone.1), dimensions={0}, to_apply=%region_10.11 | reduce | flops 1572864 | bytes 5242882 | tf_op jit(solution)/shard_map/reduce_sum | solution.py:138
  (62 shorter events, 14.3 us)
Async XLA Ops:
  2.7 27.2 %all-to-all-start.1 = ((bf16[16,4,4096]{2,1,0:T(4,128)(2,1)}), bf16[16,4,4096]{2,1,0:T(4,128)(2,1)S(1)}, u32[]{:S(2)}, u32[]{:S(2)}) async-start(bf16[16,4,4096]{2,1,0:T(4,128)(2,1)} %bitcast.12), calls=%async_computation.1 | async-start | bytes 1048576 | tf_op jit(solution)/shard_map/all_to_all | solution.py:23
  12.7 4.8 %copy-start.5 = (s32[256]{0:T(256)S(1)}, s32[256]{0:T(256)}, u32[]{:S(2)}) copy-start(s32[256]{0:T(256)} %param.14) | copy-start | bytes 3076
  12.7 4.8 %copy-start.6 = (s32[256]{0:T(256)S(1)}, s32[256]{0:T(256)}, u32[]{:S(2)}) copy-start(s32[256]{0:T(256)} %param.13) | copy-start | bytes 3076
  12.7 4.8 %copy-start.7 = (f32[256]{0:T(256)S(1)}, f32[256]{0:T(256)}, u32[]{:S(2)}) copy-start(f32[256]{0:T(256)} %param.16) | copy-start | bytes 3076
  12.7 4.8 %copy-start.8 = (f32[256]{0:T(256)S(1)}, f32[256]{0:T(256)}, u32[]{:S(2)}) copy-start(f32[256]{0:T(256)} %param.15) | copy-start | bytes 3076
  17.4 42.8 %collective-permute-start = (bf16[256,4096]{1,0:T(8,128)(2,1)}, bf16[256,4096]{1,0:T(8,128)(2,1)}, u32[]{:S(2)}, u32[]{:S(2)}) collective-permute-start(bf16[256,4096]{1,0:T(8,128)(2,1)} %get-tuple-element.23), channel_id=1, source_target_pairs={{0,4},{4,0},{1,5},{5,1},{2,6},{6,2},{3,7},{7,3},{8,12},{12,8},{9,1... | collective-permute-start | bytes 6291464 | tf_op jit(solution)/shard_map/ppermute | solution.py:54
  30.6 18.1 %all-to-all-start = ((f32[64,8,128]{2,1,0:T(8,128)}), f32[64,8,128]{2,1,0:T(8,128)S(1)}, u32[]{:S(2)}, u32[]{:S(2)}) async-start(f32[64,8,128]{2,1,0:T(8,128)} %broadcast_in_dim.20), calls=%async_computation | async-start | bytes 524288 | tf_op jit(solution)/shard_map/all_to_all | solution.py:23
  50.3 3.9 %copy-start.4 = (s32[128]{0:T(128)S(1)}, s32[128]{0:T(128)}, u32[]{:S(2)}) copy-start(s32[128]{0:T(128)} %param.17) | copy-start | bytes 1540
  50.3 29.7 %all-to-all-start.2 = ((bf16[4,64,4096]{2,1,0:T(8,128)(2,1)}), bf16[4,64,4096]{2,1,0:T(8,128)(2,1)S(1)}, u32[]{:S(2)}, u32[]{:S(2)}) async-start(bf16[4,64,4096]{2,1,0:T(8,128)(2,1)} %broadcast_in_dim.23), calls=%async_computation.2 | async-start | bytes 4194304 | tf_op jit(solution)/shard_map/all_to_all | solution.py:23
  80.0 4.1 %copy-start = (bf16[256,4096]{1,0:T(8,128)(2,1)S(1)}, bf16[256,4096]{1,0:T(8,128)(2,1)}, u32[]{:S(2)}) copy-start(bf16[256,4096]{1,0:T(8,128)(2,1)} %get-tuple-element.24) | copy-start | bytes 6291460
  82.5 2.8 %collective-permute-start.1 = (f32[256,256]{1,0:T(8,128)S(1)}, f32[256,256]{1,0:T(8,128)S(1)}, u32[]{:S(2)}, u32[]{:S(2)}) collective-permute-start(f32[256,256]{1,0:T(8,128)S(1)} %convolution_bitcast_fusion), channel_id=1, source_target_pairs={{0,4},{4,0},{1,5},{5,1},{2,6},{6,2},{3,7},{7,3},{8,12},{12,8},{9,1... | collective-permute-start | bytes 786440 | tf_op jit(solution)/shard_map/ppermute | solution.py:80
  86.1 8.2 %all-to-all-start.3 = ((f32[4,3,256]{2,1,0:T(4,128)}), f32[4,3,256]{2,1,0:T(4,128)S(1)}, u32[]{:S(2)}, u32[]{:S(2)}) async-start(f32[4,3,256]{2,1,0:T(4,128)} %broadcast_in_dim.48), calls=%async_computation.3 | async-start | bytes 32768 | tf_op jit(solution)/shard_map/all_to_all | solution.py:23
  91.4 48.4 %collective-permute-start.2 = (bf16[256,4096]{1,0:T(8,128)(2,1)S(1)}, bf16[256,4096]{1,0:T(8,128)(2,1)}, u32[]{:S(2)}, u32[]{:S(2)}) collective-permute-start(bf16[256,4096]{1,0:T(8,128)(2,1)S(1)} %bitcast.90), channel_id=1, source_target_pairs={{0,4},{4,0},{1,5},{5,1},{2,6},{6,2},{3,7},{7,3},{8,12},{12,8},{9,1... | collective-permute-start | bytes 6291464 | tf_op jit(solution)/shard_map/ppermute | solution.py:121
  94.5 2.9 %collective-permute-start.3 = (bf16[256,256]{1,0:T(8,128)(2,1)S(1)}, bf16[256,256]{1,0:T(8,128)(2,1)S(1)}, u32[]{:S(2)}, u32[]{:S(2)}) collective-permute-start(bf16[256,256]{1,0:T(8,128)(2,1)S(1)} %multiply_convert_fusion), channel_id=1, source_target_pairs={{0,4},{4,0},{1,5},{5,1},{2,6},{6,2},{3,7},{7,3},{8,12},{12,8},{9,1... | collective-permute-start | bytes 393224 | tf_op jit(solution)/shard_map/ppermute | solution.py:103
  102.2 30.6 %all-to-all-start.6 = ((bf16[4,64,4096]{2,1,0:T(8,128)(2,1)}), bf16[4,64,4096]{2,1,0:T(8,128)(2,1)}, u32[]{:S(2)}, u32[]{:S(2)}) async-start(bf16[4,64,4096]{2,1,0:T(8,128)(2,1)} %bitcast.91), calls=%async_computation.6 | async-start | bytes 4194304 | tf_op jit(solution)/shard_map/all_to_all | solution.py:23
  135.7 21.2 %all-to-all-start.7 = ((bf16[8,8,4096]{2,1,0:T(8,128)(2,1)}), bf16[8,8,4096]{2,1,0:T(8,128)(2,1)}, u32[]{:S(2)}, u32[]{:S(2)}) async-start(bf16[8,8,4096]{2,1,0:T(8,128)(2,1)} %bitcast.38), calls=%async_computation.7 | async-start | bytes 1048576 | tf_op jit(solution)/shard_map/all_to_all | solution.py:23
  157.5 15.3 %all-to-all-start.4 = ((f32[64,2,128]{2,1,0:T(2,128)}), f32[64,2,128]{2,1,0:T(2,128)S(1)}, u32[]{:S(2)}, u32[]{:S(2)}) async-start(f32[64,2,128]{2,1,0:T(2,128)} %broadcast_in_dim.49), calls=%async_computation.4 | async-start | bytes 131072 | tf_op jit(solution)/shard_map/all_to_all | solution.py:23
  174.2 18.5 %all-to-all-start.8 = ((f32[256,1,128]{2,1,0:T(1,128)}), f32[256,1,128]{2,1,0:T(1,128)S(1)}, u32[]{:S(2)}, u32[]{:S(2)}) async-start(f32[256,1,128]{2,1,0:T(1,128)} %broadcast_in_dim_broadcast_in_dim_broadcast_in_dim.3), calls=%async_computation.8 | async-start | bytes 262144 | tf_op jit(solution)/shard_map/all_to_all | solution.py:23
  183.3 23.9 %copy-start.1 = (f32[4,8192]{1,0:T(4,128)S(1)}, f32[4,8192]{1,0:T(4,128)}, u32[]{:S(2)}) copy-start(f32[4,8192]{1,0:T(4,128)} %param.10) | copy-start | bytes 393220
  183.3 23.9 %copy-start.2 = (f32[4,8192]{1,0:T(4,128)S(1)}, f32[4,8192]{1,0:T(4,128)}, u32[]{:S(2)}) copy-start(f32[4,8192]{1,0:T(4,128)} %param.12) | copy-start | bytes 393220
  183.3 23.9 %copy-start.3 = (f32[4,8192]{1,0:T(4,128)S(1)}, f32[4,8192]{1,0:T(4,128)}, u32[]{:S(2)}) copy-start(f32[4,8192]{1,0:T(4,128)} %param.11) | copy-start | bytes 393220
  192.7 52.8 %all-to-all-start.5 = ((bf16[4,256,2048]{2,1,0:T(8,128)(2,1)}), bf16[4,256,2048]{2,1,0:T(8,128)(2,1)}, u32[]{:S(2)}, u32[]{:S(2)}) async-start(bf16[4,256,2048]{2,1,0:T(8,128)(2,1)} %pad_maximum_fusion), calls=%async_computation.5 | async-start | bytes 8388608 | tf_op jit(solution)/shard_map/all_to_all | solution.py:23
  204.1 3.0 %collective-permute-start.4 = (f32[4,4096]{1,0:T(4,128)S(1)}, f32[4,4096]{1,0:T(4,128)S(1)}, u32[]{:S(2)}, u32[]{:S(2)}) collective-permute-start(f32[4,4096]{1,0:T(4,128)S(1)} %get-tuple-element.27), channel_id=1, source_target_pairs={{0,4},{4,0},{1,5},{5,1},{2,6},{6,2},{3,7},{7,3},{8,12},{12,8},{9,1... | collective-permute-start | bytes 196616 | tf_op jit(solution)/shard_map/ppermute | solution.py:116

commit v2 on v1

--- a/solution.py
+++ b/solution.py
@@ -23,6 +23,10 @@
     return lax.all_to_all(x, axes, 0, 0, tiled=True)
 
 
+def shift(x, axis, count, step):
+    return lax.ppermute(x, axis, [(i, (i + step) % count) for i in range(count)])
+
+
 def spread(x, axes, count):
     return exchange(jnp.broadcast_to(x[None], (count,) + x.shape), axes)
 
@@ -35,8 +39,9 @@
     vocab_count = lax.axis_size("vocab")
     ctx_count = NY * NZ * NC
     core = lax.axis_index("core")
+    y_place = lax.axis_index("y")
     vocab_place = lax.axis_index("vocab")
-    ctx_place = (lax.axis_index("y") * NZ + lax.axis_index("z")) * NC + core
+    ctx_place = (y_place * NZ + lax.axis_index("z")) * NC + core
     span = tok_rows // 2
     half = feat // 2
     group_rows = shard_rows * ctx_count
@@ -47,7 +52,7 @@
     cut = master.astype(bf16).reshape(shard_rows, NC, half).transpose(1, 0, 2)
     cut = jnp.broadcast_to(cut[None], (NZ,) + cut.shape).reshape(NZ * NC, shard_rows, half)
     block = exchange(cut, ("z", "core")).reshape(y_rows, half)
-    head = spread(block, "y", NY).reshape(group_rows, half)
+    head = jnp.concatenate([block] + [shift(block, "y", NY, s) for s in range(1, NY)], 0)
 
     own_half = lax.dynamic_slice_in_dim(hidden_states, core * half, half, 1)
     far_half = lax.dynamic_slice_in_dim(hidden_states, (1 - core) * half, half, 1)
@@ -82,12 +87,21 @@
 
     local_col = tgt_rows - block_total - vocab_place * group_rows
     vocab_ids = lax.broadcasted_iota(jnp.int32, (group_rows, tok_rows), 0)
+    vocab_ids = (y_place * y_rows - vocab_ids // y_rows * y_rows) % group_rows + vocab_ids % y_rows
     hits = vocab_ids == local_col[None, :]
     top_local = jnp.max(logits, axis=0)
     sum_local = jnp.sum(jnp.exp(logits - top_local[None, :]), axis=0)
     target_local = jnp.sum(jnp.where(hits, logits, 0.0), axis=0)
     stats = jnp.stack([top_local, sum_local, target_local], 0)
-    stats = spread(stats, "vocab", vocab_count)
+    heard = [stats] + [shift(stats, "vocab", vocab_count, s) for s in range(1, vocab_count)]
+    ordered = []
+    for j in range(vocab_count):
+        back = (vocab_place - j) % vocab_count
+        pick = heard[0]
+        for s in range(1, vocab_count):
+            pick = jnp.where(back == s, heard[s], pick)
+        ordered.append(pick)
+    stats = jnp.stack(ordered, 0)
     top_value = jnp.maximum(prior_rows, jnp.max(stats[:, 0], axis=0))
     sum_total = jnp.sum(stats[:, 1] * jnp.exp(stats[:, 0] - top_value[None, :]), axis=0)
     target_sum = jnp.sum(stats[:, 2], axis=0)
@@ -104,8 +118,11 @@
 
     both = jnp.concatenate([dlogits, mate_dlogits], 1)
     partial_rows = jnp.dot(both, tokens, preferred_element_type=f32).astype(bf16)
-    by_y = exchange(partial_rows.reshape(NY, y_rows, half), "y")
-    by_y = jnp.sum(by_y.astype(f32), axis=0).astype(bf16)
+    blocks = [partial_rows[s * y_rows : (s + 1) * y_rows] for s in range(NY)]
+    by_y = blocks[0].astype(f32)
+    for s in range(1, NY):
+        by_y = by_y + shift(blocks[s], "y", NY, -s).astype(f32)
+    by_y = by_y.astype(bf16)
     by_z = exchange(by_y.reshape(NZ, chip_rows, half), "z")
     chip_grad = jnp.sum(by_z.astype(f32), axis=0)
     square = jnp.sum(chip_grad * chip_grad)
@@ -119,23 +136,24 @@
     )
 
     mate_head = lax.ppermute(head, "core", SWAP)
-    low = jnp.where(core == 0, head, mate_head)
-    high = jnp.where(core == 0, mate_head, head)
     width = feat // vocab_count
-    parts = []
-    for q in range(vocab_count):
-        side = low if q < vocab_count // 2 else high
-        at = (q % (vocab_count // 2)) * width
-        parts.append(
-            lax.dot_general(
-                dlogits,
-                side[:, at : at + width],
-                (((0,), (0,)), ((), ())),
-                preferred_element_type=f32,
-            ).astype(bf16)
+    per_half = vocab_count // NC
+    hidden_sum = jnp.zeros((tok_rows, width), f32)
+    for s in range(vocab_count - 1, -1, -1):
+        q = (vocab_place + s) % vocab_count
+        at = (q % per_half) * width
+        side = jnp.where(
+            q // per_half == core,
+            lax.dynamic_slice_in_dim(head, at, width, 1),
+            lax.dynamic_slice_in_dim(mate_head, at, width, 1),
         )
-    hidden_parts = exchange(jnp.stack(parts, 0), "vocab")
-    hidden_grad = jnp.sum(hidden_parts.astype(f32), axis=0).astype(bf16)
+        part = lax.dot_general(
+            dlogits, side, (((0,), (0,)), ((), ())), preferred_element_type=f32
+        ).astype(bf16)
+        if s:
+            part = shift(part, "vocab", vocab_count, s)
+        hidden_sum = hidden_sum + part.astype(f32)
+    hidden_grad = hidden_sum.astype(bf16)
 
     losses = spread(loss_rows.reshape(2, span), CTX, ctx_count).reshape(2 * ctx_count, span)
     mean_loss = jnp.sum(losses) / token_count

time: 252 us -> 201 us (0.80)
  waiting for transfers between devices: 141 us -> 85.5 us
  other arithmetic: 19.4 us -> 9.85 us
  matrix products: 10.9 us -> 19.1 us
  starting transfers between devices: 54.2 us -> 59 us
    all_to_all x9 -> x5, waiting for transfers between devices: 140 us -> 43.3 us  [exchange(): return lax.all_to_all(x, axes, 0, 0, tiled=True)]
    ppermute x0 -> x12, waiting for transfers between devices: none -> 41.5 us  [shift(): lax.ppermute(x, axis, [(i, (i + step) % count) for i in range(count)])]
    ppermute x0 -> x12, starting transfers between devices: none -> 12.9 us  [shift(): lax.ppermute(x, axis, [(i, (i + step) % count) for i in range(count)])]
    all_to_all x9 -> x5, starting transfers between devices: 48.7 us -> 40.4 us  [exchange(): return lax.all_to_all(x, axes, 0, 0, tiled=True)]
    dot_general x4, matrix products: 2.81 us -> 10.9 us  [body(): lax.dot_general(dlogits, side, (((0,), (0,)), ((), ())), preferred_elemen...]
    reduce_sum x2 -> x0, other arithmetic: 7.11 us -> none  [the longest x1 4.25 us: body(): hidden_grad = jnp.sum(hidden_parts.astype(f32), axis=0).astype(bf16)]
    another operation x1 -> x3, other arithmetic: 3.27 us -> 0.04 us  [body(): stats = jnp.stack(ordered, 0)]
  transfers between devices with their start and end apart: 14 -> 22, of which waited for: 11 -> 11; matrix products, arithmetic and copies ran while one was open for 12% -> 16% of each run, Pallas kernels for 0% -> 0%
where the time goes in v2:
time: 201 us; the launch traced here: 200 us
  waiting for transfers between devices  85.5 us (43%)
  starting transfers between devices  59 us (29%)
  matrix products  19.1 us (10%)
  between operations  14.3 us (7%)
  local copies, waits for them, and re-layouts  12.8 us (6%)
  other arithmetic  9.85 us (5%)
    all_to_all x5, waiting for transfers between devices, exchange(): return lax.all_to_all(x, axes, 0, 0, tiled=True)  43.3 us
    ppermute x12, waiting for transfers between devices, shift(): lax.ppermute(x, axis, [(i, (i + step) % count) for i in range(count)])  41.5 us
    all_to_all x5, starting transfers between devices, exchange(): return lax.all_to_all(x, axes, 0, 0, tiled=True)  40.4 us
    ppermute x12, starting transfers between devices, shift(): lax.ppermute(x, axis, [(i, (i + step) % count) for i in range(count)])  12.9 us
    dot_general x4, matrix products, body(): lax.dot_general(dlogits, side, (((0,), (0,)), ((), ())), preferred_elemen...  10.9 us
    dynamic_slice x1, local copies, waits for them, and re-layouts, body(): own_half = lax.dynamic_slice_in_dim(hidden_states, core * half, half, 1)  4.69 us
    dot_general x2, matrix products, score(): lax.dot_general(head, tok, (((1,), (1,)), ((), ())), preferred_element_ty...  4.68 us
  transfers between devices with their start and end apart: 22, of which 11 were waited for; matrix products, arithmetic and copies ran while one was open for 16% of the time, Pallas kernels for 0%

profile of v2, /device:TPU:1, one launch (start us, length us, event | category | flops | bytes accessed | tf_op | source)
XLA Modules:
  0.0 200.4 jit_solution(2820023122021508330)
XLA Ops:
  2.7 10.0 %all-to-all-start.1 = ((bf16[16,4,4096]{2,1,0:T(4,128)(2,1)}), bf16[16,4,4096]{2,1,0:T(4,128)(2,1)S(1)}, u32[]{:S(2)}, u32[]{:S(2)}) async-start(bf16[16,4,4096]{2,1,0:T(4,128)(2,1)} %bitcast.12), calls=%async_computation.1 | async-start | bytes 1048576 | tf_op jit(solution)/shard_map/all_to_all | solution.py:23
  12.7 4.7 %constant_dynamic-slice_fusion.5 = (bf16[256,4096]{1,0:T(8,128)(2,1)}, bf16[256,4096]{1,0:T(8,128)(2,1)}) fusion(bf16[256,8192]{1,0:T(8,128)(2,1)} %param.9, s32[]{:T(128)S(6)} %select_n.282, s32[]{:T(128)S(6)} %select_n.283), kind=kLoop, calls=%fused_computation.82 | loop fusion | bytes 8388616 | tf_op jit(solution)/shard_map/dynamic_slice | solution.py:57
  17.6 12.3 %all-to-all-done.1 = bf16[16,4,4096]{2,1,0:T(4,128)(2,1)S(1)} async-done(((bf16[16,4,4096]{2,1,0:T(4,128)(2,1)}), bf16[16,4,4096]{2,1,0:T(4,128)(2,1)S(1)}, u32[]{:S(2)}, u32[]{:S(2)}) %all-to-all-start.1) | async-done | bytes 524320 | tf_op jit(solution)/shard_map/all_to_all | solution.py:23
  30.6 6.2 %all-to-all-start = ((f32[64,8,128]{2,1,0:T(8,128)}), f32[64,8,128]{2,1,0:T(8,128)S(1)}, u32[]{:S(2)}, u32[]{:S(2)}) async-start(f32[64,8,128]{2,1,0:T(8,128)} %broadcast_in_dim.14), calls=%async_computation | async-start | bytes 524288 | tf_op jit(solution)/shard_map/all_to_all | solution.py:23
  36.9 1.4 collective-permute-start
  38.3 2.6 %collective-permute-start.1 = (bf16[64,4096]{1,0:T(8,128)(2,1)S(1)}, bf16[64,4096]{1,0:T(8,128)(2,1)S(1)}, u32[]{:S(2)}, u32[]{:S(2)}) collective-permute-start(bf16[64,4096]{1,0:T(8,128)(2,1)S(1)} %reshape.114), channel_id=1, source_target_pairs={{0,128},{64,192},{128,0},{192,64},{1,129},{65,193},{129,1},{193,65... | collective-permute-start | bytes 1572872 | tf_op jit(solution)/shard_map/ppermute | solution.py:27
  42.1 12.3 %collective-permute-done = bf16[64,4096]{1,0:T(8,128)(2,1)S(1)} collective-permute-done((bf16[64,4096]{1,0:T(8,128)(2,1)S(1)}, bf16[64,4096]{1,0:T(8,128)(2,1)S(1)}, u32[]{:S(2)}, u32[]{:S(2)}) %collective-permute-start) | collective-permute-done | bytes 524320 | tf_op jit(solution)/shard_map/ppermute | solution.py:27
  54.5 11.9 %collective-permute-done.1 = bf16[64,4096]{1,0:T(8,128)(2,1)S(1)} collective-permute-done((bf16[64,4096]{1,0:T(8,128)(2,1)S(1)}, bf16[64,4096]{1,0:T(8,128)(2,1)S(1)}, u32[]{:S(2)}, u32[]{:S(2)}) %collective-permute-start.1) | collective-permute-done | bytes 524320 | tf_op jit(solution)/shard_map/ppermute | solution.py:27
  66.4 2.3 %fusion.59 = f32[256,256]{1,0:T(8,128)S(1)} fusion(bf16[256,4096]{1,0:T(8,128)(2,1)S(1)} %constant_dynamic-update-slice_fusion, bf16[256,4096]{1,0:T(8,128)(2,1)} %collective-permute-done.3), kind=kOutput, calls=%fused_computation.122 | convolution fusion | flops 536870912 | bytes 4456448 | tf_op jit(solution)/shard_map/dot_general | solution.py:83
  68.8 1.3 collective-permute-start.4
  76.1 2.3 %fusion.58 = (f32[256]{0:T(256)S(1)}, f32[256,256]{1,0:T(8,128)S(1)}) fusion(f32[256,256]{1,0:T(8,128)S(1)} %collective-permute-done.4, bf16[256,4096]{1,0:T(8,128)(2,1)S(1)} %constant_dynamic-update-slice_fusion, bf16[256,4096]{1,0:T(8,128)(2,1)} %get-tuple-element.19), kind=kOutput, calls=%fused_computation.121 | convolution fusion | flops 537001728 | bytes 4719616 | tf_op jit(solution)/shard_map/dot_general | solution.py:83
  78.8 2.5 %collective-permute-start.5 = (f32[3,256]{1,0:T(4,128)S(1)}, f32[3,256]{1,0:T(4,128)S(1)}, u32[]{:S(2)}, u32[]{:S(2)}) collective-permute-start(f32[3,256]{1,0:T(4,128)S(1)} %pad_maximum_fusion.2), channel_id=1, source_target_pairs={{0,3},{1,0},{2,1},{3,2},{4,7},{5,4},{6,5},{7,6},{8,11},{9,8},{10,9... | collective-permute-start | bytes 9224 | tf_op jit(solution)/shard_map/ppermute | solution.py:27
  83.8 1.5 collective-permute-done.6
  86.0 1.8 collective-permute-start.12
  88.8 3.5 %convolution_convert_fusion = bf16[256,4096]{1,0:T(8,128)(2,1)S(1)} fusion(bf16[256,4096]{1,0:T(8,128)(2,1)} %collective-permute-done.3, bf16[256,4096]{1,0:T(8,128)(2,1)} %get-tuple-element.19, bf16[256,256]{1,0:T(8,128)(2,1)S(1)} %collective-permute-done.12, bf16[256,256]{1,0:T(8,128)(2,1)S(1)} %multiply_convert_fusion), kind=kOutput, calls=%fused_computation | convolution fusion | flops 1083703296 | bytes 6553600 | tf_op jit(solution)/shard_map/dot_general | solution.py:120
  92.3 1.3 copy-done
  94.8 1.5 collective-permute-start.13
  98.3 10.2 %all-to-all-start.2 = ((f32[64,2,128]{2,1,0:T(2,128)}), f32[64,2,128]{2,1,0:T(2,128)S(1)}, u32[]{:S(2)}, u32[]{:S(2)}) async-start(f32[64,2,128]{2,1,0:T(2,128)} %broadcast_in_dim.17), calls=%async_computation.2 | async-start | bytes 131072 | tf_op jit(solution)/shard_map/all_to_all | solution.py:23
  108.5 2.4 %collective-permute-done.14 = bf16[64,4096]{1,0:T(8,128)(2,1)S(1)} collective-permute-done((bf16[64,4096]{1,0:T(8,128)(2,1)}, bf16[64,4096]{1,0:T(8,128)(2,1)S(1)}, u32[]{:S(2)}, u32[]{:S(2)}) %collective-permute-start.14) | collective-permute-done | bytes 524320 | tf_op jit(solution)/shard_map/ppermute | solution.py:27
  110.9 12.9 %collective-permute-done.15 = bf16[64,4096]{1,0:T(8,128)(2,1)} collective-permute-done((bf16[64,4096]{1,0:T(8,128)(2,1)}, bf16[64,4096]{1,0:T(8,128)(2,1)}, u32[]{:S(2)}, u32[]{:S(2)}) %collective-permute-start.15) | collective-permute-done | bytes 524320 | tf_op jit(solution)/shard_map/ppermute | solution.py:27
  123.8 2.3 %fusion.22 = bf16[8,8,4096]{2,1,0:T(8,128)(2,1)} fusion(bf16[64,4096]{1,0:T(8,128)(2,1)} %collective-permute-done.15, bf16[64,4096]{1,0:T(8,128)(2,1)S(1)} %collective-permute-done.14, bf16[64,4096]{1,0:T(8,128)(2,1)S(1)} %collective-permute-done.13, bf16[256,4096]{1,0:T(8,128)(2,1)} %copy-done), kind=kLoop, calls=%fused_computation.29 | loop fusion | flops 2097152 | bytes 2621440 | tf_op jit(solution)/shard_map/reshape | solution.py:126
  126.1 5.8 %all-to-all-start.3 = ((bf16[8,8,4096]{2,1,0:T(8,128)(2,1)}), bf16[8,8,4096]{2,1,0:T(8,128)(2,1)S(1)}, u32[]{:S(2)}, u32[]{:S(2)}) async-start(bf16[8,8,4096]{2,1,0:T(8,128)(2,1)} %fusion.22), calls=%async_computation.3 | async-start | bytes 1048576 | tf_op jit(solution)/shard_map/all_to_all | solution.py:23
  139.2 2.7 %convolution_convert_fusion.4 = bf16[256,2048]{1,0:T(8,128)(2,1)} fusion(bf16[256,256]{1,0:T(8,128)(2,1)S(1)} %multiply_convert_fusion, bf16[256,4096]{1,0:T(8,128)(2,1)} %collective-permute-done.8, s32[]{:T(128)S(6)} %select_n.323, bf16[256,4096]{1,0:T(8,128)(2,1)S(1)} %constant_dynamic-update-slice_fusion, pred[]{:T(512)S(6)} %eq.110), kind=kOutput, calls=%fused_computation.7 | convolution fusion | flops 269484032 | bytes 3276805 | tf_op jit(solution)/shard_map/dot_general | solution.py:150
  141.9 2.7 %convolution_convert_fusion.3 = bf16[256,2048]{1,0:T(8,128)(2,1)} fusion(bf16[256,256]{1,0:T(8,128)(2,1)S(1)} %multiply_convert_fusion, bf16[256,4096]{1,0:T(8,128)(2,1)} %collective-permute-done.8, s32[]{:T(128)S(6)} %select_n.329, bf16[256,4096]{1,0:T(8,128)(2,1)S(1)} %constant_dynamic-update-slice_fusion, pred[]{:T(512)S(6)} %eq.111), kind=kOutput, calls=%fused_computation.6 | convolution fusion | flops 269484032 | bytes 3276805 | tf_op jit(solution)/shard_map/dot_general | solution.py:150
  145.7 4.1 %all-to-all-done.3 = bf16[8,8,4096]{2,1,0:T(8,128)(2,1)S(1)} async-done(((bf16[8,8,4096]{2,1,0:T(8,128)(2,1)}), bf16[8,8,4096]{2,1,0:T(8,128)(2,1)S(1)}, u32[]{:S(2)}, u32[]{:S(2)}) %all-to-all-start.3) | async-done | bytes 524320 | tf_op jit(solution)/shard_map/all_to_all | solution.py:23
  150.6 1.4 broadcast_in_dim_broadcast_in_dim_broadcast_in_dim.3
  151.9 8.3 %all-to-all-start.4 = ((f32[256,1,128]{2,1,0:T(1,128)}), f32[256,1,128]{2,1,0:T(1,128)S(1)}, u32[]{:S(2)}, u32[]{:S(2)}) async-start(f32[256,1,128]{2,1,0:T(1,128)} %broadcast_in_dim_broadcast_in_dim_broadcast_in_dim.3), calls=%async_computation.4 | async-start | bytes 262144 | tf_op jit(solution)/shard_map/all_to_all | solution.py:23
  161.0 2.1 %collective-permute-start.16 = (f32[4,4096]{1,0:T(4,128)}, f32[4,4096]{1,0:T(4,128)}, u32[]{:S(2)}, u32[]{:S(2)}) collective-permute-start(f32[4,4096]{1,0:T(4,128)} %get-tuple-element.26), channel_id=1, source_target_pairs={{0,4},{4,0},{1,5},{5,1},{2,6},{6,2},{3,7},{7,3},{8,12},{12,8},{9,1... | collective-permute-start | bytes 196616 | tf_op jit(solution)/shard_map/ppermute | solution.py:133
  163.1 1.7 convolution_convert_fusion.2
  164.9 26.8 %all-to-all-done.4 = f32[256,1,128]{2,1,0:T(1,128)S(1)} async-done(((f32[256,1,128]{2,1,0:T(1,128)}), f32[256,1,128]{2,1,0:T(1,128)S(1)}, u32[]{:S(2)}, u32[]{:S(2)}) %all-to-all-start.4) | async-done | bytes 131104 | tf_op jit(solution)/shard_map/all_to_all | solution.py:23
  193.1 2.0 %multiply_subtract_fusion = (f32[4,8192]{1,0:T(4,128)}, f32[4,8192]{1,0:T(4,128)}, f32[4,8192]{1,0:T(4,128)}) fusion(f32[4,8192]{1,0:T(4,128)S(1)} %copy-done.1, f32[]{:T(128)S(6)} %min_shard_map.3, f32[4,4096]{1,0:T(4,128)} %get-tuple-element.27, f32[4,4096]{1,0:T(4,128)} %collective-permute-done.16, pred[]{:T(512)S(6)} %eq.114, f32[4,8192]{1,0:T(4,128)} %param.12, ...), kind=kLoop, calls=%fused_computation.46 | loop fusion | flops 557056 | bytes 917509 | tf_op jit(solution)/shard_map/sub | solution.py:172
  195.4 3.9 %add_convert_fusion = bf16[256,2048]{1,0:T(8,128)(2,1)} fusion(bf16[256,2048]{1,0:T(8,128)(2,1)} %collective-permute-done.11, bf16[256,2048]{1,0:T(8,128)(2,1)} %collective-permute-done.10, bf16[256,2048]{1,0:T(8,128)(2,1)} %collective-permute-done.9, bf16[256,256]{1,0:T(8,128)(2,1)S(1)} %multiply_convert_fusion, ...), kind=kOutput, calls=%fused_computation.9 | convolution fusion | flops 273678336 | bytes 6422533 | tf_op jit(solution)/shard_map/dot_general | solution.py:150
  (83 shorter events, 17.4 us)
Async XLA Ops:
  2.7 27.2 %all-to-all-start.1 = ((bf16[16,4,4096]{2,1,0:T(4,128)(2,1)}), bf16[16,4,4096]{2,1,0:T(4,128)(2,1)S(1)}, u32[]{:S(2)}, u32[]{:S(2)}) async-start(bf16[16,4,4096]{2,1,0:T(4,128)(2,1)} %bitcast.12), calls=%async_computation.1 | async-start | bytes 1048576 | tf_op jit(solution)/shard_map/all_to_all | solution.py:23
  12.7 4.8 %copy-start.3 = (s32[256]{0:T(256)S(1)}, s32[256]{0:T(256)}, u32[]{:S(2)}) copy-start(s32[256]{0:T(256)} %param.14) | copy-start | bytes 3076
  12.7 4.8 %copy-start.4 = (s32[256]{0:T(256)S(1)}, s32[256]{0:T(256)}, u32[]{:S(2)}) copy-start(s32[256]{0:T(256)} %param.13) | copy-start | bytes 3076
  12.7 4.9 %copy-start.5 = (f32[256]{0:T(256)S(1)}, f32[256]{0:T(256)}, u32[]{:S(2)}) copy-start(f32[256]{0:T(256)} %param.16) | copy-start | bytes 3076
  12.7 4.9 %copy-start.6 = (f32[256]{0:T(256)S(1)}, f32[256]{0:T(256)}, u32[]{:S(2)}) copy-start(f32[256]{0:T(256)} %param.15) | copy-start | bytes 3076
  17.4 49.0 %collective-permute-start.3 = (bf16[256,4096]{1,0:T(8,128)(2,1)}, bf16[256,4096]{1,0:T(8,128)(2,1)}, u32[]{:S(2)}, u32[]{:S(2)}) collective-permute-start(bf16[256,4096]{1,0:T(8,128)(2,1)} %get-tuple-element.20), channel_id=1, source_target_pairs={{0,4},{4,0},{1,5},{5,1},{2,6},{6,2},{3,7},{7,3},{8,12},{12,8},{9,1... | collective-permute-start | bytes 6291464 | tf_op jit(solution)/shard_map/ppermute | solution.py:59
  30.6 45.4 %all-to-all-start = ((f32[64,8,128]{2,1,0:T(8,128)}), f32[64,8,128]{2,1,0:T(8,128)S(1)}, u32[]{:S(2)}, u32[]{:S(2)}) async-start(f32[64,8,128]{2,1,0:T(8,128)} %broadcast_in_dim.14), calls=%async_computation | async-start | bytes 524288 | tf_op jit(solution)/shard_map/all_to_all | solution.py:23
  36.9 17.5 %collective-permute-start = (bf16[64,4096]{1,0:T(8,128)(2,1)S(1)}, bf16[64,4096]{1,0:T(8,128)(2,1)S(1)}, u32[]{:S(2)}, u32[]{:S(2)}) collective-permute-start(bf16[64,4096]{1,0:T(8,128)(2,1)S(1)} %reshape.114), channel_id=1, source_target_pairs={{0,64},{64,128},{128,192},{192,0},{1,65},{65,129},{129,193},{193,1... | collective-permute-start | bytes 1572872 | tf_op jit(solution)/shard_map/ppermute | solution.py:27
  38.3 28.0 %collective-permute-start.1 = (bf16[64,4096]{1,0:T(8,128)(2,1)S(1)}, bf16[64,4096]{1,0:T(8,128)(2,1)S(1)}, u32[]{:S(2)}, u32[]{:S(2)}) collective-permute-start(bf16[64,4096]{1,0:T(8,128)(2,1)S(1)} %reshape.114), channel_id=1, source_target_pairs={{0,128},{64,192},{128,0},{192,64},{1,129},{65,193},{129,1},{193,65... | collective-permute-start | bytes 1572872 | tf_op jit(solution)/shard_map/ppermute | solution.py:27
  41.0 25.4 %collective-permute-start.2 = (bf16[64,4096]{1,0:T(8,128)(2,1)S(1)}, bf16[64,4096]{1,0:T(8,128)(2,1)S(1)}, u32[]{:S(2)}, u32[]{:S(2)}) collective-permute-start(bf16[64,4096]{1,0:T(8,128)(2,1)S(1)} %reshape.114), channel_id=1, source_target_pairs={{0,192},{64,0},{128,64},{192,128},{1,193},{65,1},{129,65},{193,129... | collective-permute-start | bytes 1572872 | tf_op jit(solution)/shard_map/ppermute | solution.py:27
  66.4 3.6 %copy-start.2 = (s32[128]{0:T(128)S(1)}, s32[128]{0:T(128)}, u32[]{:S(2)}) copy-start(s32[128]{0:T(128)} %param.17) | copy-start | bytes 1540
  68.8 7.3 %collective-permute-start.4 = (f32[256,256]{1,0:T(8,128)S(1)}, f32[256,256]{1,0:T(8,128)S(1)}, u32[]{:S(2)}, u32[]{:S(2)}) collective-permute-start(f32[256,256]{1,0:T(8,128)S(1)} %fusion.59), channel_id=1, source_target_pairs={{0,4},{4,0},{1,5},{5,1},{2,6},{6,2},{3,7},{7,3},{8,12},{12,8},{9,1... | collective-permute-start | bytes 786440 | tf_op jit(solution)/shard_map/ppermute | solution.py:85
  78.8 5.0 %collective-permute-start.5 = (f32[3,256]{1,0:T(4,128)S(1)}, f32[3,256]{1,0:T(4,128)S(1)}, u32[]{:S(2)}, u32[]{:S(2)}) collective-permute-start(f32[3,256]{1,0:T(4,128)S(1)} %pad_maximum_fusion.2), channel_id=1, source_target_pairs={{0,3},{1,0},{2,1},{3,2},{4,7},{5,4},{6,5},{7,6},{8,11},{9,8},{10,9... | collective-permute-start | bytes 9224 | tf_op jit(solution)/shard_map/ppermute | solution.py:27
  81.3 4.0 %collective-permute-start.6 = (f32[3,256]{1,0:T(4,128)S(1)}, f32[3,256]{1,0:T(4,128)S(1)}, u32[]{:S(2)}, u32[]{:S(2)}) collective-permute-start(f32[3,256]{1,0:T(4,128)S(1)} %pad_maximum_fusion.2), channel_id=1, source_target_pairs={{0,2},{1,3},{2,0},{3,1},{4,6},{5,7},{6,4},{7,5},{8,10},{9,11},{10,... | collective-permute-start | bytes 9224 | tf_op jit(solution)/shard_map/ppermute | solution.py:27
  81.8 3.7 %collective-permute-start.7 = (f32[3,256]{1,0:T(4,128)S(1)}, f32[3,256]{1,0:T(4,128)S(1)}, u32[]{:S(2)}, u32[]{:S(2)}) collective-permute-start(f32[3,256]{1,0:T(4,128)S(1)} %pad_maximum_fusion.2), channel_id=1, source_target_pairs={{0,1},{1,2},{2,3},{3,0},{4,5},{5,6},{6,7},{7,4},{8,9},{9,10},{10,1... | collective-permute-start | bytes 9224 | tf_op jit(solution)/shard_map/ppermute | solution.py:27
  86.0 2.8 %collective-permute-start.12 = (bf16[256,256]{1,0:T(8,128)(2,1)S(1)}, bf16[256,256]{1,0:T(8,128)(2,1)S(1)}, u32[]{:S(2)}, u32[]{:S(2)}) collective-permute-start(bf16[256,256]{1,0:T(8,128)(2,1)S(1)} %multiply_convert_fusion), channel_id=1, source_target_pairs={{0,4},{4,0},{1,5},{5,1},{2,6},{6,2},{3,7},{7,3},{8,12},{12,8},{9,1... | collective-permute-start | bytes 393224 | tf_op jit(solution)/shard_map/ppermute | solution.py:117
  87.8 51.3 %collective-permute-start.8 = (bf16[256,4096]{1,0:T(8,128)(2,1)S(1)}, bf16[256,4096]{1,0:T(8,128)(2,1)}, u32[]{:S(2)}, u32[]{:S(2)}) collective-permute-start(bf16[256,4096]{1,0:T(8,128)(2,1)S(1)} %constant_dynamic-update-slice_fusion), channel_id=1, source_target_pairs={{0,4},{4,0},{1,5},{5,1},{2,6},{6,2},{3,7},{7,3},{8,12},{12,8},{9,1... | collective-permute-start | bytes 6291464 | tf_op jit(solution)/shard_map/ppermute | solution.py:138
  92.3 1.3 copy-start
  94.8 13.6 %collective-permute-start.13 = (bf16[64,4096]{1,0:T(8,128)(2,1)}, bf16[64,4096]{1,0:T(8,128)(2,1)S(1)}, u32[]{:S(2)}, u32[]{:S(2)}) collective-permute-start(bf16[64,4096]{1,0:T(8,128)(2,1)} %get-tuple-element.21), channel_id=1, source_target_pairs={{0,192},{64,0},{128,64},{192,128},{1,193},{65,1},{129,65},{193,129... | collective-permute-start | bytes 1572872 | tf_op jit(solution)/shard_map/ppermute | solution.py:27
  96.3 14.6 %collective-permute-start.14 = (bf16[64,4096]{1,0:T(8,128)(2,1)}, bf16[64,4096]{1,0:T(8,128)(2,1)S(1)}, u32[]{:S(2)}, u32[]{:S(2)}) collective-permute-start(bf16[64,4096]{1,0:T(8,128)(2,1)} %get-tuple-element.23), channel_id=1, source_target_pairs={{0,128},{64,192},{128,0},{192,64},{1,129},{65,193},{129,1},{193,65... | collective-permute-start | bytes 1572872 | tf_op jit(solution)/shard_map/ppermute | solution.py:27
  97.3 26.5 %collective-permute-start.15 = (bf16[64,4096]{1,0:T(8,128)(2,1)}, bf16[64,4096]{1,0:T(8,128)(2,1)}, u32[]{:S(2)}, u32[]{:S(2)}) collective-permute-start(bf16[64,4096]{1,0:T(8,128)(2,1)} %get-tuple-element.22), channel_id=1, source_target_pairs={{0,64},{64,128},{128,192},{192,0},{1,65},{65,129},{129,193},{193,1... | collective-permute-start | bytes 1572872 | tf_op jit(solution)/shard_map/ppermute | solution.py:27
  98.3 27.9 %all-to-all-start.2 = ((f32[64,2,128]{2,1,0:T(2,128)}), f32[64,2,128]{2,1,0:T(2,128)S(1)}, u32[]{:S(2)}, u32[]{:S(2)}) async-start(f32[64,2,128]{2,1,0:T(2,128)} %broadcast_in_dim.17), calls=%async_computation.2 | async-start | bytes 131072 | tf_op jit(solution)/shard_map/all_to_all | solution.py:23
  126.1 23.7 %all-to-all-start.3 = ((bf16[8,8,4096]{2,1,0:T(8,128)(2,1)}), bf16[8,8,4096]{2,1,0:T(8,128)(2,1)S(1)}, u32[]{:S(2)}, u32[]{:S(2)}) async-start(bf16[8,8,4096]{2,1,0:T(8,128)(2,1)} %fusion.22), calls=%async_computation.3 | async-start | bytes 1048576 | tf_op jit(solution)/shard_map/all_to_all | solution.py:23
  141.8 53.3 %collective-permute-start.9 = (bf16[256,2048]{1,0:T(8,128)(2,1)}, bf16[256,2048]{1,0:T(8,128)(2,1)}, u32[]{:S(2)}, u32[]{:S(2)}) collective-permute-start(bf16[256,2048]{1,0:T(8,128)(2,1)} %convolution_convert_fusion.4), channel_id=1, source_target_pairs={{0,3},{1,0},{2,1},{3,2},{4,7},{5,4},{6,5},{7,6},{8,11},{9,8},{10,9... | collective-permute-start | bytes 3145736 | tf_op jit(solution)/shard_map/ppermute | solution.py:27
  144.5 50.6 %collective-permute-start.10 = (bf16[256,2048]{1,0:T(8,128)(2,1)}, bf16[256,2048]{1,0:T(8,128)(2,1)}, u32[]{:S(2)}, u32[]{:S(2)}) collective-permute-start(bf16[256,2048]{1,0:T(8,128)(2,1)} %convolution_convert_fusion.3), channel_id=1, source_target_pairs={{0,2},{1,3},{2,0},{3,1},{4,6},{5,7},{6,4},{7,5},{8,10},{9,11},{10,... | collective-permute-start | bytes 3145736 | tf_op jit(solution)/shard_map/ppermute | solution.py:27
  149.9 43.2 %copy-start.1 = (f32[4,8192]{1,0:T(4,128)S(1)}, f32[4,8192]{1,0:T(4,128)}, u32[]{:S(2)}) copy-start(f32[4,8192]{1,0:T(4,128)} %param.10) | copy-start | bytes 393220
  151.9 39.8 %all-to-all-start.4 = ((f32[256,1,128]{2,1,0:T(1,128)}), f32[256,1,128]{2,1,0:T(1,128)S(1)}, u32[]{:S(2)}, u32[]{:S(2)}) async-start(f32[256,1,128]{2,1,0:T(1,128)} %broadcast_in_dim_broadcast_in_dim_broadcast_in_dim.3), calls=%async_computation.4 | async-start | bytes 262144 | tf_op jit(solution)/shard_map/all_to_all | solution.py:23
  161.0 32.1 %collective-permute-start.16 = (f32[4,4096]{1,0:T(4,128)}, f32[4,4096]{1,0:T(4,128)}, u32[]{:S(2)}, u32[]{:S(2)}) collective-permute-start(f32[4,4096]{1,0:T(4,128)} %get-tuple-element.26), channel_id=1, source_target_pairs={{0,4},{4,0},{1,5},{5,1},{2,6},{6,2},{3,7},{7,3},{8,12},{12,8},{9,1... | collective-permute-start | bytes 196616 | tf_op jit(solution)/shard_map/ppermute | solution.py:133
  164.8 30.6 %collective-permute-start.11 = (bf16[256,2048]{1,0:T(8,128)(2,1)S(1)}, bf16[256,2048]{1,0:T(8,128)(2,1)}, u32[]{:S(2)}, u32[]{:S(2)}) collective-permute-start(bf16[256,2048]{1,0:T(8,128)(2,1)S(1)} %convolution_convert_fusion.2), channel_id=1, source_target_pairs={{0,1},{1,2},{2,3},{3,0},{4,5},{5,6},{6,7},{7,4},{8,9},{9,10},{10,1... | collective-permute-start | bytes 3145736 | tf_op jit(solution)/shard_map/ppermute | solution.py:27

commit v3 on v2

--- a/solution.py
+++ b/solution.py
@@ -2,6 +2,7 @@
 import jax.numpy as jnp
 from jax import lax
 from jax.sharding import Mesh, PartitionSpec as P
+
 
 loss_scale = 1048576.0
 clip_norm = 0.004
@@ -27,11 +28,26 @@
     return lax.ppermute(x, axis, [(i, (i + step) % count) for i in range(count)])
 
 
+def pair(x, y, keep, axis):
+    return jnp.where(keep, jnp.concatenate([x, y], axis), jnp.concatenate([y, x], axis))
+
+
+def gather(x):
+    x = x[None]
+    for axis, count in (("core", NC), ("z", NZ), ("y", NY)):
+        place, bit = lax.axis_index(axis), 1
+        while bit < count:
+            other = lax.ppermute(x, axis, [(i, i ^ bit) for i in range(count)])
+            x = pair(x, other, place & bit == 0, 0)
+            bit *= 2
+    return x
+
+
 def spread(x, axes, count):
     return exchange(jnp.broadcast_to(x[None], (count,) + x.shape), axes)
 
 
-def body(
+def step(
     hidden_states, master, moment, second, targets, loss_mask, prior_lse, prior_target, span_order
 ):
     tok_rows, feat = hidden_states.shape
@@ -49,10 +65,19 @@
     y_rows = group_rows // NY
     chip_rows = y_rows // NZ
 
-    cut = master.astype(bf16).reshape(shard_rows, NC, half).transpose(1, 0, 2)
-    cut = jnp.broadcast_to(cut[None], (NZ,) + cut.shape).reshape(NZ * NC, shard_rows, half)
-    block = exchange(cut, ("z", "core")).reshape(y_rows, half)
-    head = jnp.concatenate([block] + [shift(block, "y", NY, s) for s in range(1, NY)], 0)
+    wide = half * 3 // 4
+    thin = half - wide
+    halves = master.astype(bf16).reshape(shard_rows, NC, half)
+    cut = halves[:, :, :wide].transpose(1, 0, 2)
+    cut = jnp.broadcast_to(cut[None], (NZ,) + cut.shape).reshape(NZ * NC, shard_rows, wide)
+    block = exchange(cut, ("z", "core")).reshape(y_rows, wide)
+    near_b = lax.dynamic_index_in_dim(halves[:, :, wide:], core, 1, keepdims=False)
+    far_b = lax.dynamic_index_in_dim(halves[:, :, wide:], 1 - core, 1, keepdims=False)
+    chip_b = pair(near_b, lax.ppermute(far_b, "core", SWAP), core == 0, 0)
+    chips_b = jnp.stack([chip_b] + [shift(chip_b, "y", NY, s) for s in range(1, NY)], 0)
+    head_a = jnp.concatenate([block] + [shift(block, "y", NY, s) for s in range(1, NY)], 0)
+    head_b = spread(chips_b, "z", NZ).transpose(1, 0, 2, 3).reshape(group_rows, thin)
+    head = jnp.concatenate([head_a, head_b], 1)
 
     own_half = lax.dynamic_slice_in_dim(hidden_states, core * half, half, 1)
     far_half = lax.dynamic_slice_in_dim(hidden_states, (1 - core) * half, half, 1)
@@ -68,7 +93,8 @@
         ],
         0,
     )
-    small = spread(small, CTX, ctx_count).reshape(ctx_count, 4, 2, span)
+    small = gather(small)
+    small = small.reshape(ctx_count, 4, 2, span)
     token_count = jnp.sum(small[:, 1])
     pieces = []
     for offset in (0, 1):
@@ -118,16 +144,25 @@
 
     both = jnp.concatenate([dlogits, mate_dlogits], 1)
     partial_rows = jnp.dot(both, tokens, preferred_element_type=f32).astype(bf16)
-    blocks = [partial_rows[s * y_rows : (s + 1) * y_rows] for s in range(NY)]
+    blocks = [partial_rows[s * y_rows : (s + 1) * y_rows, :wide] for s in range(NY)]
     by_y = blocks[0].astype(f32)
     for s in range(1, NY):
         by_y = by_y + shift(blocks[s], "y", NY, -s).astype(f32)
-    by_y = by_y.astype(bf16)
-    by_z = exchange(by_y.reshape(NZ, chip_rows, half), "z")
-    chip_grad = jnp.sum(by_z.astype(f32), axis=0)
+    by_y = by_y.astype(bf16).reshape(NZ, chip_rows, wide)
+    by_z = partial_rows[:, wide:].reshape(NY, NZ, chip_rows, thin).transpose(1, 0, 2, 3)
+    by_z = jnp.sum(exchange(by_z, "z").astype(f32), axis=0).astype(bf16)
+    grad_b = by_z[0].astype(f32)
+    for s in range(1, NY):
+        grad_b = grad_b + shift(by_z[s], "y", NY, -s).astype(f32)
+    grad_a = jnp.sum(exchange(by_y, "z").astype(f32), axis=0)
+    chip_grad = jnp.concatenate([grad_a, grad_b], 1)
     square = jnp.sum(chip_grad * chip_grad)
-    squares = spread(jnp.full((1, 128), square), ALL, ctx_count * vocab_count)
-    square_sum = jnp.sum(squares) / 128.0
+    lanes = tok_rows // vocab_count
+    share = lax.dynamic_slice_in_dim(loss_rows, vocab_place * lanes, lanes, 0)
+    report = jnp.concatenate([jnp.full((lanes,), square), share], 0)[None]
+    reports = spread(report, ALL, ctx_count * vocab_count)[:, 0]
+    square_sum = jnp.sum(reports[:, :lanes]) / lanes
+    mean_loss = jnp.sum(reports[:, lanes:]) / token_count
     near = lax.dynamic_slice_in_dim(chip_grad, core * shard_rows, shard_rows, 0)
     far = lax.dynamic_slice_in_dim(chip_grad, (1 - core) * shard_rows, shard_rows, 0)
     mate = lax.ppermute(far, "core", SWAP)
@@ -155,13 +190,14 @@
         hidden_sum = hidden_sum + part.astype(f32)
     hidden_grad = hidden_sum.astype(bf16)
 
-    losses = spread(loss_rows.reshape(2, span), CTX, ctx_count).reshape(2 * ctx_count, span)
-    mean_loss = jnp.sum(losses) / token_count
+    per_span = vocab_count // 2
     slot_ids = jnp.arange(span_order.shape[0], dtype=jnp.int32)
     natural = []
     for offset in (0, 1):
         slot = jnp.sum(jnp.where(span_order == 2 * ctx_place + offset, slot_ids, 0))
-        natural.append(lax.dynamic_slice_in_dim(losses, slot, 1, 0).reshape(span))
+        natural.append(
+            lax.dynamic_slice(reports, (slot * per_span, lanes), (per_span, lanes)).reshape(span)
+        )
     token_loss = jnp.concatenate(natural, 0)
 
     norm_value = jnp.sqrt(square_sum) / loss_scale
@@ -190,4 +226,4 @@
         P(),
     )
     out_specs = (P(CTX), P(), P(CTX, "vocab"), head_spec, head_spec, head_spec)
-    return jax.shard_map(body, mesh=grid, in_specs=in_specs, out_specs=out_specs, check_vma=False)
+    return jax.shard_map(step, mesh=grid, in_specs=in_specs, out_specs=out_specs, check_vma=False)

time: 201 us -> 193 us (0.960)
  waiting for transfers between devices: 85.5 us -> 57.8 us
  starting transfers between devices: 59 us -> 79.4 us
  between operations: 14.3 us -> 11.8 us
    ppermute x12 -> x18, waiting for transfers between devices: 41.5 us -> 15.8 us  [shift(): lax.ppermute(x, axis, [(i, (i + step) % count) for i in range(count)])]
    ppermute x5 -> x12, starting transfers between devices: 5.65 us -> 26.4 us  [the longest x6 14.2 us: gather(): other = lax.ppermute(x, axis, [(i, i ^ bit) for i in range(count)])]
    all_to_all x5, waiting for transfers between devices: 43.3 us -> 24.2 us  [exchange(): return lax.all_to_all(x, axes, 0, 0, tiled=True)]
    ppermute x5 -> x12, waiting for transfers between devices: 0.72 us -> 17.7 us  [the longest x6 15.7 us: gather(): other = lax.ppermute(x, axis, [(i, i ^ bit) for i in range(count)])]
    all_to_all x5, starting transfers between devices: 40.4 us -> 30.5 us  [exchange(): return lax.all_to_all(x, axes, 0, 0, tiled=True)]
    ppermute x12 -> x18, starting transfers between devices: 12.9 us -> 22.4 us  [shift(): lax.ppermute(x, axis, [(i, (i + step) % count) for i in range(count)])]
    dynamic_slice x4 -> x5, local copies, waits for them, and re-layouts: 5.97 us -> 5.49 us  [the longest x1 4.71 us: step(): own_half = lax.dynamic_slice_in_dim(hidden_states, core * half, half, 1)]
  transfers between devices with their start and end apart: 22 -> 35, of which waited for: 11 -> 13; matrix products, arithmetic and copies ran while one was open for 16% -> 18% of each run, Pallas kernels for 0% -> 0%
where the time goes in v3:
time: 193 us
  starting transfers between devices  79.4 us (41%)
  waiting for transfers between devices  57.8 us (30%)
  matrix products  18.9 us (10%)
  local copies, waits for them, and re-layouts  14 us (7%)
  between operations  11.8 us (6%)
  other arithmetic  10.7 us (6%)
    all_to_all x5, starting transfers between devices, exchange(): return lax.all_to_all(x, axes, 0, 0, tiled=True)  30.5 us
    all_to_all x5, waiting for transfers between devices, exchange(): return lax.all_to_all(x, axes, 0, 0, tiled=True)  24.2 us
    ppermute x18, starting transfers between devices, shift(): lax.ppermute(x, axis, [(i, (i + step) % count) for i in range(count)])  22.4 us
    ppermute x18, waiting for transfers between devices, shift(): lax.ppermute(x, axis, [(i, (i + step) % count) for i in range(count)])  15.8 us
    ppermute x6, waiting for transfers between devices, gather(): other = lax.ppermute(x, axis, [(i, i ^ bit) for i in range(count)])  15.7 us
    ppermute x6, starting transfers between devices, gather(): other = lax.ppermute(x, axis, [(i, i ^ bit) for i in range(count)])  14.2 us
    dot_general x4, matrix products, step(): lax.dot_general(dlogits, side, (((0,), (0,)), ((), ())), preferred_elemen...  11.9 us
    dynamic_slice x1, local copies, waits for them, and re-layouts, step(): own_half = lax.dynamic_slice_in_dim(hidden_states, core * half, half, 1)  4.71 us
  transfers between devices with their start and end apart: 35, of which 13 were waited for; matrix products, arithmetic and copies ran while one was open for 18% of the time, Pallas kernels for 0%

profile of v3, /device:TPU:1, one launch (start us, length us, event | category | flops | bytes accessed | tf_op | source)
XLA Modules:
  0.0 192.6 jit_solution(5963956366216741211)
XLA Ops:
  1.6 3.3 %collective-permute-start.9 = (bf16[4,1024]{1,0:T(4,128)(2,1)S(1)}, bf16[4,1024]{1,0:T(4,128)(2,1)S(1)}, u32[]{:S(2)}, u32[]{:S(2)}) collective-permute-start(bf16[4,1024]{1,0:T(4,128)(2,1)S(1)} %get-tuple-element.37), channel_id=1, source_target_pairs={{0,4},{4,0},{1,5},{5,1},{2,6},{6,2},{3,7},{7,3},{8,12},{12,8},{9,1... | collective-permute-start | bytes 24584 | tf_op jit(solution)/shard_map/ppermute | solution.py:76
  5.9 6.9 %all-to-all-start = ((bf16[16,4,3072]{2,1,0:T(4,128)(2,1)}), bf16[16,4,3072]{2,1,0:T(4,128)(2,1)S(1)}, u32[]{:S(2)}, u32[]{:S(2)}) async-start(bf16[16,4,3072]{2,1,0:T(4,128)(2,1)} %bitcast.17), calls=%async_computation | async-start | bytes 786432 | tf_op jit(solution)/shard_map/all_to_all | solution.py:24
  12.8 4.7 %constant_dynamic-slice_fusion.3 = (bf16[256,4096]{1,0:T(8,128)(2,1)}, bf16[256,4096]{1,0:T(8,128)(2,1)}) fusion(bf16[256,8192]{1,0:T(8,128)(2,1)} %param.9, s32[]{:T(128)S(6)} %select_n.395, s32[]{:T(128)S(6)} %select_n.396), kind=kLoop, calls=%fused_computation.99 | loop fusion | bytes 8388616 | tf_op jit(solution)/shard_map/dynamic_slice | solution.py:82
  18.2 3.9 %collective-permute-done = f32[1,8,128]{2,0,1:T(1,128)S(1)} collective-permute-done((f32[1,8,128]{2,0,1:T(1,128)S(1)}, f32[1,8,128]{2,0,1:T(1,128)S(1)}, u32[]{:S(2)}, u32[]{:S(2)}) %collective-permute-start) | collective-permute-done | bytes 4128 | tf_op jit(solution)/shard_map/ppermute | solution.py:40
  23.6 2.8 %collective-permute-start.12 = (bf16[8,1024]{1,0:T(8,128)(2,1)S(1)}, bf16[8,1024]{1,0:T(8,128)(2,1)S(1)}, u32[]{:S(2)}, u32[]{:S(2)}) collective-permute-start(bf16[8,1024]{1,0:T(8,128)(2,1)S(1)} %maximum_select_fusion.10), channel_id=1, source_target_pairs={{0,192},{64,0},{128,64},{192,128},{1,193},{65,1},{129,65},{193,129... | collective-permute-start | bytes 49160 | tf_op jit(solution)/shard_map/ppermute | solution.py:28
  27.5 3.0 %collective-permute-done.11 = bf16[8,1024]{1,0:T(8,128)(2,1)S(1)} collective-permute-done((bf16[8,1024]{1,0:T(8,128)(2,1)S(1)}, bf16[8,1024]{1,0:T(8,128)(2,1)S(1)}, u32[]{:S(2)}, u32[]{:S(2)}) %collective-permute-start.11) | collective-permute-done | bytes 16416 | tf_op jit(solution)/shard_map/ppermute | solution.py:28
  31.5 5.5 %all-to-all-start.1 = ((bf16[8,4,8,1024]{3,2,1,0:T(8,128)(2,1)}), bf16[8,4,8,1024]{3,2,1,0:T(8,128)(2,1)S(1)}, u32[]{:S(2)}, u32[]{:S(2)}) async-start(bf16[8,4,8,1024]{3,2,1,0:T(8,128)(2,1)} %broadcast_in_dim.18), calls=%async_computation.1 | async-start | bytes 1048576 | tf_op jit(solution)/shard_map/all_to_all | solution.py:24
  37.1 2.4 %collective-permute-start.2 = (f32[4,8,128]{2,0,1:T(4,128)S(1)}, f32[4,8,128]{2,0,1:T(4,128)S(1)}, u32[]{:S(2)}, u32[]{:S(2)}) collective-permute-start(f32[4,8,128]{2,0,1:T(4,128)S(1)} %maximum_select_fusion.8), channel_id=1, source_target_pairs={{0,16},{8,24},{16,0},{24,8},{32,48},{40,56},{48,32},{56,40},{1,17}... | collective-permute-start | bytes 49160 | tf_op jit(solution)/shard_map/ppermute | solution.py:40
  46.0 6.0 %collective-permute-start.3 = (f32[8,8,128]{2,0,1:T(8,128)S(1)}, f32[8,8,128]{2,0,1:T(8,128)S(1)}, u32[]{:S(2)}, u32[]{:S(2)}) collective-permute-start(f32[8,8,128]{2,0,1:T(8,128)S(1)} %maximum_select_fusion.7), channel_id=1, source_target_pairs={{0,32},{8,40},{16,48},{24,56},{32,0},{40,8},{48,16},{56,24},{1,33}... | collective-permute-start | bytes 98312 | tf_op jit(solution)/shard_map/ppermute | solution.py:40
  56.1 11.9 %collective-permute-done.4 = f32[16,8,128]{2,0,1:T(8,128)S(1)} collective-permute-done((f32[16,8,128]{2,0,1:T(8,128)S(1)}, f32[16,8,128]{2,0,1:T(8,128)S(1)}, u32[]{:S(2)}, u32[]{:S(2)}) %collective-permute-start.4) | collective-permute-done | bytes 65568 | tf_op jit(solution)/shard_map/ppermute | solution.py:40
  68.7 2.5 %collective-permute-start.5 = (f32[32,8,128]{2,0,1:T(8,128)}, f32[32,8,128]{2,0,1:T(8,128)S(1)}, u32[]{:S(2)}, u32[]{:S(2)}) collective-permute-start(f32[32,8,128]{2,0,1:T(8,128)} %maximum_select_fusion.2), channel_id=1, source_target_pairs={{0,128},{64,192},{128,0},{192,64},{1,129},{65,193},{129,1},{193,65... | collective-permute-start | bytes 393224 | tf_op jit(solution)/shard_map/ppermute | solution.py:40
  71.2 2.7 %collective-permute-done.6 = bf16[64,3072]{1,0:T(8,128)(2,1)S(1)} collective-permute-done((bf16[64,3072]{1,0:T(8,128)(2,1)S(1)}, bf16[64,3072]{1,0:T(8,128)(2,1)S(1)}, u32[]{:S(2)}, u32[]{:S(2)}) %collective-permute-start.6) | collective-permute-done | bytes 393248 | tf_op jit(solution)/shard_map/ppermute | solution.py:28
  75.8 2.5 %fusion.61 = f32[256,256]{1,0:T(8,128)S(1)} fusion(bf16[256,4096]{1,0:T(8,128)(2,1)S(1)} %pad_maximum_fusion, bf16[256,4096]{1,0:T(8,128)(2,1)} %collective-permute-done.13), kind=kOutput, calls=%fused_computation.145 | convolution fusion | flops 536870912 | bytes 4456448 | tf_op jit(solution)/shard_map/dot_general | solution.py:109
  78.3 4.3 %collective-permute-start.14 = (f32[256,256]{1,0:T(8,128)S(1)}, f32[256,256]{1,0:T(8,128)S(1)}, u32[]{:S(2)}, u32[]{:S(2)}) collective-permute-start(f32[256,256]{1,0:T(8,128)S(1)} %fusion.61), channel_id=1, source_target_pairs={{0,4},{4,0},{1,5},{5,1},{2,6},{6,2},{3,7},{7,3},{8,12},{12,8},{9,1... | collective-permute-start | bytes 786440 | tf_op jit(solution)/shard_map/ppermute | solution.py:111
  85.1 2.6 %collective-permute-start.15 = (f32[3,256]{1,0:T(4,128)S(1)}, f32[3,256]{1,0:T(4,128)S(1)}, u32[]{:S(2)}, u32[]{:S(2)}) collective-permute-start(f32[3,256]{1,0:T(4,128)S(1)} %pad_maximum_fusion.5), channel_id=1, source_target_pairs={{0,3},{1,0},{2,1},{3,2},{4,7},{5,4},{6,5},{7,6},{8,11},{9,8},{10,9... | collective-permute-start | bytes 9224 | tf_op jit(solution)/shard_map/ppermute | solution.py:28
  92.4 2.2 %collective-permute-start.18 = (bf16[256,256]{1,0:T(8,128)(2,1)S(1)}, bf16[256,256]{1,0:T(8,128)(2,1)S(1)}, u32[]{:S(2)}, u32[]{:S(2)}) collective-permute-start(bf16[256,256]{1,0:T(8,128)(2,1)S(1)} %multiply_convert_fusion), channel_id=1, source_target_pairs={{0,4},{4,0},{1,5},{5,1},{2,6},{6,2},{3,7},{7,3},{8,12},{12,8},{9,1... | collective-permute-start | bytes 393224 | tf_op jit(solution)/shard_map/ppermute | solution.py:143
  95.5 3.5 %convolution_convert_fusion = bf16[256,4096]{1,0:T(8,128)(2,1)S(1)} fusion(bf16[256,4096]{1,0:T(8,128)(2,1)} %collective-permute-done.13, bf16[256,4096]{1,0:T(8,128)(2,1)} %get-tuple-element.23, bf16[256,256]{1,0:T(8,128)(2,1)S(1)} %collective-permute-done.18, bf16[256,256]{1,0:T(8,128)(2,1)S(1)} %multiply_convert_fusion), kind=kOutput, calls=%fused_computation | convolution fusion | flops 1083703296 | bytes 6553600 | tf_op jit(solution)/shard_map/dot_general | solution.py:146
  109.3 4.2 %all-to-all-start.3 = ((bf16[8,4,8,1024]{3,2,1,0:T(8,128)(2,1)}), bf16[8,4,8,1024]{3,2,1,0:T(8,128)(2,1)S(1)}, u32[]{:S(2)}, u32[]{:S(2)}) async-start(bf16[8,4,8,1024]{3,2,1,0:T(8,128)(2,1)} %bitcast.87), calls=%async_computation.3 | async-start | bytes 1048576 | tf_op jit(solution)/shard_map/all_to_all | solution.py:24
  113.5 8.1 %collective-permute-done.20 = bf16[64,3072]{1,0:T(8,128)(2,1)} collective-permute-done((bf16[64,3072]{1,0:T(8,128)(2,1)S(1)}, bf16[64,3072]{1,0:T(8,128)(2,1)}, u32[]{:S(2)}, u32[]{:S(2)}) %collective-permute-start.20) | collective-permute-done | bytes 393248 | tf_op jit(solution)/shard_map/ppermute | solution.py:28
  121.7 2.3 %fusion.22 = bf16[8,8,3072]{2,1,0:T(8,128)(2,1)} fusion(bf16[64,3072]{1,0:T(8,128)(2,1)} %collective-permute-done.21, bf16[64,3072]{1,0:T(8,128)(2,1)} %collective-permute-done.20, bf16[64,3072]{1,0:T(8,128)(2,1)} %collective-permute-done.19, bf16[256,4096]{1,0:T(8,128)(2,1)} %copy-done.1), kind=kLoop, calls=%fused_computation.31 | loop fusion | flops 1572864 | bytes 1966080 | tf_op jit(solution)/shard_map/reshape | solution.py:151
  124.0 2.7 %convolution_convert_fusion.2 = bf16[256,2048]{1,0:T(8,128)(2,1)} fusion(bf16[256,256]{1,0:T(8,128)(2,1)S(1)} %multiply_convert_fusion, bf16[256,4096]{1,0:T(8,128)(2,1)} %collective-permute-done.25, s32[]{:T(128)S(6)} %select_n.449, bf16[256,4096]{1,0:T(8,128)(2,1)S(1)} %pad_maximum_fusion, pred[]{:T(512)S(6)} %eq.138), kind=kOutput, calls=%fused_computation.5 | convolution fusion | flops 269484032 | bytes 3276805 | tf_op jit(solution)/shard_map/dot_general | solution.py:185
  126.6 2.7 %convolution_convert_fusion.3 = bf16[256,2048]{1,0:T(8,128)(2,1)} fusion(bf16[256,256]{1,0:T(8,128)(2,1)S(1)} %multiply_convert_fusion, bf16[256,4096]{1,0:T(8,128)(2,1)} %collective-permute-done.25, s32[]{:T(128)S(6)} %select_n.443, bf16[256,4096]{1,0:T(8,128)(2,1)S(1)} %pad_maximum_fusion, pred[]{:T(512)S(6)} %eq.137), kind=kOutput, calls=%fused_computation.6 | convolution fusion | flops 269484032 | bytes 3276805 | tf_op jit(solution)/shard_map/dot_general | solution.py:185
  131.3 3.5 %all-to-all-start.2 = ((bf16[8,8,3072]{2,1,0:T(8,128)(2,1)}), bf16[8,8,3072]{2,1,0:T(8,128)(2,1)S(1)}, u32[]{:S(2)}, u32[]{:S(2)}) async-start(bf16[8,8,3072]{2,1,0:T(8,128)(2,1)} %fusion.22), calls=%async_computation.2 | async-start | bytes 786432 | tf_op jit(solution)/shard_map/all_to_all | solution.py:24
  134.9 2.2 %collective-permute-start.24 = (bf16[8,1024]{1,0:T(8,128)(2,1)S(1)}, bf16[8,1024]{1,0:T(8,128)(2,1)S(1)}, u32[]{:S(2)}, u32[]{:S(2)}) collective-permute-start(bf16[8,1024]{1,0:T(8,128)(2,1)S(1)} %get-tuple-element.33), channel_id=1, source_target_pairs={{0,64},{64,128},{128,192},{192,0},{1,65},{65,129},{129,193},{193,1... | collective-permute-start | bytes 49160 | tf_op jit(solution)/shard_map/ppermute | solution.py:28
  137.1 2.3 %collective-permute-start.23 = (bf16[8,1024]{1,0:T(8,128)(2,1)S(1)}, bf16[8,1024]{1,0:T(8,128)(2,1)S(1)}, u32[]{:S(2)}, u32[]{:S(2)}) collective-permute-start(bf16[8,1024]{1,0:T(8,128)(2,1)S(1)} %get-tuple-element.34), channel_id=1, source_target_pairs={{0,128},{64,192},{128,0},{192,64},{1,129},{65,193},{129,1},{193,65... | collective-permute-start | bytes 49160 | tf_op jit(solution)/shard_map/ppermute | solution.py:28
  139.8 2.7 %convolution_convert_fusion.4 = bf16[256,2048]{1,0:T(8,128)(2,1)} fusion(bf16[256,256]{1,0:T(8,128)(2,1)S(1)} %multiply_convert_fusion, bf16[256,4096]{1,0:T(8,128)(2,1)} %collective-permute-done.25, s32[]{:T(128)S(6)} %select_n.437, bf16[256,4096]{1,0:T(8,128)(2,1)S(1)} %pad_maximum_fusion, pred[]{:T(512)S(6)} %eq.136), kind=kOutput, calls=%fused_computation.7 | convolution fusion | flops 269484032 | bytes 3276805 | tf_op jit(solution)/shard_map/dot_general | solution.py:185
  142.5 2.1 %collective-permute-start.26 = (bf16[256,2048]{1,0:T(8,128)(2,1)}, bf16[256,2048]{1,0:T(8,128)(2,1)}, u32[]{:S(2)}, u32[]{:S(2)}) collective-permute-start(bf16[256,2048]{1,0:T(8,128)(2,1)} %convolution_convert_fusion.4), channel_id=1, source_target_pairs={{0,3},{1,0},{2,1},{3,2},{4,7},{5,4},{6,5},{7,6},{8,11},{9,8},{10,9... | collective-permute-start | bytes 3145736 | tf_op jit(solution)/shard_map/ppermute | solution.py:28
  144.6 2.5 %all-to-all-done.2 = bf16[8,8,3072]{2,1,0:T(8,128)(2,1)S(1)} async-done(((bf16[8,8,3072]{2,1,0:T(8,128)(2,1)}), bf16[8,8,3072]{2,1,0:T(8,128)(2,1)S(1)}, u32[]{:S(2)}, u32[]{:S(2)}) %all-to-all-start.2) | async-done | bytes 393248 | tf_op jit(solution)/shard_map/all_to_all | solution.py:24
  149.2 10.5 %all-to-all-start.4 = ((f32[256,1,128]{2,1,0:T(1,128)}), f32[256,1,128]{2,1,0:T(1,128)S(1)}, u32[]{:S(2)}, u32[]{:S(2)}) async-start(f32[256,1,128]{2,1,0:T(1,128)} %broadcast_in_dim.38), calls=%async_computation.4 | async-start | bytes 262144 | tf_op jit(solution)/shard_map/all_to_all | solution.py:24
  159.8 2.2 %collective-permute-start.29 = (f32[4,4096]{1,0:T(4,128)S(1)}, f32[4,4096]{1,0:T(4,128)S(1)}, u32[]{:S(2)}, u32[]{:S(2)}) collective-permute-start(f32[4,4096]{1,0:T(4,128)S(1)} %get-tuple-element.30), channel_id=1, source_target_pairs={{0,4},{4,0},{1,5},{5,1},{2,6},{6,2},{3,7},{7,3},{8,12},{12,8},{9,1... | collective-permute-start | bytes 196616 | tf_op jit(solution)/shard_map/ppermute | solution.py:168
  162.0 21.0 %all-to-all-done.4 = f32[256,1,128]{2,1,0:T(1,128)S(1)} async-done(((f32[256,1,128]{2,1,0:T(1,128)}), f32[256,1,128]{2,1,0:T(1,128)S(1)}, u32[]{:S(2)}, u32[]{:S(2)}) %all-to-all-start.4) | async-done | bytes 131104 | tf_op jit(solution)/shard_map/all_to_all | solution.py:24
  187.6 3.9 %add_convert_fusion = bf16[256,2048]{1,0:T(8,128)(2,1)} fusion(bf16[256,2048]{1,0:T(8,128)(2,1)} %collective-permute-done.28, bf16[256,2048]{1,0:T(8,128)(2,1)} %collective-permute-done.27, bf16[256,2048]{1,0:T(8,128)(2,1)} %collective-permute-done.26, bf16[256,256]{1,0:T(8,128)(2,1)S(1)} %multiply_convert_fusion, ...), kind=kOutput, calls=%fused_computation.10 | convolution fusion | flops 273678336 | bytes 6422533 | tf_op jit(solution)/shard_map/dot_general | solution.py:185
  (142 shorter events, 37.4 us)
Async XLA Ops:
  1.6 21.9 %collective-permute-start.9 = (bf16[4,1024]{1,0:T(4,128)(2,1)S(1)}, bf16[4,1024]{1,0:T(4,128)(2,1)S(1)}, u32[]{:S(2)}, u32[]{:S(2)}) collective-permute-start(bf16[4,1024]{1,0:T(4,128)(2,1)S(1)} %get-tuple-element.37), channel_id=1, source_target_pairs={{0,4},{4,0},{1,5},{5,1},{2,6},{6,2},{3,7},{7,3},{8,12},{12,8},{9,1... | collective-permute-start | bytes 24584 | tf_op jit(solution)/shard_map/ppermute | solution.py:76
  5.9 24.8 %all-to-all-start = ((bf16[16,4,3072]{2,1,0:T(4,128)(2,1)}), bf16[16,4,3072]{2,1,0:T(4,128)(2,1)S(1)}, u32[]{:S(2)}, u32[]{:S(2)}) async-start(bf16[16,4,3072]{2,1,0:T(4,128)(2,1)} %bitcast.17), calls=%async_computation | async-start | bytes 786432 | tf_op jit(solution)/shard_map/all_to_all | solution.py:24
  17.6 58.3 %collective-permute-start.13 = (bf16[256,4096]{1,0:T(8,128)(2,1)}, bf16[256,4096]{1,0:T(8,128)(2,1)}, u32[]{:S(2)}, u32[]{:S(2)}) collective-permute-start(bf16[256,4096]{1,0:T(8,128)(2,1)} %get-tuple-element.24), channel_id=1, source_target_pairs={{0,4},{4,0},{1,5},{5,1},{2,6},{6,2},{3,7},{7,3},{8,12},{12,8},{9,1... | collective-permute-start | bytes 6291464 | tf_op jit(solution)/shard_map/ppermute | solution.py:84
  17.7 4.3 %collective-permute-start = (f32[1,8,128]{2,0,1:T(1,128)S(1)}, f32[1,8,128]{2,0,1:T(1,128)S(1)}, u32[]{:S(2)}, u32[]{:S(2)}) collective-permute-start(f32[1,8,128]{2,0,1:T(1,128)S(1)} %bitcast.111), channel_id=1, source_target_pairs={{0,4},{4,0},{1,5},{5,1},{2,6},{6,2},{3,7},{7,3},{8,12},{12,8},{9,1... | collective-permute-start | bytes 12296 | tf_op jit(solution)/shard_map/ppermute | solution.py:40
  22.1 14.9 %collective-permute-start.1 = (f32[2,8,128]{2,0,1:T(2,128)S(1)}, f32[2,8,128]{2,0,1:T(2,128)S(1)}, u32[]{:S(2)}, u32[]{:S(2)}) collective-permute-start(f32[2,8,128]{2,0,1:T(2,128)S(1)} %maximum_select_fusion.11), channel_id=1, source_target_pairs={{0,8},{8,0},{16,24},{24,16},{32,40},{40,32},{48,56},{56,48},{1,9},... | collective-permute-start | bytes 24584 | tf_op jit(solution)/shard_map/ppermute | solution.py:40
  26.4 4.1 %collective-permute-start.11 = (bf16[8,1024]{1,0:T(8,128)(2,1)S(1)}, bf16[8,1024]{1,0:T(8,128)(2,1)S(1)}, u32[]{:S(2)}, u32[]{:S(2)}) collective-permute-start(bf16[8,1024]{1,0:T(8,128)(2,1)S(1)} %maximum_select_fusion.10), channel_id=1, source_target_pairs={{0,128},{64,192},{128,0},{192,64},{1,129},{65,193},{129,1},{193,65... | collective-permute-start | bytes 49160 | tf_op jit(solution)/shard_map/ppermute | solution.py:28
  26.7 3.9 %collective-permute-start.10 = (bf16[8,1024]{1,0:T(8,128)(2,1)S(1)}, bf16[8,1024]{1,0:T(8,128)(2,1)S(1)}, u32[]{:S(2)}, u32[]{:S(2)}) collective-permute-start(bf16[8,1024]{1,0:T(8,128)(2,1)S(1)} %maximum_select_fusion.10), channel_id=1, source_target_pairs={{0,64},{64,128},{128,192},{192,0},{1,65},{65,129},{129,193},{193,1... | collective-permute-start | bytes 49160 | tf_op jit(solution)/shard_map/ppermute | solution.py:28
  31.5 39.6 %all-to-all-start.1 = ((bf16[8,4,8,1024]{3,2,1,0:T(8,128)(2,1)}), bf16[8,4,8,1024]{3,2,1,0:T(8,128)(2,1)S(1)}, u32[]{:S(2)}, u32[]{:S(2)}) async-start(bf16[8,4,8,1024]{3,2,1,0:T(8,128)(2,1)} %broadcast_in_dim.18), calls=%async_computation.1 | async-start | bytes 1048576 | tf_op jit(solution)/shard_map/all_to_all | solution.py:24
  37.1 8.9 %collective-permute-start.2 = (f32[4,8,128]{2,0,1:T(4,128)S(1)}, f32[4,8,128]{2,0,1:T(4,128)S(1)}, u32[]{:S(2)}, u32[]{:S(2)}) collective-permute-start(f32[4,8,128]{2,0,1:T(4,128)S(1)} %maximum_select_fusion.8), channel_id=1, source_target_pairs={{0,16},{8,24},{16,0},{24,8},{32,48},{40,56},{48,32},{56,40},{1,17}... | collective-permute-start | bytes 49160 | tf_op jit(solution)/shard_map/ppermute | solution.py:40
  46.0 8.7 %collective-permute-start.3 = (f32[8,8,128]{2,0,1:T(8,128)S(1)}, f32[8,8,128]{2,0,1:T(8,128)S(1)}, u32[]{:S(2)}, u32[]{:S(2)}) collective-permute-start(f32[8,8,128]{2,0,1:T(8,128)S(1)} %maximum_select_fusion.7), channel_id=1, source_target_pairs={{0,32},{8,40},{16,48},{24,56},{32,0},{40,8},{48,16},{56,24},{1,33}... | collective-permute-start | bytes 98312 | tf_op jit(solution)/shard_map/ppermute | solution.py:40
  52.1 19.1 %collective-permute-start.8 = (bf16[64,3072]{1,0:T(8,128)(2,1)S(1)}, bf16[64,3072]{1,0:T(8,128)(2,1)S(1)}, u32[]{:S(2)}, u32[]{:S(2)}) collective-permute-start(bf16[64,3072]{1,0:T(8,128)(2,1)S(1)} %reshape.154), channel_id=1, source_target_pairs={{0,192},{64,0},{128,64},{192,128},{1,193},{65,1},{129,65},{193,129... | collective-permute-start | bytes 1179656 | tf_op jit(solution)/shard_map/ppermute | solution.py:28
  53.3 17.8 %collective-permute-start.7 = (bf16[64,3072]{1,0:T(8,128)(2,1)S(1)}, bf16[64,3072]{1,0:T(8,128)(2,1)S(1)}, u32[]{:S(2)}, u32[]{:S(2)}) collective-permute-start(bf16[64,3072]{1,0:T(8,128)(2,1)S(1)} %reshape.154), channel_id=1, source_target_pairs={{0,128},{64,192},{128,0},{192,64},{1,129},{65,193},{129,1},{193,65... | collective-permute-start | bytes 1179656 | tf_op jit(solution)/shard_map/ppermute | solution.py:28
  53.9 20.0 %collective-permute-start.6 = (bf16[64,3072]{1,0:T(8,128)(2,1)S(1)}, bf16[64,3072]{1,0:T(8,128)(2,1)S(1)}, u32[]{:S(2)}, u32[]{:S(2)}) collective-permute-start(bf16[64,3072]{1,0:T(8,128)(2,1)S(1)} %reshape.154), channel_id=1, source_target_pairs={{0,64},{64,128},{128,192},{192,0},{1,65},{65,129},{129,193},{193,1... | collective-permute-start | bytes 1179656 | tf_op jit(solution)/shard_map/ppermute | solution.py:28
  54.7 13.3 %collective-permute-start.4 = (f32[16,8,128]{2,0,1:T(8,128)S(1)}, f32[16,8,128]{2,0,1:T(8,128)S(1)}, u32[]{:S(2)}, u32[]{:S(2)}) collective-permute-start(f32[16,8,128]{2,0,1:T(8,128)S(1)} %maximum_select_fusion.5), channel_id=1, source_target_pairs={{0,64},{64,0},{128,192},{192,128},{1,65},{65,1},{129,193},{193,129... | collective-permute-start | bytes 196616 | tf_op jit(solution)/shard_map/ppermute | solution.py:40
  68.7 14.0 %collective-permute-start.5 = (f32[32,8,128]{2,0,1:T(8,128)}, f32[32,8,128]{2,0,1:T(8,128)S(1)}, u32[]{:S(2)}, u32[]{:S(2)}) collective-permute-start(f32[32,8,128]{2,0,1:T(8,128)} %maximum_select_fusion.2), channel_id=1, source_target_pairs={{0,128},{64,192},{128,0},{192,64},{1,129},{65,193},{129,1},{193,65... | collective-permute-start | bytes 393224 | tf_op jit(solution)/shard_map/ppermute | solution.py:40
  78.3 5.5 %collective-permute-start.14 = (f32[256,256]{1,0:T(8,128)S(1)}, f32[256,256]{1,0:T(8,128)S(1)}, u32[]{:S(2)}, u32[]{:S(2)}) collective-permute-start(f32[256,256]{1,0:T(8,128)S(1)} %fusion.61), channel_id=1, source_target_pairs={{0,4},{4,0},{1,5},{5,1},{2,6},{6,2},{3,7},{7,3},{8,12},{12,8},{9,1... | collective-permute-start | bytes 786440 | tf_op jit(solution)/shard_map/ppermute | solution.py:111
  85.1 5.0 %collective-permute-start.15 = (f32[3,256]{1,0:T(4,128)S(1)}, f32[3,256]{1,0:T(4,128)S(1)}, u32[]{:S(2)}, u32[]{:S(2)}) collective-permute-start(f32[3,256]{1,0:T(4,128)S(1)} %pad_maximum_fusion.5), channel_id=1, source_target_pairs={{0,3},{1,0},{2,1},{3,2},{4,7},{5,4},{6,5},{7,6},{8,11},{9,8},{10,9... | collective-permute-start | bytes 9224 | tf_op jit(solution)/shard_map/ppermute | solution.py:28
  87.7 4.0 %collective-permute-start.16 = (f32[3,256]{1,0:T(4,128)S(1)}, f32[3,256]{1,0:T(4,128)S(1)}, u32[]{:S(2)}, u32[]{:S(2)}) collective-permute-start(f32[3,256]{1,0:T(4,128)S(1)} %pad_maximum_fusion.5), channel_id=1, source_target_pairs={{0,2},{1,3},{2,0},{3,1},{4,6},{5,7},{6,4},{7,5},{8,10},{9,11},{10,... | collective-permute-start | bytes 9224 | tf_op jit(solution)/shard_map/ppermute | solution.py:28
  94.5 29.4 %collective-permute-start.25 = (bf16[256,4096]{1,0:T(8,128)(2,1)S(1)}, bf16[256,4096]{1,0:T(8,128)(2,1)}, u32[]{:S(2)}, u32[]{:S(2)}) collective-permute-start(bf16[256,4096]{1,0:T(8,128)(2,1)S(1)} %pad_maximum_fusion), channel_id=1, source_target_pairs={{0,4},{4,0},{1,5},{5,1},{2,6},{6,2},{3,7},{7,3},{8,12},{12,8},{9,1... | collective-permute-start | bytes 6291464 | tf_op jit(solution)/shard_map/ppermute | solution.py:173
  101.2 12.4 %collective-permute-start.21 = (bf16[64,3072]{1,0:T(8,128)(2,1)}, bf16[64,3072]{1,0:T(8,128)(2,1)}, u32[]{:S(2)}, u32[]{:S(2)}) collective-permute-start(bf16[64,3072]{1,0:T(8,128)(2,1)} %get-tuple-element.26), channel_id=1, source_target_pairs={{0,64},{64,128},{128,192},{192,0},{1,65},{65,129},{129,193},{193,1... | collective-permute-start | bytes 1179656 | tf_op jit(solution)/shard_map/ppermute | solution.py:28
  102.8 18.9 %collective-permute-start.20 = (bf16[64,3072]{1,0:T(8,128)(2,1)S(1)}, bf16[64,3072]{1,0:T(8,128)(2,1)}, u32[]{:S(2)}, u32[]{:S(2)}) collective-permute-start(bf16[64,3072]{1,0:T(8,128)(2,1)S(1)} %get-tuple-element.27), channel_id=1, source_target_pairs={{0,128},{64,192},{128,0},{192,64},{1,129},{65,193},{129,1},{193,65... | collective-permute-start | bytes 1179656 | tf_op jit(solution)/shard_map/ppermute | solution.py:28
  104.1 17.6 %collective-permute-start.19 = (bf16[64,3072]{1,0:T(8,128)(2,1)S(1)}, bf16[64,3072]{1,0:T(8,128)(2,1)}, u32[]{:S(2)}, u32[]{:S(2)}) collective-permute-start(bf16[64,3072]{1,0:T(8,128)(2,1)S(1)} %get-tuple-element.25), channel_id=1, source_target_pairs={{0,192},{64,0},{128,64},{192,128},{1,193},{65,1},{129,65},{193,129... | collective-permute-start | bytes 1179656 | tf_op jit(solution)/shard_map/ppermute | solution.py:28
  109.3 22.0 %all-to-all-start.3 = ((bf16[8,4,8,1024]{3,2,1,0:T(8,128)(2,1)}), bf16[8,4,8,1024]{3,2,1,0:T(8,128)(2,1)S(1)}, u32[]{:S(2)}, u32[]{:S(2)}) async-start(bf16[8,4,8,1024]{3,2,1,0:T(8,128)(2,1)} %bitcast.87), calls=%async_computation.3 | async-start | bytes 1048576 | tf_op jit(solution)/shard_map/all_to_all | solution.py:24
  126.6 60.9 %collective-permute-start.28 = (bf16[256,2048]{1,0:T(8,128)(2,1)}, bf16[256,2048]{1,0:T(8,128)(2,1)}, u32[]{:S(2)}, u32[]{:S(2)}) collective-permute-start(bf16[256,2048]{1,0:T(8,128)(2,1)} %convolution_convert_fusion.2), channel_id=1, source_target_pairs={{0,1},{1,2},{2,3},{3,0},{4,5},{5,6},{6,7},{7,4},{8,9},{9,10},{10,1... | collective-permute-start | bytes 3145736 | tf_op jit(solution)/shard_map/ppermute | solution.py:28
  129.3 58.2 %collective-permute-start.27 = (bf16[256,2048]{1,0:T(8,128)(2,1)}, bf16[256,2048]{1,0:T(8,128)(2,1)}, u32[]{:S(2)}, u32[]{:S(2)}) collective-permute-start(bf16[256,2048]{1,0:T(8,128)(2,1)} %convolution_convert_fusion.3), channel_id=1, source_target_pairs={{0,2},{1,3},{2,0},{3,1},{4,6},{5,7},{6,4},{7,5},{8,10},{9,11},{10,... | collective-permute-start | bytes 3145736 | tf_op jit(solution)/shard_map/ppermute | solution.py:28
  131.3 15.8 %all-to-all-start.2 = ((bf16[8,8,3072]{2,1,0:T(8,128)(2,1)}), bf16[8,8,3072]{2,1,0:T(8,128)(2,1)S(1)}, u32[]{:S(2)}, u32[]{:S(2)}) async-start(bf16[8,8,3072]{2,1,0:T(8,128)(2,1)} %fusion.22), calls=%async_computation.2 | async-start | bytes 786432 | tf_op jit(solution)/shard_map/all_to_all | solution.py:24
  134.9 7.6 %collective-permute-start.24 = (bf16[8,1024]{1,0:T(8,128)(2,1)S(1)}, bf16[8,1024]{1,0:T(8,128)(2,1)S(1)}, u32[]{:S(2)}, u32[]{:S(2)}) collective-permute-start(bf16[8,1024]{1,0:T(8,128)(2,1)S(1)} %get-tuple-element.33), channel_id=1, source_target_pairs={{0,64},{64,128},{128,192},{192,0},{1,65},{65,129},{129,193},{193,1... | collective-permute-start | bytes 49160 | tf_op jit(solution)/shard_map/ppermute | solution.py:28
  137.1 7.5 %collective-permute-start.23 = (bf16[8,1024]{1,0:T(8,128)(2,1)S(1)}, bf16[8,1024]{1,0:T(8,128)(2,1)S(1)}, u32[]{:S(2)}, u32[]{:S(2)}) collective-permute-start(bf16[8,1024]{1,0:T(8,128)(2,1)S(1)} %get-tuple-element.34), channel_id=1, source_target_pairs={{0,128},{64,192},{128,0},{192,64},{1,129},{65,193},{129,1},{193,65... | collective-permute-start | bytes 49160 | tf_op jit(solution)/shard_map/ppermute | solution.py:28
  139.4 5.2 %collective-permute-start.22 = (bf16[8,1024]{1,0:T(8,128)(2,1)S(1)}, bf16[8,1024]{1,0:T(8,128)(2,1)S(1)}, u32[]{:S(2)}, u32[]{:S(2)}) collective-permute-start(bf16[8,1024]{1,0:T(8,128)(2,1)S(1)} %get-tuple-element.32), channel_id=1, source_target_pairs={{0,192},{64,0},{128,64},{192,128},{1,193},{65,1},{129,65},{193,129... | collective-permute-start | bytes 49160 | tf_op jit(solution)/shard_map/ppermute | solution.py:28
  142.5 45.1 %collective-permute-start.26 = (bf16[256,2048]{1,0:T(8,128)(2,1)}, bf16[256,2048]{1,0:T(8,128)(2,1)}, u32[]{:S(2)}, u32[]{:S(2)}) collective-permute-start(bf16[256,2048]{1,0:T(8,128)(2,1)} %convolution_convert_fusion.4), channel_id=1, source_target_pairs={{0,3},{1,0},{2,1},{3,2},{4,7},{5,4},{6,5},{7,6},{8,11},{9,8},{10,9... | collective-permute-start | bytes 3145736 | tf_op jit(solution)/shard_map/ppermute | solution.py:28
  149.2 33.8 %all-to-all-start.4 = ((f32[256,1,128]{2,1,0:T(1,128)}), f32[256,1,128]{2,1,0:T(1,128)S(1)}, u32[]{:S(2)}, u32[]{:S(2)}) async-start(f32[256,1,128]{2,1,0:T(1,128)} %broadcast_in_dim.38), calls=%async_computation.4 | async-start | bytes 262144 | tf_op jit(solution)/shard_map/all_to_all | solution.py:24
  159.8 26.8 %collective-permute-start.29 = (f32[4,4096]{1,0:T(4,128)S(1)}, f32[4,4096]{1,0:T(4,128)S(1)}, u32[]{:S(2)}, u32[]{:S(2)}) collective-permute-start(f32[4,4096]{1,0:T(4,128)S(1)} %get-tuple-element.30), channel_id=1, source_target_pairs={{0,4},{4,0},{1,5},{5,1},{2,6},{6,2},{3,7},{7,3},{8,12},{12,8},{9,1... | collective-permute-start | bytes 196616 | tf_op jit(solution)/shard_map/ppermute | solution.py:168
  (17 other events, 216.0 us)

commit v4 on v3

--- a/solution.py
+++ b/solution.py
@@ -32,15 +32,12 @@
     return jnp.where(keep, jnp.concatenate([x, y], axis), jnp.concatenate([y, x], axis))
 
 
-def gather(x):
-    x = x[None]
-    for axis, count in (("core", NC), ("z", NZ), ("y", NY)):
-        place, bit = lax.axis_index(axis), 1
-        while bit < count:
-            other = lax.ppermute(x, axis, [(i, i ^ bit) for i in range(count)])
-            x = pair(x, other, place & bit == 0, 0)
-            bit *= 2
-    return x
+def split(x, count):
+    out = []
+    for _ in range(count):
+        out.append(lax.reduce_precision(x, 8, 7))
+        x = x - out[-1]
+    return out
 
 
 def spread(x, axes, count):
@@ -65,50 +62,64 @@
     y_rows = group_rows // NY
     chip_rows = y_rows // NZ
 
-    wide = half * 3 // 4
-    thin = half - wide
+    thin = half * 3 // 16
+    wide = half - thin
     halves = master.astype(bf16).reshape(shard_rows, NC, half)
     cut = halves[:, :, :wide].transpose(1, 0, 2)
     cut = jnp.broadcast_to(cut[None], (NZ,) + cut.shape).reshape(NZ * NC, shard_rows, wide)
     block = exchange(cut, ("z", "core")).reshape(y_rows, wide)
+    digit = 256
+    pieces = [targets // digit, targets % digit, loss_mask]
+    pieces = [p.astype(f32) for p in pieces] + split(prior_lse, 3) + split(prior_target, 2)
+    small = jnp.concatenate(
+        [jnp.stack(pieces[:4], 0), jnp.stack(pieces[4:], 0)], 1
+    ).astype(bf16)
     near_b = lax.dynamic_index_in_dim(halves[:, :, wide:], core, 1, keepdims=False)
     far_b = lax.dynamic_index_in_dim(halves[:, :, wide:], 1 - core, 1, keepdims=False)
-    chip_b = pair(near_b, lax.ppermute(far_b, "core", SWAP), core == 0, 0)
+    near_b = jnp.concatenate([near_b, small], 1)
+    far_b = jnp.concatenate([far_b, small], 1)
+    far_b = lax.ppermute(far_b, "core", SWAP)
+    chip_b = pair(near_b, far_b, core == 0, 0)
     chips_b = jnp.stack([chip_b] + [shift(chip_b, "y", NY, s) for s in range(1, NY)], 0)
     head_a = jnp.concatenate([block] + [shift(block, "y", NY, s) for s in range(1, NY)], 0)
-    head_b = spread(chips_b, "z", NZ).transpose(1, 0, 2, 3).reshape(group_rows, thin)
+    part_b = spread(chips_b, "z", NZ)
+    head_b = part_b[..., :thin].transpose(1, 0, 2, 3).reshape(group_rows, thin)
     head = jnp.concatenate([head_a, head_b], 1)
+    small = part_b[..., thin:]
 
     own_half = lax.dynamic_slice_in_dim(hidden_states, core * half, half, 1)
     far_half = lax.dynamic_slice_in_dim(hidden_states, (1 - core) * half, half, 1)
     mate_half = lax.ppermute(far_half, "core", SWAP)
     tokens = jnp.concatenate([own_half, mate_half], 0)
 
-    small = jnp.concatenate(
-        [
-            targets.astype(f32).reshape(2, span),
-            loss_mask.astype(f32).reshape(2, span),
-            prior_lse.reshape(2, span),
-            prior_target.reshape(2, span),
-        ],
-        0,
-    )
-    small = gather(small)
-    small = small.reshape(ctx_count, 4, 2, span)
-    token_count = jnp.sum(small[:, 1])
-    pieces = []
+    masks = small.reshape(NZ, NY, NC, shard_rows, 2 * tok_rows)[:, :, :, 2, :tok_rows]
+    token_count = jnp.sum(masks.astype(f32))
+    found = []
     for offset in (0, 1):
         sid = span_order[2 * ctx_place + offset]
-        piece = lax.dynamic_slice(small, (sid // 2, 0, sid % 2, 0), (1, 4, 1, span))
-        pieces.append(piece.reshape(4, span))
-    rows = jnp.concatenate(pieces, 1)
-    tgt_rows = rows[0].astype(jnp.int32)
-    mask_rows, prior_rows, outside = rows[1], rows[2], rows[3]
+        owner = sid // 2
+        at_y, at_z, at_core = owner // (NZ * NC), owner // NC % NZ, owner % NC
+        start = [at_z, (y_place - at_y) % NY, at_core * shard_rows]
+        for side in (0, 1):
+            lane = side * tok_rows + sid % 2 * span
+            found.append(
+                lax.dynamic_slice(small, start + [lane], (1, 1, shard_rows, span)).reshape(
+                    shard_rows, span
+                )
+            )
+    rows_a = jnp.concatenate([found[0], found[2]], 1).astype(f32)
+    rows_b = jnp.concatenate([found[1], found[3]], 1).astype(f32)
+    tgt_rows = (rows_a[0] * digit + rows_a[1]).astype(jnp.int32)
+    mask_rows = rows_a[2]
+    prior_rows = rows_a[3] + rows_b[0] + rows_b[1]
+    outside = rows_b[2] + rows_b[3]
 
     def score(tok):
         return lax.dot_general(head, tok, (((1,), (1,)), ((), ())), preferred_element_type=f32)
 
-    mate_part = lax.ppermute(score(mate_half), "core", SWAP)
+    mate_part = score(mate_half)
+    mate_head = lax.ppermute(head, "core", SWAP)
+    mate_part = lax.ppermute(mate_part, "core", SWAP)
     logits = score(own_half) + mate_part
 
     local_col = tgt_rows - block_total - vocab_place * group_rows
@@ -170,10 +181,9 @@
         core == 0, jnp.concatenate([near, mate], 1), jnp.concatenate([mate, near], 1)
     )
 
-    mate_head = lax.ppermute(head, "core", SWAP)
     width = feat // vocab_count
     per_half = vocab_count // NC
-    hidden_sum = jnp.zeros((tok_rows, width), f32)
+    hidden_parts = []
     for s in range(vocab_count - 1, -1, -1):
         q = (vocab_place + s) % vocab_count
         at = (q % per_half) * width
@@ -182,13 +192,14 @@
             lax.dynamic_slice_in_dim(head, at, width, 1),
             lax.dynamic_slice_in_dim(mate_head, at, width, 1),
         )
+        side = lax.optimization_barrier(side)
         part = lax.dot_general(
             dlogits, side, (((0,), (0,)), ((), ())), preferred_element_type=f32
         ).astype(bf16)
         if s:
             part = shift(part, "vocab", vocab_count, s)
-        hidden_sum = hidden_sum + part.astype(f32)
-    hidden_grad = hidden_sum.astype(bf16)
+        hidden_parts.append(part)
+    hidden_grad = sum(part.astype(f32) for part in hidden_parts).astype(bf16)
 
     per_span = vocab_count // 2
     slot_ids = jnp.arange(span_order.shape[0], dtype=jnp.int32)

time: 193 us -> 204 us (1.057)
  waiting for transfers between devices: 57.8 us -> 71.9 us
  starting transfers between devices: 79.4 us -> 70.4 us
  other arithmetic: 10.7 us -> 18.5 us
  matrix products: 18.9 us -> 14.9 us
    all_to_all x5, waiting for transfers between devices: 24.2 us -> 57.6 us  [exchange(): return lax.all_to_all(x, axes, 0, 0, tiled=True)]
    ppermute x8 -> x2, starting transfers between devices: 21.8 us -> 5.47 us  [the longest x1 3.29 us: step(): far_b = lax.ppermute(far_b, 'core', SWAP)]
    ppermute x8 -> x2, waiting for transfers between devices: 16.8 us -> 1.07 us  [the longest x1 1.07 us: step(): mate_part = lax.ppermute(mate_part, 'core', SWAP)]
    ppermute x18, starting transfers between devices: 22.4 us -> 29.6 us  [shift(): lax.ppermute(x, axis, [(i, (i + step) % count) for i in range(count)])]
    dot_general x4, matrix products: 11.9 us -> 6.79 us  [step(): lax.dot_general(dlogits, side, (((0,), (0,)), ((), ())), preferred_elemen...]
    select_n x0 -> x1, other arithmetic: none -> 4.04 us  [step(): jnp.where(q // per_half == core, lax.dynamic_slice_in_dim(head, at, width...]
    another operation x0 -> x4, other arithmetic: none -> 2.75 us
    ppermute x18, waiting for transfers between devices: 15.8 us -> 13.2 us  [shift(): lax.ppermute(x, axis, [(i, (i + step) % count) for i in range(count)])]
  transfers between devices with their start and end apart: 35 -> 29, of which waited for: 13 -> 11; matrix products, arithmetic and copies ran while one was open for 18% -> 16% of each run, Pallas kernels for 0% -> 0%
where the time goes in v4:
time: 204 us; the launch traced here: 203 us
  waiting for transfers between devices  71.9 us (35%)
  starting transfers between devices  70.4 us (35%)
  other arithmetic  18.5 us (9%)
  local copies, waits for them, and re-layouts  15.1 us (7%)
  matrix products  14.9 us (7%)
  between operations  11.8 us (6%)
    all_to_all x5, waiting for transfers between devices, exchange(): return lax.all_to_all(x, axes, 0, 0, tiled=True)  57.6 us
    all_to_all x5, starting transfers between devices, exchange(): return lax.all_to_all(x, axes, 0, 0, tiled=True)  31.4 us
    ppermute x18, starting transfers between devices, shift(): lax.ppermute(x, axis, [(i, (i + step) % count) for i in range(count)])  29.6 us
    ppermute x18, waiting for transfers between devices, shift(): lax.ppermute(x, axis, [(i, (i + step) % count) for i in range(count)])  13.2 us
    dot_general x4, matrix products, step(): lax.dot_general(dlogits, side, (((0,), (0,)), ((), ())), preferred_elemen...  6.79 us
    dynamic_slice x1, local copies, waits for them, and re-layouts, step(): own_half = lax.dynamic_slice_in_dim(hidden_states, core * half, half, 1)  4.69 us
    dot_general x2, matrix products, score(): lax.dot_general(head, tok, (((1,), (1,)), ((), ())), preferred_element_ty...  4.67 us
  transfers between devices with their start and end apart: 29, of which 11 were waited for; matrix products, arithmetic and copies ran while one was open for 16% of the time, Pallas kernels for 0%

profile of v4, /device:TPU:1, one launch (start us, length us, event | category | flops | bytes accessed | tf_op | source)
XLA Modules:
  0.0 202.7 jit_solution(14305981117444156274)
XLA Ops:
  4.4 3.3 %collective-permute-start = (bf16[4,1280]{1,0:T(4,128)(2,1)S(1)}, bf16[4,1280]{1,0:T(4,128)(2,1)S(1)}, u32[]{:S(2)}, u32[]{:S(2)}) collective-permute-start(bf16[4,1280]{1,0:T(4,128)(2,1)S(1)} %get-tuple-element.48), channel_id=1, source_target_pairs={{0,4},{4,0},{1,5},{5,1},{2,6},{6,2},{3,7},{7,3},{8,12},{12,8},{9,1... | collective-permute-start | bytes 30728 | tf_op jit(solution)/shard_map/ppermute | solution.py:81
  8.7 6.9 %all-to-all-start.1 = ((bf16[16,4,3328]{2,1,0:T(4,128)(2,1)}), bf16[16,4,3328]{2,1,0:T(4,128)(2,1)S(1)}, u32[]{:S(2)}, u32[]{:S(2)}) async-start(bf16[16,4,3328]{2,1,0:T(4,128)(2,1)} %bitcast.17), calls=%async_computation.1 | async-start | bytes 851968 | tf_op jit(solution)/shard_map/all_to_all | solution.py:24
  15.6 4.7 %constant_dynamic-slice_fusion.3 = (bf16[256,4096]{1,0:T(8,128)(2,1)}, bf16[256,4096]{1,0:T(8,128)(2,1)}) fusion(bf16[256,8192]{1,0:T(8,128)(2,1)} %param.9, s32[]{:T(128)S(6)} %select_n.406, s32[]{:T(128)S(6)} %select_n.407), kind=kLoop, calls=%fused_computation.72 | loop fusion | bytes 8388616 | tf_op jit(solution)/shard_map/dynamic_slice | solution.py:90
  21.9 2.6 %collective-permute-start.2 = (bf16[8,1280]{1,0:T(8,128)(2,1)S(1)}, bf16[8,1280]{1,0:T(8,128)(2,1)S(1)}, u32[]{:S(2)}, u32[]{:S(2)}) collective-permute-start(bf16[8,1280]{1,0:T(8,128)(2,1)S(1)} %maximum_select_fusion.2), channel_id=1, source_target_pairs={{0,128},{64,192},{128,0},{192,64},{1,129},{65,193},{129,1},{193,65... | collective-permute-start | bytes 61448 | tf_op jit(solution)/shard_map/ppermute | solution.py:28
  27.4 3.4 %all-to-all-done.1 = bf16[16,4,3328]{2,1,0:T(4,128)(2,1)S(1)} async-done(((bf16[16,4,3328]{2,1,0:T(4,128)(2,1)}), bf16[16,4,3328]{2,1,0:T(4,128)(2,1)S(1)}, u32[]{:S(2)}, u32[]{:S(2)}) %all-to-all-start.1) | async-done | bytes 426016 | tf_op jit(solution)/shard_map/all_to_all | solution.py:24
  31.7 3.5 %all-to-all-start = ((bf16[8,4,8,1280]{3,2,1,0:T(8,128)(2,1)}), bf16[8,4,8,1280]{3,2,1,0:T(8,128)(2,1)S(1)}, u32[]{:S(2)}, u32[]{:S(2)}) async-start(bf16[8,4,8,1280]{3,2,1,0:T(8,128)(2,1)} %broadcast_in_dim.14), calls=%async_computation | async-start | bytes 1310720 | tf_op jit(solution)/shard_map/all_to_all | solution.py:24
  42.8 2.6 %collective-permute-start.5 = (bf16[64,3328]{1,0:T(8,128)(2,1)S(1)}, bf16[64,3328]{1,0:T(8,128)(2,1)S(1)}, u32[]{:S(2)}, u32[]{:S(2)}) collective-permute-start(bf16[64,3328]{1,0:T(8,128)(2,1)S(1)} %reshape.137), channel_id=1, source_target_pairs={{0,128},{64,192},{128,0},{192,64},{1,129},{65,193},{129,1},{193,65... | collective-permute-start | bytes 1277960 | tf_op jit(solution)/shard_map/ppermute | solution.py:28
  46.5 7.9 %all-to-all-done = bf16[8,4,8,1280]{3,2,1,0:T(8,128)(2,1)S(1)} async-done(((bf16[8,4,8,1280]{3,2,1,0:T(8,128)(2,1)}), bf16[8,4,8,1280]{3,2,1,0:T(8,128)(2,1)S(1)}, u32[]{:S(2)}, u32[]{:S(2)}) %all-to-all-start) | async-done | bytes 655392 | tf_op jit(solution)/shard_map/all_to_all | solution.py:24
  54.7 8.6 %collective-permute-done.5 = bf16[64,3328]{1,0:T(8,128)(2,1)S(1)} collective-permute-done((bf16[64,3328]{1,0:T(8,128)(2,1)S(1)}, bf16[64,3328]{1,0:T(8,128)(2,1)S(1)}, u32[]{:S(2)}, u32[]{:S(2)}) %collective-permute-start.5) | collective-permute-done | bytes 426016 | tf_op jit(solution)/shard_map/ppermute | solution.py:28
  64.8 2.2 %pad_maximum_fusion = bf16[256,4096]{1,0:T(8,128)(2,1)S(1)} fusion(bf16[256,768]{1,0:T(8,128)(2,1)S(1)} %bitcast.88, bf16[64,3328]{1,0:T(8,128)(2,1)} %copy-done.3, bf16[64,3328]{1,0:T(8,128)(2,1)} %copy-done.2, bf16[64,3328]{1,0:T(8,128)(2,1)S(1)} %collective-permute-done.4, bf16[64,3328]{1,0:T(8,128)(2,1)S(1)} %reshape.137), kind=kLoop, calls=%fused_computation.9 | loop fusion | flops 10485760 | bytes 4194304 | tf_op jit(solution)/shard_map/concatenate | solution.py:87
  67.0 2.3 %fusion.43 = f32[256,256]{1,0:T(8,128)S(1)} fusion(bf16[256,4096]{1,0:T(8,128)(2,1)S(1)} %pad_maximum_fusion, bf16[256,4096]{1,0:T(8,128)(2,1)} %collective-permute-done.7), kind=kOutput, calls=%fused_computation.142 | convolution fusion | flops 536870912 | bytes 4456448 | tf_op jit(solution)/shard_map/dot_general | solution.py:118
  69.3 2.2 %collective-permute-start.8 = (f32[256,256]{1,0:T(8,128)S(1)}, f32[256,256]{1,0:T(8,128)S(1)}, u32[]{:S(2)}, u32[]{:S(2)}) collective-permute-start(f32[256,256]{1,0:T(8,128)S(1)} %fusion.43), channel_id=1, source_target_pairs={{0,4},{4,0},{1,5},{5,1},{2,6},{6,2},{3,7},{7,3},{8,12},{12,8},{9,1... | collective-permute-start | bytes 786440 | tf_op jit(solution)/shard_map/ppermute | solution.py:122
  72.7 2.3 %fusion.42 = (f32[256]{0:T(256)S(1)}, f32[256,256]{1,0:T(8,128)S(1)}) fusion(f32[256,256]{1,0:T(8,128)S(1)} %collective-permute-done.8, bf16[256,4096]{1,0:T(8,128)(2,1)S(1)} %pad_maximum_fusion, bf16[256,4096]{1,0:T(8,128)(2,1)} %get-tuple-element.27), kind=kOutput, calls=%fused_computation.141 | convolution fusion | flops 537001728 | bytes 4719616 | tf_op jit(solution)/shard_map/dot_general | solution.py:118
  75.3 2.8 %collective-permute-start.10 = (f32[3,256]{1,0:T(4,128)S(1)}, f32[3,256]{1,0:T(4,128)S(1)}, u32[]{:S(2)}, u32[]{:S(2)}) collective-permute-start(f32[3,256]{1,0:T(4,128)S(1)} %pad_maximum_fusion.6), channel_id=1, source_target_pairs={{0,2},{1,3},{2,0},{3,1},{4,6},{5,7},{6,4},{7,5},{8,10},{9,11},{10,... | collective-permute-start | bytes 9224 | tf_op jit(solution)/shard_map/ppermute | solution.py:28
  78.5 2.4 %collective-permute-start.9 = (f32[3,256]{1,0:T(4,128)S(1)}, f32[3,256]{1,0:T(4,128)S(1)}, u32[]{:S(2)}, u32[]{:S(2)}) collective-permute-start(f32[3,256]{1,0:T(4,128)S(1)} %pad_maximum_fusion.6), channel_id=1, source_target_pairs={{0,3},{1,0},{2,1},{3,2},{4,7},{5,4},{6,5},{7,6},{8,11},{9,8},{10,9... | collective-permute-start | bytes 9224 | tf_op jit(solution)/shard_map/ppermute | solution.py:28
  86.4 3.5 %convolution_convert_fusion = bf16[256,4096]{1,0:T(8,128)(2,1)S(1)} fusion(bf16[256,4096]{1,0:T(8,128)(2,1)} %collective-permute-done.7, bf16[256,4096]{1,0:T(8,128)(2,1)} %get-tuple-element.27, bf16[256,256]{1,0:T(8,128)(2,1)S(1)} %collective-permute-done.12, bf16[256,256]{1,0:T(8,128)(2,1)S(1)} %multiply_convert_fusion), kind=kOutput, calls=%fused_computation | convolution fusion | flops 1083703296 | bytes 6553600 | tf_op jit(solution)/shard_map/dot_general | solution.py:157
  92.0 6.5 %all-to-all-start.3 = ((bf16[8,4,8,768]{3,2,1,0:T(8,128)(2,1)}), bf16[8,4,8,768]{3,2,1,0:T(8,128)(2,1)S(1)}, u32[]{:S(2)}, u32[]{:S(2)}) async-start(bf16[8,4,8,768]{3,2,1,0:T(8,128)(2,1)} %bitcast.87), calls=%async_computation.3 | async-start | bytes 786432 | tf_op jit(solution)/shard_map/all_to_all | solution.py:24
  98.6 2.1 %fusion.40 = (bf16[64,3328]{1,0:T(8,128)(2,1)}, bf16[64,3328]{1,0:T(8,128)(2,1)S(1)}, bf16[64,3328]{1,0:T(8,128)(2,1)S(1)}) fusion(bf16[256,4096]{1,0:T(8,128)(2,1)} %copy-done), kind=kLoop, calls=%fused_computation.139 | loop fusion | bytes 2555904 | tf_op jit(solution)/shard_map/slice | solution.py:158
  103.1 10.5 %all-to-all-done.3 = bf16[8,4,8,768]{3,2,1,0:T(8,128)(2,1)S(1)} async-done(((bf16[8,4,8,768]{3,2,1,0:T(8,128)(2,1)}), bf16[8,4,8,768]{3,2,1,0:T(8,128)(2,1)S(1)}, u32[]{:S(2)}, u32[]{:S(2)}) %all-to-all-start.3) | async-done | bytes 393248 | tf_op jit(solution)/shard_map/all_to_all | solution.py:24
  115.8 5.9 %collective-permute-start.18 = (bf16[8,768]{1,0:T(8,128)(2,1)S(1)}, bf16[8,768]{1,0:T(8,128)(2,1)S(1)}, u32[]{:S(2)}, u32[]{:S(2)}) collective-permute-start(bf16[8,768]{1,0:T(8,128)(2,1)S(1)} %get-tuple-element.39), channel_id=1, source_target_pairs={{0,64},{64,128},{128,192},{192,0},{1,65},{65,129},{129,193},{193,1... | collective-permute-start | bytes 36872 | tf_op jit(solution)/shard_map/ppermute | solution.py:28
  121.7 2.7 %collective-permute-done.15 = bf16[64,3328]{1,0:T(8,128)(2,1)} collective-permute-done((bf16[64,3328]{1,0:T(8,128)(2,1)S(1)}, bf16[64,3328]{1,0:T(8,128)(2,1)}, u32[]{:S(2)}, u32[]{:S(2)}) %collective-permute-start.15) | collective-permute-done | bytes 426016 | tf_op jit(solution)/shard_map/ppermute | solution.py:28
  124.4 2.4 %fusion.4 = bf16[8,8,3328]{2,1,0:T(8,128)(2,1)} fusion(bf16[64,3328]{1,0:T(8,128)(2,1)} %collective-permute-done.15, bf16[64,3328]{1,0:T(8,128)(2,1)} %collective-permute-done.14, bf16[64,3328]{1,0:T(8,128)(2,1)} %collective-permute-done.13, bf16[256,4096]{1,0:T(8,128)(2,1)} %copy-done), kind=kLoop, calls=%fused_computation.18 | loop fusion | flops 1703936 | bytes 2129920 | tf_op jit(solution)/shard_map/reshape | solution.py:162
  126.7 6.6 %all-to-all-start.2 = ((bf16[8,8,3328]{2,1,0:T(8,128)(2,1)}), bf16[8,8,3328]{2,1,0:T(8,128)(2,1)}, u32[]{:S(2)}, u32[]{:S(2)}) async-start(bf16[8,8,3328]{2,1,0:T(8,128)(2,1)} %fusion.4), calls=%async_computation.2 | async-start | bytes 851968 | tf_op jit(solution)/shard_map/all_to_all | solution.py:24
  133.4 4.0 %dynamic-slice_select_fusion.3 = (bf16[256,2048]{1,0:T(8,128)(2,1)S(1)}, bf16[256,2048]{1,0:T(8,128)(2,1)S(1)}, bf16[256,2048]{1,0:T(8,128)(2,1)S(1)}, bf16[256,2048]{1,0:T(8,128)(2,1)S(1)}) fusion(bf16[256,4096]{1,0:T(8,128)(2,1)} %collective-permute-done.19, s32[]{:T(128)S(6)} %select_n.448, bf16[256,4096]{1,0:T(8,128)(2,1)S(1)} %pad_maximum_fusion, ...), kind=kLoop, calls=%fused_computation.15 | loop fusion | flops 2097152 | bytes 12582932 | tf_op jit(solution)/shard_map/jit(_where)/select_n | solution.py:190
  138.0 3.0 %collective-permute-start.20 = (bf16[256,2048]{1,0:T(8,128)(2,1)S(1)}, bf16[256,2048]{1,0:T(8,128)(2,1)}, u32[]{:S(2)}, u32[]{:S(2)}) collective-permute-start(bf16[256,2048]{1,0:T(8,128)(2,1)S(1)} %convolution_convert_fusion.4), channel_id=1, source_target_pairs={{0,3},{1,0},{2,1},{3,2},{4,7},{5,4},{6,5},{7,6},{8,11},{9,8},{10,9... | collective-permute-start | bytes 3145736 | tf_op jit(solution)/shard_map/ppermute | solution.py:28
  141.0 1.5 convolution_convert_fusion.3
  142.5 1.4 convolution_convert_fusion.2
  144.5 4.8 %all-to-all-done.2 = bf16[8,8,3328]{2,1,0:T(8,128)(2,1)} async-done(((bf16[8,8,3328]{2,1,0:T(8,128)(2,1)}), bf16[8,8,3328]{2,1,0:T(8,128)(2,1)}, u32[]{:S(2)}, u32[]{:S(2)}) %all-to-all-start.2) | async-done | bytes 426016 | tf_op jit(solution)/shard_map/all_to_all | solution.py:24
  152.4 7.8 %all-to-all-start.4 = ((f32[256,1,128]{2,1,0:T(1,128)}), f32[256,1,128]{2,1,0:T(1,128)S(1)}, u32[]{:S(2)}, u32[]{:S(2)}) async-start(f32[256,1,128]{2,1,0:T(1,128)} %broadcast_in_dim.17), calls=%async_computation.4 | async-start | bytes 262144 | tf_op jit(solution)/shard_map/all_to_all | solution.py:24
  160.3 2.2 %collective-permute-start.23 = (f32[4,4096]{1,0:T(4,128)S(1)}, f32[4,4096]{1,0:T(4,128)S(1)}, u32[]{:S(2)}, u32[]{:S(2)}) collective-permute-start(f32[4,4096]{1,0:T(4,128)S(1)} %get-tuple-element.36), channel_id=1, source_target_pairs={{0,4},{4,0},{1,5},{5,1},{2,6},{6,2},{3,7},{7,3},{8,12},{12,8},{9,1... | collective-permute-start | bytes 196616 | tf_op jit(solution)/shard_map/ppermute | solution.py:179
  162.5 31.0 %all-to-all-done.4 = f32[256,1,128]{2,1,0:T(1,128)S(1)} async-done(((f32[256,1,128]{2,1,0:T(1,128)}), f32[256,1,128]{2,1,0:T(1,128)S(1)}, u32[]{:S(2)}, u32[]{:S(2)}) %all-to-all-start.4) | async-done | bytes 131104 | tf_op jit(solution)/shard_map/all_to_all | solution.py:24
  198.1 3.4 %add_convert_fusion = bf16[256,2048]{1,0:T(8,128)(2,1)} fusion(bf16[256,2048]{1,0:T(8,128)(2,1)} %collective-permute-done.22, bf16[256,2048]{1,0:T(8,128)(2,1)} %collective-permute-done.21, bf16[256,2048]{1,0:T(8,128)(2,1)} %collective-permute-done.20, bf16[256,256]{1,0:T(8,128)(2,1)S(1)} %multiply_convert_fusion, bf16[256,2048]{1,0:T(8,128)(2,1)S(1)} %get-tuple-element.24), kind=kOutput, calls=%fused_computation.10 | convolution fusion | flops 273154048 | bytes 5373952 | tf_op jit(solution)/shard_map/dot_general | solution.py:196
  (123 shorter events, 33.5 us)
Async XLA Ops:
  4.4 16.0 %collective-permute-start = (bf16[4,1280]{1,0:T(4,128)(2,1)S(1)}, bf16[4,1280]{1,0:T(4,128)(2,1)S(1)}, u32[]{:S(2)}, u32[]{:S(2)}) collective-permute-start(bf16[4,1280]{1,0:T(4,128)(2,1)S(1)} %get-tuple-element.48), channel_id=1, source_target_pairs={{0,4},{4,0},{1,5},{5,1},{2,6},{6,2},{3,7},{7,3},{8,12},{12,8},{9,1... | collective-permute-start | bytes 30728 | tf_op jit(solution)/shard_map/ppermute | solution.py:81
  8.7 22.1 %all-to-all-start.1 = ((bf16[16,4,3328]{2,1,0:T(4,128)(2,1)}), bf16[16,4,3328]{2,1,0:T(4,128)(2,1)S(1)}, u32[]{:S(2)}, u32[]{:S(2)}) async-start(bf16[16,4,3328]{2,1,0:T(4,128)(2,1)} %bitcast.17), calls=%async_computation.1 | async-start | bytes 851968 | tf_op jit(solution)/shard_map/all_to_all | solution.py:24
  20.3 46.7 %collective-permute-start.7 = (bf16[256,4096]{1,0:T(8,128)(2,1)}, bf16[256,4096]{1,0:T(8,128)(2,1)}, u32[]{:S(2)}, u32[]{:S(2)}) collective-permute-start(bf16[256,4096]{1,0:T(8,128)(2,1)} %get-tuple-element.28), channel_id=1, source_target_pairs={{0,4},{4,0},{1,5},{5,1},{2,6},{6,2},{3,7},{7,3},{8,12},{12,8},{9,1... | collective-permute-start | bytes 6291464 | tf_op jit(solution)/shard_map/ppermute | solution.py:92
  20.5 5.1 %collective-permute-start.1 = (bf16[8,1280]{1,0:T(8,128)(2,1)S(1)}, bf16[8,1280]{1,0:T(8,128)(2,1)S(1)}, u32[]{:S(2)}, u32[]{:S(2)}) collective-permute-start(bf16[8,1280]{1,0:T(8,128)(2,1)S(1)} %maximum_select_fusion.2), channel_id=1, source_target_pairs={{0,64},{64,128},{128,192},{192,0},{1,65},{65,129},{129,193},{193,1... | collective-permute-start | bytes 61448 | tf_op jit(solution)/shard_map/ppermute | solution.py:28
  21.9 4.4 %collective-permute-start.2 = (bf16[8,1280]{1,0:T(8,128)(2,1)S(1)}, bf16[8,1280]{1,0:T(8,128)(2,1)S(1)}, u32[]{:S(2)}, u32[]{:S(2)}) collective-permute-start(bf16[8,1280]{1,0:T(8,128)(2,1)S(1)} %maximum_select_fusion.2), channel_id=1, source_target_pairs={{0,128},{64,192},{128,0},{192,64},{1,129},{65,193},{129,1},{193,65... | collective-permute-start | bytes 61448 | tf_op jit(solution)/shard_map/ppermute | solution.py:28
  24.5 2.9 %collective-permute-start.3 = (bf16[8,1280]{1,0:T(8,128)(2,1)S(1)}, bf16[8,1280]{1,0:T(8,128)(2,1)S(1)}, u32[]{:S(2)}, u32[]{:S(2)}) collective-permute-start(bf16[8,1280]{1,0:T(8,128)(2,1)S(1)} %maximum_select_fusion.2), channel_id=1, source_target_pairs={{0,192},{64,0},{128,64},{192,128},{1,193},{65,1},{129,65},{193,129... | collective-permute-start | bytes 61448 | tf_op jit(solution)/shard_map/ppermute | solution.py:28
  31.7 22.8 %all-to-all-start = ((bf16[8,4,8,1280]{3,2,1,0:T(8,128)(2,1)}), bf16[8,4,8,1280]{3,2,1,0:T(8,128)(2,1)S(1)}, u32[]{:S(2)}, u32[]{:S(2)}) async-start(bf16[8,4,8,1280]{3,2,1,0:T(8,128)(2,1)} %broadcast_in_dim.14), calls=%async_computation | async-start | bytes 1310720 | tf_op jit(solution)/shard_map/all_to_all | solution.py:24
  41.4 13.2 %collective-permute-start.4 = (bf16[64,3328]{1,0:T(8,128)(2,1)S(1)}, bf16[64,3328]{1,0:T(8,128)(2,1)S(1)}, u32[]{:S(2)}, u32[]{:S(2)}) collective-permute-start(bf16[64,3328]{1,0:T(8,128)(2,1)S(1)} %reshape.137), channel_id=1, source_target_pairs={{0,64},{64,128},{128,192},{192,0},{1,65},{65,129},{129,193},{193,1... | collective-permute-start | bytes 1277960 | tf_op jit(solution)/shard_map/ppermute | solution.py:28
  42.8 20.4 %collective-permute-start.5 = (bf16[64,3328]{1,0:T(8,128)(2,1)S(1)}, bf16[64,3328]{1,0:T(8,128)(2,1)S(1)}, u32[]{:S(2)}, u32[]{:S(2)}) collective-permute-start(bf16[64,3328]{1,0:T(8,128)(2,1)S(1)} %reshape.137), channel_id=1, source_target_pairs={{0,128},{64,192},{128,0},{192,64},{1,129},{65,193},{129,1},{193,65... | collective-permute-start | bytes 1277960 | tf_op jit(solution)/shard_map/ppermute | solution.py:28
  45.4 17.9 %collective-permute-start.6 = (bf16[64,3328]{1,0:T(8,128)(2,1)S(1)}, bf16[64,3328]{1,0:T(8,128)(2,1)S(1)}, u32[]{:S(2)}, u32[]{:S(2)}) collective-permute-start(bf16[64,3328]{1,0:T(8,128)(2,1)S(1)} %reshape.137), channel_id=1, source_target_pairs={{0,192},{64,0},{128,64},{192,128},{1,193},{65,1},{129,65},{193,129... | collective-permute-start | bytes 1277960 | tf_op jit(solution)/shard_map/ppermute | solution.py:28
  69.3 3.3 %collective-permute-start.8 = (f32[256,256]{1,0:T(8,128)S(1)}, f32[256,256]{1,0:T(8,128)S(1)}, u32[]{:S(2)}, u32[]{:S(2)}) collective-permute-start(f32[256,256]{1,0:T(8,128)S(1)} %fusion.43), channel_id=1, source_target_pairs={{0,4},{4,0},{1,5},{5,1},{2,6},{6,2},{3,7},{7,3},{8,12},{12,8},{9,1... | collective-permute-start | bytes 786440 | tf_op jit(solution)/shard_map/ppermute | solution.py:122
  75.3 6.9 %collective-permute-start.10 = (f32[3,256]{1,0:T(4,128)S(1)}, f32[3,256]{1,0:T(4,128)S(1)}, u32[]{:S(2)}, u32[]{:S(2)}) collective-permute-start(f32[3,256]{1,0:T(4,128)S(1)} %pad_maximum_fusion.6), channel_id=1, source_target_pairs={{0,2},{1,3},{2,0},{3,1},{4,6},{5,7},{6,4},{7,5},{8,10},{9,11},{10,... | collective-permute-start | bytes 9224 | tf_op jit(solution)/shard_map/ppermute | solution.py:28
  78.2 4.1 %collective-permute-start.11 = (f32[3,256]{1,0:T(4,128)S(1)}, f32[3,256]{1,0:T(4,128)S(1)}, u32[]{:S(2)}, u32[]{:S(2)}) collective-permute-start(f32[3,256]{1,0:T(4,128)S(1)} %pad_maximum_fusion.6), channel_id=1, source_target_pairs={{0,1},{1,2},{2,3},{3,0},{4,5},{5,6},{6,7},{7,4},{8,9},{9,10},{10,1... | collective-permute-start | bytes 9224 | tf_op jit(solution)/shard_map/ppermute | solution.py:28
  78.5 3.8 %collective-permute-start.9 = (f32[3,256]{1,0:T(4,128)S(1)}, f32[3,256]{1,0:T(4,128)S(1)}, u32[]{:S(2)}, u32[]{:S(2)}) collective-permute-start(f32[3,256]{1,0:T(4,128)S(1)} %pad_maximum_fusion.6), channel_id=1, source_target_pairs={{0,3},{1,0},{2,1},{3,2},{4,7},{5,4},{6,5},{7,6},{8,11},{9,8},{10,9... | collective-permute-start | bytes 9224 | tf_op jit(solution)/shard_map/ppermute | solution.py:28
  82.8 3.6 %collective-permute-start.12 = (bf16[256,256]{1,0:T(8,128)(2,1)S(1)}, bf16[256,256]{1,0:T(8,128)(2,1)S(1)}, u32[]{:S(2)}, u32[]{:S(2)}) collective-permute-start(bf16[256,256]{1,0:T(8,128)(2,1)S(1)} %multiply_convert_fusion), channel_id=1, source_target_pairs={{0,4},{4,0},{1,5},{5,1},{2,6},{6,2},{3,7},{7,3},{8,12},{12,8},{9,1... | collective-permute-start | bytes 393224 | tf_op jit(solution)/shard_map/ppermute | solution.py:154
  86.3 47.2 %collective-permute-start.19 = (bf16[256,4096]{1,0:T(8,128)(2,1)S(1)}, bf16[256,4096]{1,0:T(8,128)(2,1)}, u32[]{:S(2)}, u32[]{:S(2)}) collective-permute-start(bf16[256,4096]{1,0:T(8,128)(2,1)S(1)} %pad_maximum_fusion), channel_id=1, source_target_pairs={{0,4},{4,0},{1,5},{5,1},{2,6},{6,2},{3,7},{7,3},{8,12},{12,8},{9,1... | collective-permute-start | bytes 6291464 | tf_op jit(solution)/shard_map/ppermute | solution.py:121
  92.0 21.6 %all-to-all-start.3 = ((bf16[8,4,8,768]{3,2,1,0:T(8,128)(2,1)}), bf16[8,4,8,768]{3,2,1,0:T(8,128)(2,1)S(1)}, u32[]{:S(2)}, u32[]{:S(2)}) async-start(bf16[8,4,8,768]{3,2,1,0:T(8,128)(2,1)} %bitcast.87), calls=%async_computation.3 | async-start | bytes 786432 | tf_op jit(solution)/shard_map/all_to_all | solution.py:24
  100.7 14.2 %collective-permute-start.13 = (bf16[64,3328]{1,0:T(8,128)(2,1)}, bf16[64,3328]{1,0:T(8,128)(2,1)}, u32[]{:S(2)}, u32[]{:S(2)}) collective-permute-start(bf16[64,3328]{1,0:T(8,128)(2,1)} %get-tuple-element.29), channel_id=1, source_target_pairs={{0,192},{64,0},{128,64},{192,128},{1,193},{65,1},{129,65},{193,129... | collective-permute-start | bytes 1277960 | tf_op jit(solution)/shard_map/ppermute | solution.py:28
  101.8 14.0 %collective-permute-start.14 = (bf16[64,3328]{1,0:T(8,128)(2,1)S(1)}, bf16[64,3328]{1,0:T(8,128)(2,1)}, u32[]{:S(2)}, u32[]{:S(2)}) collective-permute-start(bf16[64,3328]{1,0:T(8,128)(2,1)S(1)} %get-tuple-element.31), channel_id=1, source_target_pairs={{0,128},{64,192},{128,0},{192,64},{1,129},{65,193},{129,1},{193,65... | collective-permute-start | bytes 1277960 | tf_op jit(solution)/shard_map/ppermute | solution.py:28
  102.6 21.7 %collective-permute-start.15 = (bf16[64,3328]{1,0:T(8,128)(2,1)S(1)}, bf16[64,3328]{1,0:T(8,128)(2,1)}, u32[]{:S(2)}, u32[]{:S(2)}) collective-permute-start(bf16[64,3328]{1,0:T(8,128)(2,1)S(1)} %get-tuple-element.30), channel_id=1, source_target_pairs={{0,64},{64,128},{128,192},{192,0},{1,65},{65,129},{129,193},{193,1... | collective-permute-start | bytes 1277960 | tf_op jit(solution)/shard_map/ppermute | solution.py:28
  113.7 19.7 %collective-permute-start.16 = (bf16[8,768]{1,0:T(8,128)(2,1)S(1)}, bf16[8,768]{1,0:T(8,128)(2,1)S(1)}, u32[]{:S(2)}, u32[]{:S(2)}) collective-permute-start(bf16[8,768]{1,0:T(8,128)(2,1)S(1)} %get-tuple-element.38), channel_id=1, source_target_pairs={{0,192},{64,0},{128,64},{192,128},{1,193},{65,1},{129,65},{193,129... | collective-permute-start | bytes 36872 | tf_op jit(solution)/shard_map/ppermute | solution.py:28
  114.9 18.5 %collective-permute-start.17 = (bf16[8,768]{1,0:T(8,128)(2,1)S(1)}, bf16[8,768]{1,0:T(8,128)(2,1)S(1)}, u32[]{:S(2)}, u32[]{:S(2)}) collective-permute-start(bf16[8,768]{1,0:T(8,128)(2,1)S(1)} %get-tuple-element.40), channel_id=1, source_target_pairs={{0,128},{64,192},{128,0},{192,64},{1,129},{65,193},{129,1},{193,65... | collective-permute-start | bytes 36872 | tf_op jit(solution)/shard_map/ppermute | solution.py:28
  115.8 17.6 %collective-permute-start.18 = (bf16[8,768]{1,0:T(8,128)(2,1)S(1)}, bf16[8,768]{1,0:T(8,128)(2,1)S(1)}, u32[]{:S(2)}, u32[]{:S(2)}) collective-permute-start(bf16[8,768]{1,0:T(8,128)(2,1)S(1)} %get-tuple-element.39), channel_id=1, source_target_pairs={{0,64},{64,128},{128,192},{192,0},{1,65},{65,129},{129,193},{193,1... | collective-permute-start | bytes 36872 | tf_op jit(solution)/shard_map/ppermute | solution.py:28
  126.7 22.5 %all-to-all-start.2 = ((bf16[8,8,3328]{2,1,0:T(8,128)(2,1)}), bf16[8,8,3328]{2,1,0:T(8,128)(2,1)}, u32[]{:S(2)}, u32[]{:S(2)}) async-start(bf16[8,8,3328]{2,1,0:T(8,128)(2,1)} %fusion.4), calls=%async_computation.2 | async-start | bytes 851968 | tf_op jit(solution)/shard_map/all_to_all | solution.py:24
  138.0 60.1 %collective-permute-start.20 = (bf16[256,2048]{1,0:T(8,128)(2,1)S(1)}, bf16[256,2048]{1,0:T(8,128)(2,1)}, u32[]{:S(2)}, u32[]{:S(2)}) collective-permute-start(bf16[256,2048]{1,0:T(8,128)(2,1)S(1)} %convolution_convert_fusion.4), channel_id=1, source_target_pairs={{0,3},{1,0},{2,1},{3,2},{4,7},{5,4},{6,5},{7,6},{8,11},{9,8},{10,9... | collective-permute-start | bytes 3145736 | tf_op jit(solution)/shard_map/ppermute | solution.py:28
  142.5 54.7 %copy-start.1 = (f32[4,8192]{1,0:T(4,128)S(1)}, f32[4,8192]{1,0:T(4,128)}, u32[]{:S(2)}) copy-start(f32[4,8192]{1,0:T(4,128)} %param.10) | copy-start | bytes 393220
  142.5 54.7 %copy-start.4 = (f32[4,8192]{1,0:T(4,128)S(1)}, f32[4,8192]{1,0:T(4,128)}, u32[]{:S(2)}) copy-start(f32[4,8192]{1,0:T(4,128)} %param.12) | copy-start | bytes 393220
  142.5 54.7 %copy-start.5 = (f32[4,8192]{1,0:T(4,128)S(1)}, f32[4,8192]{1,0:T(4,128)}, u32[]{:S(2)}) copy-start(f32[4,8192]{1,0:T(4,128)} %param.11) | copy-start | bytes 393220
  142.5 55.6 %collective-permute-start.21 = (bf16[256,2048]{1,0:T(8,128)(2,1)}, bf16[256,2048]{1,0:T(8,128)(2,1)}, u32[]{:S(2)}, u32[]{:S(2)}) collective-permute-start(bf16[256,2048]{1,0:T(8,128)(2,1)} %convolution_convert_fusion.3), channel_id=1, source_target_pairs={{0,2},{1,3},{2,0},{3,1},{4,6},{5,7},{6,4},{7,5},{8,10},{9,11},{10,... | collective-permute-start | bytes 3145736 | tf_op jit(solution)/shard_map/ppermute | solution.py:28
  143.9 54.2 %collective-permute-start.22 = (bf16[256,2048]{1,0:T(8,128)(2,1)}, bf16[256,2048]{1,0:T(8,128)(2,1)}, u32[]{:S(2)}, u32[]{:S(2)}) collective-permute-start(bf16[256,2048]{1,0:T(8,128)(2,1)} %convolution_convert_fusion.2), channel_id=1, source_target_pairs={{0,1},{1,2},{2,3},{3,0},{4,5},{5,6},{6,7},{7,4},{8,9},{9,10},{10,1... | collective-permute-start | bytes 3145736 | tf_op jit(solution)/shard_map/ppermute | solution.py:28
  152.4 41.1 %all-to-all-start.4 = ((f32[256,1,128]{2,1,0:T(1,128)}), f32[256,1,128]{2,1,0:T(1,128)S(1)}, u32[]{:S(2)}, u32[]{:S(2)}) async-start(f32[256,1,128]{2,1,0:T(1,128)} %broadcast_in_dim.17), calls=%async_computation.4 | async-start | bytes 262144 | tf_op jit(solution)/shard_map/all_to_all | solution.py:24
  160.3 36.9 %collective-permute-start.23 = (f32[4,4096]{1,0:T(4,128)S(1)}, f32[4,4096]{1,0:T(4,128)S(1)}, u32[]{:S(2)}, u32[]{:S(2)}) collective-permute-start(f32[4,4096]{1,0:T(4,128)S(1)} %get-tuple-element.36), channel_id=1, source_target_pairs={{0,4},{4,0},{1,5},{5,1},{2,6},{6,2},{3,7},{7,3},{8,12},{12,8},{9,1... | collective-permute-start | bytes 196616 | tf_op jit(solution)/shard_map/ppermute | solution.py:179
  (4 other events, 17.8 us)

commit v5 on v4

--- a/solution.py
+++ b/solution.py
@@ -62,8 +62,10 @@
     y_rows = group_rows // NY
     chip_rows = y_rows // NZ
 
-    thin = half * 3 // 16
+    thin = half // 8
     wide = half - thin
+    thin_g = half * 3 // 16
+    wide_g = half - thin_g
     halves = master.astype(bf16).reshape(shard_rows, NC, half)
     cut = halves[:, :, :wide].transpose(1, 0, 2)
     cut = jnp.broadcast_to(cut[None], (NZ,) + cut.shape).reshape(NZ * NC, shard_rows, wide)
@@ -83,6 +85,23 @@
     chips_b = jnp.stack([chip_b] + [shift(chip_b, "y", NY, s) for s in range(1, NY)], 0)
     head_a = jnp.concatenate([block] + [shift(block, "y", NY, s) for s in range(1, NY)], 0)
     part_b = spread(chips_b, "z", NZ)
+    sids = lax.dynamic_slice(
+        span_order, (2 * ctx_place,), (2,), allow_negative_indices=False
+    )
+    owner = sids >> 1
+    starts = [
+        (owner >> 1) & (NZ - 1),
+        (y_place - (owner >> 4)) & (NY - 1),
+        (owner & 1) * shard_rows,
+        (sids & 1) * span,
+    ]
+    starts = lax.optimization_barrier([[v[i] for v in starts] for i in (0, 1)])
+    slot_ids = jnp.arange(span_order.shape[0], dtype=jnp.int32)
+    slots = [
+        jnp.sum(jnp.where(span_order == 2 * ctx_place + offset, slot_ids, 0))
+        for offset in (0, 1)
+    ]
+    slots = lax.optimization_barrier([slot * (vocab_count // 2) for slot in slots])
     head_b = part_b[..., :thin].transpose(1, 0, 2, 3).reshape(group_rows, thin)
     head = jnp.concatenate([head_a, head_b], 1)
     small = part_b[..., thin:]
@@ -94,19 +113,16 @@
 
     masks = small.reshape(NZ, NY, NC, shard_rows, 2 * tok_rows)[:, :, :, 2, :tok_rows]
     token_count = jnp.sum(masks.astype(f32))
-    found = []
-    for offset in (0, 1):
-        sid = span_order[2 * ctx_place + offset]
-        owner = sid // 2
-        at_y, at_z, at_core = owner // (NZ * NC), owner // NC % NZ, owner % NC
-        start = [at_z, (y_place - at_y) % NY, at_core * shard_rows]
-        for side in (0, 1):
-            lane = side * tok_rows + sid % 2 * span
-            found.append(
-                lax.dynamic_slice(small, start + [lane], (1, 1, shard_rows, span)).reshape(
-                    shard_rows, span
-                )
-            )
+    found = [
+        lax.dynamic_slice(
+            small,
+            (at[0], at[1], at[2], at[3] + side * tok_rows),
+            (1, 1, shard_rows, span),
+            allow_negative_indices=False,
+        ).reshape(shard_rows, span)
+        for at in starts
+        for side in (0, 1)
+    ]
     rows_a = jnp.concatenate([found[0], found[2]], 1).astype(f32)
     rows_b = jnp.concatenate([found[1], found[3]], 1).astype(f32)
     tgt_rows = (rows_a[0] * digit + rows_a[1]).astype(jnp.int32)
@@ -124,7 +140,8 @@
 
     local_col = tgt_rows - block_total - vocab_place * group_rows
     vocab_ids = lax.broadcasted_iota(jnp.int32, (group_rows, tok_rows), 0)
-    vocab_ids = (y_place * y_rows - vocab_ids // y_rows * y_rows) % group_rows + vocab_ids % y_rows
+    within = vocab_ids & (y_rows - 1)
+    vocab_ids = ((y_place * y_rows - (vocab_ids - within)) & (group_rows - 1)) + within
     hits = vocab_ids == local_col[None, :]
     top_local = jnp.max(logits, axis=0)
     sum_local = jnp.sum(jnp.exp(logits - top_local[None, :]), axis=0)
@@ -155,12 +172,12 @@
 
     both = jnp.concatenate([dlogits, mate_dlogits], 1)
     partial_rows = jnp.dot(both, tokens, preferred_element_type=f32).astype(bf16)
-    blocks = [partial_rows[s * y_rows : (s + 1) * y_rows, :wide] for s in range(NY)]
+    blocks = [partial_rows[s * y_rows : (s + 1) * y_rows, :wide_g] for s in range(NY)]
     by_y = blocks[0].astype(f32)
     for s in range(1, NY):
         by_y = by_y + shift(blocks[s], "y", NY, -s).astype(f32)
-    by_y = by_y.astype(bf16).reshape(NZ, chip_rows, wide)
-    by_z = partial_rows[:, wide:].reshape(NY, NZ, chip_rows, thin).transpose(1, 0, 2, 3)
+    by_y = by_y.astype(bf16).reshape(NZ, chip_rows, wide_g)
+    by_z = partial_rows[:, wide_g:].reshape(NY, NZ, chip_rows, thin_g).transpose(1, 0, 2, 3)
     by_z = jnp.sum(exchange(by_z, "z").astype(f32), axis=0).astype(bf16)
     grad_b = by_z[0].astype(f32)
     for s in range(1, NY):
@@ -170,10 +187,11 @@
     square = jnp.sum(chip_grad * chip_grad)
     lanes = tok_rows // vocab_count
     share = lax.dynamic_slice_in_dim(loss_rows, vocab_place * lanes, lanes, 0)
-    report = jnp.concatenate([jnp.full((lanes,), square), share], 0)[None]
-    reports = spread(report, ALL, ctx_count * vocab_count)[:, 0]
-    square_sum = jnp.sum(reports[:, :lanes]) / lanes
-    mean_loss = jnp.sum(reports[:, lanes:]) / token_count
+    share = jnp.pad(share, (0, span - lanes))
+    report = jnp.concatenate([jnp.full((1, span), square), share[None]], 0)
+    reports = spread(report, ALL, ctx_count * vocab_count)
+    square_sum = jnp.sum(reports[:, 0], axis=0)
+    mean_loss = jnp.sum(reports[:, 1]) * (1.0 / token_count)
     near = lax.dynamic_slice_in_dim(chip_grad, core * shard_rows, shard_rows, 0)
     far = lax.dynamic_slice_in_dim(chip_grad, (1 - core) * shard_rows, shard_rows, 0)
     mate = lax.ppermute(far, "core", SWAP)
@@ -185,35 +203,40 @@
     per_half = vocab_count // NC
     hidden_parts = []
     for s in range(vocab_count - 1, -1, -1):
-        q = (vocab_place + s) % vocab_count
-        at = (q % per_half) * width
+        q = (vocab_place + s) & (vocab_count - 1)
+        at = (q & (per_half - 1)) * width
         side = jnp.where(
-            q // per_half == core,
-            lax.dynamic_slice_in_dim(head, at, width, 1),
-            lax.dynamic_slice_in_dim(mate_head, at, width, 1),
+            (q >= per_half) == (core == 1),
+            lax.dynamic_slice(head, (0, at), (group_rows, width), allow_negative_indices=False),
+            lax.dynamic_slice(
+                mate_head, (0, at), (group_rows, width), allow_negative_indices=False
+            ),
         )
-        side = lax.optimization_barrier(side)
+        if s == 2:
+            side = lax.optimization_barrier(side)
         part = lax.dot_general(
             dlogits, side, (((0,), (0,)), ((), ())), preferred_element_type=f32
         ).astype(bf16)
         if s:
             part = shift(part, "vocab", vocab_count, s)
+        else:
+            part = lax.optimization_barrier(part)
         hidden_parts.append(part)
     hidden_grad = sum(part.astype(f32) for part in hidden_parts).astype(bf16)
 
     per_span = vocab_count // 2
-    slot_ids = jnp.arange(span_order.shape[0], dtype=jnp.int32)
-    natural = []
-    for offset in (0, 1):
-        slot = jnp.sum(jnp.where(span_order == 2 * ctx_place + offset, slot_ids, 0))
-        natural.append(
-            lax.dynamic_slice(reports, (slot * per_span, lanes), (per_span, lanes)).reshape(span)
-        )
+    natural = [
+        lax.dynamic_slice(
+            reports, (slot, 1, 0), (per_span, 1, lanes), allow_negative_indices=False
+        ).reshape(span)
+        for slot in slots
+    ]
     token_loss = jnp.concatenate(natural, 0)
 
     norm_value = jnp.sqrt(square_sum) / loss_scale
     clip_factor = jnp.minimum(1.0, clip_norm / (norm_value + 1e-06))
-    clipped = row_grad * clip_factor
+    clip_factor = jnp.broadcast_to(clip_factor, (shard_rows, feat // span, span))
+    clipped = row_grad * clip_factor.reshape(shard_rows, feat)
     new_moment = beta_one * moment + (1.0 - beta_one) * clipped
     new_second = beta_two * second + (1.0 - beta_two) * clipped * clipped
     new_master = master - learn_rate * (

time: 204 us -> 199 us (0.975)
  starting transfers between devices: 70.4 us -> 61.9 us
  local copies, waits for them, and re-layouts: 15.1 us -> 20.7 us
  between operations: 11.8 us -> 6.92 us
    ppermute x18, starting transfers between devices: 29.6 us -> 19.4 us  [shift(): lax.ppermute(x, axis, [(i, (i + step) % count) for i in range(count)])]
    ppermute x18, waiting for transfers between devices: 13.2 us -> 20.3 us  [shift(): lax.ppermute(x, axis, [(i, (i + step) % count) for i in range(count)])]
    all_to_all x5, waiting for transfers between devices: 57.6 us -> 51.6 us  [exchange(): return lax.all_to_all(x, axes, 0, 0, tiled=True)]
    reshape x4, local copies, waits for them, and re-layouts: 1.06 us -> 6.24 us  [the longest x1 5.28 us: step(): found = [lax.dynamic_slice(small, (at[0], at[1], at[2], at[3] + side * to...]
    all_to_all x5, starting transfers between devices: 31.4 us -> 35.4 us  [exchange(): return lax.all_to_all(x, axes, 0, 0, tiled=True)]
    convert_element_type x0 -> x2, other arithmetic: none -> 3.21 us  [the longest x1 3.2 us: step(): hidden_grad = sum((part.astype(f32) for part in hidden_parts)).astype(bf16)]
    select_n x1, other arithmetic: 4.04 us -> 1.61 us  [step(): jnp.where((q >= per_half) == (core == 1), lax.dynamic_slice(head, (0, at)...]
  transfers between devices with their start and end apart: 29 -> 29, of which waited for: 11 -> 15; matrix products, arithmetic and copies ran while one was open for 16% -> 22% of each run, Pallas kernels for 0% -> 0%
where the time goes in v5:
time: 199 us; the launch traced here: 198 us
  waiting for transfers between devices  73 us (37%)
  starting transfers between devices  61.9 us (31%)
  local copies, waits for them, and re-layouts  20.7 us (10%)
  other arithmetic  19.5 us (10%)
  matrix products  15.5 us (8%)
  between operations  6.92 us (3%)
    all_to_all x5, waiting for transfers between devices, exchange(): return lax.all_to_all(x, axes, 0, 0, tiled=True)  51.6 us
    all_to_all x5, starting transfers between devices, exchange(): return lax.all_to_all(x, axes, 0, 0, tiled=True)  35.4 us
    ppermute x18, waiting for transfers between devices, shift(): lax.ppermute(x, axis, [(i, (i + step) % count) for i in range(count)])  20.3 us
    ppermute x18, starting transfers between devices, shift(): lax.ppermute(x, axis, [(i, (i + step) % count) for i in range(count)])  19.4 us
    dot_general x4, matrix products, step(): lax.dot_general(dlogits, side, (((0,), (0,)), ((), ())), preferred_elemen...  8.59 us
    reshape x1, local copies, waits for them, and re-layouts, step(): found = [lax.dynamic_slice(small, (at[0], at[1], at[2], at[3] + side * to...  5.28 us
    dynamic_slice x1, local copies, waits for them, and re-layouts, step(): own_half = lax.dynamic_slice_in_dim(hidden_states, core * half, half, 1)  4.69 us
  transfers between devices with their start and end apart: 29, of which 15 were waited for; matrix products, arithmetic and copies ran while one was open for 22% of the time, Pallas kernels for 0%

profile of v5, /device:TPU:1, one launch (start us, length us, event | category | flops | bytes accessed | tf_op | source)
XLA Modules:
  0.0 197.6 jit_solution(14352656644037387260)
XLA Ops:
  4.4 3.3 %collective-permute-start = (bf16[4,1024]{1,0:T(4,128)(2,1)S(1)}, bf16[4,1024]{1,0:T(4,128)(2,1)S(1)}, u32[]{:S(2)}, u32[]{:S(2)}) collective-permute-start(bf16[4,1024]{1,0:T(4,128)(2,1)S(1)} %get-tuple-element.66), channel_id=1, source_target_pairs={{0,4},{4,0},{1,5},{5,1},{2,6},{6,2},{3,7},{7,3},{8,12},{12,8},{9,1... | collective-permute-start | bytes 24584 | tf_op jit(solution)/shard_map/ppermute | solution.py:83
  8.8 6.9 %all-to-all-start.1 = ((bf16[16,4,3584]{2,1,0:T(4,128)(2,1)}), bf16[16,4,3584]{2,1,0:T(4,128)(2,1)S(1)}, u32[]{:S(2)}, u32[]{:S(2)}) async-start(bf16[16,4,3584]{2,1,0:T(4,128)(2,1)} %bitcast.23), calls=%async_computation.1 | async-start | bytes 917504 | tf_op jit(solution)/shard_map/all_to_all | solution.py:24
  15.7 4.7 %constant_dynamic-slice_fusion.3 = (bf16[256,4096]{1,0:T(8,128)(2,1)}, bf16[256,4096]{1,0:T(8,128)(2,1)}) fusion(bf16[256,8192]{1,0:T(8,128)(2,1)} %param.9, s32[]{:T(128)S(6)} %select_n.204, s32[]{:T(128)S(6)} %select_n.205), kind=kLoop, calls=%fused_computation.81 | loop fusion | bytes 8388616 | tf_op jit(solution)/shard_map/dynamic_slice | solution.py:109
  20.5 2.8 %collective-permute-start.3 = (bf16[8,1024]{1,0:T(8,128)(2,1)S(1)}, bf16[8,1024]{1,0:T(8,128)(2,1)S(1)}, u32[]{:S(2)}, u32[]{:S(2)}) collective-permute-start(bf16[8,1024]{1,0:T(8,128)(2,1)S(1)} %maximum_select_fusion.2), channel_id=1, source_target_pairs={{0,192},{64,0},{128,64},{192,128},{1,193},{65,1},{129,65},{193,129... | collective-permute-start | bytes 49160 | tf_op jit(solution)/shard_map/ppermute | solution.py:28
  24.4 3.0 %collective-permute-done.2 = bf16[8,1024]{1,0:T(8,128)(2,1)S(1)} collective-permute-done((bf16[8,1024]{1,0:T(8,128)(2,1)S(1)}, bf16[8,1024]{1,0:T(8,128)(2,1)S(1)}, u32[]{:S(2)}, u32[]{:S(2)}) %collective-permute-start.2) | collective-permute-done | bytes 16416 | tf_op jit(solution)/shard_map/ppermute | solution.py:28
  27.9 3.6 %all-to-all-done.1 = bf16[16,4,3584]{2,1,0:T(4,128)(2,1)S(1)} async-done(((bf16[16,4,3584]{2,1,0:T(4,128)(2,1)}), bf16[16,4,3584]{2,1,0:T(4,128)(2,1)S(1)}, u32[]{:S(2)}, u32[]{:S(2)}) %all-to-all-start.1) | async-done | bytes 458784 | tf_op jit(solution)/shard_map/all_to_all | solution.py:24
  32.4 3.5 %all-to-all-start = ((bf16[8,4,8,1024]{3,2,1,0:T(8,128)(2,1)}), bf16[8,4,8,1024]{3,2,1,0:T(8,128)(2,1)S(1)}, u32[]{:S(2)}, u32[]{:S(2)}) async-start(bf16[8,4,8,1024]{3,2,1,0:T(8,128)(2,1)} %broadcast_in_dim.42), calls=%async_computation | async-start | bytes 1048576 | tf_op jit(solution)/shard_map/all_to_all | solution.py:24
  39.3 2.8 %collective-permute-start.6 = (bf16[64,3584]{1,0:T(8,128)(2,1)S(1)}, bf16[64,3584]{1,0:T(8,128)(2,1)S(1)}, u32[]{:S(2)}, u32[]{:S(2)}) collective-permute-start(bf16[64,3584]{1,0:T(8,128)(2,1)S(1)} %reshape.133), channel_id=1, source_target_pairs={{0,192},{64,0},{128,64},{192,128},{1,193},{65,1},{129,65},{193,129... | collective-permute-start | bytes 1376264 | tf_op jit(solution)/shard_map/ppermute | solution.py:28
  43.2 9.2 %all-to-all-done = bf16[8,4,8,1024]{3,2,1,0:T(8,128)(2,1)S(1)} async-done(((bf16[8,4,8,1024]{3,2,1,0:T(8,128)(2,1)}), bf16[8,4,8,1024]{3,2,1,0:T(8,128)(2,1)S(1)}, u32[]{:S(2)}, u32[]{:S(2)}) %all-to-all-start) | async-done | bytes 524320 | tf_op jit(solution)/shard_map/all_to_all | solution.py:24
  52.5 5.3 %dynamic-slice_bitcast_fusion.1 = (bf16[4,128]{1,0:T(4,128)(2,1)S(1)}, bf16[4,128]{1,0:T(4,128)(2,1)S(1)}, bf16[4,128]{1,0:T(4,128)(2,1)S(1)}, bf16[4,128]{1,0:T(4,128)(2,1)S(1)}) fusion(bf16[8,4,8,512]{3,2,1,0:T(8,128)(2,1)S(1)} %get-tuple-element.51, s32[]{:T(128)} %bitcast.8, s32[]{:T(128)} %bitcast.9, s32[]{:T(128)} %bitcast.10, s32[]{:T(128)S(6)} %add.173, ...), kind=kLoop, calls=%fused_computation.137 | loop fusion | bytes 8232 | tf_op jit(solution)/shard_map/reshape | solution.py:122
  58.5 3.5 %collective-permute-done.6 = bf16[64,3584]{1,0:T(8,128)(2,1)S(1)} collective-permute-done((bf16[64,3584]{1,0:T(8,128)(2,1)S(1)}, bf16[64,3584]{1,0:T(8,128)(2,1)S(1)}, u32[]{:S(2)}, u32[]{:S(2)}) %collective-permute-start.6) | collective-permute-done | bytes 458784 | tf_op jit(solution)/shard_map/ppermute | solution.py:28
  62.1 4.0 %collective-permute-done.4 = bf16[64,3584]{1,0:T(8,128)(2,1)} collective-permute-done((bf16[64,3584]{1,0:T(8,128)(2,1)S(1)}, bf16[64,3584]{1,0:T(8,128)(2,1)}, u32[]{:S(2)}, u32[]{:S(2)}) %collective-permute-start.4) | collective-permute-done | bytes 458784 | tf_op jit(solution)/shard_map/ppermute | solution.py:28
  67.5 2.5 %fusion.66 = f32[256,256]{1,0:T(8,128)S(1)} fusion(bf16[256,4096]{1,0:T(8,128)(2,1)S(1)} %pad_maximum_fusion, bf16[256,4096]{1,0:T(8,128)(2,1)} %collective-permute-done.7), kind=kOutput, calls=%fused_computation.163 | convolution fusion | flops 536870912 | bytes 4456448 | tf_op jit(solution)/shard_map/dot_general | solution.py:134
  72.8 2.6 %collective-permute-start.9 = (f32[3,256]{1,0:T(4,128)S(1)}, f32[3,256]{1,0:T(4,128)S(1)}, u32[]{:S(2)}, u32[]{:S(2)}) collective-permute-start(f32[3,256]{1,0:T(4,128)S(1)} %pad_maximum_fusion.6), channel_id=1, source_target_pairs={{0,3},{1,0},{2,1},{3,2},{4,7},{5,4},{6,5},{7,6},{8,11},{9,8},{10,9... | collective-permute-start | bytes 9224 | tf_op jit(solution)/shard_map/ppermute | solution.py:28
  77.2 2.1 %collective-permute-done.10 = f32[3,256]{1,0:T(4,128)S(1)} collective-permute-done((f32[3,256]{1,0:T(4,128)S(1)}, f32[3,256]{1,0:T(4,128)S(1)}, u32[]{:S(2)}, u32[]{:S(2)}) %collective-permute-start.10) | collective-permute-done | bytes 3104 | tf_op jit(solution)/shard_map/ppermute | solution.py:28
  79.9 2.4 %collective-permute-start.12 = (bf16[256,256]{1,0:T(8,128)(2,1)S(1)}, bf16[256,256]{1,0:T(8,128)(2,1)S(1)}, u32[]{:S(2)}, u32[]{:S(2)}) collective-permute-start(bf16[256,256]{1,0:T(8,128)(2,1)S(1)} %fusion.20), channel_id=1, source_target_pairs={{0,4},{4,0},{1,5},{5,1},{2,6},{6,2},{3,7},{7,3},{8,12},{12,8},{9,1... | collective-permute-start | bytes 393224 | tf_op jit(solution)/shard_map/ppermute | solution.py:171
  85.0 3.5 %convolution_convert_fusion = bf16[256,4096]{1,0:T(8,128)(2,1)S(1)} fusion(bf16[256,4096]{1,0:T(8,128)(2,1)} %collective-permute-done.7, bf16[256,4096]{1,0:T(8,128)(2,1)} %get-tuple-element.45, bf16[256,256]{1,0:T(8,128)(2,1)S(1)} %collective-permute-done.12, bf16[256,256]{1,0:T(8,128)(2,1)S(1)} %fusion.20), kind=kOutput, calls=%fused_computation | convolution fusion | flops 1083703296 | bytes 6553600 | tf_op jit(solution)/shard_map/dot_general | solution.py:174
  90.6 6.5 %all-to-all-start.3 = ((bf16[8,4,8,768]{3,2,1,0:T(8,128)(2,1)}), bf16[8,4,8,768]{3,2,1,0:T(8,128)(2,1)S(1)}, u32[]{:S(2)}, u32[]{:S(2)}) async-start(bf16[8,4,8,768]{3,2,1,0:T(8,128)(2,1)} %bitcast.93), calls=%async_computation.3 | async-start | bytes 786432 | tf_op jit(solution)/shard_map/all_to_all | solution.py:24
  97.1 2.1 %fusion.59 = (bf16[64,3328]{1,0:T(8,128)(2,1)S(1)}, bf16[64,3328]{1,0:T(8,128)(2,1)}, bf16[64,3328]{1,0:T(8,128)(2,1)S(1)}) fusion(bf16[256,4096]{1,0:T(8,128)(2,1)} %copy-done.1), kind=kLoop, calls=%fused_computation.156 | loop fusion | bytes 2555904 | tf_op jit(solution)/shard_map/slice | solution.py:175
  102.0 10.2 %all-to-all-done.3 = bf16[8,4,8,768]{3,2,1,0:T(8,128)(2,1)S(1)} async-done(((bf16[8,4,8,768]{3,2,1,0:T(8,128)(2,1)}), bf16[8,4,8,768]{3,2,1,0:T(8,128)(2,1)S(1)}, u32[]{:S(2)}, u32[]{:S(2)}) %all-to-all-start.3) | async-done | bytes 393248 | tf_op jit(solution)/shard_map/all_to_all | solution.py:24
  113.9 5.5 %collective-permute-done.14 = bf16[64,3328]{1,0:T(8,128)(2,1)} collective-permute-done((bf16[64,3328]{1,0:T(8,128)(2,1)S(1)}, bf16[64,3328]{1,0:T(8,128)(2,1)}, u32[]{:S(2)}, u32[]{:S(2)}) %collective-permute-start.14) | collective-permute-done | bytes 426016 | tf_op jit(solution)/shard_map/ppermute | solution.py:28
  120.6 2.4 %fusion.15 = bf16[8,8,3328]{2,1,0:T(8,128)(2,1)} fusion(bf16[64,3328]{1,0:T(8,128)(2,1)} %collective-permute-done.15, bf16[64,3328]{1,0:T(8,128)(2,1)} %collective-permute-done.14, bf16[64,3328]{1,0:T(8,128)(2,1)} %collective-permute-done.13, bf16[256,4096]{1,0:T(8,128)(2,1)} %copy-done.1), kind=kLoop, calls=%fused_computation.26 | loop fusion | flops 1703936 | bytes 2129920 | tf_op jit(solution)/shard_map/reshape | solution.py:179
  123.1 6.4 %all-to-all-start.2 = ((bf16[8,8,3328]{2,1,0:T(8,128)(2,1)}), bf16[8,8,3328]{2,1,0:T(8,128)(2,1)}, u32[]{:S(2)}, u32[]{:S(2)}) async-start(bf16[8,8,3328]{2,1,0:T(8,128)(2,1)} %fusion.15), calls=%async_computation.2 | async-start | bytes 851968 | tf_op jit(solution)/shard_map/all_to_all | solution.py:24
  129.5 1.7 convolution_convert_fusion.1
  131.2 2.7 %convolution_convert_fusion.2 = bf16[256,2048]{1,0:T(8,128)(2,1)} fusion(bf16[256,256]{1,0:T(8,128)(2,1)S(1)} %fusion.20, bf16[256,4096]{1,0:T(8,128)(2,1)} %collective-permute-done.19, s32[]{:T(128)S(6)} %mul.150, bf16[256,4096]{1,0:T(8,128)(2,1)S(1)} %pad_maximum_fusion, pred[]{:T(512)S(6)} %eq.110), kind=kOutput, calls=%fused_computation.5 | convolution fusion | flops 269484032 | bytes 3276805 | tf_op jit(solution)/shard_map/dot_general | solution.py:217
  138.2 3.8 %all-to-all-done.2 = bf16[8,8,3328]{2,1,0:T(8,128)(2,1)} async-done(((bf16[8,8,3328]{2,1,0:T(8,128)(2,1)}), bf16[8,8,3328]{2,1,0:T(8,128)(2,1)}, u32[]{:S(2)}, u32[]{:S(2)}) %all-to-all-start.2) | async-done | bytes 426016 | tf_op jit(solution)/shard_map/all_to_all | solution.py:24
  145.8 12.2 %all-to-all-start.4 = ((f32[256,2,128]{2,1,0:T(2,128)}), f32[256,2,128]{2,1,0:T(2,128)S(1)}, u32[]{:S(2)}, u32[]{:S(2)}) async-start(f32[256,2,128]{2,1,0:T(2,128)} %broadcast_in_dim.46), calls=%async_computation.4 | async-start | bytes 524288 | tf_op jit(solution)/shard_map/all_to_all | solution.py:24
  158.0 2.8 %convolution_convert_fusion.4 = bf16[256,2048]{1,0:T(8,128)(2,1)} fusion(bf16[256,256]{1,0:T(8,128)(2,1)S(1)} %fusion.20, bf16[256,4096]{1,0:T(8,128)(2,1)} %collective-permute-done.19, s32[]{:T(128)S(6)} %mul.148, bf16[256,4096]{1,0:T(8,128)(2,1)S(1)} %pad_maximum_fusion, pred[]{:T(512)S(6)} %eq.108), kind=kOutput, calls=%fused_computation.7 | convolution fusion | flops 269484032 | bytes 3276805 | tf_op jit(solution)/shard_map/dot_general | solution.py:217
  160.8 2.6 %collective-permute-start.20 = (bf16[256,2048]{1,0:T(8,128)(2,1)}, bf16[256,2048]{1,0:T(8,128)(2,1)S(1)}, u32[]{:S(2)}, u32[]{:S(2)}) collective-permute-start(bf16[256,2048]{1,0:T(8,128)(2,1)} %convolution_convert_fusion.4), channel_id=1, source_target_pairs={{0,3},{1,0},{2,1},{3,2},{4,7},{5,4},{6,5},{7,6},{8,11},{9,8},{10,9... | collective-permute-start | bytes 3145736 | tf_op jit(solution)/shard_map/ppermute | solution.py:28
  164.1 24.9 %all-to-all-done.4 = f32[256,2,128]{2,1,0:T(2,128)S(1)} async-done(((f32[256,2,128]{2,1,0:T(2,128)}), f32[256,2,128]{2,1,0:T(2,128)S(1)}, u32[]{:S(2)}, u32[]{:S(2)}) %all-to-all-start.4) | async-done | bytes 262176 | tf_op jit(solution)/shard_map/all_to_all | solution.py:24
  191.3 2.0 multiply_subtract_fusion
  193.3 3.2 %add_convert_fusion = bf16[256,2048]{1,0:T(8,128)(2,1)} fusion(bf16[256,2048]{1,0:T(8,128)(2,1)S(1)} %convolution_convert_fusion.1, bf16[256,2048]{1,0:T(8,128)(2,1)} %collective-permute-done.22, bf16[256,2048]{1,0:T(8,128)(2,1)} %collective-permute-done.21, bf16[256,2048]{1,0:T(8,128)(2,1)S(1)} %collective-permute-done.20), kind=kLoop, calls=%fused_computation.9 | loop fusion | flops 4194304 | bytes 5242880 | tf_op jit(solution)/shard_map/convert_element_type | solution.py:225
  (131 shorter events, 36.3 us)
Async XLA Ops:
  4.4 16.0 %collective-permute-start = (bf16[4,1024]{1,0:T(4,128)(2,1)S(1)}, bf16[4,1024]{1,0:T(4,128)(2,1)S(1)}, u32[]{:S(2)}, u32[]{:S(2)}) collective-permute-start(bf16[4,1024]{1,0:T(4,128)(2,1)S(1)} %get-tuple-element.66), channel_id=1, source_target_pairs={{0,4},{4,0},{1,5},{5,1},{2,6},{6,2},{3,7},{7,3},{8,12},{12,8},{9,1... | collective-permute-start | bytes 24584 | tf_op jit(solution)/shard_map/ppermute | solution.py:83
  8.8 22.7 %all-to-all-start.1 = ((bf16[16,4,3584]{2,1,0:T(4,128)(2,1)}), bf16[16,4,3584]{2,1,0:T(4,128)(2,1)S(1)}, u32[]{:S(2)}, u32[]{:S(2)}) async-start(bf16[16,4,3584]{2,1,0:T(4,128)(2,1)} %bitcast.23), calls=%async_computation.1 | async-start | bytes 917504 | tf_op jit(solution)/shard_map/all_to_all | solution.py:24
  15.7 20.3 %copy-start.7 = (s32[128]{0:T(128)S(1)}, s32[128]{0:T(128)}, u32[]{:S(2)}) copy-start(s32[128]{0:T(128)} %param.17) | copy-start | bytes 1540
  20.4 47.1 %collective-permute-start.7 = (bf16[256,4096]{1,0:T(8,128)(2,1)}, bf16[256,4096]{1,0:T(8,128)(2,1)}, u32[]{:S(2)}, u32[]{:S(2)}) collective-permute-start(bf16[256,4096]{1,0:T(8,128)(2,1)} %get-tuple-element.46), channel_id=1, source_target_pairs={{0,4},{4,0},{1,5},{5,1},{2,6},{6,2},{3,7},{7,3},{8,12},{12,8},{9,1... | collective-permute-start | bytes 6291464 | tf_op jit(solution)/shard_map/ppermute | solution.py:111
  20.5 3.9 %collective-permute-start.3 = (bf16[8,1024]{1,0:T(8,128)(2,1)S(1)}, bf16[8,1024]{1,0:T(8,128)(2,1)S(1)}, u32[]{:S(2)}, u32[]{:S(2)}) collective-permute-start(bf16[8,1024]{1,0:T(8,128)(2,1)S(1)} %maximum_select_fusion.2), channel_id=1, source_target_pairs={{0,192},{64,0},{128,64},{192,128},{1,193},{65,1},{129,65},{193,129... | collective-permute-start | bytes 49160 | tf_op jit(solution)/shard_map/ppermute | solution.py:28
  23.3 4.1 %collective-permute-start.2 = (bf16[8,1024]{1,0:T(8,128)(2,1)S(1)}, bf16[8,1024]{1,0:T(8,128)(2,1)S(1)}, u32[]{:S(2)}, u32[]{:S(2)}) collective-permute-start(bf16[8,1024]{1,0:T(8,128)(2,1)S(1)} %maximum_select_fusion.2), channel_id=1, source_target_pairs={{0,128},{64,192},{128,0},{192,64},{1,129},{65,193},{129,1},{193,65... | collective-permute-start | bytes 49160 | tf_op jit(solution)/shard_map/ppermute | solution.py:28
  23.7 4.2 %collective-permute-start.1 = (bf16[8,1024]{1,0:T(8,128)(2,1)S(1)}, bf16[8,1024]{1,0:T(8,128)(2,1)S(1)}, u32[]{:S(2)}, u32[]{:S(2)}) collective-permute-start(bf16[8,1024]{1,0:T(8,128)(2,1)S(1)} %maximum_select_fusion.2), channel_id=1, source_target_pairs={{0,64},{64,128},{128,192},{192,0},{1,65},{65,129},{129,193},{193,1... | collective-permute-start | bytes 49160 | tf_op jit(solution)/shard_map/ppermute | solution.py:28
  32.4 20.0 %all-to-all-start = ((bf16[8,4,8,1024]{3,2,1,0:T(8,128)(2,1)}), bf16[8,4,8,1024]{3,2,1,0:T(8,128)(2,1)S(1)}, u32[]{:S(2)}, u32[]{:S(2)}) async-start(bf16[8,4,8,1024]{3,2,1,0:T(8,128)(2,1)} %broadcast_in_dim.42), calls=%async_computation | async-start | bytes 1048576 | tf_op jit(solution)/shard_map/all_to_all | solution.py:24
  39.3 22.8 %collective-permute-start.6 = (bf16[64,3584]{1,0:T(8,128)(2,1)S(1)}, bf16[64,3584]{1,0:T(8,128)(2,1)S(1)}, u32[]{:S(2)}, u32[]{:S(2)}) collective-permute-start(bf16[64,3584]{1,0:T(8,128)(2,1)S(1)} %reshape.133), channel_id=1, source_target_pairs={{0,192},{64,0},{128,64},{192,128},{1,193},{65,1},{129,65},{193,129... | collective-permute-start | bytes 1376264 | tf_op jit(solution)/shard_map/ppermute | solution.py:28
  42.1 20.0 %collective-permute-start.5 = (bf16[64,3584]{1,0:T(8,128)(2,1)S(1)}, bf16[64,3584]{1,0:T(8,128)(2,1)S(1)}, u32[]{:S(2)}, u32[]{:S(2)}) collective-permute-start(bf16[64,3584]{1,0:T(8,128)(2,1)S(1)} %reshape.133), channel_id=1, source_target_pairs={{0,128},{64,192},{128,0},{192,64},{1,129},{65,193},{129,1},{193,65... | collective-permute-start | bytes 1376264 | tf_op jit(solution)/shard_map/ppermute | solution.py:28
  42.5 23.6 %collective-permute-start.4 = (bf16[64,3584]{1,0:T(8,128)(2,1)S(1)}, bf16[64,3584]{1,0:T(8,128)(2,1)}, u32[]{:S(2)}, u32[]{:S(2)}) collective-permute-start(bf16[64,3584]{1,0:T(8,128)(2,1)S(1)} %reshape.133), channel_id=1, source_target_pairs={{0,64},{64,128},{128,192},{192,0},{1,65},{65,129},{129,193},{193,1... | collective-permute-start | bytes 1376264 | tf_op jit(solution)/shard_map/ppermute | solution.py:28
  70.0 1.7 collective-permute-start.8
  72.8 4.4 %collective-permute-start.9 = (f32[3,256]{1,0:T(4,128)S(1)}, f32[3,256]{1,0:T(4,128)S(1)}, u32[]{:S(2)}, u32[]{:S(2)}) collective-permute-start(f32[3,256]{1,0:T(4,128)S(1)} %pad_maximum_fusion.6), channel_id=1, source_target_pairs={{0,3},{1,0},{2,1},{3,2},{4,7},{5,4},{6,5},{7,6},{8,11},{9,8},{10,9... | collective-permute-start | bytes 9224 | tf_op jit(solution)/shard_map/ppermute | solution.py:28
  75.3 4.0 %collective-permute-start.10 = (f32[3,256]{1,0:T(4,128)S(1)}, f32[3,256]{1,0:T(4,128)S(1)}, u32[]{:S(2)}, u32[]{:S(2)}) collective-permute-start(f32[3,256]{1,0:T(4,128)S(1)} %pad_maximum_fusion.6), channel_id=1, source_target_pairs={{0,2},{1,3},{2,0},{3,1},{4,6},{5,7},{6,4},{7,5},{8,10},{9,11},{10,... | collective-permute-start | bytes 9224 | tf_op jit(solution)/shard_map/ppermute | solution.py:28
  75.9 3.7 %collective-permute-start.11 = (f32[3,256]{1,0:T(4,128)S(1)}, f32[3,256]{1,0:T(4,128)S(1)}, u32[]{:S(2)}, u32[]{:S(2)}) collective-permute-start(f32[3,256]{1,0:T(4,128)S(1)} %pad_maximum_fusion.6), channel_id=1, source_target_pairs={{0,1},{1,2},{2,3},{3,0},{4,5},{5,6},{6,7},{7,4},{8,9},{9,10},{10,1... | collective-permute-start | bytes 9224 | tf_op jit(solution)/shard_map/ppermute | solution.py:28
  79.9 5.1 %collective-permute-start.12 = (bf16[256,256]{1,0:T(8,128)(2,1)S(1)}, bf16[256,256]{1,0:T(8,128)(2,1)S(1)}, u32[]{:S(2)}, u32[]{:S(2)}) collective-permute-start(bf16[256,256]{1,0:T(8,128)(2,1)S(1)} %fusion.20), channel_id=1, source_target_pairs={{0,4},{4,0},{1,5},{5,1},{2,6},{6,2},{3,7},{7,3},{8,12},{12,8},{9,1... | collective-permute-start | bytes 393224 | tf_op jit(solution)/shard_map/ppermute | solution.py:171
  84.9 44.6 %collective-permute-start.19 = (bf16[256,4096]{1,0:T(8,128)(2,1)S(1)}, bf16[256,4096]{1,0:T(8,128)(2,1)}, u32[]{:S(2)}, u32[]{:S(2)}) collective-permute-start(bf16[256,4096]{1,0:T(8,128)(2,1)S(1)} %pad_maximum_fusion), channel_id=1, source_target_pairs={{0,4},{4,0},{1,5},{5,1},{2,6},{6,2},{3,7},{7,3},{8,12},{12,8},{9,1... | collective-permute-start | bytes 6291464 | tf_op jit(solution)/shard_map/ppermute | solution.py:137
  90.6 21.5 %all-to-all-start.3 = ((bf16[8,4,8,768]{3,2,1,0:T(8,128)(2,1)}), bf16[8,4,8,768]{3,2,1,0:T(8,128)(2,1)S(1)}, u32[]{:S(2)}, u32[]{:S(2)}) async-start(bf16[8,4,8,768]{3,2,1,0:T(8,128)(2,1)} %bitcast.93), calls=%async_computation.3 | async-start | bytes 786432 | tf_op jit(solution)/shard_map/all_to_all | solution.py:24
  99.2 13.3 %collective-permute-start.15 = (bf16[64,3328]{1,0:T(8,128)(2,1)}, bf16[64,3328]{1,0:T(8,128)(2,1)}, u32[]{:S(2)}, u32[]{:S(2)}) collective-permute-start(bf16[64,3328]{1,0:T(8,128)(2,1)} %get-tuple-element.48), channel_id=1, source_target_pairs={{0,64},{64,128},{128,192},{192,0},{1,65},{65,129},{129,193},{193,1... | collective-permute-start | bytes 1277960 | tf_op jit(solution)/shard_map/ppermute | solution.py:28
  99.2 20.2 %collective-permute-start.14 = (bf16[64,3328]{1,0:T(8,128)(2,1)S(1)}, bf16[64,3328]{1,0:T(8,128)(2,1)}, u32[]{:S(2)}, u32[]{:S(2)}) collective-permute-start(bf16[64,3328]{1,0:T(8,128)(2,1)S(1)} %get-tuple-element.49), channel_id=1, source_target_pairs={{0,128},{64,192},{128,0},{192,64},{1,129},{65,193},{129,1},{193,65... | collective-permute-start | bytes 1277960 | tf_op jit(solution)/shard_map/ppermute | solution.py:28
  100.8 19.9 %collective-permute-start.13 = (bf16[64,3328]{1,0:T(8,128)(2,1)S(1)}, bf16[64,3328]{1,0:T(8,128)(2,1)}, u32[]{:S(2)}, u32[]{:S(2)}) collective-permute-start(bf16[64,3328]{1,0:T(8,128)(2,1)S(1)} %get-tuple-element.47), channel_id=1, source_target_pairs={{0,192},{64,0},{128,64},{192,128},{1,193},{65,1},{129,65},{193,129... | collective-permute-start | bytes 1277960 | tf_op jit(solution)/shard_map/ppermute | solution.py:28
  112.3 17.2 %collective-permute-start.18 = (bf16[8,768]{1,0:T(8,128)(2,1)S(1)}, bf16[8,768]{1,0:T(8,128)(2,1)S(1)}, u32[]{:S(2)}, u32[]{:S(2)}) collective-permute-start(bf16[8,768]{1,0:T(8,128)(2,1)S(1)} %get-tuple-element.59), channel_id=1, source_target_pairs={{0,64},{64,128},{128,192},{192,0},{1,65},{65,129},{129,193},{193,1... | collective-permute-start | bytes 36872 | tf_op jit(solution)/shard_map/ppermute | solution.py:28
  112.5 17.0 %collective-permute-start.17 = (bf16[8,768]{1,0:T(8,128)(2,1)S(1)}, bf16[8,768]{1,0:T(8,128)(2,1)S(1)}, u32[]{:S(2)}, u32[]{:S(2)}) collective-permute-start(bf16[8,768]{1,0:T(8,128)(2,1)S(1)} %get-tuple-element.60), channel_id=1, source_target_pairs={{0,128},{64,192},{128,0},{192,64},{1,129},{65,193},{129,1},{193,65... | collective-permute-start | bytes 36872 | tf_op jit(solution)/shard_map/ppermute | solution.py:28
  119.4 10.1 %collective-permute-start.16 = (bf16[8,768]{1,0:T(8,128)(2,1)S(1)}, bf16[8,768]{1,0:T(8,128)(2,1)S(1)}, u32[]{:S(2)}, u32[]{:S(2)}) collective-permute-start(bf16[8,768]{1,0:T(8,128)(2,1)S(1)} %get-tuple-element.58), channel_id=1, source_target_pairs={{0,192},{64,0},{128,64},{192,128},{1,193},{65,1},{129,65},{193,129... | collective-permute-start | bytes 36872 | tf_op jit(solution)/shard_map/ppermute | solution.py:28
  123.1 18.9 %all-to-all-start.2 = ((bf16[8,8,3328]{2,1,0:T(8,128)(2,1)}), bf16[8,8,3328]{2,1,0:T(8,128)(2,1)}, u32[]{:S(2)}, u32[]{:S(2)}) async-start(bf16[8,8,3328]{2,1,0:T(8,128)(2,1)} %fusion.15), calls=%async_computation.2 | async-start | bytes 851968 | tf_op jit(solution)/shard_map/all_to_all | solution.py:24
  129.5 13.6 %copy-start.5 = (f32[8,768]{1,0:T(8,128)}, f32[8,768]{1,0:T(8,128)S(1)}, u32[]{:S(2)}) copy-start(f32[8,768]{1,0:T(8,128)S(1)} %fusion.32) | copy-start | bytes 73732
  133.9 59.4 %collective-permute-start.22 = (bf16[256,2048]{1,0:T(8,128)(2,1)}, bf16[256,2048]{1,0:T(8,128)(2,1)}, u32[]{:S(2)}, u32[]{:S(2)}) collective-permute-start(bf16[256,2048]{1,0:T(8,128)(2,1)} %convolution_convert_fusion.2), channel_id=1, source_target_pairs={{0,1},{1,2},{2,3},{3,0},{4,5},{5,6},{6,7},{7,4},{8,9},{9,10},{10,1... | collective-permute-start | bytes 3145736 | tf_op jit(solution)/shard_map/ppermute | solution.py:28
  137.0 56.3 %collective-permute-start.21 = (bf16[256,2048]{1,0:T(8,128)(2,1)}, bf16[256,2048]{1,0:T(8,128)(2,1)}, u32[]{:S(2)}, u32[]{:S(2)}) collective-permute-start(bf16[256,2048]{1,0:T(8,128)(2,1)} %convolution_convert_fusion.3), channel_id=1, source_target_pairs={{0,2},{1,3},{2,0},{3,1},{4,6},{5,7},{6,4},{7,5},{8,10},{9,11},{10,... | collective-permute-start | bytes 3145736 | tf_op jit(solution)/shard_map/ppermute | solution.py:28
  145.8 43.2 %all-to-all-start.4 = ((f32[256,2,128]{2,1,0:T(2,128)}), f32[256,2,128]{2,1,0:T(2,128)S(1)}, u32[]{:S(2)}, u32[]{:S(2)}) async-start(f32[256,2,128]{2,1,0:T(2,128)} %broadcast_in_dim.46), calls=%async_computation.4 | async-start | bytes 524288 | tf_op jit(solution)/shard_map/all_to_all | solution.py:24
  158.0 5.4 %copy-start.3 = (f32[8,3328]{1,0:T(8,128)S(1)}, f32[8,3328]{1,0:T(8,128)}, u32[]{:S(2)}) copy-start(f32[8,3328]{1,0:T(8,128)} %copy-done.2) | copy-start | bytes 319492
  160.8 32.5 %collective-permute-start.20 = (bf16[256,2048]{1,0:T(8,128)(2,1)}, bf16[256,2048]{1,0:T(8,128)(2,1)S(1)}, u32[]{:S(2)}, u32[]{:S(2)}) collective-permute-start(bf16[256,2048]{1,0:T(8,128)(2,1)} %convolution_convert_fusion.4), channel_id=1, source_target_pairs={{0,3},{1,0},{2,1},{3,2},{4,7},{5,4},{6,5},{7,6},{8,11},{9,8},{10,9... | collective-permute-start | bytes 3145736 | tf_op jit(solution)/shard_map/ppermute | solution.py:28
  163.4 27.9 %collective-permute-start.23 = (f32[4,4096]{1,0:T(4,128)S(1)}, f32[4,4096]{1,0:T(4,128)S(1)}, u32[]{:S(2)}, u32[]{:S(2)}) collective-permute-start(f32[4,4096]{1,0:T(4,128)S(1)} %get-tuple-element.56), channel_id=1, source_target_pairs={{0,4},{4,0},{1,5},{5,1},{2,6},{6,2},{3,7},{7,3},{8,12},{12,8},{9,1... | collective-permute-start | bytes 196616 | tf_op jit(solution)/shard_map/ppermute | solution.py:197
  (5 other events, 15.5 us)

commit v6 on v5

--- a/solution.py
+++ b/solution.py
@@ -1,6 +1,10 @@
+import functools
+
 import jax
 import jax.numpy as jnp
 from jax import lax
+from jax.experimental import pallas as pl
+from jax.experimental.pallas import tpu as pltpu
 from jax.sharding import Mesh, PartitionSpec as P
 
 
@@ -42,6 +46,71 @@
 
 def spread(x, axes, count):
     return exchange(jnp.broadcast_to(x[None], (count,) + x.shape), axes)
+
+
+def front_kernel(
+    group, y_rows, span_ref, place_ref, small_ref, own_ref, mate_ref, logit_ref, stat_ref, row_ref
+):
+    ctx, y_place, vocab_place = place_ref[0], place_ref[1], place_ref[2]
+    tok = own_ref.shape[1]
+    span = tok // 2
+    quads = small_ref.shape[2] // NC
+    left, right = [], []
+    for offset in (0, 1):
+        sid = span_ref[2 * ctx + offset]
+        at_z = (sid >> 2) & (NZ - 1)
+        at_y = (y_place - (sid >> 5)) & (NY - 1)
+        chip = small_ref[at_z, at_y].astype(f32)
+        mine = jnp.where((sid & 2) == 0, chip[:quads], chip[quads:])
+        odd = (sid & 1) == 1
+        left.append(jnp.where(odd, mine[:, span:tok], mine[:, :span]))
+        right.append(jnp.where(odd, mine[:, tok + span :], mine[:, tok : tok + span]))
+    left = jnp.concatenate(left, 1)
+    right = jnp.concatenate(right, 1)
+    marks = jnp.sum(small_ref[:, :, :, :tok].astype(f32), axis=(0, 1))
+    marks = marks[2:3] + marks[quads + 2 : quads + 3]
+    token_count = jnp.sum(marks, axis=1, keepdims=True)
+    target = left[0:1] * 256.0 + left[1:2]
+    mask = left[2:3]
+    local = target.astype(jnp.int32) - group * 4 - vocab_place * group
+    ids = lax.broadcasted_iota(jnp.int32, (group, tok), 0)
+    within = ids & (y_rows - 1)
+    ids = ((y_place * y_rows - (ids - within)) & (group - 1)) + within
+    hits = ids == local
+    logits = own_ref[...] + mate_ref[...]
+    logit_ref[...] = logits
+    top = jnp.max(logits, axis=0, keepdims=True)
+    stat_ref[0:1, :] = top
+    stat_ref[1:2, :] = jnp.sum(jnp.exp(logits - top), axis=0, keepdims=True)
+    stat_ref[2:3, :] = jnp.sum(jnp.where(hits, logits, 0.0), axis=0, keepdims=True)
+    stat_ref[3:8, :] = jnp.zeros((5, tok), f32)
+    row_ref[0:1, :] = target
+    row_ref[1:2, :] = mask
+    row_ref[2:3, :] = left[3:4] + right[0:1] + right[1:2]
+    row_ref[3:4, :] = right[2:3] + right[3:4]
+    row_ref[4:5, :] = mask * (loss_scale / token_count)
+    row_ref[5:6, :] = jnp.broadcast_to(1.0 / token_count, (1, tok))
+    row_ref[6:8, :] = jnp.zeros((2, tok), f32)
+
+
+def square_kernel(a_ref, b0_ref, b1_ref, b2_ref, b3_ref, share_ref, grad_ref, report_ref):
+    wide = a_ref.shape[2]
+    part_a = a_ref[0].astype(f32)
+    for i in range(1, a_ref.shape[0]):
+        part_a = part_a + a_ref[i].astype(f32)
+    part_b = b0_ref[...].astype(f32) + b1_ref[...].astype(f32)
+    part_b = part_b + b2_ref[...].astype(f32) + b3_ref[...].astype(f32)
+    grad_ref[:, :wide] = part_a
+    grad_ref[:, wide:] = part_b
+    total = jnp.sum(part_a * part_a, axis=1, keepdims=True)
+    total = total + jnp.sum(part_b * part_b, axis=1, keepdims=True)
+    total = jnp.sum(total, axis=0, keepdims=True)
+    row = jnp.concatenate([jnp.broadcast_to(total, (1, 128)), share_ref[...]], 0)
+    report_ref[...] = jnp.broadcast_to(row[None], report_ref.shape)
+
+
+VMEM = pl.BlockSpec(memory_space=pltpu.VMEM)
+SMEM = pl.BlockSpec(memory_space=pltpu.SMEM)
 
 
 def step(
@@ -85,17 +154,6 @@
     chips_b = jnp.stack([chip_b] + [shift(chip_b, "y", NY, s) for s in range(1, NY)], 0)
     head_a = jnp.concatenate([block] + [shift(block, "y", NY, s) for s in range(1, NY)], 0)
     part_b = spread(chips_b, "z", NZ)
-    sids = lax.dynamic_slice(
-        span_order, (2 * ctx_place,), (2,), allow_negative_indices=False
-    )
-    owner = sids >> 1
-    starts = [
-        (owner >> 1) & (NZ - 1),
-        (y_place - (owner >> 4)) & (NY - 1),
-        (owner & 1) * shard_rows,
-        (sids & 1) * span,
-    ]
-    starts = lax.optimization_barrier([[v[i] for v in starts] for i in (0, 1)])
     slot_ids = jnp.arange(span_order.shape[0], dtype=jnp.int32)
     slots = [
         jnp.sum(jnp.where(span_order == 2 * ctx_place + offset, slot_ids, 0))
@@ -106,29 +164,14 @@
     head = jnp.concatenate([head_a, head_b], 1)
     small = part_b[..., thin:]
 
-    own_half = lax.dynamic_slice_in_dim(hidden_states, core * half, half, 1)
-    far_half = lax.dynamic_slice_in_dim(hidden_states, (1 - core) * half, half, 1)
+    own_half = lax.dynamic_slice(
+        hidden_states, (0, core * half), (tok_rows, half), allow_negative_indices=False
+    )
+    far_half = lax.dynamic_slice(
+        hidden_states, (0, (1 - core) * half), (tok_rows, half), allow_negative_indices=False
+    )
     mate_half = lax.ppermute(far_half, "core", SWAP)
     tokens = jnp.concatenate([own_half, mate_half], 0)
-
-    masks = small.reshape(NZ, NY, NC, shard_rows, 2 * tok_rows)[:, :, :, 2, :tok_rows]
-    token_count = jnp.sum(masks.astype(f32))
-    found = [
-        lax.dynamic_slice(
-            small,
-            (at[0], at[1], at[2], at[3] + side * tok_rows),
-            (1, 1, shard_rows, span),
-            allow_negative_indices=False,
-        ).reshape(shard_rows, span)
-        for at in starts
-        for side in (0, 1)
-    ]
-    rows_a = jnp.concatenate([found[0], found[2]], 1).astype(f32)
-    rows_b = jnp.concatenate([found[1], found[3]], 1).astype(f32)
-    tgt_rows = (rows_a[0] * digit + rows_a[1]).astype(jnp.int32)
-    mask_rows = rows_a[2]
-    prior_rows = rows_a[3] + rows_b[0] + rows_b[1]
-    outside = rows_b[2] + rows_b[3]
 
     def score(tok):
         return lax.dot_general(head, tok, (((1,), (1,)), ((), ())), preferred_element_type=f32)
@@ -136,17 +179,26 @@
     mate_part = score(mate_half)
     mate_head = lax.ppermute(head, "core", SWAP)
     mate_part = lax.ppermute(mate_part, "core", SWAP)
-    logits = score(own_half) + mate_part
-
+    own_part = score(own_half)
+    place = jnp.stack([ctx_place, y_place, vocab_place])
+    logits, stats, rows = pl.pallas_call(
+        functools.partial(front_kernel, group_rows, y_rows),
+        out_shape=(
+            jax.ShapeDtypeStruct((group_rows, tok_rows), f32),
+            jax.ShapeDtypeStruct((8, tok_rows), f32),
+            jax.ShapeDtypeStruct((8, tok_rows), f32),
+        ),
+        in_specs=[SMEM, SMEM, VMEM, VMEM, VMEM],
+        out_specs=(VMEM, VMEM, VMEM),
+        name="front",
+    )(span_order, place, small, own_part, mate_part)
+    tgt_rows = rows[0].astype(jnp.int32)
+    mask_rows, prior_rows, outside, mask_scale = rows[1], rows[2], rows[3], rows[4]
     local_col = tgt_rows - block_total - vocab_place * group_rows
     vocab_ids = lax.broadcasted_iota(jnp.int32, (group_rows, tok_rows), 0)
     within = vocab_ids & (y_rows - 1)
     vocab_ids = ((y_place * y_rows - (vocab_ids - within)) & (group_rows - 1)) + within
     hits = vocab_ids == local_col[None, :]
-    top_local = jnp.max(logits, axis=0)
-    sum_local = jnp.sum(jnp.exp(logits - top_local[None, :]), axis=0)
-    target_local = jnp.sum(jnp.where(hits, logits, 0.0), axis=0)
-    stats = jnp.stack([top_local, sum_local, target_local], 0)
     heard = [stats] + [shift(stats, "vocab", vocab_count, s) for s in range(1, vocab_count)]
     ordered = []
     for j in range(vocab_count):
@@ -162,11 +214,8 @@
     log_total = top_value + jnp.log(jnp.exp(prior_rows - top_value) + sum_total)
     target_logit = jnp.where(tgt_rows >= block_total, target_sum, outside)
     loss_rows = mask_rows * (log_total - target_logit)
-    grad_scale = loss_scale / token_count
     dlogits = (
-        mask_rows[None, :]
-        * (jnp.exp(logits - log_total[None, :]) - hits.astype(f32))
-        * grad_scale
+        mask_scale[None, :] * (jnp.exp(logits - log_total[None, :]) - hits.astype(f32))
     ).astype(bf16)
     mate_dlogits = lax.ppermute(dlogits, "core", SWAP)
 
@@ -179,19 +228,24 @@
     by_y = by_y.astype(bf16).reshape(NZ, chip_rows, wide_g)
     by_z = partial_rows[:, wide_g:].reshape(NY, NZ, chip_rows, thin_g).transpose(1, 0, 2, 3)
     by_z = jnp.sum(exchange(by_z, "z").astype(f32), axis=0).astype(bf16)
-    grad_b = by_z[0].astype(f32)
-    for s in range(1, NY):
-        grad_b = grad_b + shift(by_z[s], "y", NY, -s).astype(f32)
-    grad_a = jnp.sum(exchange(by_y, "z").astype(f32), axis=0)
-    chip_grad = jnp.concatenate([grad_a, grad_b], 1)
-    square = jnp.sum(chip_grad * chip_grad)
+    pieces_b = [by_z[0]] + [shift(by_z[s], "y", NY, -s) for s in range(1, NY)]
+    pieces_a = exchange(by_y, "z")
     lanes = tok_rows // vocab_count
     share = lax.dynamic_slice_in_dim(loss_rows, vocab_place * lanes, lanes, 0)
-    share = jnp.pad(share, (0, span - lanes))
-    report = jnp.concatenate([jnp.full((1, span), square), share[None]], 0)
-    reports = spread(report, ALL, ctx_count * vocab_count)
+    share = jnp.pad(share, (0, span - lanes))[None]
+    chip_grad, report = pl.pallas_call(
+        square_kernel,
+        out_shape=(
+            jax.ShapeDtypeStruct((chip_rows, half), f32),
+            jax.ShapeDtypeStruct((ctx_count * vocab_count, 2, span), f32),
+        ),
+        in_specs=[VMEM] * (NY + 2),
+        out_specs=(VMEM, VMEM),
+        name="square",
+    )(pieces_a, *pieces_b, share)
+    reports = exchange(report, ALL)
     square_sum = jnp.sum(reports[:, 0], axis=0)
-    mean_loss = jnp.sum(reports[:, 1]) * (1.0 / token_count)
+    mean_loss = jnp.sum(reports[:, 1]) * rows[5, 0]
     near = lax.dynamic_slice_in_dim(chip_grad, core * shard_rows, shard_rows, 0)
     far = lax.dynamic_slice_in_dim(chip_grad, (1 - core) * shard_rows, shard_rows, 0)
     mate = lax.ppermute(far, "core", SWAP)

time: 199 us -> 197 us (0.990)
  local copies, waits for them, and re-layouts: 20.7 us -> 13.6 us
  Pallas kernels: 0 us -> 3.91 us
  starting transfers between devices: 61.9 us -> 64.8 us
  between operations: 6.92 us -> 4.93 us
    reshape x2 -> x0, local copies, waits for them, and re-layouts: 5.35 us -> none  [the longest x1 5.28 us: step(): found = [lax.dynamic_slice(small, (at[0], at[1], at[2], at[3] + side * to...]
    ppermute x18, waiting for transfers between devices: 20.3 us -> 24.7 us  [shift(): lax.ppermute(x, axis, [(i, (i + step) % count) for i in range(count)])]
    pallas_call x0 -> x2, Pallas kernels: none -> 3.91 us  [the longest x1 2 us: step(): pl.pallas_call(square_kernel, out_shape=(jax.ShapeDtypeStruct((chip_rows,...]
    all_to_all x5, waiting for transfers between devices: 51.6 us -> 47.7 us  [exchange(): return lax.all_to_all(x, axes, 0, 0, tiled=True)]
    ppermute x1, starting transfers between devices: 3.29 us -> 0.19 us  [step(): far_b = lax.ppermute(far_b, 'core', SWAP)]
    ppermute x1, starting transfers between devices: 0.11 us -> 3.2 us  [step(): mate_half = lax.ppermute(far_half, 'core', SWAP)]
    reduce_sum x4 -> x1, other arithmetic: 2.56 us -> 0.03 us  [step(): target_sum = jnp.sum(stats[:, 2], axis=0)]
    another operation x5, other arithmetic: 2.76 us -> 0.7 us  [the longest x1 0.67 us: step(): place = jnp.stack([ctx_place, y_place, vocab_place])]
  transfers between devices with their start and end apart: 29 -> 29, of which waited for: 15 -> 14; matrix products, arithmetic and copies ran while one was open for 22% -> 17% of each run, Pallas kernels for 0% -> 1%
where the time goes in v6:
time: 197 us; the launch traced here: 196 us
  waiting for transfers between devices  73.5 us (37%)
  starting transfers between devices  64.8 us (33%)
  other arithmetic  19.2 us (10%)
  matrix products  16.3 us (8%)
  local copies, waits for them, and re-layouts  13.6 us (7%)
  between operations  4.93 us (3%)
  Pallas kernels  3.91 us (2%)
    all_to_all x5, waiting for transfers between devices, exchange(): return lax.all_to_all(x, axes, 0, 0, tiled=True)  47.7 us
    all_to_all x5, starting transfers between devices, exchange(): return lax.all_to_all(x, axes, 0, 0, tiled=True)  36.8 us
    ppermute x18, waiting for transfers between devices, shift(): lax.ppermute(x, axis, [(i, (i + step) % count) for i in range(count)])  24.7 us
    ppermute x18, starting transfers between devices, shift(): lax.ppermute(x, axis, [(i, (i + step) % count) for i in range(count)])  21.2 us
    dot_general x4, matrix products, step(): lax.dot_general(dlogits, side, (((0,), (0,)), ((), ())), preferred_elemen...  8.64 us
    dynamic_slice x1, local copies, waits for them, and re-layouts, step(): lax.dynamic_slice(hidden_states, (0, core * half), (tok_rows, half), allo...  4.8 us
    dot_general x2, matrix products, score(): lax.dot_general(head, tok, (((1,), (1,)), ((), ())), preferred_element_ty...  4.14 us
  transfers between devices with their start and end apart: 29, of which 14 were waited for; matrix products, arithmetic and copies ran while one was open for 17% of the time, Pallas kernels for 1%

profile of v6, /device:TPU:1, one launch (start us, length us, event | category | flops | bytes accessed | tf_op | source)
XLA Modules:
  0.0 196.2 jit_solution(18141093015246317297)
XLA Ops:
  0.7 4.8 %constant_dynamic-slice_fusion.5 = (bf16[256,4096]{1,0:T(8,128)(2,1)}, bf16[256,4096]{1,0:T(8,128)(2,1)}) fusion(bf16[256,8192]{1,0:T(8,128)(2,1)} %param.9, s32[]{:T(128)S(6)} %mul.106, s32[]{:T(128)S(6)} %mul.107), kind=kLoop, calls=%fused_computation.76 | loop fusion | bytes 8388616 | tf_op jit(solution)/shard_map/dynamic_slice | solution.py:167
  5.5 3.2 %collective-permute-start.7 = (bf16[256,4096]{1,0:T(8,128)(2,1)}, bf16[256,4096]{1,0:T(8,128)(2,1)}, u32[]{:S(2)}, u32[]{:S(2)}) collective-permute-start(bf16[256,4096]{1,0:T(8,128)(2,1)} %get-tuple-element.32), channel_id=1, source_target_pairs={{0,4},{4,0},{1,5},{5,1},{2,6},{6,2},{3,7},{7,3},{8,12},{12,8},{9,1... | collective-permute-start | bytes 6291464 | tf_op jit(solution)/shard_map/ppermute | solution.py:173
  9.8 6.9 %all-to-all-start.1 = ((bf16[16,4,3584]{2,1,0:T(4,128)(2,1)}), bf16[16,4,3584]{2,1,0:T(4,128)(2,1)S(1)}, u32[]{:S(2)}, u32[]{:S(2)}) async-start(bf16[16,4,3584]{2,1,0:T(4,128)(2,1)} %bitcast.12), calls=%async_computation.1 | async-start | bytes 917504 | tf_op jit(solution)/shard_map/all_to_all | solution.py:28
  18.2 2.8 %collective-permute-start.3 = (bf16[8,1024]{1,0:T(8,128)(2,1)S(1)}, bf16[8,1024]{1,0:T(8,128)(2,1)S(1)}, u32[]{:S(2)}, u32[]{:S(2)}) collective-permute-start(bf16[8,1024]{1,0:T(8,128)(2,1)S(1)} %maximum_select_fusion.2), channel_id=1, source_target_pairs={{0,192},{64,0},{128,64},{192,128},{1,193},{65,1},{129,65},{193,129... | collective-permute-start | bytes 49160 | tf_op jit(solution)/shard_map/ppermute | solution.py:32
  22.1 3.3 %collective-permute-done.2 = bf16[8,1024]{1,0:T(8,128)(2,1)S(1)} collective-permute-done((bf16[8,1024]{1,0:T(8,128)(2,1)S(1)}, bf16[8,1024]{1,0:T(8,128)(2,1)S(1)}, u32[]{:S(2)}, u32[]{:S(2)}) %collective-permute-start.2) | collective-permute-done | bytes 16416 | tf_op jit(solution)/shard_map/ppermute | solution.py:32
  25.6 6.9 %all-to-all-done.1 = bf16[16,4,3584]{2,1,0:T(4,128)(2,1)S(1)} async-done(((bf16[16,4,3584]{2,1,0:T(4,128)(2,1)}), bf16[16,4,3584]{2,1,0:T(4,128)(2,1)S(1)}, u32[]{:S(2)}, u32[]{:S(2)}) %all-to-all-start.1) | async-done | bytes 458784 | tf_op jit(solution)/shard_map/all_to_all | solution.py:28
  33.4 3.5 %all-to-all-start = ((bf16[8,4,8,1024]{3,2,1,0:T(8,128)(2,1)}), bf16[8,4,8,1024]{3,2,1,0:T(8,128)(2,1)S(1)}, u32[]{:S(2)}, u32[]{:S(2)}) async-start(bf16[8,4,8,1024]{3,2,1,0:T(8,128)(2,1)} %broadcast_in_dim.30), calls=%async_computation | async-start | bytes 1048576 | tf_op jit(solution)/shard_map/all_to_all | solution.py:28
  37.1 2.8 %collective-permute-start.6 = (bf16[64,3584]{1,0:T(8,128)(2,1)S(1)}, bf16[64,3584]{1,0:T(8,128)(2,1)S(1)}, u32[]{:S(2)}, u32[]{:S(2)}) collective-permute-start(bf16[64,3584]{1,0:T(8,128)(2,1)S(1)} %reshape.103), channel_id=1, source_target_pairs={{0,192},{64,0},{128,64},{192,128},{1,193},{65,1},{129,65},{193,129... | collective-permute-start | bytes 1376264 | tf_op jit(solution)/shard_map/ppermute | solution.py:32
  41.6 13.2 %all-to-all-done = bf16[8,4,8,1024]{3,2,1,0:T(8,128)(2,1)S(1)} async-done(((bf16[8,4,8,1024]{3,2,1,0:T(8,128)(2,1)}), bf16[8,4,8,1024]{3,2,1,0:T(8,128)(2,1)S(1)}, u32[]{:S(2)}, u32[]{:S(2)}) %all-to-all-start) | async-done | bytes 524320 | tf_op jit(solution)/shard_map/all_to_all | solution.py:28
  55.6 4.2 %collective-permute-done.6 = bf16[64,3584]{1,0:T(8,128)(2,1)S(1)} collective-permute-done((bf16[64,3584]{1,0:T(8,128)(2,1)S(1)}, bf16[64,3584]{1,0:T(8,128)(2,1)S(1)}, u32[]{:S(2)}, u32[]{:S(2)}) %collective-permute-start.6) | collective-permute-done | bytes 458784 | tf_op jit(solution)/shard_map/ppermute | solution.py:32
  59.8 3.9 %collective-permute-done.4 = bf16[64,3584]{1,0:T(8,128)(2,1)S(1)} collective-permute-done((bf16[64,3584]{1,0:T(8,128)(2,1)S(1)}, bf16[64,3584]{1,0:T(8,128)(2,1)S(1)}, u32[]{:S(2)}, u32[]{:S(2)}) %collective-permute-start.4) | collective-permute-done | bytes 458784 | tf_op jit(solution)/shard_map/ppermute | solution.py:32
  64.5 2.3 %pad_maximum_fusion = bf16[256,4096]{1,0:T(8,128)(2,1)S(1)} fusion(bf16[256,512]{1,0:T(8,128)(2,1)S(1)} %bitcast.78, bf16[64,3584]{1,0:T(8,128)(2,1)S(1)} %collective-permute-done.6, bf16[64,3584]{1,0:T(8,128)(2,1)S(1)} %collective-permute-done.5, bf16[64,3584]{1,0:T(8,128)(2,1)} %copy-done.3, bf16[64,3584]{1,0:T(8,128)(2,1)S(1)} %reshape.103), kind=kLoop, calls=%fused_computation.8 | loop fusion | flops 10485760 | bytes 4194304 | tf_op jit(solution)/shard_map/concatenate | solution.py:164
  66.8 2.5 %fusion.48 = f32[256,256]{1,0:T(8,128)S(1)} fusion(bf16[256,4096]{1,0:T(8,128)(2,1)S(1)} %pad_maximum_fusion, bf16[256,4096]{1,0:T(8,128)(2,1)} %collective-permute-done.7), kind=kOutput, calls=%fused_computation.124 | convolution fusion | flops 536870912 | bytes 4456448 | tf_op jit(solution)/shard_map/dot_general | solution.py:177
  72.2 1.9 front.1
  74.1 2.5 %collective-permute-start.9 = (f32[8,256]{1,0:T(8,128)}, f32[8,256]{1,0:T(8,128)S(1)}, u32[]{:S(2)}, u32[]{:S(2)}) collective-permute-start(f32[8,256]{1,0:T(8,128)} %get-tuple-element.15), channel_id=1, source_target_pairs={{0,3},{1,0},{2,1},{3,2},{4,7},{5,4},{6,5},{7,6},{8,11},{9,8},{10,9... | collective-permute-start | bytes 24584 | tf_op jit(solution)/shard_map/ppermute | solution.py:32
  78.4 2.4 %collective-permute-done.10 = f32[8,256]{1,0:T(8,128)S(1)} collective-permute-done((f32[8,256]{1,0:T(8,128)}, f32[8,256]{1,0:T(8,128)S(1)}, u32[]{:S(2)}, u32[]{:S(2)}) %collective-permute-start.10) | collective-permute-done | bytes 8224 | tf_op jit(solution)/shard_map/ppermute | solution.py:32
  84.4 2.1 %collective-permute-start.12 = (bf16[256,256]{1,0:T(8,128)(2,1)S(1)}, bf16[256,256]{1,0:T(8,128)(2,1)S(1)}, u32[]{:S(2)}, u32[]{:S(2)}) collective-permute-start(bf16[256,256]{1,0:T(8,128)(2,1)S(1)} %multiply_convert_fusion), channel_id=1, source_target_pairs={{0,4},{4,0},{1,5},{5,1},{2,6},{6,2},{3,7},{7,3},{8,12},{12,8},{9,1... | collective-permute-start | bytes 393224 | tf_op jit(solution)/shard_map/ppermute | solution.py:220
  89.8 3.5 %convolution_convert_fusion = bf16[256,4096]{1,0:T(8,128)(2,1)S(1)} fusion(bf16[256,4096]{1,0:T(8,128)(2,1)} %collective-permute-done.7, bf16[256,4096]{1,0:T(8,128)(2,1)} %get-tuple-element.31, bf16[256,256]{1,0:T(8,128)(2,1)S(1)} %collective-permute-done.12, bf16[256,256]{1,0:T(8,128)(2,1)S(1)} %multiply_convert_fusion), kind=kOutput, calls=%fused_computation | convolution fusion | flops 1083703296 | bytes 6553600 | tf_op jit(solution)/shard_map/dot_general | solution.py:223
  99.1 6.4 %all-to-all-start.3 = ((bf16[8,4,8,768]{3,2,1,0:T(8,128)(2,1)}), bf16[8,4,8,768]{3,2,1,0:T(8,128)(2,1)S(1)}, u32[]{:S(2)}, u32[]{:S(2)}) async-start(bf16[8,4,8,768]{3,2,1,0:T(8,128)(2,1)} %bitcast.76), calls=%async_computation.3 | async-start | bytes 786432 | tf_op jit(solution)/shard_map/all_to_all | solution.py:28
  105.5 10.3 %collective-permute-done.15 = bf16[64,3328]{1,0:T(8,128)(2,1)} collective-permute-done((bf16[64,3328]{1,0:T(8,128)(2,1)}, bf16[64,3328]{1,0:T(8,128)(2,1)}, u32[]{:S(2)}, u32[]{:S(2)}) %collective-permute-start.15) | collective-permute-done | bytes 426016 | tf_op jit(solution)/shard_map/ppermute | solution.py:32
  116.0 2.4 %fusion.15 = bf16[8,8,3328]{2,1,0:T(8,128)(2,1)} fusion(bf16[64,3328]{1,0:T(8,128)(2,1)} %collective-permute-done.15, bf16[64,3328]{1,0:T(8,128)(2,1)} %collective-permute-done.14, bf16[64,3328]{1,0:T(8,128)(2,1)} %collective-permute-done.13, bf16[256,4096]{1,0:T(8,128)(2,1)} %copy-done.1), kind=kLoop, calls=%fused_computation.24 | loop fusion | flops 1703936 | bytes 2129920 | tf_op jit(solution)/shard_map/reshape | solution.py:228
  118.9 5.9 %all-to-all-start.2 = ((bf16[8,8,3328]{2,1,0:T(8,128)(2,1)}), bf16[8,8,3328]{2,1,0:T(8,128)(2,1)}, u32[]{:S(2)}, u32[]{:S(2)}) async-start(bf16[8,8,3328]{2,1,0:T(8,128)(2,1)} %fusion.15), calls=%async_computation.2 | async-start | bytes 851968 | tf_op jit(solution)/shard_map/all_to_all | solution.py:28
  125.5 2.8 %collective-permute-start.16 = (bf16[8,768]{1,0:T(8,128)(2,1)S(1)}, bf16[8,768]{1,0:T(8,128)(2,1)S(1)}, u32[]{:S(2)}, u32[]{:S(2)}) collective-permute-start(bf16[8,768]{1,0:T(8,128)(2,1)S(1)} %get-tuple-element.42), channel_id=1, source_target_pairs={{0,192},{64,0},{128,64},{192,128},{1,193},{65,1},{129,65},{193,129... | collective-permute-start | bytes 36872 | tf_op jit(solution)/shard_map/ppermute | solution.py:32
  128.9 1.7 convolution_convert_fusion.1
  130.6 2.7 %convolution_convert_fusion.2 = bf16[256,2048]{1,0:T(8,128)(2,1)} fusion(bf16[256,256]{1,0:T(8,128)(2,1)S(1)} %multiply_convert_fusion, bf16[256,4096]{1,0:T(8,128)(2,1)} %collective-permute-done.19, s32[]{:T(128)S(6)} %mul.122, bf16[256,4096]{1,0:T(8,128)(2,1)S(1)} %pad_maximum_fusion, pred[]{:T(512)S(6)} %eq.110), kind=kOutput, calls=%fused_computation.5 | convolution fusion | flops 269484032 | bytes 3276805 | tf_op jit(solution)/shard_map/dot_general | solution.py:271
  138.4 2.0 %square.1 = (f32[8,4096]{1,0:T(8,128)}, f32[256,2,128]{2,1,0:T(2,128)}) custom-call(bf16[8,8,3328]{2,1,0:T(8,128)(2,1)} %all-to-all-done.2.a_ref, bf16[8,768]{1,0:T(8,128)(2,1)} %get-tuple-element.43.b0_ref, bf16[8,768]{1,0:T(8,128)(2,1)} %copy-done.6, bf16[8,768]{1,0:T(8,128)(2,1)} %copy-done.7, bf16[8,768]{1,0:T(8,128)(2,1)} %copy-done.8, ...), custom_call_target="tpu_custom_call" | custom-call | tf_op jit(solution)/shard_map/square/pallas_call | solution.py:236
  140.4 14.0 %all-to-all-start.4 = ((f32[256,2,128]{2,1,0:T(2,128)}), f32[256,2,128]{2,1,0:T(2,128)S(1)}, u32[]{:S(2)}, u32[]{:S(2)}) async-start(f32[256,2,128]{2,1,0:T(2,128)} %get-tuple-element.16), calls=%async_computation.4 | async-start | bytes 524288 | tf_op jit(solution)/shard_map/all_to_all | solution.py:28
  154.5 2.7 %convolution_convert_fusion.4 = bf16[256,2048]{1,0:T(8,128)(2,1)} fusion(bf16[256,256]{1,0:T(8,128)(2,1)S(1)} %multiply_convert_fusion, bf16[256,4096]{1,0:T(8,128)(2,1)} %collective-permute-done.19, s32[]{:T(128)S(6)} %mul.120, bf16[256,4096]{1,0:T(8,128)(2,1)S(1)} %pad_maximum_fusion, pred[]{:T(512)S(6)} %eq.108), kind=kOutput, calls=%fused_computation.7 | convolution fusion | flops 269484032 | bytes 3276805 | tf_op jit(solution)/shard_map/dot_general | solution.py:271
  157.2 2.6 %collective-permute-start.20 = (bf16[256,2048]{1,0:T(8,128)(2,1)}, bf16[256,2048]{1,0:T(8,128)(2,1)S(1)}, u32[]{:S(2)}, u32[]{:S(2)}) collective-permute-start(bf16[256,2048]{1,0:T(8,128)(2,1)} %convolution_convert_fusion.4), channel_id=1, source_target_pairs={{0,3},{1,0},{2,1},{3,2},{4,7},{5,4},{6,5},{7,6},{8,11},{9,8},{10,9... | collective-permute-start | bytes 3145736 | tf_op jit(solution)/shard_map/ppermute | solution.py:32
  160.6 26.4 %all-to-all-done.4 = f32[256,2,128]{2,1,0:T(2,128)S(1)} async-done(((f32[256,2,128]{2,1,0:T(2,128)}), f32[256,2,128]{2,1,0:T(2,128)S(1)}, u32[]{:S(2)}, u32[]{:S(2)}) %all-to-all-start.4) | async-done | bytes 262176 | tf_op jit(solution)/shard_map/all_to_all | solution.py:28
  189.9 2.0 multiply_subtract_fusion
  191.9 3.2 %add_convert_fusion = bf16[256,2048]{1,0:T(8,128)(2,1)} fusion(bf16[256,2048]{1,0:T(8,128)(2,1)S(1)} %convolution_convert_fusion.1, bf16[256,2048]{1,0:T(8,128)(2,1)} %collective-permute-done.22, bf16[256,2048]{1,0:T(8,128)(2,1)} %collective-permute-done.21, bf16[256,2048]{1,0:T(8,128)(2,1)S(1)} %collective-permute-done.20), kind=kLoop, calls=%fused_computation.9 | loop fusion | flops 4194304 | bytes 5242880 | tf_op jit(solution)/shard_map/convert_element_type | solution.py:279
  (124 shorter events, 33.5 us)
Async XLA Ops:
  0.7 16.0 %copy-start.13 = (s32[256]{0:T(256)S(1)}, s32[256]{0:T(256)}, u32[]{:S(2)}) copy-start(s32[256]{0:T(256)} %param.14) | copy-start | bytes 3076
  0.7 16.1 %copy-start.12 = (f32[256]{0:T(256)S(1)}, f32[256]{0:T(256)}, u32[]{:S(2)}) copy-start(f32[256]{0:T(256)} %param.16) | copy-start | bytes 3076
  5.5 61.3 %collective-permute-start.7 = (bf16[256,4096]{1,0:T(8,128)(2,1)}, bf16[256,4096]{1,0:T(8,128)(2,1)}, u32[]{:S(2)}, u32[]{:S(2)}) collective-permute-start(bf16[256,4096]{1,0:T(8,128)(2,1)} %get-tuple-element.32), channel_id=1, source_target_pairs={{0,4},{4,0},{1,5},{5,1},{2,6},{6,2},{3,7},{7,3},{8,12},{12,8},{9,1... | collective-permute-start | bytes 6291464 | tf_op jit(solution)/shard_map/ppermute | solution.py:173
  9.8 22.7 %all-to-all-start.1 = ((bf16[16,4,3584]{2,1,0:T(4,128)(2,1)}), bf16[16,4,3584]{2,1,0:T(4,128)(2,1)S(1)}, u32[]{:S(2)}, u32[]{:S(2)}) async-start(bf16[16,4,3584]{2,1,0:T(4,128)(2,1)} %bitcast.12), calls=%async_computation.1 | async-start | bytes 917504 | tf_op jit(solution)/shard_map/all_to_all | solution.py:28
  16.9 1.3 collective-permute-start
  18.2 3.9 %collective-permute-start.3 = (bf16[8,1024]{1,0:T(8,128)(2,1)S(1)}, bf16[8,1024]{1,0:T(8,128)(2,1)S(1)}, u32[]{:S(2)}, u32[]{:S(2)}) collective-permute-start(bf16[8,1024]{1,0:T(8,128)(2,1)S(1)} %maximum_select_fusion.2), channel_id=1, source_target_pairs={{0,192},{64,0},{128,64},{192,128},{1,193},{65,1},{129,65},{193,129... | collective-permute-start | bytes 49160 | tf_op jit(solution)/shard_map/ppermute | solution.py:32
  21.0 4.4 %collective-permute-start.2 = (bf16[8,1024]{1,0:T(8,128)(2,1)S(1)}, bf16[8,1024]{1,0:T(8,128)(2,1)S(1)}, u32[]{:S(2)}, u32[]{:S(2)}) collective-permute-start(bf16[8,1024]{1,0:T(8,128)(2,1)S(1)} %maximum_select_fusion.2), channel_id=1, source_target_pairs={{0,128},{64,192},{128,0},{192,64},{1,129},{65,193},{129,1},{193,65... | collective-permute-start | bytes 49160 | tf_op jit(solution)/shard_map/ppermute | solution.py:32
  21.4 4.2 %collective-permute-start.1 = (bf16[8,1024]{1,0:T(8,128)(2,1)S(1)}, bf16[8,1024]{1,0:T(8,128)(2,1)S(1)}, u32[]{:S(2)}, u32[]{:S(2)}) collective-permute-start(bf16[8,1024]{1,0:T(8,128)(2,1)S(1)} %maximum_select_fusion.2), channel_id=1, source_target_pairs={{0,64},{64,128},{128,192},{192,0},{1,65},{65,129},{129,193},{193,1... | collective-permute-start | bytes 49160 | tf_op jit(solution)/shard_map/ppermute | solution.py:32
  33.4 21.5 %all-to-all-start = ((bf16[8,4,8,1024]{3,2,1,0:T(8,128)(2,1)}), bf16[8,4,8,1024]{3,2,1,0:T(8,128)(2,1)S(1)}, u32[]{:S(2)}, u32[]{:S(2)}) async-start(bf16[8,4,8,1024]{3,2,1,0:T(8,128)(2,1)} %broadcast_in_dim.30), calls=%async_computation | async-start | bytes 1048576 | tf_op jit(solution)/shard_map/all_to_all | solution.py:28
  37.1 22.8 %collective-permute-start.6 = (bf16[64,3584]{1,0:T(8,128)(2,1)S(1)}, bf16[64,3584]{1,0:T(8,128)(2,1)S(1)}, u32[]{:S(2)}, u32[]{:S(2)}) collective-permute-start(bf16[64,3584]{1,0:T(8,128)(2,1)S(1)} %reshape.103), channel_id=1, source_target_pairs={{0,192},{64,0},{128,64},{192,128},{1,193},{65,1},{129,65},{193,129... | collective-permute-start | bytes 1376264 | tf_op jit(solution)/shard_map/ppermute | solution.py:32
  39.9 20.0 %collective-permute-start.5 = (bf16[64,3584]{1,0:T(8,128)(2,1)S(1)}, bf16[64,3584]{1,0:T(8,128)(2,1)S(1)}, u32[]{:S(2)}, u32[]{:S(2)}) collective-permute-start(bf16[64,3584]{1,0:T(8,128)(2,1)S(1)} %reshape.103), channel_id=1, source_target_pairs={{0,128},{64,192},{128,0},{192,64},{1,129},{65,193},{129,1},{193,65... | collective-permute-start | bytes 1376264 | tf_op jit(solution)/shard_map/ppermute | solution.py:32
  40.2 23.5 %collective-permute-start.4 = (bf16[64,3584]{1,0:T(8,128)(2,1)S(1)}, bf16[64,3584]{1,0:T(8,128)(2,1)S(1)}, u32[]{:S(2)}, u32[]{:S(2)}) collective-permute-start(bf16[64,3584]{1,0:T(8,128)(2,1)S(1)} %reshape.103), channel_id=1, source_target_pairs={{0,64},{64,128},{128,192},{192,0},{1,65},{65,129},{129,193},{193,1... | collective-permute-start | bytes 1376264 | tf_op jit(solution)/shard_map/ppermute | solution.py:32
  69.3 2.2 %collective-permute-start.8 = (f32[256,256]{1,0:T(8,128)S(1)}, f32[256,256]{1,0:T(8,128)S(1)}, u32[]{:S(2)}, u32[]{:S(2)}) collective-permute-start(f32[256,256]{1,0:T(8,128)S(1)} %fusion.48), channel_id=1, source_target_pairs={{0,4},{4,0},{1,5},{5,1},{2,6},{6,2},{3,7},{7,3},{8,12},{12,8},{9,1... | collective-permute-start | bytes 786440 | tf_op jit(solution)/shard_map/ppermute | solution.py:181
  69.8 16.7 %copy-start.9 = (s32[128]{0:T(128)S(1)}, s32[128]{0:T(128)}, u32[]{:S(2)}) copy-start(s32[128]{0:T(128)} %span_ref.1) | copy-start | bytes 1540
  74.1 4.3 %collective-permute-start.9 = (f32[8,256]{1,0:T(8,128)}, f32[8,256]{1,0:T(8,128)S(1)}, u32[]{:S(2)}, u32[]{:S(2)}) collective-permute-start(f32[8,256]{1,0:T(8,128)} %get-tuple-element.15), channel_id=1, source_target_pairs={{0,3},{1,0},{2,1},{3,2},{4,7},{5,4},{6,5},{7,6},{8,11},{9,8},{10,9... | collective-permute-start | bytes 24584 | tf_op jit(solution)/shard_map/ppermute | solution.py:32
  76.6 4.2 %collective-permute-start.10 = (f32[8,256]{1,0:T(8,128)}, f32[8,256]{1,0:T(8,128)S(1)}, u32[]{:S(2)}, u32[]{:S(2)}) collective-permute-start(f32[8,256]{1,0:T(8,128)} %get-tuple-element.15), channel_id=1, source_target_pairs={{0,2},{1,3},{2,0},{3,1},{4,6},{5,7},{6,4},{7,5},{8,10},{9,11},{10,... | collective-permute-start | bytes 24584 | tf_op jit(solution)/shard_map/ppermute | solution.py:32
  77.1 3.9 %collective-permute-start.11 = (f32[8,256]{1,0:T(8,128)}, f32[8,256]{1,0:T(8,128)S(1)}, u32[]{:S(2)}, u32[]{:S(2)}) collective-permute-start(f32[8,256]{1,0:T(8,128)} %get-tuple-element.15), channel_id=1, source_target_pairs={{0,1},{1,2},{2,3},{3,0},{4,5},{5,6},{6,7},{7,4},{8,9},{9,10},{10,1... | collective-permute-start | bytes 24584 | tf_op jit(solution)/shard_map/ppermute | solution.py:32
  84.4 5.4 %collective-permute-start.12 = (bf16[256,256]{1,0:T(8,128)(2,1)S(1)}, bf16[256,256]{1,0:T(8,128)(2,1)S(1)}, u32[]{:S(2)}, u32[]{:S(2)}) collective-permute-start(bf16[256,256]{1,0:T(8,128)(2,1)S(1)} %multiply_convert_fusion), channel_id=1, source_target_pairs={{0,4},{4,0},{1,5},{5,1},{2,6},{6,2},{3,7},{7,3},{8,12},{12,8},{9,1... | collective-permute-start | bytes 393224 | tf_op jit(solution)/shard_map/ppermute | solution.py:220
  88.4 40.5 %collective-permute-start.19 = (bf16[256,4096]{1,0:T(8,128)(2,1)S(1)}, bf16[256,4096]{1,0:T(8,128)(2,1)}, u32[]{:S(2)}, u32[]{:S(2)}) collective-permute-start(bf16[256,4096]{1,0:T(8,128)(2,1)S(1)} %pad_maximum_fusion), channel_id=1, source_target_pairs={{0,4},{4,0},{1,5},{5,1},{2,6},{6,2},{3,7},{7,3},{8,12},{12,8},{9,1... | collective-permute-start | bytes 6291464 | tf_op jit(solution)/shard_map/ppermute | solution.py:180
  94.3 21.6 %collective-permute-start.15 = (bf16[64,3328]{1,0:T(8,128)(2,1)}, bf16[64,3328]{1,0:T(8,128)(2,1)}, u32[]{:S(2)}, u32[]{:S(2)}) collective-permute-start(bf16[64,3328]{1,0:T(8,128)(2,1)} %get-tuple-element.34), channel_id=1, source_target_pairs={{0,64},{64,128},{128,192},{192,0},{1,65},{65,129},{129,193},{193,1... | collective-permute-start | bytes 1277960 | tf_op jit(solution)/shard_map/ppermute | solution.py:32
  94.3 21.6 %collective-permute-start.14 = (bf16[64,3328]{1,0:T(8,128)(2,1)S(1)}, bf16[64,3328]{1,0:T(8,128)(2,1)}, u32[]{:S(2)}, u32[]{:S(2)}) collective-permute-start(bf16[64,3328]{1,0:T(8,128)(2,1)S(1)} %get-tuple-element.35), channel_id=1, source_target_pairs={{0,128},{64,192},{128,0},{192,64},{1,129},{65,193},{129,1},{193,65... | collective-permute-start | bytes 1277960 | tf_op jit(solution)/shard_map/ppermute | solution.py:32
  95.8 20.3 %collective-permute-start.13 = (bf16[64,3328]{1,0:T(8,128)(2,1)S(1)}, bf16[64,3328]{1,0:T(8,128)(2,1)}, u32[]{:S(2)}, u32[]{:S(2)}) collective-permute-start(bf16[64,3328]{1,0:T(8,128)(2,1)S(1)} %get-tuple-element.33), channel_id=1, source_target_pairs={{0,192},{64,0},{128,64},{192,128},{1,193},{65,1},{129,65},{193,129... | collective-permute-start | bytes 1277960 | tf_op jit(solution)/shard_map/ppermute | solution.py:32
  99.1 19.8 %all-to-all-start.3 = ((bf16[8,4,8,768]{3,2,1,0:T(8,128)(2,1)}), bf16[8,4,8,768]{3,2,1,0:T(8,128)(2,1)S(1)}, u32[]{:S(2)}, u32[]{:S(2)}) async-start(bf16[8,4,8,768]{3,2,1,0:T(8,128)(2,1)} %bitcast.76), calls=%async_computation.3 | async-start | bytes 786432 | tf_op jit(solution)/shard_map/all_to_all | solution.py:28
  118.9 19.5 %all-to-all-start.2 = ((bf16[8,8,3328]{2,1,0:T(8,128)(2,1)}), bf16[8,8,3328]{2,1,0:T(8,128)(2,1)}, u32[]{:S(2)}, u32[]{:S(2)}) async-start(bf16[8,8,3328]{2,1,0:T(8,128)(2,1)} %fusion.15), calls=%async_computation.2 | async-start | bytes 851968 | tf_op jit(solution)/shard_map/all_to_all | solution.py:28
  125.5 12.2 %collective-permute-start.16 = (bf16[8,768]{1,0:T(8,128)(2,1)S(1)}, bf16[8,768]{1,0:T(8,128)(2,1)S(1)}, u32[]{:S(2)}, u32[]{:S(2)}) collective-permute-start(bf16[8,768]{1,0:T(8,128)(2,1)S(1)} %get-tuple-element.42), channel_id=1, source_target_pairs={{0,192},{64,0},{128,64},{192,128},{1,193},{65,1},{129,65},{193,129... | collective-permute-start | bytes 36872 | tf_op jit(solution)/shard_map/ppermute | solution.py:32
  128.3 9.4 %collective-permute-start.17 = (bf16[8,768]{1,0:T(8,128)(2,1)S(1)}, bf16[8,768]{1,0:T(8,128)(2,1)S(1)}, u32[]{:S(2)}, u32[]{:S(2)}) collective-permute-start(bf16[8,768]{1,0:T(8,128)(2,1)S(1)} %get-tuple-element.41), channel_id=1, source_target_pairs={{0,128},{64,192},{128,0},{192,64},{1,129},{65,193},{129,1},{193,65... | collective-permute-start | bytes 36872 | tf_op jit(solution)/shard_map/ppermute | solution.py:32
  128.3 9.4 %collective-permute-start.18 = (bf16[8,768]{1,0:T(8,128)(2,1)S(1)}, bf16[8,768]{1,0:T(8,128)(2,1)S(1)}, u32[]{:S(2)}, u32[]{:S(2)}) collective-permute-start(bf16[8,768]{1,0:T(8,128)(2,1)S(1)} %get-tuple-element.40), channel_id=1, source_target_pairs={{0,64},{64,128},{128,192},{192,0},{1,65},{65,129},{129,193},{193,1... | collective-permute-start | bytes 36872 | tf_op jit(solution)/shard_map/ppermute | solution.py:32
  133.3 58.6 %collective-permute-start.22 = (bf16[256,2048]{1,0:T(8,128)(2,1)}, bf16[256,2048]{1,0:T(8,128)(2,1)}, u32[]{:S(2)}, u32[]{:S(2)}) collective-permute-start(bf16[256,2048]{1,0:T(8,128)(2,1)} %convolution_convert_fusion.2), channel_id=1, source_target_pairs={{0,1},{1,2},{2,3},{3,0},{4,5},{5,6},{6,7},{7,4},{8,9},{9,10},{10,1... | collective-permute-start | bytes 3145736 | tf_op jit(solution)/shard_map/ppermute | solution.py:32
  136.4 55.4 %collective-permute-start.21 = (bf16[256,2048]{1,0:T(8,128)(2,1)}, bf16[256,2048]{1,0:T(8,128)(2,1)}, u32[]{:S(2)}, u32[]{:S(2)}) collective-permute-start(bf16[256,2048]{1,0:T(8,128)(2,1)} %convolution_convert_fusion.3), channel_id=1, source_target_pairs={{0,2},{1,3},{2,0},{3,1},{4,6},{5,7},{6,4},{7,5},{8,10},{9,11},{10,... | collective-permute-start | bytes 3145736 | tf_op jit(solution)/shard_map/ppermute | solution.py:32
  140.4 46.5 %all-to-all-start.4 = ((f32[256,2,128]{2,1,0:T(2,128)}), f32[256,2,128]{2,1,0:T(2,128)S(1)}, u32[]{:S(2)}, u32[]{:S(2)}) async-start(f32[256,2,128]{2,1,0:T(2,128)} %get-tuple-element.16), calls=%async_computation.4 | async-start | bytes 524288 | tf_op jit(solution)/shard_map/all_to_all | solution.py:28
  157.2 34.6 %collective-permute-start.20 = (bf16[256,2048]{1,0:T(8,128)(2,1)}, bf16[256,2048]{1,0:T(8,128)(2,1)S(1)}, u32[]{:S(2)}, u32[]{:S(2)}) collective-permute-start(bf16[256,2048]{1,0:T(8,128)(2,1)} %convolution_convert_fusion.4), channel_id=1, source_target_pairs={{0,3},{1,0},{2,1},{3,2},{4,7},{5,4},{6,5},{7,6},{8,11},{9,8},{10,9... | collective-permute-start | bytes 3145736 | tf_op jit(solution)/shard_map/ppermute | solution.py:32
  159.8 30.1 %collective-permute-start.23 = (f32[4,4096]{1,0:T(4,128)S(1)}, f32[4,4096]{1,0:T(4,128)S(1)}, u32[]{:S(2)}, u32[]{:S(2)}) collective-permute-start(f32[4,4096]{1,0:T(4,128)S(1)} %get-tuple-element.38), channel_id=1, source_target_pairs={{0,4},{4,0},{1,5},{5,1},{2,6},{6,2},{3,7},{7,3},{8,12},{12,8},{9,1... | collective-permute-start | bytes 196616 | tf_op jit(solution)/shard_map/ppermute | solution.py:251
  (11 other events, 57.1 us)

commit v7 on v6

--- a/solution.py
+++ b/solution.py
@@ -48,13 +48,55 @@
     return exchange(jnp.broadcast_to(x[None], (count,) + x.shape), axes)
 
 
+def score_kernel(thin, a0_ref, a1_ref, a2_ref, a3_ref, b_ref, tok_ref, head_ref, part_ref):
+    wide = a0_ref.shape[1]
+    y_rows = a0_ref.shape[0]
+    for s, a_ref in enumerate((a0_ref, a1_ref, a2_ref, a3_ref)):
+        head_ref[s * y_rows : (s + 1) * y_rows, :wide] = a_ref[...]
+        for z in range(NZ):
+            at = s * y_rows + z * (y_rows // NZ)
+            head_ref[at : at + y_rows // NZ, wide:] = b_ref[z, s, :, :thin]
+    part_ref[...] = lax.dot_general(
+        head_ref[...], tok_ref[...], (((1,), (1,)), ((), ())), preferred_element_type=f32
+    )
+
+
+def final_kernel(
+    place_ref, report_ref, row_ref, near_ref, mate_ref, master_ref, moment_ref, second_ref,
+    loss_ref, mean_ref, new_master_ref, new_moment_ref, new_second_ref,
+):
+    sums = jnp.sum(report_ref[...], axis=0)
+    norm_value = jnp.sqrt(sums[0:1, 0:1]) / loss_scale
+    clip_factor = jnp.minimum(1.0, clip_norm / (norm_value + 1e-06))
+    lanes = report_ref.shape[2] // 2
+    mean_ref[...] = jnp.sum(sums[:, lanes:], axis=1, keepdims=True) * row_ref[5:6, 0:1]
+    for i in (0, 1):
+        slot = place_ref[3 + i]
+        for j in (0, 1):
+            loss_ref[i : i + 1, j * lanes : (j + 1) * lanes] = report_ref[2 * slot + j, :, lanes:]
+    half = near_ref.shape[1]
+    for h in (0, 1):
+        cols = slice(h * half, (h + 1) * half)
+        row_grad = jnp.where(place_ref[5] == h, near_ref[...], mate_ref[...])
+        clipped = row_grad * clip_factor
+        new_moment = beta_one * moment_ref[:, cols] + (1.0 - beta_one) * clipped
+        new_second = beta_two * second_ref[:, cols] + (1.0 - beta_two) * clipped * clipped
+        master = master_ref[:, cols]
+        new_master_ref[:, cols] = master - learn_rate * (
+            new_moment / (jnp.sqrt(new_second) + adam_eps) + weight_decay * master
+        )
+        new_moment_ref[:, cols] = new_moment
+        new_second_ref[:, cols] = new_second
+
+
 def front_kernel(
-    group, y_rows, span_ref, place_ref, small_ref, own_ref, mate_ref, logit_ref, stat_ref, row_ref
+    group, y_rows, span_ref, place_ref, b_ref, own_ref, mate_ref, logit_ref, stat_ref, row_ref
 ):
     ctx, y_place, vocab_place = place_ref[0], place_ref[1], place_ref[2]
     tok = own_ref.shape[1]
     span = tok // 2
-    quads = small_ref.shape[2] // NC
+    quads = b_ref.shape[2] // NC
+    small_ref = b_ref.at[:, :, :, b_ref.shape[3] - 2 * tok :]
     left, right = [], []
     for offset in (0, 1):
         sid = span_ref[2 * ctx + offset]
@@ -105,7 +147,8 @@
     total = jnp.sum(part_a * part_a, axis=1, keepdims=True)
     total = total + jnp.sum(part_b * part_b, axis=1, keepdims=True)
     total = jnp.sum(total, axis=0, keepdims=True)
-    row = jnp.concatenate([jnp.broadcast_to(total, (1, 128)), share_ref[...]], 0)
+    share = share_ref[...]
+    row = jnp.concatenate([jnp.broadcast_to(total, share.shape), share], 1)
     report_ref[...] = jnp.broadcast_to(row[None], report_ref.shape)
 
 
@@ -131,7 +174,7 @@
     y_rows = group_rows // NY
     chip_rows = y_rows // NZ
 
-    thin = half // 8
+    thin = half // 16
     wide = half - thin
     thin_g = half * 3 // 16
     wide_g = half - thin_g
@@ -152,18 +195,17 @@
     far_b = lax.ppermute(far_b, "core", SWAP)
     chip_b = pair(near_b, far_b, core == 0, 0)
     chips_b = jnp.stack([chip_b] + [shift(chip_b, "y", NY, s) for s in range(1, NY)], 0)
-    head_a = jnp.concatenate([block] + [shift(block, "y", NY, s) for s in range(1, NY)], 0)
+    parts_a = [block] + [shift(block, "y", NY, s) for s in range(1, NY)]
     part_b = spread(chips_b, "z", NZ)
     slot_ids = jnp.arange(span_order.shape[0], dtype=jnp.int32)
     slots = [
         jnp.sum(jnp.where(span_order == 2 * ctx_place + offset, slot_ids, 0))
         for offset in (0, 1)
     ]
-    slots = lax.optimization_barrier([slot * (vocab_count // 2) for slot in slots])
-    head_b = part_b[..., :thin].transpose(1, 0, 2, 3).reshape(group_rows, thin)
-    head = jnp.concatenate([head_a, head_b], 1)
-    small = part_b[..., thin:]
-
+    at = jnp.arange(8, dtype=jnp.int32)
+    place = jnp.where(at == 0, ctx_place, jnp.where(at == 1, y_place, vocab_place))
+    place = jnp.where(at == 3, slots[0], jnp.where(at == 4, slots[1], place))
+    place = lax.optimization_barrier(jnp.where(at == 5, core, place))
     own_half = lax.dynamic_slice(
         hidden_states, (0, core * half), (tok_rows, half), allow_negative_indices=False
     )
@@ -176,11 +218,19 @@
     def score(tok):
         return lax.dot_general(head, tok, (((1,), (1,)), ((), ())), preferred_element_type=f32)
 
-    mate_part = score(mate_half)
+    head, mate_part = pl.pallas_call(
+        functools.partial(score_kernel, thin),
+        out_shape=(
+            jax.ShapeDtypeStruct((group_rows, half), bf16),
+            jax.ShapeDtypeStruct((group_rows, tok_rows), f32),
+        ),
+        in_specs=[VMEM] * (NY + 2),
+        out_specs=(VMEM, VMEM),
+        name="score",
+    )(*parts_a, part_b, mate_half)
     mate_head = lax.ppermute(head, "core", SWAP)
     mate_part = lax.ppermute(mate_part, "core", SWAP)
     own_part = score(own_half)
-    place = jnp.stack([ctx_place, y_place, vocab_place])
     logits, stats, rows = pl.pallas_call(
         functools.partial(front_kernel, group_rows, y_rows),
         out_shape=(
@@ -191,7 +241,7 @@
         in_specs=[SMEM, SMEM, VMEM, VMEM, VMEM],
         out_specs=(VMEM, VMEM, VMEM),
         name="front",
-    )(span_order, place, small, own_part, mate_part)
+    )(span_order, place, part_b, own_part, mate_part)
     tgt_rows = rows[0].astype(jnp.int32)
     mask_rows, prior_rows, outside, mask_scale = rows[1], rows[2], rows[3], rows[4]
     local_col = tgt_rows - block_total - vocab_place * group_rows
@@ -232,26 +282,21 @@
     pieces_a = exchange(by_y, "z")
     lanes = tok_rows // vocab_count
     share = lax.dynamic_slice_in_dim(loss_rows, vocab_place * lanes, lanes, 0)
-    share = jnp.pad(share, (0, span - lanes))[None]
+    share = share[None]
     chip_grad, report = pl.pallas_call(
         square_kernel,
         out_shape=(
             jax.ShapeDtypeStruct((chip_rows, half), f32),
-            jax.ShapeDtypeStruct((ctx_count * vocab_count, 2, span), f32),
+            jax.ShapeDtypeStruct((ctx_count * vocab_count, 1, 2 * lanes), f32),
         ),
         in_specs=[VMEM] * (NY + 2),
         out_specs=(VMEM, VMEM),
         name="square",
     )(pieces_a, *pieces_b, share)
     reports = exchange(report, ALL)
-    square_sum = jnp.sum(reports[:, 0], axis=0)
-    mean_loss = jnp.sum(reports[:, 1]) * rows[5, 0]
     near = lax.dynamic_slice_in_dim(chip_grad, core * shard_rows, shard_rows, 0)
     far = lax.dynamic_slice_in_dim(chip_grad, (1 - core) * shard_rows, shard_rows, 0)
     mate = lax.ppermute(far, "core", SWAP)
-    row_grad = jnp.where(
-        core == 0, jnp.concatenate([near, mate], 1), jnp.concatenate([mate, near], 1)
-    )
 
     width = feat // vocab_count
     per_half = vocab_count // NC
@@ -278,24 +323,22 @@
         hidden_parts.append(part)
     hidden_grad = sum(part.astype(f32) for part in hidden_parts).astype(bf16)
 
-    per_span = vocab_count // 2
-    natural = [
-        lax.dynamic_slice(
-            reports, (slot, 1, 0), (per_span, 1, lanes), allow_negative_indices=False
-        ).reshape(span)
-        for slot in slots
-    ]
-    token_loss = jnp.concatenate(natural, 0)
-
-    norm_value = jnp.sqrt(square_sum) / loss_scale
-    clip_factor = jnp.minimum(1.0, clip_norm / (norm_value + 1e-06))
-    clip_factor = jnp.broadcast_to(clip_factor, (shard_rows, feat // span, span))
-    clipped = row_grad * clip_factor.reshape(shard_rows, feat)
-    new_moment = beta_one * moment + (1.0 - beta_one) * clipped
-    new_second = beta_two * second + (1.0 - beta_two) * clipped * clipped
-    new_master = master - learn_rate * (
-        new_moment / (jnp.sqrt(new_second) + adam_eps) + weight_decay * master
-    )
+    state = jax.ShapeDtypeStruct((shard_rows, feat), f32)
+    token_loss, mean_loss, new_master, new_moment, new_second = pl.pallas_call(
+        final_kernel,
+        out_shape=(
+            jax.ShapeDtypeStruct((2, span), f32),
+            jax.ShapeDtypeStruct((1, 1), f32),
+            state,
+            state,
+            state,
+        ),
+        in_specs=[SMEM] + [VMEM] * 7,
+        out_specs=(VMEM,) * 5,
+        name="final",
+    )(place, reports, rows, near, mate, master, moment, second)
+    token_loss = token_loss.reshape(tok_rows)
+    mean_loss = mean_loss[0, 0]
     return (token_loss, mean_loss, hidden_grad, new_master, new_moment, new_second)
 
 

time: 197 us -> 194 us (0.985)
  Pallas kernels: 3.91 us -> 10.5 us
  waiting for transfers between devices: 73.5 us -> 69.2 us
  other arithmetic: 19.2 us -> 15 us
  between operations: 4.93 us -> 1.02 us
    all_to_all x5, waiting for transfers between devices: 47.7 us -> 37.1 us  [exchange(): return lax.all_to_all(x, axes, 0, 0, tiled=True)]
    pallas_call x0 -> x2, Pallas kernels: none -> 6.65 us  [the longest x1 4.35 us: step(): pl.pallas_call(functools.partial(score_kernel, thin), out_shape=(jax.Shap...]
    ppermute x18, waiting for transfers between devices: 24.7 us -> 29.5 us  [shift(): lax.ppermute(x, axis, [(i, (i + step) % count) for i in range(count)])]
    concatenate x2 -> x0, other arithmetic: 2.85 us -> none  [the longest x1 2.28 us: step(): head = jnp.concatenate([head_a, head_b], 1)]
    ppermute x18, starting transfers between devices: 21.2 us -> 24 us  [shift(): lax.ppermute(x, axis, [(i, (i + step) % count) for i in range(count)])]
    all_to_all x5, starting transfers between devices: 36.8 us -> 34.4 us  [exchange(): return lax.all_to_all(x, axes, 0, 0, tiled=True)]
    unnamed x28 -> x36, local copies, waits for them, and re-layouts: 1.51 us -> 3.55 us
    dot_general x2 -> x1, matrix products: 4.14 us -> 3.82 us  [score(): lax.dot_general(head, tok, (((1,), (1,)), ((), ())), preferred_element_ty...]
  transfers between devices with their start and end apart: 29 -> 29, of which waited for: 14 -> 15; matrix products, arithmetic and copies ran while one was open for 17% -> 16% of each run, Pallas kernels for 1% -> 2%
where the time goes in v7:
time: 194 us; the launch traced here: 193 us
  waiting for transfers between devices  69.2 us (36%)
  starting transfers between devices  66.6 us (34%)
  matrix products  15.8 us (8%)
  local copies, waits for them, and re-layouts  15.1 us (8%)
  other arithmetic  15 us (8%)
  Pallas kernels  10.5 us (5%)
    all_to_all x5, waiting for transfers between devices, exchange(): return lax.all_to_all(x, axes, 0, 0, tiled=True)  37.1 us
    all_to_all x5, starting transfers between devices, exchange(): return lax.all_to_all(x, axes, 0, 0, tiled=True)  34.4 us
    ppermute x18, waiting for transfers between devices, shift(): lax.ppermute(x, axis, [(i, (i + step) % count) for i in range(count)])  29.5 us
    ppermute x18, starting transfers between devices, shift(): lax.ppermute(x, axis, [(i, (i + step) % count) for i in range(count)])  24 us
    dot_general x4, matrix products, step(): lax.dot_general(dlogits, side, (((0,), (0,)), ((), ())), preferred_elemen...  8.48 us
    pallas_call x1, Pallas kernels, step(): pl.pallas_call(functools.partial(score_kernel, thin), out_shape=(jax.Shap...  4.35 us
    dynamic_slice x1, local copies, waits for them, and re-layouts, step(): lax.dynamic_slice(hidden_states, (0, core * half), (tok_rows, half), allo...  3.98 us
  transfers between devices with their start and end apart: 29, of which 15 were waited for; matrix products, arithmetic and copies ran while one was open for 16% of the time, Pallas kernels for 2%

profile of v7, /device:TPU:1, one launch (start us, length us, event | category | flops | bytes accessed | tf_op | source)
XLA Modules:
  0.0 193.2 jit_solution(6696676805983546402)
XLA Ops:
  0.7 4.0 %constant_dynamic-slice_fusion.2 = (bf16[256,4096]{1,0:T(8,128)(2,1)}, bf16[256,4096]{1,0:T(8,128)(2,1)S(1)}) fusion(bf16[256,8192]{1,0:T(8,128)(2,1)} %param.9, s32[]{:T(128)S(6)} %mul.63, s32[]{:T(128)S(6)} %mul.62), kind=kLoop, calls=%fused_computation.62 | loop fusion | bytes 8388616 | tf_op jit(solution)/shard_map/dynamic_slice | solution.py:209
  4.6 3.3 %collective-permute-start.7 = (bf16[256,4096]{1,0:T(8,128)(2,1)S(1)}, bf16[256,4096]{1,0:T(8,128)(2,1)}, u32[]{:S(2)}, u32[]{:S(2)}) collective-permute-start(bf16[256,4096]{1,0:T(8,128)(2,1)S(1)} %get-tuple-element.35), channel_id=1, source_target_pairs={{0,4},{4,0},{1,5},{5,1},{2,6},{6,2},{3,7},{7,3},{8,12},{12,8},{9,1... | collective-permute-start | bytes 6291464 | tf_op jit(solution)/shard_map/ppermute | solution.py:215
  9.1 6.9 %all-to-all-start.1 = ((bf16[16,4,3840]{2,1,0:T(4,128)(2,1)}), bf16[16,4,3840]{2,1,0:T(4,128)(2,1)S(1)}, u32[]{:S(2)}, u32[]{:S(2)}) async-start(bf16[16,4,3840]{2,1,0:T(4,128)(2,1)} %bitcast.9), calls=%async_computation.1 | async-start | bytes 983040 | tf_op jit(solution)/shard_map/all_to_all | solution.py:28
  17.5 2.8 %collective-permute-start.3 = (bf16[8,768]{1,0:T(8,128)(2,1)S(1)}, bf16[8,768]{1,0:T(8,128)(2,1)S(1)}, u32[]{:S(2)}, u32[]{:S(2)}) collective-permute-start(bf16[8,768]{1,0:T(8,128)(2,1)S(1)} %maximum_select_fusion.1), channel_id=1, source_target_pairs={{0,192},{64,0},{128,64},{192,128},{1,193},{65,1},{129,65},{193,129... | collective-permute-start | bytes 36872 | tf_op jit(solution)/shard_map/ppermute | solution.py:32
  21.4 3.3 %collective-permute-done.2 = bf16[8,768]{1,0:T(8,128)(2,1)S(1)} collective-permute-done((bf16[8,768]{1,0:T(8,128)(2,1)S(1)}, bf16[8,768]{1,0:T(8,128)(2,1)S(1)}, u32[]{:S(2)}, u32[]{:S(2)}) %collective-permute-start.2) | collective-permute-done | bytes 12320 | tf_op jit(solution)/shard_map/ppermute | solution.py:32
  24.8 7.7 %all-to-all-done.1 = bf16[16,4,3840]{2,1,0:T(4,128)(2,1)S(1)} async-done(((bf16[16,4,3840]{2,1,0:T(4,128)(2,1)}), bf16[16,4,3840]{2,1,0:T(4,128)(2,1)S(1)}, u32[]{:S(2)}, u32[]{:S(2)}) %all-to-all-start.1) | async-done | bytes 491552 | tf_op jit(solution)/shard_map/all_to_all | solution.py:28
  33.2 3.5 %all-to-all-start = ((bf16[8,4,8,768]{3,2,1,0:T(8,128)(2,1)}), bf16[8,4,8,768]{3,2,1,0:T(8,128)(2,1)S(1)}, u32[]{:S(2)}, u32[]{:S(2)}) async-start(bf16[8,4,8,768]{3,2,1,0:T(8,128)(2,1)} %broadcast_in_dim.51), calls=%async_computation | async-start | bytes 786432 | tf_op jit(solution)/shard_map/all_to_all | solution.py:28
  38.2 2.6 %collective-permute-start.5 = (bf16[64,3840]{1,0:T(8,128)(2,1)S(1)}, bf16[64,3840]{1,0:T(8,128)(2,1)}, u32[]{:S(2)}, u32[]{:S(2)}) collective-permute-start(bf16[64,3840]{1,0:T(8,128)(2,1)S(1)} %reshape.95.a0_ref), channel_id=1, source_target_pairs={{0,128},{64,192},{128,0},{192,64},{1,129},{65,193},{129,1},{193,65... | collective-permute-start | bytes 1474568 | tf_op jit(solution)/shard_map/ppermute | solution.py:32
  44.4 7.5 %all-to-all-done.b_ref = bf16[8,4,8,768]{3,2,1,0:T(8,128)(2,1)S(1)} async-done(((bf16[8,4,8,768]{3,2,1,0:T(8,128)(2,1)}), bf16[8,4,8,768]{3,2,1,0:T(8,128)(2,1)S(1)}, u32[]{:S(2)}, u32[]{:S(2)}) %all-to-all-start) | async-done | bytes 393248 | tf_op jit(solution)/shard_map/all_to_all | solution.py:28
  51.9 11.2 %collective-permute-done.5.a2_ref = bf16[64,3840]{1,0:T(8,128)(2,1)} collective-permute-done((bf16[64,3840]{1,0:T(8,128)(2,1)S(1)}, bf16[64,3840]{1,0:T(8,128)(2,1)}, u32[]{:S(2)}, u32[]{:S(2)}) %collective-permute-start.5) | collective-permute-done | bytes 491552 | tf_op jit(solution)/shard_map/ppermute | solution.py:32
  63.2 4.4 %score.1 = (bf16[256,4096]{1,0:T(8,128)(2,1)}, f32[256,256]{1,0:T(8,128)}) custom-call(bf16[64,3840]{1,0:T(8,128)(2,1)} %copy-done.3, bf16[64,3840]{1,0:T(8,128)(2,1)} %copy-done.7, bf16[64,3840]{1,0:T(8,128)(2,1)} %collective-permute-done.5.a2_ref, bf16[64,3840]{1,0:T(8,128)(2,1)} %collective-permute-done.6.a3_ref, bf16[8,4,8,768]{3,2,1,0:T(8,128)(2,1)} %copy-done.1, ...), custom_call_target="tpu_custom_call" | custom-call | tf_op jit(solution)/shard_map/score/pallas_call | solution.py:221
  67.9 3.8 %fusion.44.own_ref = f32[256,256]{1,0:T(8,128)} fusion(bf16[256,4096]{1,0:T(8,128)(2,1)} %get-tuple-element.18, bf16[256,4096]{1,0:T(8,128)(2,1)} %get-tuple-element.34), kind=kOutput, calls=%fused_computation.112 | convolution fusion | flops 536870912 | bytes 4456448 | tf_op jit(solution)/shard_map/dot_general | solution.py:219
  72.4 1.9 %front.1 = (f32[256,256]{1,0:T(8,128)}, f32[8,256]{1,0:T(8,128)}, f32[8,256]{1,0:T(8,128)}) custom-call(s32[128]{0:T(128)} %span_ref.1, s32[8]{0:T(128)} %compare_select_fusion.6.place_ref, bf16[8,4,8,768]{3,2,1,0:T(8,128)(2,1)} %copy-done.1, f32[256,256]{1,0:T(8,128)} %fusion.44.own_ref, f32[256,256]{1,0:T(8,128)} %copy-done.8), custom_call_target="tpu_custom_call" | custom-call | tf_op jit(solution)/shard_map/front/pallas_call | solution.py:234
  74.4 2.5 %collective-permute-start.9 = (f32[8,256]{1,0:T(8,128)}, f32[8,256]{1,0:T(8,128)S(1)}, u32[]{:S(2)}, u32[]{:S(2)}) collective-permute-start(f32[8,256]{1,0:T(8,128)} %get-tuple-element.22), channel_id=1, source_target_pairs={{0,3},{1,0},{2,1},{3,2},{4,7},{5,4},{6,5},{7,6},{8,11},{9,8},{10,9... | collective-permute-start | bytes 24584 | tf_op jit(solution)/shard_map/ppermute | solution.py:32
  78.7 2.4 %collective-permute-done.10 = f32[8,256]{1,0:T(8,128)S(1)} collective-permute-done((f32[8,256]{1,0:T(8,128)}, f32[8,256]{1,0:T(8,128)S(1)}, u32[]{:S(2)}, u32[]{:S(2)}) %collective-permute-start.10) | collective-permute-done | bytes 8224 | tf_op jit(solution)/shard_map/ppermute | solution.py:32
  87.6 3.5 %convolution_convert_fusion = bf16[256,4096]{1,0:T(8,128)(2,1)S(1)} fusion(bf16[256,4096]{1,0:T(8,128)(2,1)} %collective-permute-done.7.tok_ref, bf16[256,4096]{1,0:T(8,128)(2,1)} %get-tuple-element.34, bf16[256,256]{1,0:T(8,128)(2,1)S(1)} %collective-permute-done.12, bf16[256,256]{1,0:T(8,128)(2,1)S(1)} %multiply_convert_fusion), kind=kOutput, calls=%fused_computation | convolution fusion | flops 1083703296 | bytes 6553600 | tf_op jit(solution)/shard_map/dot_general | solution.py:273
  94.3 2.2 %collective-permute-start.14 = (bf16[64,3328]{1,0:T(8,128)(2,1)S(1)}, bf16[64,3328]{1,0:T(8,128)(2,1)}, u32[]{:S(2)}, u32[]{:S(2)}) collective-permute-start(bf16[64,3328]{1,0:T(8,128)(2,1)S(1)} %get-tuple-element.38), channel_id=1, source_target_pairs={{0,128},{64,192},{128,0},{192,64},{1,129},{65,193},{129,1},{193,65... | collective-permute-start | bytes 1277960 | tf_op jit(solution)/shard_map/ppermute | solution.py:32
  100.2 6.6 %all-to-all-start.3 = ((bf16[8,4,8,768]{3,2,1,0:T(8,128)(2,1)}), bf16[8,4,8,768]{3,2,1,0:T(8,128)(2,1)S(1)}, u32[]{:S(2)}, u32[]{:S(2)}) async-start(bf16[8,4,8,768]{3,2,1,0:T(8,128)(2,1)} %bitcast.67), calls=%async_computation.3 | async-start | bytes 786432 | tf_op jit(solution)/shard_map/all_to_all | solution.py:28
  106.8 8.7 %collective-permute-done.14 = bf16[64,3328]{1,0:T(8,128)(2,1)} collective-permute-done((bf16[64,3328]{1,0:T(8,128)(2,1)S(1)}, bf16[64,3328]{1,0:T(8,128)(2,1)}, u32[]{:S(2)}, u32[]{:S(2)}) %collective-permute-start.14) | collective-permute-done | bytes 426016 | tf_op jit(solution)/shard_map/ppermute | solution.py:32
  115.4 2.4 %fusion.15 = bf16[8,8,3328]{2,1,0:T(8,128)(2,1)} fusion(bf16[64,3328]{1,0:T(8,128)(2,1)} %collective-permute-done.15, bf16[64,3328]{1,0:T(8,128)(2,1)} %collective-permute-done.14, bf16[64,3328]{1,0:T(8,128)(2,1)} %collective-permute-done.13, bf16[256,4096]{1,0:T(8,128)(2,1)} %copy-done.2), kind=kLoop, calls=%fused_computation.23 | loop fusion | flops 1703936 | bytes 2129920 | tf_op jit(solution)/shard_map/reshape | solution.py:278
  117.8 2.0 %all-to-all-done.3 = bf16[8,4,8,768]{3,2,1,0:T(8,128)(2,1)S(1)} async-done(((bf16[8,4,8,768]{3,2,1,0:T(8,128)(2,1)}), bf16[8,4,8,768]{3,2,1,0:T(8,128)(2,1)S(1)}, u32[]{:S(2)}, u32[]{:S(2)}) %all-to-all-start.3) | async-done | bytes 393248 | tf_op jit(solution)/shard_map/all_to_all | solution.py:28
  119.9 4.5 %all-to-all-start.2 = ((bf16[8,8,3328]{2,1,0:T(8,128)(2,1)}), bf16[8,8,3328]{2,1,0:T(8,128)(2,1)S(1)}, u32[]{:S(2)}, u32[]{:S(2)}) async-start(bf16[8,8,3328]{2,1,0:T(8,128)(2,1)} %fusion.15), calls=%async_computation.2 | async-start | bytes 851968 | tf_op jit(solution)/shard_map/all_to_all | solution.py:28
  125.0 3.1 %collective-permute-start.16 = (bf16[8,768]{1,0:T(8,128)(2,1)S(1)}, bf16[8,768]{1,0:T(8,128)(2,1)S(1)}, u32[]{:S(2)}, u32[]{:S(2)}) collective-permute-start(bf16[8,768]{1,0:T(8,128)(2,1)S(1)} %get-tuple-element.43), channel_id=1, source_target_pairs={{0,192},{64,0},{128,64},{192,128},{1,193},{65,1},{129,65},{193,129... | collective-permute-start | bytes 36872 | tf_op jit(solution)/shard_map/ppermute | solution.py:32
  128.1 2.7 %convolution_convert_fusion.2 = bf16[256,2048]{1,0:T(8,128)(2,1)} fusion(bf16[256,256]{1,0:T(8,128)(2,1)S(1)} %multiply_convert_fusion, bf16[256,4096]{1,0:T(8,128)(2,1)} %collective-permute-done.20, s32[]{:T(128)S(6)} %mul.76, bf16[256,4096]{1,0:T(8,128)(2,1)S(1)} %copy-done, pred[]{:T(512)S(6)} %eq.129), kind=kOutput, calls=%fused_computation.5 | convolution fusion | flops 269484032 | bytes 3276805 | tf_op jit(solution)/shard_map/dot_general | solution.py:316
  135.1 2.7 %convolution_convert_fusion.4 = bf16[256,2048]{1,0:T(8,128)(2,1)} fusion(bf16[256,256]{1,0:T(8,128)(2,1)S(1)} %multiply_convert_fusion, bf16[256,4096]{1,0:T(8,128)(2,1)} %collective-permute-done.20, s32[]{:T(128)S(6)} %mul.74, bf16[256,4096]{1,0:T(8,128)(2,1)S(1)} %copy-done, pred[]{:T(512)S(6)} %eq.127), kind=kOutput, calls=%fused_computation.7 | convolution fusion | flops 269484032 | bytes 3276805 | tf_op jit(solution)/shard_map/dot_general | solution.py:316
  137.8 2.1 %collective-permute-start.21 = (bf16[256,2048]{1,0:T(8,128)(2,1)}, bf16[256,2048]{1,0:T(8,128)(2,1)}, u32[]{:S(2)}, u32[]{:S(2)}) collective-permute-start(bf16[256,2048]{1,0:T(8,128)(2,1)} %convolution_convert_fusion.4), channel_id=1, source_target_pairs={{0,3},{1,0},{2,1},{3,2},{4,7},{5,4},{6,5},{7,6},{8,11},{9,8},{10,9... | collective-permute-start | bytes 3145736 | tf_op jit(solution)/shard_map/ppermute | solution.py:32
  141.2 2.8 %collective-permute-done.17.b2_ref = bf16[8,768]{1,0:T(8,128)(2,1)S(1)} collective-permute-done((bf16[8,768]{1,0:T(8,128)(2,1)S(1)}, bf16[8,768]{1,0:T(8,128)(2,1)S(1)}, u32[]{:S(2)}, u32[]{:S(2)}) %collective-permute-start.17) | collective-permute-done | bytes 12320 | tf_op jit(solution)/shard_map/ppermute | solution.py:32
  147.5 13.0 %all-to-all-start.4 = ((f32[256,1,128]{2,1,0:T(1,128)}), f32[256,1,128]{2,1,0:T(1,128)S(1)}, u32[]{:S(2)}, u32[]{:S(2)}) async-start(f32[256,1,128]{2,1,0:T(1,128)} %get-tuple-element.23), calls=%async_computation.4 | async-start | bytes 262144 | tf_op jit(solution)/shard_map/all_to_all | solution.py:28
  162.2 2.1 %collective-permute-start.19 = (f32[4,4096]{1,0:T(4,128)S(1)}, f32[4,4096]{1,0:T(4,128)S(1)}, u32[]{:S(2)}, u32[]{:S(2)}) collective-permute-start(f32[4,4096]{1,0:T(4,128)S(1)} %get-tuple-element.39), channel_id=1, source_target_pairs={{0,4},{4,0},{1,5},{5,1},{2,6},{6,2},{3,7},{7,3},{8,12},{12,8},{9,1... | collective-permute-start | bytes 196616 | tf_op jit(solution)/shard_map/ppermute | solution.py:299
  165.2 19.8 %all-to-all-done.4.report_ref = f32[256,1,128]{2,1,0:T(1,128)S(1)} async-done(((f32[256,1,128]{2,1,0:T(1,128)}), f32[256,1,128]{2,1,0:T(1,128)S(1)}, u32[]{:S(2)}, u32[]{:S(2)}) %all-to-all-start.4) | async-done | bytes 131104 | tf_op jit(solution)/shard_map/all_to_all | solution.py:28
  185.7 2.3 %final.1 = (f32[2,128]{1,0:T(2,128)}, f32[1,1]{1,0:T(1,128)}, f32[4,8192]{1,0:T(4,128)}, f32[4,8192]{1,0:T(4,128)}, f32[4,8192]{1,0:T(4,128)}) custom-call(s32[8]{0:T(128)} %compare_select_fusion.6.place_ref, f32[256,1,128]{2,1,0:T(1,128)} %copy-done.6, f32[8,256]{1,0:T(8,128)} %get-tuple-element.20.row_ref, f32[4,4096]{1,0:T(4,128)} %get-tuple-element.40.near_ref, ...), custom_call_target="tpu_custom_call" | custom-call | tf_op jit(solution)/shard_map/final/pallas_call | solution.py:327
  189.7 3.5 %add_convert_fusion = bf16[256,2048]{1,0:T(8,128)(2,1)} fusion(bf16[256,2048]{1,0:T(8,128)(2,1)S(1)} %convolution_convert_fusion.1, bf16[256,2048]{1,0:T(8,128)(2,1)} %collective-permute-done.23, bf16[256,2048]{1,0:T(8,128)(2,1)} %collective-permute-done.22, bf16[256,2048]{1,0:T(8,128)(2,1)} %collective-permute-done.21), kind=kLoop, calls=%fused_computation.8 | loop fusion | flops 4194304 | bytes 5242880 | tf_op jit(solution)/shard_map/convert_element_type | solution.py:324
  (120 shorter events, 40.6 us)
Async XLA Ops:
  4.6 58.5 %collective-permute-start.7 = (bf16[256,4096]{1,0:T(8,128)(2,1)S(1)}, bf16[256,4096]{1,0:T(8,128)(2,1)}, u32[]{:S(2)}, u32[]{:S(2)}) collective-permute-start(bf16[256,4096]{1,0:T(8,128)(2,1)S(1)} %get-tuple-element.35), channel_id=1, source_target_pairs={{0,4},{4,0},{1,5},{5,1},{2,6},{6,2},{3,7},{7,3},{8,12},{12,8},{9,1... | collective-permute-start | bytes 6291464 | tf_op jit(solution)/shard_map/ppermute | solution.py:215
  8.1 33.8 %copy-start.13 = (s32[128]{0:T(128)S(1)}, s32[128]{0:T(128)}, u32[]{:S(2)}) copy-start(s32[128]{0:T(128)} %span_ref.1) | copy-start | bytes 1540
  9.1 23.4 %all-to-all-start.1 = ((bf16[16,4,3840]{2,1,0:T(4,128)(2,1)}), bf16[16,4,3840]{2,1,0:T(4,128)(2,1)S(1)}, u32[]{:S(2)}, u32[]{:S(2)}) async-start(bf16[16,4,3840]{2,1,0:T(4,128)(2,1)} %bitcast.9), calls=%async_computation.1 | async-start | bytes 983040 | tf_op jit(solution)/shard_map/all_to_all | solution.py:28
  16.2 1.3 collective-permute-start
  17.5 3.9 %collective-permute-start.3 = (bf16[8,768]{1,0:T(8,128)(2,1)S(1)}, bf16[8,768]{1,0:T(8,128)(2,1)S(1)}, u32[]{:S(2)}, u32[]{:S(2)}) collective-permute-start(bf16[8,768]{1,0:T(8,128)(2,1)S(1)} %maximum_select_fusion.1), channel_id=1, source_target_pairs={{0,192},{64,0},{128,64},{192,128},{1,193},{65,1},{129,65},{193,129... | collective-permute-start | bytes 36872 | tf_op jit(solution)/shard_map/ppermute | solution.py:32
  20.3 4.3 %collective-permute-start.2 = (bf16[8,768]{1,0:T(8,128)(2,1)S(1)}, bf16[8,768]{1,0:T(8,128)(2,1)S(1)}, u32[]{:S(2)}, u32[]{:S(2)}) collective-permute-start(bf16[8,768]{1,0:T(8,128)(2,1)S(1)} %maximum_select_fusion.1), channel_id=1, source_target_pairs={{0,128},{64,192},{128,0},{192,64},{1,129},{65,193},{129,1},{193,65... | collective-permute-start | bytes 36872 | tf_op jit(solution)/shard_map/ppermute | solution.py:32
  20.6 4.1 %collective-permute-start.1 = (bf16[8,768]{1,0:T(8,128)(2,1)S(1)}, bf16[8,768]{1,0:T(8,128)(2,1)S(1)}, u32[]{:S(2)}, u32[]{:S(2)}) collective-permute-start(bf16[8,768]{1,0:T(8,128)(2,1)S(1)} %maximum_select_fusion.1), channel_id=1, source_target_pairs={{0,64},{64,128},{128,192},{192,0},{1,65},{65,129},{129,193},{193,1... | collective-permute-start | bytes 36872 | tf_op jit(solution)/shard_map/ppermute | solution.py:32
  33.2 18.7 %all-to-all-start = ((bf16[8,4,8,768]{3,2,1,0:T(8,128)(2,1)}), bf16[8,4,8,768]{3,2,1,0:T(8,128)(2,1)S(1)}, u32[]{:S(2)}, u32[]{:S(2)}) async-start(bf16[8,4,8,768]{3,2,1,0:T(8,128)(2,1)} %broadcast_in_dim.51), calls=%async_computation | async-start | bytes 786432 | tf_op jit(solution)/shard_map/all_to_all | solution.py:28
  36.8 26.3 %copy-start.3 = (bf16[64,3840]{1,0:T(8,128)(2,1)}, bf16[64,3840]{1,0:T(8,128)(2,1)S(1)}, u32[]{:S(2)}) copy-start(bf16[64,3840]{1,0:T(8,128)(2,1)S(1)} %reshape.95.a0_ref) | copy-start | bytes 1474564
  36.8 15.1 %collective-permute-start.4 = (bf16[64,3840]{1,0:T(8,128)(2,1)S(1)}, bf16[64,3840]{1,0:T(8,128)(2,1)S(1)}, u32[]{:S(2)}, u32[]{:S(2)}) collective-permute-start(bf16[64,3840]{1,0:T(8,128)(2,1)S(1)} %reshape.95.a0_ref), channel_id=1, source_target_pairs={{0,64},{64,128},{128,192},{192,0},{1,65},{65,129},{129,193},{193,1... | collective-permute-start | bytes 1474568 | tf_op jit(solution)/shard_map/ppermute | solution.py:32
  38.2 24.9 %collective-permute-start.5 = (bf16[64,3840]{1,0:T(8,128)(2,1)S(1)}, bf16[64,3840]{1,0:T(8,128)(2,1)}, u32[]{:S(2)}, u32[]{:S(2)}) collective-permute-start(bf16[64,3840]{1,0:T(8,128)(2,1)S(1)} %reshape.95.a0_ref), channel_id=1, source_target_pairs={{0,128},{64,192},{128,0},{192,64},{1,129},{65,193},{129,1},{193,65... | collective-permute-start | bytes 1474568 | tf_op jit(solution)/shard_map/ppermute | solution.py:32
  40.8 22.3 %collective-permute-start.6 = (bf16[64,3840]{1,0:T(8,128)(2,1)S(1)}, bf16[64,3840]{1,0:T(8,128)(2,1)}, u32[]{:S(2)}, u32[]{:S(2)}) collective-permute-start(bf16[64,3840]{1,0:T(8,128)(2,1)S(1)} %reshape.95.a0_ref), channel_id=1, source_target_pairs={{0,192},{64,0},{128,64},{192,128},{1,193},{65,1},{129,65},{193,129... | collective-permute-start | bytes 1474568 | tf_op jit(solution)/shard_map/ppermute | solution.py:32
  67.5 4.2 %collective-permute-start.8 = (f32[256,256]{1,0:T(8,128)}, f32[256,256]{1,0:T(8,128)S(1)}, u32[]{:S(2)}, u32[]{:S(2)}) collective-permute-start(f32[256,256]{1,0:T(8,128)} %get-tuple-element.19), channel_id=1, source_target_pairs={{0,4},{4,0},{1,5},{5,1},{2,6},{6,2},{3,7},{7,3},{8,12},{12,8},{9,1... | collective-permute-start | bytes 786440 | tf_op jit(solution)/shard_map/ppermute | solution.py:232
  74.4 4.3 %collective-permute-start.9 = (f32[8,256]{1,0:T(8,128)}, f32[8,256]{1,0:T(8,128)S(1)}, u32[]{:S(2)}, u32[]{:S(2)}) collective-permute-start(f32[8,256]{1,0:T(8,128)} %get-tuple-element.22), channel_id=1, source_target_pairs={{0,3},{1,0},{2,1},{3,2},{4,7},{5,4},{6,5},{7,6},{8,11},{9,8},{10,9... | collective-permute-start | bytes 24584 | tf_op jit(solution)/shard_map/ppermute | solution.py:32
  76.9 4.2 %collective-permute-start.10 = (f32[8,256]{1,0:T(8,128)}, f32[8,256]{1,0:T(8,128)S(1)}, u32[]{:S(2)}, u32[]{:S(2)}) collective-permute-start(f32[8,256]{1,0:T(8,128)} %get-tuple-element.22), channel_id=1, source_target_pairs={{0,2},{1,3},{2,0},{3,1},{4,6},{5,7},{6,4},{7,5},{8,10},{9,11},{10,... | collective-permute-start | bytes 24584 | tf_op jit(solution)/shard_map/ppermute | solution.py:32
  77.4 3.9 %collective-permute-start.11 = (f32[8,256]{1,0:T(8,128)}, f32[8,256]{1,0:T(8,128)S(1)}, u32[]{:S(2)}, u32[]{:S(2)}) collective-permute-start(f32[8,256]{1,0:T(8,128)} %get-tuple-element.22), channel_id=1, source_target_pairs={{0,1},{1,2},{2,3},{3,0},{4,5},{5,6},{6,7},{7,4},{8,9},{9,10},{10,1... | collective-permute-start | bytes 24584 | tf_op jit(solution)/shard_map/ppermute | solution.py:32
  84.7 2.9 %collective-permute-start.12 = (bf16[256,256]{1,0:T(8,128)(2,1)S(1)}, bf16[256,256]{1,0:T(8,128)(2,1)S(1)}, u32[]{:S(2)}, u32[]{:S(2)}) collective-permute-start(bf16[256,256]{1,0:T(8,128)(2,1)S(1)} %multiply_convert_fusion), channel_id=1, source_target_pairs={{0,4},{4,0},{1,5},{5,1},{2,6},{6,2},{3,7},{7,3},{8,12},{12,8},{9,1... | collective-permute-start | bytes 393224 | tf_op jit(solution)/shard_map/ppermute | solution.py:270
  86.6 41.5 %collective-permute-start.20 = (bf16[256,4096]{1,0:T(8,128)(2,1)S(1)}, bf16[256,4096]{1,0:T(8,128)(2,1)}, u32[]{:S(2)}, u32[]{:S(2)}) collective-permute-start(bf16[256,4096]{1,0:T(8,128)(2,1)S(1)} %copy-done), channel_id=1, source_target_pairs={{0,4},{4,0},{1,5},{5,1},{2,6},{6,2},{3,7},{7,3},{8,12},{12,8},{9,1... | collective-permute-start | bytes 6291464 | tf_op jit(solution)/shard_map/ppermute | solution.py:231
  93.3 13.5 %collective-permute-start.15 = (bf16[64,3328]{1,0:T(8,128)(2,1)}, bf16[64,3328]{1,0:T(8,128)(2,1)}, u32[]{:S(2)}, u32[]{:S(2)}) collective-permute-start(bf16[64,3328]{1,0:T(8,128)(2,1)} %get-tuple-element.37), channel_id=1, source_target_pairs={{0,64},{64,128},{128,192},{192,0},{1,65},{65,129},{129,193},{193,1... | collective-permute-start | bytes 1277960 | tf_op jit(solution)/shard_map/ppermute | solution.py:32
  94.3 21.2 %collective-permute-start.14 = (bf16[64,3328]{1,0:T(8,128)(2,1)S(1)}, bf16[64,3328]{1,0:T(8,128)(2,1)}, u32[]{:S(2)}, u32[]{:S(2)}) collective-permute-start(bf16[64,3328]{1,0:T(8,128)(2,1)S(1)} %get-tuple-element.38), channel_id=1, source_target_pairs={{0,128},{64,192},{128,0},{192,64},{1,129},{65,193},{129,1},{193,65... | collective-permute-start | bytes 1277960 | tf_op jit(solution)/shard_map/ppermute | solution.py:32
  96.4 19.0 %collective-permute-start.13 = (bf16[64,3328]{1,0:T(8,128)(2,1)S(1)}, bf16[64,3328]{1,0:T(8,128)(2,1)}, u32[]{:S(2)}, u32[]{:S(2)}) collective-permute-start(bf16[64,3328]{1,0:T(8,128)(2,1)S(1)} %get-tuple-element.36), channel_id=1, source_target_pairs={{0,192},{64,0},{128,64},{192,128},{1,193},{65,1},{129,65},{193,129... | collective-permute-start | bytes 1277960 | tf_op jit(solution)/shard_map/ppermute | solution.py:32
  100.2 19.7 %all-to-all-start.3 = ((bf16[8,4,8,768]{3,2,1,0:T(8,128)(2,1)}), bf16[8,4,8,768]{3,2,1,0:T(8,128)(2,1)S(1)}, u32[]{:S(2)}, u32[]{:S(2)}) async-start(bf16[8,4,8,768]{3,2,1,0:T(8,128)(2,1)} %bitcast.67), calls=%async_computation.3 | async-start | bytes 786432 | tf_op jit(solution)/shard_map/all_to_all | solution.py:28
  119.9 24.9 %all-to-all-start.2 = ((bf16[8,8,3328]{2,1,0:T(8,128)(2,1)}), bf16[8,8,3328]{2,1,0:T(8,128)(2,1)S(1)}, u32[]{:S(2)}, u32[]{:S(2)}) async-start(bf16[8,8,3328]{2,1,0:T(8,128)(2,1)} %fusion.15), calls=%async_computation.2 | async-start | bytes 851968 | tf_op jit(solution)/shard_map/all_to_all | solution.py:28
  125.0 15.5 %collective-permute-start.16 = (bf16[8,768]{1,0:T(8,128)(2,1)S(1)}, bf16[8,768]{1,0:T(8,128)(2,1)S(1)}, u32[]{:S(2)}, u32[]{:S(2)}) collective-permute-start(bf16[8,768]{1,0:T(8,128)(2,1)S(1)} %get-tuple-element.43), channel_id=1, source_target_pairs={{0,192},{64,0},{128,64},{192,128},{1,193},{65,1},{129,65},{193,129... | collective-permute-start | bytes 36872 | tf_op jit(solution)/shard_map/ppermute | solution.py:32
  130.8 58.9 %collective-permute-start.23 = (bf16[256,2048]{1,0:T(8,128)(2,1)}, bf16[256,2048]{1,0:T(8,128)(2,1)}, u32[]{:S(2)}, u32[]{:S(2)}) collective-permute-start(bf16[256,2048]{1,0:T(8,128)(2,1)} %convolution_convert_fusion.2), channel_id=1, source_target_pairs={{0,1},{1,2},{2,3},{3,0},{4,5},{5,6},{6,7},{7,4},{8,9},{9,10},{10,1... | collective-permute-start | bytes 3145736 | tf_op jit(solution)/shard_map/ppermute | solution.py:32
  133.8 55.8 %collective-permute-start.22 = (bf16[256,2048]{1,0:T(8,128)(2,1)}, bf16[256,2048]{1,0:T(8,128)(2,1)}, u32[]{:S(2)}, u32[]{:S(2)}) collective-permute-start(bf16[256,2048]{1,0:T(8,128)(2,1)} %convolution_convert_fusion.3), channel_id=1, source_target_pairs={{0,2},{1,3},{2,0},{3,1},{4,6},{5,7},{6,4},{7,5},{8,10},{9,11},{10,... | collective-permute-start | bytes 3145736 | tf_op jit(solution)/shard_map/ppermute | solution.py:32
  137.8 51.9 %collective-permute-start.21 = (bf16[256,2048]{1,0:T(8,128)(2,1)}, bf16[256,2048]{1,0:T(8,128)(2,1)}, u32[]{:S(2)}, u32[]{:S(2)}) collective-permute-start(bf16[256,2048]{1,0:T(8,128)(2,1)} %convolution_convert_fusion.4), channel_id=1, source_target_pairs={{0,3},{1,0},{2,1},{3,2},{4,7},{5,4},{6,5},{7,6},{8,11},{9,8},{10,9... | collective-permute-start | bytes 3145736 | tf_op jit(solution)/shard_map/ppermute | solution.py:32
  139.9 4.1 %collective-permute-start.17 = (bf16[8,768]{1,0:T(8,128)(2,1)S(1)}, bf16[8,768]{1,0:T(8,128)(2,1)S(1)}, u32[]{:S(2)}, u32[]{:S(2)}) collective-permute-start(bf16[8,768]{1,0:T(8,128)(2,1)S(1)} %get-tuple-element.42), channel_id=1, source_target_pairs={{0,128},{64,192},{128,0},{192,64},{1,129},{65,193},{129,1},{193,65... | collective-permute-start | bytes 36872 | tf_op jit(solution)/shard_map/ppermute | solution.py:32
  140.6 4.2 %collective-permute-start.18 = (bf16[8,768]{1,0:T(8,128)(2,1)S(1)}, bf16[8,768]{1,0:T(8,128)(2,1)S(1)}, u32[]{:S(2)}, u32[]{:S(2)}) collective-permute-start(bf16[8,768]{1,0:T(8,128)(2,1)S(1)} %get-tuple-element.41), channel_id=1, source_target_pairs={{0,64},{64,128},{128,192},{192,0},{1,65},{65,129},{129,193},{193,1... | collective-permute-start | bytes 36872 | tf_op jit(solution)/shard_map/ppermute | solution.py:32
  147.5 37.5 %all-to-all-start.4 = ((f32[256,1,128]{2,1,0:T(1,128)}), f32[256,1,128]{2,1,0:T(1,128)S(1)}, u32[]{:S(2)}, u32[]{:S(2)}) async-start(f32[256,1,128]{2,1,0:T(1,128)} %get-tuple-element.23), calls=%async_computation.4 | async-start | bytes 262144 | tf_op jit(solution)/shard_map/all_to_all | solution.py:28
  162.2 3.0 %collective-permute-start.19 = (f32[4,4096]{1,0:T(4,128)S(1)}, f32[4,4096]{1,0:T(4,128)S(1)}, u32[]{:S(2)}, u32[]{:S(2)}) collective-permute-start(f32[4,4096]{1,0:T(4,128)S(1)} %get-tuple-element.39), channel_id=1, source_target_pairs={{0,4},{4,0},{1,5},{5,1},{2,6},{6,2},{3,7},{7,3},{8,12},{12,8},{9,1... | collective-permute-start | bytes 196616 | tf_op jit(solution)/shard_map/ppermute | solution.py:299
  165.2 19.8 %copy-start.9 = (f32[4,4096]{1,0:T(4,128)}, f32[4,4096]{1,0:T(4,128)S(1)}, u32[]{:S(2)}) copy-start(f32[4,4096]{1,0:T(4,128)S(1)} %collective-permute-done.19.mate_ref) | copy-start | bytes 196612
  (15 other events, 103.0 us)

commit v8 on v7

--- a/solution.py
+++ b/solution.py
@@ -48,7 +48,9 @@
     return exchange(jnp.broadcast_to(x[None], (count,) + x.shape), axes)
 
 
-def score_kernel(thin, a0_ref, a1_ref, a2_ref, a3_ref, b_ref, tok_ref, head_ref, part_ref):
+def score_kernel(
+    thin, a0_ref, a1_ref, a2_ref, a3_ref, b_ref, own_ref, mate_ref, head_ref, own_part_ref, mate_part_ref
+):
     wide = a0_ref.shape[1]
     y_rows = a0_ref.shape[0]
     for s, a_ref in enumerate((a0_ref, a1_ref, a2_ref, a3_ref)):
@@ -56,9 +58,33 @@
         for z in range(NZ):
             at = s * y_rows + z * (y_rows // NZ)
             head_ref[at : at + y_rows // NZ, wide:] = b_ref[z, s, :, :thin]
-    part_ref[...] = lax.dot_general(
-        head_ref[...], tok_ref[...], (((1,), (1,)), ((), ())), preferred_element_type=f32
-    )
+    for tok_ref, part_ref in ((mate_ref, mate_part_ref), (own_ref, own_part_ref)):
+        part_ref[...] = lax.dot_general(
+            head_ref[...], tok_ref[...], (((1,), (1,)), ((), ())), preferred_element_type=f32
+        )
+
+
+def grad_kernel(own_d_ref, mate_d_ref, own_ref, mate_ref, a0_ref, a1_ref, a2_ref, a3_ref, b_ref):
+    step = pl.program_id(0)
+    cols = own_ref.shape[1]
+    y_rows, wide = a0_ref.shape
+    full, rest = wide // cols, wide % cols
+    total = jnp.dot(own_d_ref[...], own_ref[...], preferred_element_type=f32)
+    total = total + jnp.dot(mate_d_ref[...], mate_ref[...], preferred_element_type=f32)
+
+    @pl.when(step < full)
+    def _():
+        at = pl.multiple_of(jnp.minimum(step, full - 1) * cols, cols)
+        for s, a_ref in enumerate((a0_ref, a1_ref, a2_ref, a3_ref)):
+            a_ref[:, pl.ds(at, cols)] = total[s * y_rows : (s + 1) * y_rows].astype(bf16)
+
+    @pl.when(step == full)
+    def _():
+        for s, a_ref in enumerate((a0_ref, a1_ref, a2_ref, a3_ref)):
+            a_ref[:, full * cols :] = total[s * y_rows : (s + 1) * y_rows, :rest].astype(bf16)
+            for z in range(NZ):
+                at = s * y_rows + z * (y_rows // NZ)
+                b_ref[z, s] = total[at : at + y_rows // NZ, rest:].astype(bf16)
 
 
 def final_kernel(
@@ -213,24 +239,20 @@
         hidden_states, (0, (1 - core) * half), (tok_rows, half), allow_negative_indices=False
     )
     mate_half = lax.ppermute(far_half, "core", SWAP)
-    tokens = jnp.concatenate([own_half, mate_half], 0)
-
-    def score(tok):
-        return lax.dot_general(head, tok, (((1,), (1,)), ((), ())), preferred_element_type=f32)
-
-    head, mate_part = pl.pallas_call(
+
+    head, own_part, mate_part = pl.pallas_call(
         functools.partial(score_kernel, thin),
         out_shape=(
             jax.ShapeDtypeStruct((group_rows, half), bf16),
             jax.ShapeDtypeStruct((group_rows, tok_rows), f32),
+            jax.ShapeDtypeStruct((group_rows, tok_rows), f32),
         ),
-        in_specs=[VMEM] * (NY + 2),
-        out_specs=(VMEM, VMEM),
+        in_specs=[VMEM] * (NY + 3),
+        out_specs=(VMEM, VMEM, VMEM),
         name="score",
-    )(*parts_a, part_b, mate_half)
+    )(*parts_a, part_b, own_half, mate_half)
     mate_head = lax.ppermute(head, "core", SWAP)
     mate_part = lax.ppermute(mate_part, "core", SWAP)
-    own_part = score(own_half)
     logits, stats, rows = pl.pallas_call(
         functools.partial(front_kernel, group_rows, y_rows),
         out_shape=(
@@ -269,14 +291,25 @@
     ).astype(bf16)
     mate_dlogits = lax.ppermute(dlogits, "core", SWAP)
 
-    both = jnp.concatenate([dlogits, mate_dlogits], 1)
-    partial_rows = jnp.dot(both, tokens, preferred_element_type=f32).astype(bf16)
-    blocks = [partial_rows[s * y_rows : (s + 1) * y_rows, :wide_g] for s in range(NY)]
+    cols = half // 4
+    block_shape = jax.ShapeDtypeStruct((y_rows, wide_g), bf16)
+    fixed = pl.BlockSpec((y_rows, wide_g), lambda i: (0, 0))
+    dlog_spec = pl.BlockSpec((group_rows, tok_rows), lambda i: (0, 0))
+    tok_spec = pl.BlockSpec((tok_rows, cols), lambda i: (0, i))
+    *blocks, by_z = pl.pallas_call(
+        grad_kernel,
+        grid=(half // cols,),
+        out_shape=[block_shape] * NY
+        + [jax.ShapeDtypeStruct((NZ, NY, chip_rows, thin_g), bf16)],
+        in_specs=[dlog_spec, dlog_spec, tok_spec, tok_spec],
+        out_specs=[fixed] * NY
+        + [pl.BlockSpec((NZ, NY, chip_rows, thin_g), lambda i: (0, 0, 0, 0))],
+        name="grad",
+    )(dlogits, mate_dlogits, own_half, mate_half)
     by_y = blocks[0].astype(f32)
     for s in range(1, NY):
         by_y = by_y + shift(blocks[s], "y", NY, -s).astype(f32)
     by_y = by_y.astype(bf16).reshape(NZ, chip_rows, wide_g)
-    by_z = partial_rows[:, wide_g:].reshape(NY, NZ, chip_rows, thin_g).transpose(1, 0, 2, 3)
     by_z = jnp.sum(exchange(by_z, "z").astype(f32), axis=0).astype(bf16)
     pieces_b = [by_z[0]] + [shift(by_z[s], "y", NY, -s) for s in range(1, NY)]
     pieces_a = exchange(by_y, "z")

time: 194 us -> 196 us (1.010)
  matrix products: 15.8 us -> 8.5 us
  Pallas kernels: 10.5 us -> 17.2 us
  starting transfers between devices: 66.6 us -> 71.6 us
  waiting for transfers between devices: 69.2 us -> 66.6 us
    all_to_all x5, waiting for transfers between devices: 37.1 us -> 28.4 us  [exchange(): return lax.all_to_all(x, axes, 0, 0, tiled=True)]
    all_to_all x5, starting transfers between devices: 34.4 us -> 42.9 us  [exchange(): return lax.all_to_all(x, axes, 0, 0, tiled=True)]
    dot_general x2 -> x0, matrix products: 7.29 us -> none  [the longest x1 3.82 us: score(): lax.dot_general(head, tok, (((1,), (1,)), ((), ())), preferred_element_ty...]
    pallas_call x0 -> x1, Pallas kernels: none -> 5.43 us  [step(): pl.pallas_call(grad_kernel, grid=(half // cols,), out_shape=[block_shape]...]
    ppermute x18, waiting for transfers between devices: 29.5 us -> 32.8 us  [shift(): lax.ppermute(x, axis, [(i, (i + step) % count) for i in range(count)])]
    ppermute x1, starting transfers between devices: 3.29 us -> 0.11 us  [step(): mate_half = lax.ppermute(far_half, 'core', SWAP)]
    ppermute x1, waiting for transfers between devices: 1.06 us -> 3.55 us  [step(): far_b = lax.ppermute(far_b, 'core', SWAP)]
    ppermute x18, starting transfers between devices: 24 us -> 21.8 us  [shift(): lax.ppermute(x, axis, [(i, (i + step) % count) for i in range(count)])]
  transfers between devices with their start and end apart: 29 -> 29, of which waited for: 15 -> 17; matrix products, arithmetic and copies ran while one was open for 16% -> 15% of each run, Pallas kernels for 2% -> 6%
where the time goes in v8:
time: 196 us; the launch traced here: 194 us
  starting transfers between devices  71.6 us (37%)
  waiting for transfers between devices  66.6 us (34%)
  Pallas kernels  17.2 us (9%)
  other arithmetic  15.7 us (8%)
  local copies, waits for them, and re-layouts  13.9 us (7%)
  matrix products  8.5 us (4%)
    all_to_all x5, starting transfers between devices, exchange(): return lax.all_to_all(x, axes, 0, 0, tiled=True)  42.9 us
    ppermute x18, waiting for transfers between devices, shift(): lax.ppermute(x, axis, [(i, (i + step) % count) for i in range(count)])  32.8 us
    all_to_all x5, waiting for transfers between devices, exchange(): return lax.all_to_all(x, axes, 0, 0, tiled=True)  28.4 us
    ppermute x18, starting transfers between devices, shift(): lax.ppermute(x, axis, [(i, (i + step) % count) for i in range(count)])  21.8 us
    dot_general x4, matrix products, step(): lax.dot_general(dlogits, side, (((0,), (0,)), ((), ())), preferred_elemen...  8.5 us
    pallas_call x1, Pallas kernels, step(): pl.pallas_call(functools.partial(score_kernel, thin), out_shape=(jax.Shap...  5.58 us
    pallas_call x1, Pallas kernels, step(): pl.pallas_call(grad_kernel, grid=(half // cols,), out_shape=[block_shape]...  5.43 us
    dynamic_slice x1, local copies, waits for them, and re-layouts, step(): lax.dynamic_slice(hidden_states, (0, (1 - core) * half), (tok_rows, half)...  4.77 us
  transfers between devices with their start and end apart: 29, of which 17 were waited for; matrix products, arithmetic and copies ran while one was open for 15% of the time, Pallas kernels for 6%

profile of v8, /device:TPU:1, one launch (start us, length us, event | category | flops | bytes accessed | tf_op | source)
XLA Modules:
  0.0 194.5 jit_solution(5598964953849404260)
XLA Ops:
  2.6 10.0 %all-to-all-start.1 = ((bf16[16,4,3840]{2,1,0:T(4,128)(2,1)}), bf16[16,4,3840]{2,1,0:T(4,128)(2,1)S(1)}, u32[]{:S(2)}, u32[]{:S(2)}) async-start(bf16[16,4,3840]{2,1,0:T(4,128)(2,1)} %bitcast.9), calls=%async_computation.1 | async-start | bytes 983040 | tf_op jit(solution)/shard_map/all_to_all | solution.py:28
  12.7 4.8 %constant_dynamic-slice_fusion.2 = (bf16[256,4096]{1,0:T(8,128)(2,1)}, bf16[256,4096]{1,0:T(8,128)(2,1)}) fusion(bf16[256,8192]{1,0:T(8,128)(2,1)} %param.9, s32[]{:T(128)S(6)} %mul.63, s32[]{:T(128)S(6)} %mul.62), kind=kLoop, calls=%fused_computation.54 | loop fusion | bytes 8388616 | tf_op jit(solution)/shard_map/dynamic_slice | solution.py:238
  18.3 3.6 %collective-permute-done = bf16[4,768]{1,0:T(4,128)(2,1)S(1)} collective-permute-done((bf16[4,768]{1,0:T(4,128)(2,1)S(1)}, bf16[4,768]{1,0:T(4,128)(2,1)S(1)}, u32[]{:S(2)}, u32[]{:S(2)}) %collective-permute-start) | collective-permute-done | bytes 6176 | tf_op jit(solution)/shard_map/ppermute | solution.py:221
  21.8 2.8 %collective-permute-start.3 = (bf16[8,768]{1,0:T(8,128)(2,1)S(1)}, bf16[8,768]{1,0:T(8,128)(2,1)S(1)}, u32[]{:S(2)}, u32[]{:S(2)}) collective-permute-start(bf16[8,768]{1,0:T(8,128)(2,1)S(1)} %maximum_select_fusion.1), channel_id=1, source_target_pairs={{0,192},{64,0},{128,64},{192,128},{1,193},{65,1},{129,65},{193,129... | collective-permute-start | bytes 36872 | tf_op jit(solution)/shard_map/ppermute | solution.py:32
  25.7 3.0 %collective-permute-done.2 = bf16[8,768]{1,0:T(8,128)(2,1)S(1)} collective-permute-done((bf16[8,768]{1,0:T(8,128)(2,1)S(1)}, bf16[8,768]{1,0:T(8,128)(2,1)S(1)}, u32[]{:S(2)}, u32[]{:S(2)}) %collective-permute-start.2) | collective-permute-done | bytes 12320 | tf_op jit(solution)/shard_map/ppermute | solution.py:32
  29.9 6.3 %all-to-all-start = ((bf16[8,4,8,768]{3,2,1,0:T(8,128)(2,1)}), bf16[8,4,8,768]{3,2,1,0:T(8,128)(2,1)S(1)}, u32[]{:S(2)}, u32[]{:S(2)}) async-start(bf16[8,4,8,768]{3,2,1,0:T(8,128)(2,1)} %broadcast_in_dim.51), calls=%async_computation | async-start | bytes 786432 | tf_op jit(solution)/shard_map/all_to_all | solution.py:28
  38.2 1.9 collective-permute-start.6
  40.1 8.3 %all-to-all-done.b_ref = bf16[8,4,8,768]{3,2,1,0:T(8,128)(2,1)S(1)} async-done(((bf16[8,4,8,768]{3,2,1,0:T(8,128)(2,1)}), bf16[8,4,8,768]{3,2,1,0:T(8,128)(2,1)S(1)}, u32[]{:S(2)}, u32[]{:S(2)}) %all-to-all-start) | async-done | bytes 393248 | tf_op jit(solution)/shard_map/all_to_all | solution.py:28
  48.6 9.8 %collective-permute-done.5.a2_ref = bf16[64,3840]{1,0:T(8,128)(2,1)} collective-permute-done((bf16[64,3840]{1,0:T(8,128)(2,1)S(1)}, bf16[64,3840]{1,0:T(8,128)(2,1)}, u32[]{:S(2)}, u32[]{:S(2)}) %collective-permute-start.5) | collective-permute-done | bytes 491552 | tf_op jit(solution)/shard_map/ppermute | solution.py:32
  58.3 2.5 %collective-permute-done.6.a3_ref = bf16[64,3840]{1,0:T(8,128)(2,1)} collective-permute-done((bf16[64,3840]{1,0:T(8,128)(2,1)S(1)}, bf16[64,3840]{1,0:T(8,128)(2,1)}, u32[]{:S(2)}, u32[]{:S(2)}) %collective-permute-start.6) | collective-permute-done | bytes 491552 | tf_op jit(solution)/shard_map/ppermute | solution.py:32
  62.3 5.6 %score.1 = (bf16[256,4096]{1,0:T(8,128)(2,1)}, f32[256,256]{1,0:T(8,128)}, f32[256,256]{1,0:T(8,128)}) custom-call(bf16[64,3840]{1,0:T(8,128)(2,1)} %copy-done.5, bf16[64,3840]{1,0:T(8,128)(2,1)} %copy-done.8, bf16[64,3840]{1,0:T(8,128)(2,1)} %collective-permute-done.5.a2_ref, bf16[64,3840]{1,0:T(8,128)(2,1)} %collective-permute-done.6.a3_ref, ...), custom_call_target="tpu_custom_call" | custom-call | tf_op jit(solution)/shard_map/score/pallas_call | solution.py:243
  72.7 2.0 %front.1 = (f32[256,256]{1,0:T(8,128)}, f32[8,256]{1,0:T(8,128)}, f32[8,256]{1,0:T(8,128)}) custom-call(s32[128]{0:T(128)} %span_ref.1, s32[8]{0:T(128)} %compare_select_fusion.6.place_ref, bf16[8,4,8,768]{3,2,1,0:T(8,128)(2,1)} %copy-done.4, f32[256,256]{1,0:T(8,128)} %get-tuple-element.24.own_ref, f32[256,256]{1,0:T(8,128)} %copy-done.9), custom_call_target="tpu_custom_call" | custom-call | tf_op jit(solution)/shard_map/front/pallas_call | solution.py:256
  74.7 2.5 %collective-permute-start.9 = (f32[8,256]{1,0:T(8,128)}, f32[8,256]{1,0:T(8,128)S(1)}, u32[]{:S(2)}, u32[]{:S(2)}) collective-permute-start(f32[8,256]{1,0:T(8,128)} %get-tuple-element.28), channel_id=1, source_target_pairs={{0,3},{1,0},{2,1},{3,2},{4,7},{5,4},{6,5},{7,6},{8,11},{9,8},{10,9... | collective-permute-start | bytes 24584 | tf_op jit(solution)/shard_map/ppermute | solution.py:32
  79.0 2.4 %collective-permute-done.10 = f32[8,256]{1,0:T(8,128)S(1)} collective-permute-done((f32[8,256]{1,0:T(8,128)}, f32[8,256]{1,0:T(8,128)S(1)}, u32[]{:S(2)}, u32[]{:S(2)}) %collective-permute-start.10) | collective-permute-done | bytes 8224 | tf_op jit(solution)/shard_map/ppermute | solution.py:32
  85.0 2.5 %collective-permute-start.12 = (bf16[256,256]{1,0:T(8,128)(2,1)S(1)}, bf16[256,256]{1,0:T(8,128)(2,1)S(1)}, u32[]{:S(2)}, u32[]{:S(2)}) collective-permute-start(bf16[256,256]{1,0:T(8,128)(2,1)S(1)} %multiply_convert_fusion.own_d_ref), channel_id=1, source_target_pairs={{0,4},{4,0},{1,5},{5,1},{2,6},{6,2},{3,7},{7,3},{8,12},{12,8},{9,1... | collective-permute-start | bytes 393224 | tf_op jit(solution)/shard_map/ppermute | solution.py:292
  89.1 5.4 %grad.1 = (bf16[64,3328]{1,0:T(8,128)(2,1)}, bf16[64,3328]{1,0:T(8,128)(2,1)}, bf16[64,3328]{1,0:T(8,128)(2,1)}, bf16[64,3328]{1,0:T(8,128)(2,1)}, bf16[8,4,8,768]{3,2,1,0:T(8,128)(2,1)}) custom-call(bf16[256,256]{1,0:T(8,128)(2,1)} %copy-done.2, bf16[256,256]{1,0:T(8,128)(2,1)} %copy-done.10, bf16[256,4096]{1,0:T(8,128)(2,1)} %get-tuple-element.47.own_ref, ...), custom_call_target="tpu_custom_call" | custom-call | tf_op jit(solution)/shard_map/grad/pallas_call | solution.py:299
  95.5 2.6 %collective-permute-start.14 = (bf16[64,3328]{1,0:T(8,128)(2,1)}, bf16[64,3328]{1,0:T(8,128)(2,1)S(1)}, u32[]{:S(2)}, u32[]{:S(2)}) collective-permute-start(bf16[64,3328]{1,0:T(8,128)(2,1)} %get-tuple-element.31), channel_id=1, source_target_pairs={{0,128},{64,192},{128,0},{192,64},{1,129},{65,193},{129,1},{193,65... | collective-permute-start | bytes 1277960 | tf_op jit(solution)/shard_map/ppermute | solution.py:32
  99.0 6.8 %all-to-all-start.3 = ((bf16[8,4,8,768]{3,2,1,0:T(8,128)(2,1)}), bf16[8,4,8,768]{3,2,1,0:T(8,128)(2,1)S(1)}, u32[]{:S(2)}, u32[]{:S(2)}) async-start(bf16[8,4,8,768]{3,2,1,0:T(8,128)(2,1)} %get-tuple-element.33), calls=%async_computation.3 | async-start | bytes 786432 | tf_op jit(solution)/shard_map/all_to_all | solution.py:28
  107.0 10.0 %collective-permute-done.14 = bf16[64,3328]{1,0:T(8,128)(2,1)S(1)} collective-permute-done((bf16[64,3328]{1,0:T(8,128)(2,1)}, bf16[64,3328]{1,0:T(8,128)(2,1)S(1)}, u32[]{:S(2)}, u32[]{:S(2)}) %collective-permute-start.14) | collective-permute-done | bytes 426016 | tf_op jit(solution)/shard_map/ppermute | solution.py:32
  117.0 2.1 %fusion.12 = bf16[8,8,3328]{2,1,0:T(8,128)(2,1)} fusion(bf16[64,3328]{1,0:T(8,128)(2,1)S(1)} %collective-permute-done.15, bf16[64,3328]{1,0:T(8,128)(2,1)S(1)} %collective-permute-done.14, bf16[64,3328]{1,0:T(8,128)(2,1)} %collective-permute-done.13, bf16[64,3328]{1,0:T(8,128)(2,1)} %get-tuple-element.29), kind=kLoop, calls=%fused_computation.19 | loop fusion | flops 1703936 | bytes 2129920 | tf_op jit(solution)/shard_map/reshape | solution.py:312
  119.1 6.7 %all-to-all-start.2 = ((bf16[8,8,3328]{2,1,0:T(8,128)(2,1)}), bf16[8,8,3328]{2,1,0:T(8,128)(2,1)S(1)}, u32[]{:S(2)}, u32[]{:S(2)}) async-start(bf16[8,8,3328]{2,1,0:T(8,128)(2,1)} %fusion.12), calls=%async_computation.2 | async-start | bytes 851968 | tf_op jit(solution)/shard_map/all_to_all | solution.py:28
  126.4 2.9 %collective-permute-start.16 = (bf16[8,768]{1,0:T(8,128)(2,1)S(1)}, bf16[8,768]{1,0:T(8,128)(2,1)S(1)}, u32[]{:S(2)}, u32[]{:S(2)}) collective-permute-start(bf16[8,768]{1,0:T(8,128)(2,1)S(1)} %get-tuple-element.52), channel_id=1, source_target_pairs={{0,192},{64,0},{128,64},{192,128},{1,193},{65,1},{129,65},{193,129... | collective-permute-start | bytes 36872 | tf_op jit(solution)/shard_map/ppermute | solution.py:32
  129.4 2.7 %convolution_convert_fusion.1 = bf16[256,2048]{1,0:T(8,128)(2,1)} fusion(bf16[256,256]{1,0:T(8,128)(2,1)S(1)} %copy-done.3, bf16[256,4096]{1,0:T(8,128)(2,1)} %collective-permute-done.20, s32[]{:T(128)S(6)} %mul.76, bf16[256,4096]{1,0:T(8,128)(2,1)S(1)} %copy-done.1, pred[]{:T(512)S(6)} %eq.129), kind=kOutput, calls=%fused_computation.1 | convolution fusion | flops 269484032 | bytes 3276805 | tf_op jit(solution)/shard_map/dot_general | solution.py:349
  136.4 2.7 %convolution_convert_fusion.3 = bf16[256,2048]{1,0:T(8,128)(2,1)} fusion(bf16[256,256]{1,0:T(8,128)(2,1)S(1)} %copy-done.3, bf16[256,4096]{1,0:T(8,128)(2,1)} %collective-permute-done.20, s32[]{:T(128)S(6)} %mul.74, bf16[256,4096]{1,0:T(8,128)(2,1)S(1)} %copy-done.1, pred[]{:T(512)S(6)} %eq.127), kind=kOutput, calls=%fused_computation.3 | convolution fusion | flops 269484032 | bytes 3276805 | tf_op jit(solution)/shard_map/dot_general | solution.py:349
  139.0 2.1 %collective-permute-start.21 = (bf16[256,2048]{1,0:T(8,128)(2,1)}, bf16[256,2048]{1,0:T(8,128)(2,1)}, u32[]{:S(2)}, u32[]{:S(2)}) collective-permute-start(bf16[256,2048]{1,0:T(8,128)(2,1)} %convolution_convert_fusion.3), channel_id=1, source_target_pairs={{0,3},{1,0},{2,1},{3,2},{4,7},{5,4},{6,5},{7,6},{8,11},{9,8},{10,9... | collective-permute-start | bytes 3145736 | tf_op jit(solution)/shard_map/ppermute | solution.py:32
  142.4 2.9 %collective-permute-done.17.b2_ref = bf16[8,768]{1,0:T(8,128)(2,1)S(1)} collective-permute-done((bf16[8,768]{1,0:T(8,128)(2,1)S(1)}, bf16[8,768]{1,0:T(8,128)(2,1)S(1)}, u32[]{:S(2)}, u32[]{:S(2)}) %collective-permute-start.17) | collective-permute-done | bytes 12320 | tf_op jit(solution)/shard_map/ppermute | solution.py:32
  146.6 1.9 square.1
  148.5 13.2 %all-to-all-start.4 = ((f32[256,1,128]{2,1,0:T(1,128)}), f32[256,1,128]{2,1,0:T(1,128)S(1)}, u32[]{:S(2)}, u32[]{:S(2)}) async-start(f32[256,1,128]{2,1,0:T(1,128)} %get-tuple-element.34), calls=%async_computation.4 | async-start | bytes 262144 | tf_op jit(solution)/shard_map/all_to_all | solution.py:28
  163.4 2.1 %collective-permute-start.19 = (f32[4,4096]{1,0:T(4,128)S(1)}, f32[4,4096]{1,0:T(4,128)S(1)}, u32[]{:S(2)}, u32[]{:S(2)}) collective-permute-start(f32[4,4096]{1,0:T(4,128)S(1)} %get-tuple-element.48), channel_id=1, source_target_pairs={{0,4},{4,0},{1,5},{5,1},{2,6},{6,2},{3,7},{7,3},{8,12},{12,8},{9,1... | collective-permute-start | bytes 196616 | tf_op jit(solution)/shard_map/ppermute | solution.py:332
  166.5 19.8 %all-to-all-done.4.report_ref = f32[256,1,128]{2,1,0:T(1,128)S(1)} async-done(((f32[256,1,128]{2,1,0:T(1,128)}), f32[256,1,128]{2,1,0:T(1,128)S(1)}, u32[]{:S(2)}, u32[]{:S(2)}) %all-to-all-start.4) | async-done | bytes 131104 | tf_op jit(solution)/shard_map/all_to_all | solution.py:28
  186.9 2.3 %final.1 = (f32[2,128]{1,0:T(2,128)}, f32[1,1]{1,0:T(1,128)}, f32[4,8192]{1,0:T(4,128)}, f32[4,8192]{1,0:T(4,128)}, f32[4,8192]{1,0:T(4,128)}) custom-call(s32[8]{0:T(128)} %compare_select_fusion.6.place_ref, f32[256,1,128]{2,1,0:T(1,128)} %copy-done.7, f32[8,256]{1,0:T(8,128)} %get-tuple-element.26.row_ref, f32[4,4096]{1,0:T(4,128)} %get-tuple-element.49.near_ref, ...), custom_call_target="tpu_custom_call" | custom-call | tf_op jit(solution)/shard_map/final/pallas_call | solution.py:360
  190.9 3.5 %add_convert_fusion = bf16[256,2048]{1,0:T(8,128)(2,1)} fusion(bf16[256,2048]{1,0:T(8,128)(2,1)S(1)} %convolution_convert_fusion, bf16[256,2048]{1,0:T(8,128)(2,1)} %collective-permute-done.23, bf16[256,2048]{1,0:T(8,128)(2,1)} %collective-permute-done.22, bf16[256,2048]{1,0:T(8,128)(2,1)} %collective-permute-done.21), kind=kLoop, calls=%fused_computation.4 | loop fusion | flops 4194304 | bytes 5242880 | tf_op jit(solution)/shard_map/convert_element_type | solution.py:357
  (120 shorter events, 36.0 us)
Async XLA Ops:
  2.6 26.5 %all-to-all-start.1 = ((bf16[16,4,3840]{2,1,0:T(4,128)(2,1)}), bf16[16,4,3840]{2,1,0:T(4,128)(2,1)S(1)}, u32[]{:S(2)}, u32[]{:S(2)}) async-start(bf16[16,4,3840]{2,1,0:T(4,128)(2,1)} %bitcast.9), calls=%async_computation.1 | async-start | bytes 983040 | tf_op jit(solution)/shard_map/all_to_all | solution.py:28
  17.4 43.4 %collective-permute-start.7 = (bf16[256,4096]{1,0:T(8,128)(2,1)}, bf16[256,4096]{1,0:T(8,128)(2,1)S(1)}, u32[]{:S(2)}, u32[]{:S(2)}) collective-permute-start(bf16[256,4096]{1,0:T(8,128)(2,1)} %get-tuple-element.46), channel_id=1, source_target_pairs={{0,4},{4,0},{1,5},{5,1},{2,6},{6,2},{3,7},{7,3},{8,12},{12,8},{9,1... | collective-permute-start | bytes 6291464 | tf_op jit(solution)/shard_map/ppermute | solution.py:241
  17.8 4.0 %collective-permute-start = (bf16[4,768]{1,0:T(4,128)(2,1)S(1)}, bf16[4,768]{1,0:T(4,128)(2,1)S(1)}, u32[]{:S(2)}, u32[]{:S(2)}) collective-permute-start(bf16[4,768]{1,0:T(4,128)(2,1)S(1)} %get-tuple-element.68), channel_id=1, source_target_pairs={{0,4},{4,0},{1,5},{5,1},{2,6},{6,2},{3,7},{7,3},{8,12},{12,8},{9,1... | collective-permute-start | bytes 18440 | tf_op jit(solution)/shard_map/ppermute | solution.py:221
  21.8 3.9 %collective-permute-start.3 = (bf16[8,768]{1,0:T(8,128)(2,1)S(1)}, bf16[8,768]{1,0:T(8,128)(2,1)S(1)}, u32[]{:S(2)}, u32[]{:S(2)}) collective-permute-start(bf16[8,768]{1,0:T(8,128)(2,1)S(1)} %maximum_select_fusion.1), channel_id=1, source_target_pairs={{0,192},{64,0},{128,64},{192,128},{1,193},{65,1},{129,65},{193,129... | collective-permute-start | bytes 36872 | tf_op jit(solution)/shard_map/ppermute | solution.py:32
  24.7 4.1 %collective-permute-start.2 = (bf16[8,768]{1,0:T(8,128)(2,1)S(1)}, bf16[8,768]{1,0:T(8,128)(2,1)S(1)}, u32[]{:S(2)}, u32[]{:S(2)}) collective-permute-start(bf16[8,768]{1,0:T(8,128)(2,1)S(1)} %maximum_select_fusion.1), channel_id=1, source_target_pairs={{0,128},{64,192},{128,0},{192,64},{1,129},{65,193},{129,1},{193,65... | collective-permute-start | bytes 36872 | tf_op jit(solution)/shard_map/ppermute | solution.py:32
  25.0 3.8 %collective-permute-start.1 = (bf16[8,768]{1,0:T(8,128)(2,1)S(1)}, bf16[8,768]{1,0:T(8,128)(2,1)S(1)}, u32[]{:S(2)}, u32[]{:S(2)}) collective-permute-start(bf16[8,768]{1,0:T(8,128)(2,1)S(1)} %maximum_select_fusion.1), channel_id=1, source_target_pairs={{0,64},{64,128},{128,192},{192,0},{1,65},{65,129},{129,193},{193,1... | collective-permute-start | bytes 36872 | tf_op jit(solution)/shard_map/ppermute | solution.py:32
  29.9 18.5 %all-to-all-start = ((bf16[8,4,8,768]{3,2,1,0:T(8,128)(2,1)}), bf16[8,4,8,768]{3,2,1,0:T(8,128)(2,1)S(1)}, u32[]{:S(2)}, u32[]{:S(2)}) async-start(bf16[8,4,8,768]{3,2,1,0:T(8,128)(2,1)} %broadcast_in_dim.51), calls=%async_computation | async-start | bytes 786432 | tf_op jit(solution)/shard_map/all_to_all | solution.py:28
  36.3 24.5 %copy-start.5 = (bf16[64,3840]{1,0:T(8,128)(2,1)}, bf16[64,3840]{1,0:T(8,128)(2,1)S(1)}, u32[]{:S(2)}) copy-start(bf16[64,3840]{1,0:T(8,128)(2,1)S(1)} %reshape.92.a0_ref) | copy-start | bytes 1474564
  36.3 12.2 %collective-permute-start.4 = (bf16[64,3840]{1,0:T(8,128)(2,1)S(1)}, bf16[64,3840]{1,0:T(8,128)(2,1)S(1)}, u32[]{:S(2)}, u32[]{:S(2)}) collective-permute-start(bf16[64,3840]{1,0:T(8,128)(2,1)S(1)} %reshape.92.a0_ref), channel_id=1, source_target_pairs={{0,64},{64,128},{128,192},{192,0},{1,65},{65,129},{129,193},{193,1... | collective-permute-start | bytes 1474568 | tf_op jit(solution)/shard_map/ppermute | solution.py:32
  36.4 21.9 %collective-permute-start.5 = (bf16[64,3840]{1,0:T(8,128)(2,1)S(1)}, bf16[64,3840]{1,0:T(8,128)(2,1)}, u32[]{:S(2)}, u32[]{:S(2)}) collective-permute-start(bf16[64,3840]{1,0:T(8,128)(2,1)S(1)} %reshape.92.a0_ref), channel_id=1, source_target_pairs={{0,128},{64,192},{128,0},{192,64},{1,129},{65,193},{129,1},{193,65... | collective-permute-start | bytes 1474568 | tf_op jit(solution)/shard_map/ppermute | solution.py:32
  38.2 22.7 %collective-permute-start.6 = (bf16[64,3840]{1,0:T(8,128)(2,1)S(1)}, bf16[64,3840]{1,0:T(8,128)(2,1)}, u32[]{:S(2)}, u32[]{:S(2)}) collective-permute-start(bf16[64,3840]{1,0:T(8,128)(2,1)S(1)} %reshape.92.a0_ref), channel_id=1, source_target_pairs={{0,192},{64,0},{128,64},{192,128},{1,193},{65,1},{129,65},{193,129... | collective-permute-start | bytes 1474568 | tf_op jit(solution)/shard_map/ppermute | solution.py:32
  67.8 4.1 %collective-permute-start.8 = (f32[256,256]{1,0:T(8,128)}, f32[256,256]{1,0:T(8,128)S(1)}, u32[]{:S(2)}, u32[]{:S(2)}) collective-permute-start(f32[256,256]{1,0:T(8,128)} %get-tuple-element.25), channel_id=1, source_target_pairs={{0,4},{4,0},{1,5},{5,1},{2,6},{6,2},{3,7},{7,3},{8,12},{12,8},{9,1... | collective-permute-start | bytes 786440 | tf_op jit(solution)/shard_map/ppermute | solution.py:255
  72.0 57.4 %collective-permute-start.20 = (bf16[256,4096]{1,0:T(8,128)(2,1)}, bf16[256,4096]{1,0:T(8,128)(2,1)}, u32[]{:S(2)}, u32[]{:S(2)}) collective-permute-start(bf16[256,4096]{1,0:T(8,128)(2,1)} %get-tuple-element.38), channel_id=1, source_target_pairs={{0,4},{4,0},{1,5},{5,1},{2,6},{6,2},{3,7},{7,3},{8,12},{12,8},{9,1... | collective-permute-start | bytes 6291464 | tf_op jit(solution)/shard_map/ppermute | solution.py:254
  74.7 4.3 %collective-permute-start.9 = (f32[8,256]{1,0:T(8,128)}, f32[8,256]{1,0:T(8,128)S(1)}, u32[]{:S(2)}, u32[]{:S(2)}) collective-permute-start(f32[8,256]{1,0:T(8,128)} %get-tuple-element.28), channel_id=1, source_target_pairs={{0,3},{1,0},{2,1},{3,2},{4,7},{5,4},{6,5},{7,6},{8,11},{9,8},{10,9... | collective-permute-start | bytes 24584 | tf_op jit(solution)/shard_map/ppermute | solution.py:32
  77.1 4.2 %collective-permute-start.10 = (f32[8,256]{1,0:T(8,128)}, f32[8,256]{1,0:T(8,128)S(1)}, u32[]{:S(2)}, u32[]{:S(2)}) collective-permute-start(f32[8,256]{1,0:T(8,128)} %get-tuple-element.28), channel_id=1, source_target_pairs={{0,2},{1,3},{2,0},{3,1},{4,6},{5,7},{6,4},{7,5},{8,10},{9,11},{10,... | collective-permute-start | bytes 24584 | tf_op jit(solution)/shard_map/ppermute | solution.py:32
  77.7 3.9 %collective-permute-start.11 = (f32[8,256]{1,0:T(8,128)}, f32[8,256]{1,0:T(8,128)S(1)}, u32[]{:S(2)}, u32[]{:S(2)}) collective-permute-start(f32[8,256]{1,0:T(8,128)} %get-tuple-element.28), channel_id=1, source_target_pairs={{0,1},{1,2},{2,3},{3,0},{4,5},{5,6},{6,7},{7,4},{8,9},{9,10},{10,1... | collective-permute-start | bytes 24584 | tf_op jit(solution)/shard_map/ppermute | solution.py:32
  85.0 3.5 %collective-permute-start.12 = (bf16[256,256]{1,0:T(8,128)(2,1)S(1)}, bf16[256,256]{1,0:T(8,128)(2,1)S(1)}, u32[]{:S(2)}, u32[]{:S(2)}) collective-permute-start(bf16[256,256]{1,0:T(8,128)(2,1)S(1)} %multiply_convert_fusion.own_d_ref), channel_id=1, source_target_pairs={{0,4},{4,0},{1,5},{5,1},{2,6},{6,2},{3,7},{7,3},{8,12},{12,8},{9,1... | collective-permute-start | bytes 393224 | tf_op jit(solution)/shard_map/ppermute | solution.py:292
  94.5 12.4 %collective-permute-start.15 = (bf16[64,3328]{1,0:T(8,128)(2,1)}, bf16[64,3328]{1,0:T(8,128)(2,1)S(1)}, u32[]{:S(2)}, u32[]{:S(2)}) collective-permute-start(bf16[64,3328]{1,0:T(8,128)(2,1)} %get-tuple-element.32), channel_id=1, source_target_pairs={{0,64},{64,128},{128,192},{192,0},{1,65},{65,129},{129,193},{193,1... | collective-permute-start | bytes 1277960 | tf_op jit(solution)/shard_map/ppermute | solution.py:32
  95.5 21.4 %collective-permute-start.14 = (bf16[64,3328]{1,0:T(8,128)(2,1)}, bf16[64,3328]{1,0:T(8,128)(2,1)S(1)}, u32[]{:S(2)}, u32[]{:S(2)}) collective-permute-start(bf16[64,3328]{1,0:T(8,128)(2,1)} %get-tuple-element.31), channel_id=1, source_target_pairs={{0,128},{64,192},{128,0},{192,64},{1,129},{65,193},{129,1},{193,65... | collective-permute-start | bytes 1277960 | tf_op jit(solution)/shard_map/ppermute | solution.py:32
  98.1 18.9 %collective-permute-start.13 = (bf16[64,3328]{1,0:T(8,128)(2,1)}, bf16[64,3328]{1,0:T(8,128)(2,1)}, u32[]{:S(2)}, u32[]{:S(2)}) collective-permute-start(bf16[64,3328]{1,0:T(8,128)(2,1)} %get-tuple-element.30), channel_id=1, source_target_pairs={{0,192},{64,0},{128,64},{192,128},{1,193},{65,1},{129,65},{193,129... | collective-permute-start | bytes 1277960 | tf_op jit(solution)/shard_map/ppermute | solution.py:32
  98.9 30.4 %copy-start.1 = (bf16[256,4096]{1,0:T(8,128)(2,1)S(1)}, bf16[256,4096]{1,0:T(8,128)(2,1)}, u32[]{:S(2)}) copy-start(bf16[256,4096]{1,0:T(8,128)(2,1)} %get-tuple-element.38) | copy-start | bytes 6291460
  99.0 30.4 %copy-start.3 = (bf16[256,256]{1,0:T(8,128)(2,1)S(1)}, bf16[256,256]{1,0:T(8,128)(2,1)}, u32[]{:S(2)}) copy-start(bf16[256,256]{1,0:T(8,128)(2,1)} %copy-done.2) | copy-start | bytes 393220
  99.0 20.1 %all-to-all-start.3 = ((bf16[8,4,8,768]{3,2,1,0:T(8,128)(2,1)}), bf16[8,4,8,768]{3,2,1,0:T(8,128)(2,1)S(1)}, u32[]{:S(2)}, u32[]{:S(2)}) async-start(bf16[8,4,8,768]{3,2,1,0:T(8,128)(2,1)} %get-tuple-element.33), calls=%async_computation.3 | async-start | bytes 786432 | tf_op jit(solution)/shard_map/all_to_all | solution.py:28
  119.1 26.7 %all-to-all-start.2 = ((bf16[8,8,3328]{2,1,0:T(8,128)(2,1)}), bf16[8,8,3328]{2,1,0:T(8,128)(2,1)S(1)}, u32[]{:S(2)}, u32[]{:S(2)}) async-start(bf16[8,8,3328]{2,1,0:T(8,128)(2,1)} %fusion.12), calls=%async_computation.2 | async-start | bytes 851968 | tf_op jit(solution)/shard_map/all_to_all | solution.py:28
  126.4 15.2 %collective-permute-start.16 = (bf16[8,768]{1,0:T(8,128)(2,1)S(1)}, bf16[8,768]{1,0:T(8,128)(2,1)S(1)}, u32[]{:S(2)}, u32[]{:S(2)}) collective-permute-start(bf16[8,768]{1,0:T(8,128)(2,1)S(1)} %get-tuple-element.52), channel_id=1, source_target_pairs={{0,192},{64,0},{128,64},{192,128},{1,193},{65,1},{129,65},{193,129... | collective-permute-start | bytes 36872 | tf_op jit(solution)/shard_map/ppermute | solution.py:32
  132.0 58.9 %collective-permute-start.23 = (bf16[256,2048]{1,0:T(8,128)(2,1)}, bf16[256,2048]{1,0:T(8,128)(2,1)}, u32[]{:S(2)}, u32[]{:S(2)}) collective-permute-start(bf16[256,2048]{1,0:T(8,128)(2,1)} %convolution_convert_fusion.1), channel_id=1, source_target_pairs={{0,1},{1,2},{2,3},{3,0},{4,5},{5,6},{6,7},{7,4},{8,9},{9,10},{10,1... | collective-permute-start | bytes 3145736 | tf_op jit(solution)/shard_map/ppermute | solution.py:32
  135.1 55.8 %collective-permute-start.22 = (bf16[256,2048]{1,0:T(8,128)(2,1)}, bf16[256,2048]{1,0:T(8,128)(2,1)}, u32[]{:S(2)}, u32[]{:S(2)}) collective-permute-start(bf16[256,2048]{1,0:T(8,128)(2,1)} %convolution_convert_fusion.2), channel_id=1, source_target_pairs={{0,2},{1,3},{2,0},{3,1},{4,6},{5,7},{6,4},{7,5},{8,10},{9,11},{10,... | collective-permute-start | bytes 3145736 | tf_op jit(solution)/shard_map/ppermute | solution.py:32
  139.0 51.9 %collective-permute-start.21 = (bf16[256,2048]{1,0:T(8,128)(2,1)}, bf16[256,2048]{1,0:T(8,128)(2,1)}, u32[]{:S(2)}, u32[]{:S(2)}) collective-permute-start(bf16[256,2048]{1,0:T(8,128)(2,1)} %convolution_convert_fusion.3), channel_id=1, source_target_pairs={{0,3},{1,0},{2,1},{3,2},{4,7},{5,4},{6,5},{7,6},{8,11},{9,8},{10,9... | collective-permute-start | bytes 3145736 | tf_op jit(solution)/shard_map/ppermute | solution.py:32
  141.1 4.1 %collective-permute-start.17 = (bf16[8,768]{1,0:T(8,128)(2,1)S(1)}, bf16[8,768]{1,0:T(8,128)(2,1)S(1)}, u32[]{:S(2)}, u32[]{:S(2)}) collective-permute-start(bf16[8,768]{1,0:T(8,128)(2,1)S(1)} %get-tuple-element.51), channel_id=1, source_target_pairs={{0,128},{64,192},{128,0},{192,64},{1,129},{65,193},{129,1},{193,65... | collective-permute-start | bytes 36872 | tf_op jit(solution)/shard_map/ppermute | solution.py:32
  141.6 4.2 %collective-permute-start.18 = (bf16[8,768]{1,0:T(8,128)(2,1)S(1)}, bf16[8,768]{1,0:T(8,128)(2,1)S(1)}, u32[]{:S(2)}, u32[]{:S(2)}) collective-permute-start(bf16[8,768]{1,0:T(8,128)(2,1)S(1)} %get-tuple-element.50), channel_id=1, source_target_pairs={{0,64},{64,128},{128,192},{192,0},{1,65},{65,129},{129,193},{193,1... | collective-permute-start | bytes 36872 | tf_op jit(solution)/shard_map/ppermute | solution.py:32
  148.5 37.7 %all-to-all-start.4 = ((f32[256,1,128]{2,1,0:T(1,128)}), f32[256,1,128]{2,1,0:T(1,128)S(1)}, u32[]{:S(2)}, u32[]{:S(2)}) async-start(f32[256,1,128]{2,1,0:T(1,128)} %get-tuple-element.34), calls=%async_computation.4 | async-start | bytes 262144 | tf_op jit(solution)/shard_map/all_to_all | solution.py:28
  163.4 3.0 %collective-permute-start.19 = (f32[4,4096]{1,0:T(4,128)S(1)}, f32[4,4096]{1,0:T(4,128)S(1)}, u32[]{:S(2)}, u32[]{:S(2)}) collective-permute-start(f32[4,4096]{1,0:T(4,128)S(1)} %get-tuple-element.48), channel_id=1, source_target_pairs={{0,4},{4,0},{1,5},{5,1},{2,6},{6,2},{3,7},{7,3},{8,12},{12,8},{9,1... | collective-permute-start | bytes 196616 | tf_op jit(solution)/shard_map/ppermute | solution.py:332
  (17 other events, 84.7 us)

commit v9 on v7

--- a/solution.py
+++ b/solution.py
@@ -48,17 +48,34 @@
     return exchange(jnp.broadcast_to(x[None], (count,) + x.shape), axes)
 
 
-def score_kernel(thin, a0_ref, a1_ref, a2_ref, a3_ref, b_ref, tok_ref, head_ref, part_ref):
-    wide = a0_ref.shape[1]
-    y_rows = a0_ref.shape[0]
-    for s, a_ref in enumerate((a0_ref, a1_ref, a2_ref, a3_ref)):
-        head_ref[s * y_rows : (s + 1) * y_rows, :wide] = a_ref[...]
-        for z in range(NZ):
-            at = s * y_rows + z * (y_rows // NZ)
-            head_ref[at : at + y_rows // NZ, wide:] = b_ref[z, s, :, :thin]
-    part_ref[...] = lax.dot_general(
-        head_ref[...], tok_ref[...], (((1,), (1,)), ((), ())), preferred_element_type=f32
-    )
+def score_kernel(
+    a0_ref, a1_ref, a2_ref, a3_ref, b_ref, own_ref, mate_ref, head_ref, own_part_ref, mate_part_ref
+):
+    step = pl.program_id(0)
+    last = pl.num_programs(0) - 1
+    y_rows, cols = a0_ref.shape
+
+    @pl.when(step < last)
+    def _():
+        for s, a_ref in enumerate((a0_ref, a1_ref, a2_ref, a3_ref)):
+            head_ref[s * y_rows : (s + 1) * y_rows, :] = a_ref[...]
+
+    @pl.when(step == last)
+    def _():
+        for s in range(NY):
+            for z in range(NZ):
+                at = s * y_rows + z * (y_rows // NZ)
+                head_ref[at : at + y_rows // NZ, :] = b_ref[z, s, :, :cols]
+
+    @pl.when(step == 0)
+    def _():
+        own_part_ref[...] = jnp.zeros(own_part_ref.shape, f32)
+        mate_part_ref[...] = jnp.zeros(mate_part_ref.shape, f32)
+
+    for tok_ref, part_ref in ((mate_ref, mate_part_ref), (own_ref, own_part_ref)):
+        part_ref[...] += lax.dot_general(
+            head_ref[...], tok_ref[...], (((1,), (1,)), ((), ())), preferred_element_type=f32
+        )
 
 
 def final_kernel(
@@ -174,7 +191,7 @@
     y_rows = group_rows // NY
     chip_rows = y_rows // NZ
 
-    thin = half // 16
+    thin = half // 8
     wide = half - thin
     thin_g = half * 3 // 16
     wide_g = half - thin_g
@@ -215,22 +232,25 @@
     mate_half = lax.ppermute(far_half, "core", SWAP)
     tokens = jnp.concatenate([own_half, mate_half], 0)
 
-    def score(tok):
-        return lax.dot_general(head, tok, (((1,), (1,)), ((), ())), preferred_element_type=f32)
-
-    head, mate_part = pl.pallas_call(
-        functools.partial(score_kernel, thin),
+    steps = half // thin
+    block_a = pl.BlockSpec((y_rows, thin), lambda i: (0, jnp.minimum(i, steps - 2)))
+    block_t = pl.BlockSpec((tok_rows, thin), lambda i: (0, i))
+    block_p = pl.BlockSpec((group_rows, tok_rows), lambda i: (0, 0))
+    head, own_part, mate_part = pl.pallas_call(
+        score_kernel,
+        grid=(steps,),
         out_shape=(
             jax.ShapeDtypeStruct((group_rows, half), bf16),
             jax.ShapeDtypeStruct((group_rows, tok_rows), f32),
+            jax.ShapeDtypeStruct((group_rows, tok_rows), f32),
         ),
-        in_specs=[VMEM] * (NY + 2),
-        out_specs=(VMEM, VMEM),
+        in_specs=[block_a] * NY
+        + [pl.BlockSpec(part_b.shape, lambda i: (0, 0, 0, 0)), block_t, block_t],
+        out_specs=(pl.BlockSpec((group_rows, thin), lambda i: (0, i)), block_p, block_p),
         name="score",
-    )(*parts_a, part_b, mate_half)
+    )(*parts_a, part_b, own_half, mate_half)
+    mate_part = lax.ppermute(mate_part, "core", SWAP)
     mate_head = lax.ppermute(head, "core", SWAP)
-    mate_part = lax.ppermute(mate_part, "core", SWAP)
-    own_part = score(own_half)
     logits, stats, rows = pl.pallas_call(
         functools.partial(front_kernel, group_rows, y_rows),
         out_shape=(

time: 194 us -> 197 us (1.015)
  matrix products: 15.8 us -> 11.3 us
  Pallas kernels: 10.5 us -> 14.3 us
  local copies, waits for them, and re-layouts: 15.1 us -> 17.4 us
    all_to_all x5, waiting for transfers between devices: 37.1 us -> 41.7 us  [exchange(): return lax.all_to_all(x, axes, 0, 0, tiled=True)]
    ppermute x18, waiting for transfers between devices: 29.5 us -> 25.1 us  [shift(): lax.ppermute(x, axis, [(i, (i + step) % count) for i in range(count)])]
    dot_general x1 -> x0, matrix products: 3.82 us -> none  [score(): lax.dot_general(head, tok, (((1,), (1,)), ((), ())), preferred_element_ty...]
    pallas_call x1, Pallas kernels: 4.35 us -> 8.1 us  [step(): pl.pallas_call(score_kernel, grid=(steps,), out_shape=(jax.ShapeDtypeStru...]
    unnamed x36 -> x40, local copies, waits for them, and re-layouts: 3.55 us -> 4.95 us
  transfers between devices with their start and end apart: 29 -> 29, of which waited for: 15 -> 15; matrix products, arithmetic and copies ran while one was open for 16% -> 14% of each run, Pallas kernels for 2% -> 2%
where the time goes in v9:
time: 197 us; the launch traced here: 195 us
  waiting for transfers between devices  69.5 us (35%)
  starting transfers between devices  66.7 us (34%)
  local copies, waits for them, and re-layouts  17.4 us (9%)
  other arithmetic  15.1 us (8%)
  Pallas kernels  14.3 us (7%)
  matrix products  11.3 us (6%)
    all_to_all x5, waiting for transfers between devices, exchange(): return lax.all_to_all(x, axes, 0, 0, tiled=True)  41.7 us
    all_to_all x5, starting transfers between devices, exchange(): return lax.all_to_all(x, axes, 0, 0, tiled=True)  34.4 us
    ppermute x18, waiting for transfers between devices, shift(): lax.ppermute(x, axis, [(i, (i + step) % count) for i in range(count)])  25.1 us
    ppermute x18, starting transfers between devices, shift(): lax.ppermute(x, axis, [(i, (i + step) % count) for i in range(count)])  24.1 us
    dot_general x4, matrix products, step(): lax.dot_general(dlogits, side, (((0,), (0,)), ((), ())), preferred_elemen...  8.5 us
    pallas_call x1, Pallas kernels, step(): pl.pallas_call(score_kernel, grid=(steps,), out_shape=(jax.ShapeDtypeStru...  8.1 us
    unnamed x40, local copies, waits for them, and re-layouts  4.95 us
    dynamic_slice x1, local copies, waits for them, and re-layouts, step(): lax.dynamic_slice(hidden_states, (0, core * half), (tok_rows, half), allo...  4.82 us
  transfers between devices with their start and end apart: 29, of which 15 were waited for; matrix products, arithmetic and copies ran while one was open for 14% of the time, Pallas kernels for 2%

profile of v9, /device:TPU:1, one launch (start us, length us, event | category | flops | bytes accessed | tf_op | source)
XLA Modules:
  0.0 195.4 jit_solution(13764163439050910060)
XLA Ops:
  0.7 4.8 %constant_dynamic-slice_fusion.3 = (bf16[256,4096]{1,0:T(8,128)(2,1)}, bf16[256,4096]{1,0:T(8,128)(2,1)}) fusion(bf16[256,8192]{1,0:T(8,128)(2,1)} %param.9, s32[]{:T(128)S(6)} %mul.62, s32[]{:T(128)S(6)} %mul.63), kind=kLoop, calls=%fused_computation.65 | loop fusion | bytes 8388616 | tf_op jit(solution)/shard_map/dynamic_slice | solution.py:226
  5.5 3.2 %collective-permute-start.7 = (bf16[256,4096]{1,0:T(8,128)(2,1)}, bf16[256,4096]{1,0:T(8,128)(2,1)S(1)}, u32[]{:S(2)}, u32[]{:S(2)}) collective-permute-start(bf16[256,4096]{1,0:T(8,128)(2,1)} %get-tuple-element.37), channel_id=1, source_target_pairs={{0,4},{4,0},{1,5},{5,1},{2,6},{6,2},{3,7},{7,3},{8,12},{12,8},{9,1... | collective-permute-start | bytes 6291464 | tf_op jit(solution)/shard_map/ppermute | solution.py:232
  9.8 6.9 %all-to-all-start.1 = ((bf16[16,4,3584]{2,1,0:T(4,128)(2,1)}), bf16[16,4,3584]{2,1,0:T(4,128)(2,1)S(1)}, u32[]{:S(2)}, u32[]{:S(2)}) async-start(bf16[16,4,3584]{2,1,0:T(4,128)(2,1)} %bitcast.9), calls=%async_computation.1 | async-start | bytes 917504 | tf_op jit(solution)/shard_map/all_to_all | solution.py:28
  18.2 2.8 %collective-permute-start.3 = (bf16[8,1024]{1,0:T(8,128)(2,1)S(1)}, bf16[8,1024]{1,0:T(8,128)(2,1)S(1)}, u32[]{:S(2)}, u32[]{:S(2)}) collective-permute-start(bf16[8,1024]{1,0:T(8,128)(2,1)S(1)} %maximum_select_fusion.1), channel_id=1, source_target_pairs={{0,192},{64,0},{128,64},{192,128},{1,193},{65,1},{129,65},{193,129... | collective-permute-start | bytes 49160 | tf_op jit(solution)/shard_map/ppermute | solution.py:32
  22.1 3.3 %collective-permute-done.2 = bf16[8,1024]{1,0:T(8,128)(2,1)S(1)} collective-permute-done((bf16[8,1024]{1,0:T(8,128)(2,1)S(1)}, bf16[8,1024]{1,0:T(8,128)(2,1)S(1)}, u32[]{:S(2)}, u32[]{:S(2)}) %collective-permute-start.2) | collective-permute-done | bytes 16416 | tf_op jit(solution)/shard_map/ppermute | solution.py:32
  25.6 6.9 %all-to-all-done.1 = bf16[16,4,3584]{2,1,0:T(4,128)(2,1)S(1)} async-done(((bf16[16,4,3584]{2,1,0:T(4,128)(2,1)}), bf16[16,4,3584]{2,1,0:T(4,128)(2,1)S(1)}, u32[]{:S(2)}, u32[]{:S(2)}) %all-to-all-start.1) | async-done | bytes 458784 | tf_op jit(solution)/shard_map/all_to_all | solution.py:28
  33.4 3.5 %all-to-all-start = ((bf16[8,4,8,1024]{3,2,1,0:T(8,128)(2,1)}), bf16[8,4,8,1024]{3,2,1,0:T(8,128)(2,1)S(1)}, u32[]{:S(2)}, u32[]{:S(2)}) async-start(bf16[8,4,8,1024]{3,2,1,0:T(8,128)(2,1)} %broadcast_in_dim.51), calls=%async_computation | async-start | bytes 1048576 | tf_op jit(solution)/shard_map/all_to_all | solution.py:28
  38.4 2.6 %collective-permute-start.5 = (bf16[64,3584]{1,0:T(8,128)(2,1)S(1)}, bf16[64,3584]{1,0:T(8,128)(2,1)}, u32[]{:S(2)}, u32[]{:S(2)}) collective-permute-start(bf16[64,3584]{1,0:T(8,128)(2,1)S(1)} %reshape.95.a0_ref), channel_id=1, source_target_pairs={{0,128},{64,192},{128,0},{192,64},{1,129},{65,193},{129,1},{193,65... | collective-permute-start | bytes 1376264 | tf_op jit(solution)/shard_map/ppermute | solution.py:32
  42.1 12.8 %all-to-all-done.b_ref = bf16[8,4,8,1024]{3,2,1,0:T(8,128)(2,1)S(1)} async-done(((bf16[8,4,8,1024]{3,2,1,0:T(8,128)(2,1)}), bf16[8,4,8,1024]{3,2,1,0:T(8,128)(2,1)S(1)}, u32[]{:S(2)}, u32[]{:S(2)}) %all-to-all-start) | async-done | bytes 524320 | tf_op jit(solution)/shard_map/all_to_all | solution.py:28
  54.9 6.9 %collective-permute-done.5.a2_ref = bf16[64,3584]{1,0:T(8,128)(2,1)} collective-permute-done((bf16[64,3584]{1,0:T(8,128)(2,1)S(1)}, bf16[64,3584]{1,0:T(8,128)(2,1)}, u32[]{:S(2)}, u32[]{:S(2)}) %collective-permute-start.5) | collective-permute-done | bytes 458784 | tf_op jit(solution)/shard_map/ppermute | solution.py:32
  63.2 8.1 %score.1 = (bf16[256,4096]{1,0:T(8,128)(2,1)}, f32[256,256]{1,0:T(8,128)}, f32[256,256]{1,0:T(8,128)}) custom-call(bf16[64,3584]{1,0:T(8,128)(2,1)} %copy-done.5, bf16[64,3584]{1,0:T(8,128)(2,1)} %copy-done.9, bf16[64,3584]{1,0:T(8,128)(2,1)} %collective-permute-done.5.a2_ref, bf16[64,3584]{1,0:T(8,128)(2,1)} %collective-permute-done.6.a3_ref, ...), custom_call_target="tpu_custom_call" | custom-call | tf_op jit(solution)/shard_map/score/pallas_call | solution.py:239
  75.0 2.0 %front.1 = (f32[256,256]{1,0:T(8,128)}, f32[8,256]{1,0:T(8,128)}, f32[8,256]{1,0:T(8,128)}) custom-call(s32[128]{0:T(128)} %span_ref.1, s32[8]{0:T(128)} %compare_select_fusion.6.place_ref, bf16[8,4,8,1024]{3,2,1,0:T(8,128)(2,1)} %copy-done.2, f32[256,256]{1,0:T(8,128)} %get-tuple-element.19.own_ref, f32[256,256]{1,0:T(8,128)} %copy-done.10), custom_call_target="tpu_custom_call" | custom-call | tf_op jit(solution)/shard_map/front/pallas_call | solution.py:254
  77.0 2.5 %collective-permute-start.9 = (f32[8,256]{1,0:T(8,128)}, f32[8,256]{1,0:T(8,128)S(1)}, u32[]{:S(2)}, u32[]{:S(2)}) collective-permute-start(f32[8,256]{1,0:T(8,128)} %get-tuple-element.23), channel_id=1, source_target_pairs={{0,3},{1,0},{2,1},{3,2},{4,7},{5,4},{6,5},{7,6},{8,11},{9,8},{10,9... | collective-permute-start | bytes 24584 | tf_op jit(solution)/shard_map/ppermute | solution.py:32
  81.3 2.4 %collective-permute-done.10 = f32[8,256]{1,0:T(8,128)S(1)} collective-permute-done((f32[8,256]{1,0:T(8,128)}, f32[8,256]{1,0:T(8,128)S(1)}, u32[]{:S(2)}, u32[]{:S(2)}) %collective-permute-start.10) | collective-permute-done | bytes 8224 | tf_op jit(solution)/shard_map/ppermute | solution.py:32
  90.2 2.8 %convolution_convert_fusion = bf16[256,4096]{1,0:T(8,128)(2,1)S(1)} fusion(bf16[256,4096]{1,0:T(8,128)(2,1)} %copy-done.3, bf16[256,4096]{1,0:T(8,128)(2,1)S(1)} %copy-done, bf16[256,256]{1,0:T(8,128)(2,1)S(1)} %collective-permute-done.12, bf16[256,256]{1,0:T(8,128)(2,1)S(1)} %multiply_convert_fusion), kind=kOutput, calls=%fused_computation | convolution fusion | flops 1083703296 | bytes 6553600 | tf_op jit(solution)/shard_map/dot_general | solution.py:293
  96.4 2.2 %collective-permute-start.14 = (bf16[64,3328]{1,0:T(8,128)(2,1)S(1)}, bf16[64,3328]{1,0:T(8,128)(2,1)}, u32[]{:S(2)}, u32[]{:S(2)}) collective-permute-start(bf16[64,3328]{1,0:T(8,128)(2,1)S(1)} %get-tuple-element.40), channel_id=1, source_target_pairs={{0,128},{64,192},{128,0},{192,64},{1,129},{65,193},{129,1},{193,65... | collective-permute-start | bytes 1277960 | tf_op jit(solution)/shard_map/ppermute | solution.py:32
  102.4 6.7 %all-to-all-start.3 = ((bf16[8,4,8,768]{3,2,1,0:T(8,128)(2,1)}), bf16[8,4,8,768]{3,2,1,0:T(8,128)(2,1)S(1)}, u32[]{:S(2)}, u32[]{:S(2)}) async-start(bf16[8,4,8,768]{3,2,1,0:T(8,128)(2,1)} %bitcast.65), calls=%async_computation.3 | async-start | bytes 786432 | tf_op jit(solution)/shard_map/all_to_all | solution.py:28
  109.1 8.5 %collective-permute-done.14 = bf16[64,3328]{1,0:T(8,128)(2,1)} collective-permute-done((bf16[64,3328]{1,0:T(8,128)(2,1)S(1)}, bf16[64,3328]{1,0:T(8,128)(2,1)}, u32[]{:S(2)}, u32[]{:S(2)}) %collective-permute-start.14) | collective-permute-done | bytes 426016 | tf_op jit(solution)/shard_map/ppermute | solution.py:32
  117.6 2.4 %fusion.15 = bf16[8,8,3328]{2,1,0:T(8,128)(2,1)} fusion(bf16[64,3328]{1,0:T(8,128)(2,1)} %collective-permute-done.15, bf16[64,3328]{1,0:T(8,128)(2,1)} %collective-permute-done.14, bf16[64,3328]{1,0:T(8,128)(2,1)} %collective-permute-done.13, bf16[256,4096]{1,0:T(8,128)(2,1)} %copy-done.4), kind=kLoop, calls=%fused_computation.23 | loop fusion | flops 1703936 | bytes 2129920 | tf_op jit(solution)/shard_map/reshape | solution.py:298
  120.0 2.2 %all-to-all-done.3 = bf16[8,4,8,768]{3,2,1,0:T(8,128)(2,1)S(1)} async-done(((bf16[8,4,8,768]{3,2,1,0:T(8,128)(2,1)}), bf16[8,4,8,768]{3,2,1,0:T(8,128)(2,1)S(1)}, u32[]{:S(2)}, u32[]{:S(2)}) %all-to-all-start.3) | async-done | bytes 393248 | tf_op jit(solution)/shard_map/all_to_all | solution.py:28
  122.2 4.3 %all-to-all-start.2 = ((bf16[8,8,3328]{2,1,0:T(8,128)(2,1)}), bf16[8,8,3328]{2,1,0:T(8,128)(2,1)S(1)}, u32[]{:S(2)}, u32[]{:S(2)}) async-start(bf16[8,8,3328]{2,1,0:T(8,128)(2,1)} %fusion.15), calls=%async_computation.2 | async-start | bytes 851968 | tf_op jit(solution)/shard_map/all_to_all | solution.py:28
  127.2 3.1 %collective-permute-start.16 = (bf16[8,768]{1,0:T(8,128)(2,1)S(1)}, bf16[8,768]{1,0:T(8,128)(2,1)S(1)}, u32[]{:S(2)}, u32[]{:S(2)}) collective-permute-start(bf16[8,768]{1,0:T(8,128)(2,1)S(1)} %get-tuple-element.45), channel_id=1, source_target_pairs={{0,192},{64,0},{128,64},{192,128},{1,193},{65,1},{129,65},{193,129... | collective-permute-start | bytes 36872 | tf_op jit(solution)/shard_map/ppermute | solution.py:32
  130.3 2.7 %convolution_convert_fusion.2 = bf16[256,2048]{1,0:T(8,128)(2,1)} fusion(bf16[256,256]{1,0:T(8,128)(2,1)S(1)} %multiply_convert_fusion, bf16[256,4096]{1,0:T(8,128)(2,1)} %collective-permute-done.20, s32[]{:T(128)S(6)} %mul.76, bf16[256,4096]{1,0:T(8,128)(2,1)S(1)} %copy-done.1, pred[]{:T(512)S(6)} %eq.129), kind=kOutput, calls=%fused_computation.5 | convolution fusion | flops 269484032 | bytes 3276805 | tf_op jit(solution)/shard_map/dot_general | solution.py:336
  137.3 2.7 %convolution_convert_fusion.4 = bf16[256,2048]{1,0:T(8,128)(2,1)} fusion(bf16[256,256]{1,0:T(8,128)(2,1)S(1)} %multiply_convert_fusion, bf16[256,4096]{1,0:T(8,128)(2,1)} %collective-permute-done.20, s32[]{:T(128)S(6)} %mul.74, bf16[256,4096]{1,0:T(8,128)(2,1)S(1)} %copy-done.1, pred[]{:T(512)S(6)} %eq.127), kind=kOutput, calls=%fused_computation.7 | convolution fusion | flops 269484032 | bytes 3276805 | tf_op jit(solution)/shard_map/dot_general | solution.py:336
  139.9 2.1 %collective-permute-start.21 = (bf16[256,2048]{1,0:T(8,128)(2,1)}, bf16[256,2048]{1,0:T(8,128)(2,1)}, u32[]{:S(2)}, u32[]{:S(2)}) collective-permute-start(bf16[256,2048]{1,0:T(8,128)(2,1)} %convolution_convert_fusion.4), channel_id=1, source_target_pairs={{0,3},{1,0},{2,1},{3,2},{4,7},{5,4},{6,5},{7,6},{8,11},{9,8},{10,9... | collective-permute-start | bytes 3145736 | tf_op jit(solution)/shard_map/ppermute | solution.py:32
  143.3 2.8 %collective-permute-done.17.b2_ref = bf16[8,768]{1,0:T(8,128)(2,1)S(1)} collective-permute-done((bf16[8,768]{1,0:T(8,128)(2,1)S(1)}, bf16[8,768]{1,0:T(8,128)(2,1)S(1)}, u32[]{:S(2)}, u32[]{:S(2)}) %collective-permute-start.17) | collective-permute-done | bytes 12320 | tf_op jit(solution)/shard_map/ppermute | solution.py:32
  147.7 1.9 square.1
  149.6 13.0 %all-to-all-start.4 = ((f32[256,1,128]{2,1,0:T(1,128)}), f32[256,1,128]{2,1,0:T(1,128)S(1)}, u32[]{:S(2)}, u32[]{:S(2)}) async-start(f32[256,1,128]{2,1,0:T(1,128)} %get-tuple-element.24), calls=%async_computation.4 | async-start | bytes 262144 | tf_op jit(solution)/shard_map/all_to_all | solution.py:28
  164.3 2.1 %collective-permute-start.19 = (f32[4,4096]{1,0:T(4,128)S(1)}, f32[4,4096]{1,0:T(4,128)S(1)}, u32[]{:S(2)}, u32[]{:S(2)}) collective-permute-start(f32[4,4096]{1,0:T(4,128)S(1)} %get-tuple-element.41), channel_id=1, source_target_pairs={{0,4},{4,0},{1,5},{5,1},{2,6},{6,2},{3,7},{7,3},{8,12},{12,8},{9,1... | collective-permute-start | bytes 196616 | tf_op jit(solution)/shard_map/ppermute | solution.py:319
  167.4 19.8 %all-to-all-done.4.report_ref = f32[256,1,128]{2,1,0:T(1,128)S(1)} async-done(((f32[256,1,128]{2,1,0:T(1,128)}), f32[256,1,128]{2,1,0:T(1,128)S(1)}, u32[]{:S(2)}, u32[]{:S(2)}) %all-to-all-start.4) | async-done | bytes 131104 | tf_op jit(solution)/shard_map/all_to_all | solution.py:28
  187.8 2.3 %final.1 = (f32[2,128]{1,0:T(2,128)}, f32[1,1]{1,0:T(1,128)}, f32[4,8192]{1,0:T(4,128)}, f32[4,8192]{1,0:T(4,128)}, f32[4,8192]{1,0:T(4,128)}) custom-call(s32[8]{0:T(128)} %compare_select_fusion.6.place_ref, f32[256,1,128]{2,1,0:T(1,128)} %copy-done.8, f32[8,256]{1,0:T(8,128)} %get-tuple-element.21.row_ref, f32[4,4096]{1,0:T(4,128)} %get-tuple-element.42.near_ref, ...), custom_call_target="tpu_custom_call" | custom-call | tf_op jit(solution)/shard_map/final/pallas_call | solution.py:347
  191.9 3.5 %add_convert_fusion = bf16[256,2048]{1,0:T(8,128)(2,1)} fusion(bf16[256,2048]{1,0:T(8,128)(2,1)S(1)} %convolution_convert_fusion.1, bf16[256,2048]{1,0:T(8,128)(2,1)} %collective-permute-done.23, bf16[256,2048]{1,0:T(8,128)(2,1)} %collective-permute-done.22, bf16[256,2048]{1,0:T(8,128)(2,1)} %collective-permute-done.21), kind=kLoop, calls=%fused_computation.8 | loop fusion | flops 4194304 | bytes 5242880 | tf_op jit(solution)/shard_map/convert_element_type | solution.py:344
  (123 shorter events, 40.5 us)
Async XLA Ops:
  5.5 56.3 %collective-permute-start.7 = (bf16[256,4096]{1,0:T(8,128)(2,1)}, bf16[256,4096]{1,0:T(8,128)(2,1)S(1)}, u32[]{:S(2)}, u32[]{:S(2)}) collective-permute-start(bf16[256,4096]{1,0:T(8,128)(2,1)} %get-tuple-element.37), channel_id=1, source_target_pairs={{0,4},{4,0},{1,5},{5,1},{2,6},{6,2},{3,7},{7,3},{8,12},{12,8},{9,1... | collective-permute-start | bytes 6291464 | tf_op jit(solution)/shard_map/ppermute | solution.py:232
  9.8 22.7 %all-to-all-start.1 = ((bf16[16,4,3584]{2,1,0:T(4,128)(2,1)}), bf16[16,4,3584]{2,1,0:T(4,128)(2,1)S(1)}, u32[]{:S(2)}, u32[]{:S(2)}) async-start(bf16[16,4,3584]{2,1,0:T(4,128)(2,1)} %bitcast.9), calls=%async_computation.1 | async-start | bytes 917504 | tf_op jit(solution)/shard_map/all_to_all | solution.py:28
  16.9 1.3 collective-permute-start
  18.2 3.9 %collective-permute-start.3 = (bf16[8,1024]{1,0:T(8,128)(2,1)S(1)}, bf16[8,1024]{1,0:T(8,128)(2,1)S(1)}, u32[]{:S(2)}, u32[]{:S(2)}) collective-permute-start(bf16[8,1024]{1,0:T(8,128)(2,1)S(1)} %maximum_select_fusion.1), channel_id=1, source_target_pairs={{0,192},{64,0},{128,64},{192,128},{1,193},{65,1},{129,65},{193,129... | collective-permute-start | bytes 49160 | tf_op jit(solution)/shard_map/ppermute | solution.py:32
  21.0 4.4 %collective-permute-start.2 = (bf16[8,1024]{1,0:T(8,128)(2,1)S(1)}, bf16[8,1024]{1,0:T(8,128)(2,1)S(1)}, u32[]{:S(2)}, u32[]{:S(2)}) collective-permute-start(bf16[8,1024]{1,0:T(8,128)(2,1)S(1)} %maximum_select_fusion.1), channel_id=1, source_target_pairs={{0,128},{64,192},{128,0},{192,64},{1,129},{65,193},{129,1},{193,65... | collective-permute-start | bytes 49160 | tf_op jit(solution)/shard_map/ppermute | solution.py:32
  21.4 4.2 %collective-permute-start.1 = (bf16[8,1024]{1,0:T(8,128)(2,1)S(1)}, bf16[8,1024]{1,0:T(8,128)(2,1)S(1)}, u32[]{:S(2)}, u32[]{:S(2)}) collective-permute-start(bf16[8,1024]{1,0:T(8,128)(2,1)S(1)} %maximum_select_fusion.1), channel_id=1, source_target_pairs={{0,64},{64,128},{128,192},{192,0},{1,65},{65,129},{129,193},{193,1... | collective-permute-start | bytes 49160 | tf_op jit(solution)/shard_map/ppermute | solution.py:32
  33.4 21.5 %all-to-all-start = ((bf16[8,4,8,1024]{3,2,1,0:T(8,128)(2,1)}), bf16[8,4,8,1024]{3,2,1,0:T(8,128)(2,1)S(1)}, u32[]{:S(2)}, u32[]{:S(2)}) async-start(bf16[8,4,8,1024]{3,2,1,0:T(8,128)(2,1)} %broadcast_in_dim.51), calls=%async_computation | async-start | bytes 1048576 | tf_op jit(solution)/shard_map/all_to_all | solution.py:28
  37.0 26.2 %copy-start.5 = (bf16[64,3584]{1,0:T(8,128)(2,1)}, bf16[64,3584]{1,0:T(8,128)(2,1)S(1)}, u32[]{:S(2)}) copy-start(bf16[64,3584]{1,0:T(8,128)(2,1)S(1)} %reshape.95.a0_ref) | copy-start | bytes 1376260
  37.0 17.9 %collective-permute-start.4 = (bf16[64,3584]{1,0:T(8,128)(2,1)S(1)}, bf16[64,3584]{1,0:T(8,128)(2,1)S(1)}, u32[]{:S(2)}, u32[]{:S(2)}) collective-permute-start(bf16[64,3584]{1,0:T(8,128)(2,1)S(1)} %reshape.95.a0_ref), channel_id=1, source_target_pairs={{0,64},{64,128},{128,192},{192,0},{1,65},{65,129},{129,193},{193,1... | collective-permute-start | bytes 1376264 | tf_op jit(solution)/shard_map/ppermute | solution.py:32
  38.4 23.4 %collective-permute-start.5 = (bf16[64,3584]{1,0:T(8,128)(2,1)S(1)}, bf16[64,3584]{1,0:T(8,128)(2,1)}, u32[]{:S(2)}, u32[]{:S(2)}) collective-permute-start(bf16[64,3584]{1,0:T(8,128)(2,1)S(1)} %reshape.95.a0_ref), channel_id=1, source_target_pairs={{0,128},{64,192},{128,0},{192,64},{1,129},{65,193},{129,1},{193,65... | collective-permute-start | bytes 1376264 | tf_op jit(solution)/shard_map/ppermute | solution.py:32
  41.0 20.8 %collective-permute-start.6 = (bf16[64,3584]{1,0:T(8,128)(2,1)S(1)}, bf16[64,3584]{1,0:T(8,128)(2,1)}, u32[]{:S(2)}, u32[]{:S(2)}) collective-permute-start(bf16[64,3584]{1,0:T(8,128)(2,1)S(1)} %reshape.95.a0_ref), channel_id=1, source_target_pairs={{0,192},{64,0},{128,64},{192,128},{1,193},{65,1},{129,65},{193,129... | collective-permute-start | bytes 1376264 | tf_op jit(solution)/shard_map/ppermute | solution.py:32
  63.2 27.0 %copy-start = (bf16[256,4096]{1,0:T(8,128)(2,1)S(1)}, bf16[256,4096]{1,0:T(8,128)(2,1)}, u32[]{:S(2)}) copy-start(bf16[256,4096]{1,0:T(8,128)(2,1)} %get-tuple-element.36.own_ref) | copy-start | bytes 6291460
  71.3 3.0 %collective-permute-start.8 = (f32[256,256]{1,0:T(8,128)}, f32[256,256]{1,0:T(8,128)S(1)}, u32[]{:S(2)}, u32[]{:S(2)}) collective-permute-start(f32[256,256]{1,0:T(8,128)} %get-tuple-element.20), channel_id=1, source_target_pairs={{0,4},{4,0},{1,5},{5,1},{2,6},{6,2},{3,7},{7,3},{8,12},{12,8},{9,1... | collective-permute-start | bytes 786440 | tf_op jit(solution)/shard_map/ppermute | solution.py:252
  77.0 4.3 %collective-permute-start.9 = (f32[8,256]{1,0:T(8,128)}, f32[8,256]{1,0:T(8,128)S(1)}, u32[]{:S(2)}, u32[]{:S(2)}) collective-permute-start(f32[8,256]{1,0:T(8,128)} %get-tuple-element.23), channel_id=1, source_target_pairs={{0,3},{1,0},{2,1},{3,2},{4,7},{5,4},{6,5},{7,6},{8,11},{9,8},{10,9... | collective-permute-start | bytes 24584 | tf_op jit(solution)/shard_map/ppermute | solution.py:32
  79.5 4.2 %collective-permute-start.10 = (f32[8,256]{1,0:T(8,128)}, f32[8,256]{1,0:T(8,128)S(1)}, u32[]{:S(2)}, u32[]{:S(2)}) collective-permute-start(f32[8,256]{1,0:T(8,128)} %get-tuple-element.23), channel_id=1, source_target_pairs={{0,2},{1,3},{2,0},{3,1},{4,6},{5,7},{6,4},{7,5},{8,10},{9,11},{10,... | collective-permute-start | bytes 24584 | tf_op jit(solution)/shard_map/ppermute | solution.py:32
  80.0 3.9 %collective-permute-start.11 = (f32[8,256]{1,0:T(8,128)}, f32[8,256]{1,0:T(8,128)S(1)}, u32[]{:S(2)}, u32[]{:S(2)}) collective-permute-start(f32[8,256]{1,0:T(8,128)} %get-tuple-element.23), channel_id=1, source_target_pairs={{0,1},{1,2},{2,3},{3,0},{4,5},{5,6},{6,7},{7,4},{8,9},{9,10},{10,1... | collective-permute-start | bytes 24584 | tf_op jit(solution)/shard_map/ppermute | solution.py:32
  87.3 2.9 %collective-permute-start.12 = (bf16[256,256]{1,0:T(8,128)(2,1)S(1)}, bf16[256,256]{1,0:T(8,128)(2,1)S(1)}, u32[]{:S(2)}, u32[]{:S(2)}) collective-permute-start(bf16[256,256]{1,0:T(8,128)(2,1)S(1)} %multiply_convert_fusion), channel_id=1, source_target_pairs={{0,4},{4,0},{1,5},{5,1},{2,6},{6,2},{3,7},{7,3},{8,12},{12,8},{9,1... | collective-permute-start | bytes 393224 | tf_op jit(solution)/shard_map/ppermute | solution.py:290
  89.3 41.0 %collective-permute-start.20 = (bf16[256,4096]{1,0:T(8,128)(2,1)}, bf16[256,4096]{1,0:T(8,128)(2,1)}, u32[]{:S(2)}, u32[]{:S(2)}) collective-permute-start(bf16[256,4096]{1,0:T(8,128)(2,1)} %get-tuple-element.28), channel_id=1, source_target_pairs={{0,4},{4,0},{1,5},{5,1},{2,6},{6,2},{3,7},{7,3},{8,12},{12,8},{9,1... | collective-permute-start | bytes 6291464 | tf_op jit(solution)/shard_map/ppermute | solution.py:253
  95.3 13.8 %collective-permute-start.15 = (bf16[64,3328]{1,0:T(8,128)(2,1)}, bf16[64,3328]{1,0:T(8,128)(2,1)}, u32[]{:S(2)}, u32[]{:S(2)}) collective-permute-start(bf16[64,3328]{1,0:T(8,128)(2,1)} %get-tuple-element.39), channel_id=1, source_target_pairs={{0,64},{64,128},{128,192},{192,0},{1,65},{65,129},{129,193},{193,1... | collective-permute-start | bytes 1277960 | tf_op jit(solution)/shard_map/ppermute | solution.py:32
  96.4 21.2 %collective-permute-start.14 = (bf16[64,3328]{1,0:T(8,128)(2,1)S(1)}, bf16[64,3328]{1,0:T(8,128)(2,1)}, u32[]{:S(2)}, u32[]{:S(2)}) collective-permute-start(bf16[64,3328]{1,0:T(8,128)(2,1)S(1)} %get-tuple-element.40), channel_id=1, source_target_pairs={{0,128},{64,192},{128,0},{192,64},{1,129},{65,193},{129,1},{193,65... | collective-permute-start | bytes 1277960 | tf_op jit(solution)/shard_map/ppermute | solution.py:32
  98.6 19.0 %collective-permute-start.13 = (bf16[64,3328]{1,0:T(8,128)(2,1)S(1)}, bf16[64,3328]{1,0:T(8,128)(2,1)}, u32[]{:S(2)}, u32[]{:S(2)}) collective-permute-start(bf16[64,3328]{1,0:T(8,128)(2,1)S(1)} %get-tuple-element.38), channel_id=1, source_target_pairs={{0,192},{64,0},{128,64},{192,128},{1,193},{65,1},{129,65},{193,129... | collective-permute-start | bytes 1277960 | tf_op jit(solution)/shard_map/ppermute | solution.py:32
  102.4 27.9 %copy-start.1 = (bf16[256,4096]{1,0:T(8,128)(2,1)S(1)}, bf16[256,4096]{1,0:T(8,128)(2,1)}, u32[]{:S(2)}) copy-start(bf16[256,4096]{1,0:T(8,128)(2,1)} %get-tuple-element.28) | copy-start | bytes 6291460
  102.4 19.8 %all-to-all-start.3 = ((bf16[8,4,8,768]{3,2,1,0:T(8,128)(2,1)}), bf16[8,4,8,768]{3,2,1,0:T(8,128)(2,1)S(1)}, u32[]{:S(2)}, u32[]{:S(2)}) async-start(bf16[8,4,8,768]{3,2,1,0:T(8,128)(2,1)} %bitcast.65), calls=%async_computation.3 | async-start | bytes 786432 | tf_op jit(solution)/shard_map/all_to_all | solution.py:28
  122.2 24.7 %all-to-all-start.2 = ((bf16[8,8,3328]{2,1,0:T(8,128)(2,1)}), bf16[8,8,3328]{2,1,0:T(8,128)(2,1)S(1)}, u32[]{:S(2)}, u32[]{:S(2)}) async-start(bf16[8,8,3328]{2,1,0:T(8,128)(2,1)} %fusion.15), calls=%async_computation.2 | async-start | bytes 851968 | tf_op jit(solution)/shard_map/all_to_all | solution.py:28
  127.2 15.5 %collective-permute-start.16 = (bf16[8,768]{1,0:T(8,128)(2,1)S(1)}, bf16[8,768]{1,0:T(8,128)(2,1)S(1)}, u32[]{:S(2)}, u32[]{:S(2)}) collective-permute-start(bf16[8,768]{1,0:T(8,128)(2,1)S(1)} %get-tuple-element.45), channel_id=1, source_target_pairs={{0,192},{64,0},{128,64},{192,128},{1,193},{65,1},{129,65},{193,129... | collective-permute-start | bytes 36872 | tf_op jit(solution)/shard_map/ppermute | solution.py:32
  132.9 58.9 %collective-permute-start.23 = (bf16[256,2048]{1,0:T(8,128)(2,1)}, bf16[256,2048]{1,0:T(8,128)(2,1)}, u32[]{:S(2)}, u32[]{:S(2)}) collective-permute-start(bf16[256,2048]{1,0:T(8,128)(2,1)} %convolution_convert_fusion.2), channel_id=1, source_target_pairs={{0,1},{1,2},{2,3},{3,0},{4,5},{5,6},{6,7},{7,4},{8,9},{9,10},{10,1... | collective-permute-start | bytes 3145736 | tf_op jit(solution)/shard_map/ppermute | solution.py:32
  136.0 55.8 %collective-permute-start.22 = (bf16[256,2048]{1,0:T(8,128)(2,1)}, bf16[256,2048]{1,0:T(8,128)(2,1)}, u32[]{:S(2)}, u32[]{:S(2)}) collective-permute-start(bf16[256,2048]{1,0:T(8,128)(2,1)} %convolution_convert_fusion.3), channel_id=1, source_target_pairs={{0,2},{1,3},{2,0},{3,1},{4,6},{5,7},{6,4},{7,5},{8,10},{9,11},{10,... | collective-permute-start | bytes 3145736 | tf_op jit(solution)/shard_map/ppermute | solution.py:32
  139.9 51.9 %collective-permute-start.21 = (bf16[256,2048]{1,0:T(8,128)(2,1)}, bf16[256,2048]{1,0:T(8,128)(2,1)}, u32[]{:S(2)}, u32[]{:S(2)}) collective-permute-start(bf16[256,2048]{1,0:T(8,128)(2,1)} %convolution_convert_fusion.4), channel_id=1, source_target_pairs={{0,3},{1,0},{2,1},{3,2},{4,7},{5,4},{6,5},{7,6},{8,11},{9,8},{10,9... | collective-permute-start | bytes 3145736 | tf_op jit(solution)/shard_map/ppermute | solution.py:32
  142.0 4.1 %collective-permute-start.17 = (bf16[8,768]{1,0:T(8,128)(2,1)S(1)}, bf16[8,768]{1,0:T(8,128)(2,1)S(1)}, u32[]{:S(2)}, u32[]{:S(2)}) collective-permute-start(bf16[8,768]{1,0:T(8,128)(2,1)S(1)} %get-tuple-element.44), channel_id=1, source_target_pairs={{0,128},{64,192},{128,0},{192,64},{1,129},{65,193},{129,1},{193,65... | collective-permute-start | bytes 36872 | tf_op jit(solution)/shard_map/ppermute | solution.py:32
  142.7 4.2 %collective-permute-start.18 = (bf16[8,768]{1,0:T(8,128)(2,1)S(1)}, bf16[8,768]{1,0:T(8,128)(2,1)S(1)}, u32[]{:S(2)}, u32[]{:S(2)}) collective-permute-start(bf16[8,768]{1,0:T(8,128)(2,1)S(1)} %get-tuple-element.43), channel_id=1, source_target_pairs={{0,64},{64,128},{128,192},{192,0},{1,65},{65,129},{129,193},{193,1... | collective-permute-start | bytes 36872 | tf_op jit(solution)/shard_map/ppermute | solution.py:32
  149.6 37.5 %all-to-all-start.4 = ((f32[256,1,128]{2,1,0:T(1,128)}), f32[256,1,128]{2,1,0:T(1,128)S(1)}, u32[]{:S(2)}, u32[]{:S(2)}) async-start(f32[256,1,128]{2,1,0:T(1,128)} %get-tuple-element.24), calls=%async_computation.4 | async-start | bytes 262144 | tf_op jit(solution)/shard_map/all_to_all | solution.py:28
  164.3 3.0 %collective-permute-start.19 = (f32[4,4096]{1,0:T(4,128)S(1)}, f32[4,4096]{1,0:T(4,128)S(1)}, u32[]{:S(2)}, u32[]{:S(2)}) collective-permute-start(f32[4,4096]{1,0:T(4,128)S(1)} %get-tuple-element.41), channel_id=1, source_target_pairs={{0,4},{4,0},{1,5},{5,1},{2,6},{6,2},{3,7},{7,3},{8,12},{12,8},{9,1... | collective-permute-start | bytes 196616 | tf_op jit(solution)/shard_map/ppermute | solution.py:319
  (17 other events, 127.8 us)

commit v10 on v7

--- a/solution.py
+++ b/solution.py
@@ -48,7 +48,9 @@
     return exchange(jnp.broadcast_to(x[None], (count,) + x.shape), axes)
 
 
-def score_kernel(thin, a0_ref, a1_ref, a2_ref, a3_ref, b_ref, tok_ref, head_ref, part_ref):
+def score_kernel(
+    thin, a0_ref, a1_ref, a2_ref, a3_ref, b_ref, own_ref, mate_ref, head_ref, own_part_ref, mate_part_ref
+):
     wide = a0_ref.shape[1]
     y_rows = a0_ref.shape[0]
     for s, a_ref in enumerate((a0_ref, a1_ref, a2_ref, a3_ref)):
@@ -56,9 +58,10 @@
         for z in range(NZ):
             at = s * y_rows + z * (y_rows // NZ)
             head_ref[at : at + y_rows // NZ, wide:] = b_ref[z, s, :, :thin]
-    part_ref[...] = lax.dot_general(
-        head_ref[...], tok_ref[...], (((1,), (1,)), ((), ())), preferred_element_type=f32
-    )
+    for tok_ref, part_ref in ((mate_ref, mate_part_ref), (own_ref, own_part_ref)):
+        part_ref[...] = lax.dot_general(
+            head_ref[...], tok_ref[...], (((1,), (1,)), ((), ())), preferred_element_type=f32
+        )
 
 
 def final_kernel(
@@ -215,22 +218,19 @@
     mate_half = lax.ppermute(far_half, "core", SWAP)
     tokens = jnp.concatenate([own_half, mate_half], 0)
 
-    def score(tok):
-        return lax.dot_general(head, tok, (((1,), (1,)), ((), ())), preferred_element_type=f32)
-
-    head, mate_part = pl.pallas_call(
+    head, own_part, mate_part = pl.pallas_call(
         functools.partial(score_kernel, thin),
         out_shape=(
             jax.ShapeDtypeStruct((group_rows, half), bf16),
             jax.ShapeDtypeStruct((group_rows, tok_rows), f32),
+            jax.ShapeDtypeStruct((group_rows, tok_rows), f32),
         ),
-        in_specs=[VMEM] * (NY + 2),
-        out_specs=(VMEM, VMEM),
+        in_specs=[VMEM] * (NY + 3),
+        out_specs=(VMEM, VMEM, VMEM),
         name="score",
-    )(*parts_a, part_b, mate_half)
+    )(*parts_a, part_b, own_half, mate_half)
+    mate_part = lax.ppermute(mate_part, "core", SWAP)
     mate_head = lax.ppermute(head, "core", SWAP)
-    mate_part = lax.ppermute(mate_part, "core", SWAP)
-    own_part = score(own_half)
     logits, stats, rows = pl.pallas_call(
         functools.partial(front_kernel, group_rows, y_rows),
         out_shape=(

time: 194 us -> 196 us (1.010)
  matrix products: 15.8 us -> 11.3 us
  waiting for transfers between devices: 69.2 us -> 71.7 us
  local copies, waits for them, and re-layouts: 15.1 us -> 17.2 us
    dot_general x1 -> x0, matrix products: 3.82 us -> none  [score(): lax.dot_general(head, tok, (((1,), (1,)), ((), ())), preferred_element_ty...]
    all_to_all x5, waiting for transfers between devices: 37.1 us -> 39.8 us  [exchange(): return lax.all_to_all(x, axes, 0, 0, tiled=True)]
    unnamed x36 -> x40, local copies, waits for them, and re-layouts: 3.55 us -> 4.95 us
  transfers between devices with their start and end apart: 29 -> 29, of which waited for: 15 -> 15; matrix products, arithmetic and copies ran while one was open for 16% -> 14% of each run, Pallas kernels for 2% -> 2%
where the time goes in v10:
time: 196 us; the launch traced here: 195 us
  waiting for transfers between devices  71.7 us (37%)
  starting transfers between devices  66.5 us (34%)
  local copies, waits for them, and re-layouts  17.2 us (9%)
  other arithmetic  15.1 us (8%)
  Pallas kernels  11.9 us (6%)
  matrix products  11.3 us (6%)
    all_to_all x5, waiting for transfers between devices, exchange(): return lax.all_to_all(x, axes, 0, 0, tiled=True)  39.8 us
    all_to_all x5, starting transfers between devices, exchange(): return lax.all_to_all(x, axes, 0, 0, tiled=True)  34.3 us
    ppermute x18, waiting for transfers between devices, shift(): lax.ppermute(x, axis, [(i, (i + step) % count) for i in range(count)])  29.3 us
    ppermute x18, starting transfers between devices, shift(): lax.ppermute(x, axis, [(i, (i + step) % count) for i in range(count)])  24 us
    dot_general x4, matrix products, step(): lax.dot_general(dlogits, side, (((0,), (0,)), ((), ())), preferred_elemen...  8.49 us
    pallas_call x1, Pallas kernels, step(): pl.pallas_call(functools.partial(score_kernel, thin), out_shape=(jax.Shap...  5.67 us
    unnamed x40, local copies, waits for them, and re-layouts  4.95 us
    dynamic_slice x1, local copies, waits for them, and re-layouts, step(): lax.dynamic_slice(hidden_states, (0, core * half), (tok_rows, half), allo...  4.71 us
  transfers between devices with their start and end apart: 29, of which 15 were waited for; matrix products, arithmetic and copies ran while one was open for 14% of the time, Pallas kernels for 2%

profile of v10, /device:TPU:1, one launch (start us, length us, event | category | flops | bytes accessed | tf_op | source)
XLA Modules:
  0.0 194.8 jit_solution(15657718131344866672)
XLA Ops:
  0.7 4.7 %constant_dynamic-slice_fusion.3 = (bf16[256,4096]{1,0:T(8,128)(2,1)}, bf16[256,4096]{1,0:T(8,128)(2,1)}) fusion(bf16[256,8192]{1,0:T(8,128)(2,1)} %param.9, s32[]{:T(128)S(6)} %mul.62, s32[]{:T(128)S(6)} %mul.63), kind=kLoop, calls=%fused_computation.63 | loop fusion | bytes 8388616 | tf_op jit(solution)/shard_map/dynamic_slice | solution.py:212
  5.4 3.3 %collective-permute-start.7 = (bf16[256,4096]{1,0:T(8,128)(2,1)}, bf16[256,4096]{1,0:T(8,128)(2,1)S(1)}, u32[]{:S(2)}, u32[]{:S(2)}) collective-permute-start(bf16[256,4096]{1,0:T(8,128)(2,1)} %get-tuple-element.37), channel_id=1, source_target_pairs={{0,4},{4,0},{1,5},{5,1},{2,6},{6,2},{3,7},{7,3},{8,12},{12,8},{9,1... | collective-permute-start | bytes 6291464 | tf_op jit(solution)/shard_map/ppermute | solution.py:218
  9.8 6.9 %all-to-all-start.1 = ((bf16[16,4,3840]{2,1,0:T(4,128)(2,1)}), bf16[16,4,3840]{2,1,0:T(4,128)(2,1)S(1)}, u32[]{:S(2)}, u32[]{:S(2)}) async-start(bf16[16,4,3840]{2,1,0:T(4,128)(2,1)} %bitcast.9), calls=%async_computation.1 | async-start | bytes 983040 | tf_op jit(solution)/shard_map/all_to_all | solution.py:28
  18.2 2.8 %collective-permute-start.3 = (bf16[8,768]{1,0:T(8,128)(2,1)S(1)}, bf16[8,768]{1,0:T(8,128)(2,1)S(1)}, u32[]{:S(2)}, u32[]{:S(2)}) collective-permute-start(bf16[8,768]{1,0:T(8,128)(2,1)S(1)} %maximum_select_fusion.1), channel_id=1, source_target_pairs={{0,192},{64,0},{128,64},{192,128},{1,193},{65,1},{129,65},{193,129... | collective-permute-start | bytes 36872 | tf_op jit(solution)/shard_map/ppermute | solution.py:32
  22.1 3.3 %collective-permute-done.2 = bf16[8,768]{1,0:T(8,128)(2,1)S(1)} collective-permute-done((bf16[8,768]{1,0:T(8,128)(2,1)S(1)}, bf16[8,768]{1,0:T(8,128)(2,1)S(1)}, u32[]{:S(2)}, u32[]{:S(2)}) %collective-permute-start.2) | collective-permute-done | bytes 12320 | tf_op jit(solution)/shard_map/ppermute | solution.py:32
  25.5 7.7 %all-to-all-done.1 = bf16[16,4,3840]{2,1,0:T(4,128)(2,1)S(1)} async-done(((bf16[16,4,3840]{2,1,0:T(4,128)(2,1)}), bf16[16,4,3840]{2,1,0:T(4,128)(2,1)S(1)}, u32[]{:S(2)}, u32[]{:S(2)}) %all-to-all-start.1) | async-done | bytes 491552 | tf_op jit(solution)/shard_map/all_to_all | solution.py:28
  34.0 3.5 %all-to-all-start = ((bf16[8,4,8,768]{3,2,1,0:T(8,128)(2,1)}), bf16[8,4,8,768]{3,2,1,0:T(8,128)(2,1)S(1)}, u32[]{:S(2)}, u32[]{:S(2)}) async-start(bf16[8,4,8,768]{3,2,1,0:T(8,128)(2,1)} %broadcast_in_dim.51), calls=%async_computation | async-start | bytes 786432 | tf_op jit(solution)/shard_map/all_to_all | solution.py:28
  38.9 2.6 %collective-permute-start.5 = (bf16[64,3840]{1,0:T(8,128)(2,1)S(1)}, bf16[64,3840]{1,0:T(8,128)(2,1)}, u32[]{:S(2)}, u32[]{:S(2)}) collective-permute-start(bf16[64,3840]{1,0:T(8,128)(2,1)S(1)} %reshape.95.a0_ref), channel_id=1, source_target_pairs={{0,128},{64,192},{128,0},{192,64},{1,129},{65,193},{129,1},{193,65... | collective-permute-start | bytes 1474568 | tf_op jit(solution)/shard_map/ppermute | solution.py:32
  42.6 10.0 %all-to-all-done.b_ref = bf16[8,4,8,768]{3,2,1,0:T(8,128)(2,1)S(1)} async-done(((bf16[8,4,8,768]{3,2,1,0:T(8,128)(2,1)}), bf16[8,4,8,768]{3,2,1,0:T(8,128)(2,1)S(1)}, u32[]{:S(2)}, u32[]{:S(2)}) %all-to-all-start) | async-done | bytes 393248 | tf_op jit(solution)/shard_map/all_to_all | solution.py:28
  52.6 11.2 %collective-permute-done.5.a2_ref = bf16[64,3840]{1,0:T(8,128)(2,1)} collective-permute-done((bf16[64,3840]{1,0:T(8,128)(2,1)S(1)}, bf16[64,3840]{1,0:T(8,128)(2,1)}, u32[]{:S(2)}, u32[]{:S(2)}) %collective-permute-start.5) | collective-permute-done | bytes 491552 | tf_op jit(solution)/shard_map/ppermute | solution.py:32
  65.3 5.7 %score.1 = (bf16[256,4096]{1,0:T(8,128)(2,1)}, f32[256,256]{1,0:T(8,128)}, f32[256,256]{1,0:T(8,128)}) custom-call(bf16[64,3840]{1,0:T(8,128)(2,1)} %copy-done.5, bf16[64,3840]{1,0:T(8,128)(2,1)} %copy-done.9, bf16[64,3840]{1,0:T(8,128)(2,1)} %collective-permute-done.5.a2_ref, bf16[64,3840]{1,0:T(8,128)(2,1)} %collective-permute-done.6.a3_ref, ...), custom_call_target="tpu_custom_call" | custom-call | tf_op jit(solution)/shard_map/score/pallas_call | solution.py:221
  74.6 2.0 %front.1 = (f32[256,256]{1,0:T(8,128)}, f32[8,256]{1,0:T(8,128)}, f32[8,256]{1,0:T(8,128)}) custom-call(s32[128]{0:T(128)} %span_ref.1, s32[8]{0:T(128)} %compare_select_fusion.6.place_ref, bf16[8,4,8,768]{3,2,1,0:T(8,128)(2,1)} %copy-done.2, f32[256,256]{1,0:T(8,128)} %get-tuple-element.19.own_ref, f32[256,256]{1,0:T(8,128)} %copy-done.10), custom_call_target="tpu_custom_call" | custom-call | tf_op jit(solution)/shard_map/front/pallas_call | solution.py:234
  76.5 2.5 %collective-permute-start.9 = (f32[8,256]{1,0:T(8,128)}, f32[8,256]{1,0:T(8,128)S(1)}, u32[]{:S(2)}, u32[]{:S(2)}) collective-permute-start(f32[8,256]{1,0:T(8,128)} %get-tuple-element.23), channel_id=1, source_target_pairs={{0,3},{1,0},{2,1},{3,2},{4,7},{5,4},{6,5},{7,6},{8,11},{9,8},{10,9... | collective-permute-start | bytes 24584 | tf_op jit(solution)/shard_map/ppermute | solution.py:32
  80.8 2.4 %collective-permute-done.10 = f32[8,256]{1,0:T(8,128)S(1)} collective-permute-done((f32[8,256]{1,0:T(8,128)}, f32[8,256]{1,0:T(8,128)S(1)}, u32[]{:S(2)}, u32[]{:S(2)}) %collective-permute-start.10) | collective-permute-done | bytes 8224 | tf_op jit(solution)/shard_map/ppermute | solution.py:32
  89.7 2.8 %convolution_convert_fusion = bf16[256,4096]{1,0:T(8,128)(2,1)S(1)} fusion(bf16[256,4096]{1,0:T(8,128)(2,1)} %copy-done.3, bf16[256,4096]{1,0:T(8,128)(2,1)S(1)} %copy-done, bf16[256,256]{1,0:T(8,128)(2,1)S(1)} %collective-permute-done.12, bf16[256,256]{1,0:T(8,128)(2,1)S(1)} %multiply_convert_fusion), kind=kOutput, calls=%fused_computation | convolution fusion | flops 1083703296 | bytes 6553600 | tf_op jit(solution)/shard_map/dot_general | solution.py:273
  95.8 2.2 %collective-permute-start.14 = (bf16[64,3328]{1,0:T(8,128)(2,1)S(1)}, bf16[64,3328]{1,0:T(8,128)(2,1)}, u32[]{:S(2)}, u32[]{:S(2)}) collective-permute-start(bf16[64,3328]{1,0:T(8,128)(2,1)S(1)} %get-tuple-element.40), channel_id=1, source_target_pairs={{0,128},{64,192},{128,0},{192,64},{1,129},{65,193},{129,1},{193,65... | collective-permute-start | bytes 1277960 | tf_op jit(solution)/shard_map/ppermute | solution.py:32
  101.8 6.7 %all-to-all-start.3 = ((bf16[8,4,8,768]{3,2,1,0:T(8,128)(2,1)}), bf16[8,4,8,768]{3,2,1,0:T(8,128)(2,1)S(1)}, u32[]{:S(2)}, u32[]{:S(2)}) async-start(bf16[8,4,8,768]{3,2,1,0:T(8,128)(2,1)} %bitcast.65), calls=%async_computation.3 | async-start | bytes 786432 | tf_op jit(solution)/shard_map/all_to_all | solution.py:28
  108.5 8.5 %collective-permute-done.14 = bf16[64,3328]{1,0:T(8,128)(2,1)} collective-permute-done((bf16[64,3328]{1,0:T(8,128)(2,1)S(1)}, bf16[64,3328]{1,0:T(8,128)(2,1)}, u32[]{:S(2)}, u32[]{:S(2)}) %collective-permute-start.14) | collective-permute-done | bytes 426016 | tf_op jit(solution)/shard_map/ppermute | solution.py:32
  117.0 2.4 %fusion.15 = bf16[8,8,3328]{2,1,0:T(8,128)(2,1)} fusion(bf16[64,3328]{1,0:T(8,128)(2,1)} %collective-permute-done.15, bf16[64,3328]{1,0:T(8,128)(2,1)} %collective-permute-done.14, bf16[64,3328]{1,0:T(8,128)(2,1)} %collective-permute-done.13, bf16[256,4096]{1,0:T(8,128)(2,1)} %copy-done.4), kind=kLoop, calls=%fused_computation.23 | loop fusion | flops 1703936 | bytes 2129920 | tf_op jit(solution)/shard_map/reshape | solution.py:278
  119.4 2.2 %all-to-all-done.3 = bf16[8,4,8,768]{3,2,1,0:T(8,128)(2,1)S(1)} async-done(((bf16[8,4,8,768]{3,2,1,0:T(8,128)(2,1)}), bf16[8,4,8,768]{3,2,1,0:T(8,128)(2,1)S(1)}, u32[]{:S(2)}, u32[]{:S(2)}) %all-to-all-start.3) | async-done | bytes 393248 | tf_op jit(solution)/shard_map/all_to_all | solution.py:28
  121.6 4.3 %all-to-all-start.2 = ((bf16[8,8,3328]{2,1,0:T(8,128)(2,1)}), bf16[8,8,3328]{2,1,0:T(8,128)(2,1)S(1)}, u32[]{:S(2)}, u32[]{:S(2)}) async-start(bf16[8,8,3328]{2,1,0:T(8,128)(2,1)} %fusion.15), calls=%async_computation.2 | async-start | bytes 851968 | tf_op jit(solution)/shard_map/all_to_all | solution.py:28
  126.6 3.1 %collective-permute-start.16 = (bf16[8,768]{1,0:T(8,128)(2,1)S(1)}, bf16[8,768]{1,0:T(8,128)(2,1)S(1)}, u32[]{:S(2)}, u32[]{:S(2)}) collective-permute-start(bf16[8,768]{1,0:T(8,128)(2,1)S(1)} %get-tuple-element.45), channel_id=1, source_target_pairs={{0,192},{64,0},{128,64},{192,128},{1,193},{65,1},{129,65},{193,129... | collective-permute-start | bytes 36872 | tf_op jit(solution)/shard_map/ppermute | solution.py:32
  129.6 2.7 %convolution_convert_fusion.2 = bf16[256,2048]{1,0:T(8,128)(2,1)} fusion(bf16[256,256]{1,0:T(8,128)(2,1)S(1)} %multiply_convert_fusion, bf16[256,4096]{1,0:T(8,128)(2,1)} %collective-permute-done.20, s32[]{:T(128)S(6)} %mul.76, bf16[256,4096]{1,0:T(8,128)(2,1)S(1)} %copy-done.1, pred[]{:T(512)S(6)} %eq.129), kind=kOutput, calls=%fused_computation.5 | convolution fusion | flops 269484032 | bytes 3276805 | tf_op jit(solution)/shard_map/dot_general | solution.py:316
  136.6 2.7 %convolution_convert_fusion.4 = bf16[256,2048]{1,0:T(8,128)(2,1)} fusion(bf16[256,256]{1,0:T(8,128)(2,1)S(1)} %multiply_convert_fusion, bf16[256,4096]{1,0:T(8,128)(2,1)} %collective-permute-done.20, s32[]{:T(128)S(6)} %mul.74, bf16[256,4096]{1,0:T(8,128)(2,1)S(1)} %copy-done.1, pred[]{:T(512)S(6)} %eq.127), kind=kOutput, calls=%fused_computation.7 | convolution fusion | flops 269484032 | bytes 3276805 | tf_op jit(solution)/shard_map/dot_general | solution.py:316
  139.3 2.1 %collective-permute-start.21 = (bf16[256,2048]{1,0:T(8,128)(2,1)}, bf16[256,2048]{1,0:T(8,128)(2,1)}, u32[]{:S(2)}, u32[]{:S(2)}) collective-permute-start(bf16[256,2048]{1,0:T(8,128)(2,1)} %convolution_convert_fusion.4), channel_id=1, source_target_pairs={{0,3},{1,0},{2,1},{3,2},{4,7},{5,4},{6,5},{7,6},{8,11},{9,8},{10,9... | collective-permute-start | bytes 3145736 | tf_op jit(solution)/shard_map/ppermute | solution.py:32
  142.7 2.8 %collective-permute-done.17.b2_ref = bf16[8,768]{1,0:T(8,128)(2,1)S(1)} collective-permute-done((bf16[8,768]{1,0:T(8,128)(2,1)S(1)}, bf16[8,768]{1,0:T(8,128)(2,1)S(1)}, u32[]{:S(2)}, u32[]{:S(2)}) %collective-permute-start.17) | collective-permute-done | bytes 12320 | tf_op jit(solution)/shard_map/ppermute | solution.py:32
  147.1 1.9 square.1
  149.0 13.0 %all-to-all-start.4 = ((f32[256,1,128]{2,1,0:T(1,128)}), f32[256,1,128]{2,1,0:T(1,128)S(1)}, u32[]{:S(2)}, u32[]{:S(2)}) async-start(f32[256,1,128]{2,1,0:T(1,128)} %get-tuple-element.24), calls=%async_computation.4 | async-start | bytes 262144 | tf_op jit(solution)/shard_map/all_to_all | solution.py:28
  163.7 2.1 %collective-permute-start.19 = (f32[4,4096]{1,0:T(4,128)S(1)}, f32[4,4096]{1,0:T(4,128)S(1)}, u32[]{:S(2)}, u32[]{:S(2)}) collective-permute-start(f32[4,4096]{1,0:T(4,128)S(1)} %get-tuple-element.41), channel_id=1, source_target_pairs={{0,4},{4,0},{1,5},{5,1},{2,6},{6,2},{3,7},{7,3},{8,12},{12,8},{9,1... | collective-permute-start | bytes 196616 | tf_op jit(solution)/shard_map/ppermute | solution.py:299
  166.7 19.8 %all-to-all-done.4.report_ref = f32[256,1,128]{2,1,0:T(1,128)S(1)} async-done(((f32[256,1,128]{2,1,0:T(1,128)}), f32[256,1,128]{2,1,0:T(1,128)S(1)}, u32[]{:S(2)}, u32[]{:S(2)}) %all-to-all-start.4) | async-done | bytes 131104 | tf_op jit(solution)/shard_map/all_to_all | solution.py:28
  187.2 2.3 %final.1 = (f32[2,128]{1,0:T(2,128)}, f32[1,1]{1,0:T(1,128)}, f32[4,8192]{1,0:T(4,128)}, f32[4,8192]{1,0:T(4,128)}, f32[4,8192]{1,0:T(4,128)}) custom-call(s32[8]{0:T(128)} %compare_select_fusion.6.place_ref, f32[256,1,128]{2,1,0:T(1,128)} %copy-done.8, f32[8,256]{1,0:T(8,128)} %get-tuple-element.21.row_ref, f32[4,4096]{1,0:T(4,128)} %get-tuple-element.42.near_ref, ...), custom_call_target="tpu_custom_call" | custom-call | tf_op jit(solution)/shard_map/final/pallas_call | solution.py:327
  191.2 3.5 %add_convert_fusion = bf16[256,2048]{1,0:T(8,128)(2,1)} fusion(bf16[256,2048]{1,0:T(8,128)(2,1)S(1)} %convolution_convert_fusion.1, bf16[256,2048]{1,0:T(8,128)(2,1)} %collective-permute-done.23, bf16[256,2048]{1,0:T(8,128)(2,1)} %collective-permute-done.22, bf16[256,2048]{1,0:T(8,128)(2,1)} %collective-permute-done.21), kind=kLoop, calls=%fused_computation.8 | loop fusion | flops 4194304 | bytes 5242880 | tf_op jit(solution)/shard_map/convert_element_type | solution.py:324
  (123 shorter events, 40.2 us)
Async XLA Ops:
  5.4 58.5 %collective-permute-start.7 = (bf16[256,4096]{1,0:T(8,128)(2,1)}, bf16[256,4096]{1,0:T(8,128)(2,1)S(1)}, u32[]{:S(2)}, u32[]{:S(2)}) collective-permute-start(bf16[256,4096]{1,0:T(8,128)(2,1)} %get-tuple-element.37), channel_id=1, source_target_pairs={{0,4},{4,0},{1,5},{5,1},{2,6},{6,2},{3,7},{7,3},{8,12},{12,8},{9,1... | collective-permute-start | bytes 6291464 | tf_op jit(solution)/shard_map/ppermute | solution.py:218
  9.8 23.4 %all-to-all-start.1 = ((bf16[16,4,3840]{2,1,0:T(4,128)(2,1)}), bf16[16,4,3840]{2,1,0:T(4,128)(2,1)S(1)}, u32[]{:S(2)}, u32[]{:S(2)}) async-start(bf16[16,4,3840]{2,1,0:T(4,128)(2,1)} %bitcast.9), calls=%async_computation.1 | async-start | bytes 983040 | tf_op jit(solution)/shard_map/all_to_all | solution.py:28
  16.9 1.3 collective-permute-start
  18.2 3.9 %collective-permute-start.3 = (bf16[8,768]{1,0:T(8,128)(2,1)S(1)}, bf16[8,768]{1,0:T(8,128)(2,1)S(1)}, u32[]{:S(2)}, u32[]{:S(2)}) collective-permute-start(bf16[8,768]{1,0:T(8,128)(2,1)S(1)} %maximum_select_fusion.1), channel_id=1, source_target_pairs={{0,192},{64,0},{128,64},{192,128},{1,193},{65,1},{129,65},{193,129... | collective-permute-start | bytes 36872 | tf_op jit(solution)/shard_map/ppermute | solution.py:32
  21.0 4.3 %collective-permute-start.2 = (bf16[8,768]{1,0:T(8,128)(2,1)S(1)}, bf16[8,768]{1,0:T(8,128)(2,1)S(1)}, u32[]{:S(2)}, u32[]{:S(2)}) collective-permute-start(bf16[8,768]{1,0:T(8,128)(2,1)S(1)} %maximum_select_fusion.1), channel_id=1, source_target_pairs={{0,128},{64,192},{128,0},{192,64},{1,129},{65,193},{129,1},{193,65... | collective-permute-start | bytes 36872 | tf_op jit(solution)/shard_map/ppermute | solution.py:32
  21.4 4.1 %collective-permute-start.1 = (bf16[8,768]{1,0:T(8,128)(2,1)S(1)}, bf16[8,768]{1,0:T(8,128)(2,1)S(1)}, u32[]{:S(2)}, u32[]{:S(2)}) collective-permute-start(bf16[8,768]{1,0:T(8,128)(2,1)S(1)} %maximum_select_fusion.1), channel_id=1, source_target_pairs={{0,64},{64,128},{128,192},{192,0},{1,65},{65,129},{129,193},{193,1... | collective-permute-start | bytes 36872 | tf_op jit(solution)/shard_map/ppermute | solution.py:32
  34.0 18.7 %all-to-all-start = ((bf16[8,4,8,768]{3,2,1,0:T(8,128)(2,1)}), bf16[8,4,8,768]{3,2,1,0:T(8,128)(2,1)S(1)}, u32[]{:S(2)}, u32[]{:S(2)}) async-start(bf16[8,4,8,768]{3,2,1,0:T(8,128)(2,1)} %broadcast_in_dim.51), calls=%async_computation | async-start | bytes 786432 | tf_op jit(solution)/shard_map/all_to_all | solution.py:28
  37.5 27.7 %copy-start.5 = (bf16[64,3840]{1,0:T(8,128)(2,1)}, bf16[64,3840]{1,0:T(8,128)(2,1)S(1)}, u32[]{:S(2)}) copy-start(bf16[64,3840]{1,0:T(8,128)(2,1)S(1)} %reshape.95.a0_ref) | copy-start | bytes 1474564
  37.6 15.1 %collective-permute-start.4 = (bf16[64,3840]{1,0:T(8,128)(2,1)S(1)}, bf16[64,3840]{1,0:T(8,128)(2,1)S(1)}, u32[]{:S(2)}, u32[]{:S(2)}) collective-permute-start(bf16[64,3840]{1,0:T(8,128)(2,1)S(1)} %reshape.95.a0_ref), channel_id=1, source_target_pairs={{0,64},{64,128},{128,192},{192,0},{1,65},{65,129},{129,193},{193,1... | collective-permute-start | bytes 1474568 | tf_op jit(solution)/shard_map/ppermute | solution.py:32
  38.9 24.9 %collective-permute-start.5 = (bf16[64,3840]{1,0:T(8,128)(2,1)S(1)}, bf16[64,3840]{1,0:T(8,128)(2,1)}, u32[]{:S(2)}, u32[]{:S(2)}) collective-permute-start(bf16[64,3840]{1,0:T(8,128)(2,1)S(1)} %reshape.95.a0_ref), channel_id=1, source_target_pairs={{0,128},{64,192},{128,0},{192,64},{1,129},{65,193},{129,1},{193,65... | collective-permute-start | bytes 1474568 | tf_op jit(solution)/shard_map/ppermute | solution.py:32
  41.5 22.3 %collective-permute-start.6 = (bf16[64,3840]{1,0:T(8,128)(2,1)S(1)}, bf16[64,3840]{1,0:T(8,128)(2,1)}, u32[]{:S(2)}, u32[]{:S(2)}) collective-permute-start(bf16[64,3840]{1,0:T(8,128)(2,1)S(1)} %reshape.95.a0_ref), channel_id=1, source_target_pairs={{0,192},{64,0},{128,64},{192,128},{1,193},{65,1},{129,65},{193,129... | collective-permute-start | bytes 1474568 | tf_op jit(solution)/shard_map/ppermute | solution.py:32
  65.3 24.5 %copy-start = (bf16[256,4096]{1,0:T(8,128)(2,1)S(1)}, bf16[256,4096]{1,0:T(8,128)(2,1)}, u32[]{:S(2)}) copy-start(bf16[256,4096]{1,0:T(8,128)(2,1)} %get-tuple-element.36.own_ref) | copy-start | bytes 6291460
  70.9 2.9 %collective-permute-start.8 = (f32[256,256]{1,0:T(8,128)}, f32[256,256]{1,0:T(8,128)S(1)}, u32[]{:S(2)}, u32[]{:S(2)}) collective-permute-start(f32[256,256]{1,0:T(8,128)} %get-tuple-element.20), channel_id=1, source_target_pairs={{0,4},{4,0},{1,5},{5,1},{2,6},{6,2},{3,7},{7,3},{8,12},{12,8},{9,1... | collective-permute-start | bytes 786440 | tf_op jit(solution)/shard_map/ppermute | solution.py:232
  76.5 4.3 %collective-permute-start.9 = (f32[8,256]{1,0:T(8,128)}, f32[8,256]{1,0:T(8,128)S(1)}, u32[]{:S(2)}, u32[]{:S(2)}) collective-permute-start(f32[8,256]{1,0:T(8,128)} %get-tuple-element.23), channel_id=1, source_target_pairs={{0,3},{1,0},{2,1},{3,2},{4,7},{5,4},{6,5},{7,6},{8,11},{9,8},{10,9... | collective-permute-start | bytes 24584 | tf_op jit(solution)/shard_map/ppermute | solution.py:32
  79.0 4.2 %collective-permute-start.10 = (f32[8,256]{1,0:T(8,128)}, f32[8,256]{1,0:T(8,128)S(1)}, u32[]{:S(2)}, u32[]{:S(2)}) collective-permute-start(f32[8,256]{1,0:T(8,128)} %get-tuple-element.23), channel_id=1, source_target_pairs={{0,2},{1,3},{2,0},{3,1},{4,6},{5,7},{6,4},{7,5},{8,10},{9,11},{10,... | collective-permute-start | bytes 24584 | tf_op jit(solution)/shard_map/ppermute | solution.py:32
  79.5 3.9 %collective-permute-start.11 = (f32[8,256]{1,0:T(8,128)}, f32[8,256]{1,0:T(8,128)S(1)}, u32[]{:S(2)}, u32[]{:S(2)}) collective-permute-start(f32[8,256]{1,0:T(8,128)} %get-tuple-element.23), channel_id=1, source_target_pairs={{0,1},{1,2},{2,3},{3,0},{4,5},{5,6},{6,7},{7,4},{8,9},{9,10},{10,1... | collective-permute-start | bytes 24584 | tf_op jit(solution)/shard_map/ppermute | solution.py:32
  86.8 2.9 %collective-permute-start.12 = (bf16[256,256]{1,0:T(8,128)(2,1)S(1)}, bf16[256,256]{1,0:T(8,128)(2,1)S(1)}, u32[]{:S(2)}, u32[]{:S(2)}) collective-permute-start(bf16[256,256]{1,0:T(8,128)(2,1)S(1)} %multiply_convert_fusion), channel_id=1, source_target_pairs={{0,4},{4,0},{1,5},{5,1},{2,6},{6,2},{3,7},{7,3},{8,12},{12,8},{9,1... | collective-permute-start | bytes 393224 | tf_op jit(solution)/shard_map/ppermute | solution.py:270
  88.7 40.9 %collective-permute-start.20 = (bf16[256,4096]{1,0:T(8,128)(2,1)}, bf16[256,4096]{1,0:T(8,128)(2,1)}, u32[]{:S(2)}, u32[]{:S(2)}) collective-permute-start(bf16[256,4096]{1,0:T(8,128)(2,1)} %get-tuple-element.28), channel_id=1, source_target_pairs={{0,4},{4,0},{1,5},{5,1},{2,6},{6,2},{3,7},{7,3},{8,12},{12,8},{9,1... | collective-permute-start | bytes 6291464 | tf_op jit(solution)/shard_map/ppermute | solution.py:233
  94.8 13.6 %collective-permute-start.15 = (bf16[64,3328]{1,0:T(8,128)(2,1)}, bf16[64,3328]{1,0:T(8,128)(2,1)}, u32[]{:S(2)}, u32[]{:S(2)}) collective-permute-start(bf16[64,3328]{1,0:T(8,128)(2,1)} %get-tuple-element.39), channel_id=1, source_target_pairs={{0,64},{64,128},{128,192},{192,0},{1,65},{65,129},{129,193},{193,1... | collective-permute-start | bytes 1277960 | tf_op jit(solution)/shard_map/ppermute | solution.py:32
  95.8 21.2 %collective-permute-start.14 = (bf16[64,3328]{1,0:T(8,128)(2,1)S(1)}, bf16[64,3328]{1,0:T(8,128)(2,1)}, u32[]{:S(2)}, u32[]{:S(2)}) collective-permute-start(bf16[64,3328]{1,0:T(8,128)(2,1)S(1)} %get-tuple-element.40), channel_id=1, source_target_pairs={{0,128},{64,192},{128,0},{192,64},{1,129},{65,193},{129,1},{193,65... | collective-permute-start | bytes 1277960 | tf_op jit(solution)/shard_map/ppermute | solution.py:32
  98.0 19.0 %collective-permute-start.13 = (bf16[64,3328]{1,0:T(8,128)(2,1)S(1)}, bf16[64,3328]{1,0:T(8,128)(2,1)}, u32[]{:S(2)}, u32[]{:S(2)}) collective-permute-start(bf16[64,3328]{1,0:T(8,128)(2,1)S(1)} %get-tuple-element.38), channel_id=1, source_target_pairs={{0,192},{64,0},{128,64},{192,128},{1,193},{65,1},{129,65},{193,129... | collective-permute-start | bytes 1277960 | tf_op jit(solution)/shard_map/ppermute | solution.py:32
  101.8 27.9 %copy-start.1 = (bf16[256,4096]{1,0:T(8,128)(2,1)S(1)}, bf16[256,4096]{1,0:T(8,128)(2,1)}, u32[]{:S(2)}) copy-start(bf16[256,4096]{1,0:T(8,128)(2,1)} %get-tuple-element.28) | copy-start | bytes 6291460
  101.8 19.8 %all-to-all-start.3 = ((bf16[8,4,8,768]{3,2,1,0:T(8,128)(2,1)}), bf16[8,4,8,768]{3,2,1,0:T(8,128)(2,1)S(1)}, u32[]{:S(2)}, u32[]{:S(2)}) async-start(bf16[8,4,8,768]{3,2,1,0:T(8,128)(2,1)} %bitcast.65), calls=%async_computation.3 | async-start | bytes 786432 | tf_op jit(solution)/shard_map/all_to_all | solution.py:28
  121.6 24.7 %all-to-all-start.2 = ((bf16[8,8,3328]{2,1,0:T(8,128)(2,1)}), bf16[8,8,3328]{2,1,0:T(8,128)(2,1)S(1)}, u32[]{:S(2)}, u32[]{:S(2)}) async-start(bf16[8,8,3328]{2,1,0:T(8,128)(2,1)} %fusion.15), calls=%async_computation.2 | async-start | bytes 851968 | tf_op jit(solution)/shard_map/all_to_all | solution.py:28
  126.6 15.5 %collective-permute-start.16 = (bf16[8,768]{1,0:T(8,128)(2,1)S(1)}, bf16[8,768]{1,0:T(8,128)(2,1)S(1)}, u32[]{:S(2)}, u32[]{:S(2)}) collective-permute-start(bf16[8,768]{1,0:T(8,128)(2,1)S(1)} %get-tuple-element.45), channel_id=1, source_target_pairs={{0,192},{64,0},{128,64},{192,128},{1,193},{65,1},{129,65},{193,129... | collective-permute-start | bytes 36872 | tf_op jit(solution)/shard_map/ppermute | solution.py:32
  132.3 58.9 %collective-permute-start.23 = (bf16[256,2048]{1,0:T(8,128)(2,1)}, bf16[256,2048]{1,0:T(8,128)(2,1)}, u32[]{:S(2)}, u32[]{:S(2)}) collective-permute-start(bf16[256,2048]{1,0:T(8,128)(2,1)} %convolution_convert_fusion.2), channel_id=1, source_target_pairs={{0,1},{1,2},{2,3},{3,0},{4,5},{5,6},{6,7},{7,4},{8,9},{9,10},{10,1... | collective-permute-start | bytes 3145736 | tf_op jit(solution)/shard_map/ppermute | solution.py:32
  135.4 55.8 %collective-permute-start.22 = (bf16[256,2048]{1,0:T(8,128)(2,1)}, bf16[256,2048]{1,0:T(8,128)(2,1)}, u32[]{:S(2)}, u32[]{:S(2)}) collective-permute-start(bf16[256,2048]{1,0:T(8,128)(2,1)} %convolution_convert_fusion.3), channel_id=1, source_target_pairs={{0,2},{1,3},{2,0},{3,1},{4,6},{5,7},{6,4},{7,5},{8,10},{9,11},{10,... | collective-permute-start | bytes 3145736 | tf_op jit(solution)/shard_map/ppermute | solution.py:32
  139.3 51.9 %collective-permute-start.21 = (bf16[256,2048]{1,0:T(8,128)(2,1)}, bf16[256,2048]{1,0:T(8,128)(2,1)}, u32[]{:S(2)}, u32[]{:S(2)}) collective-permute-start(bf16[256,2048]{1,0:T(8,128)(2,1)} %convolution_convert_fusion.4), channel_id=1, source_target_pairs={{0,3},{1,0},{2,1},{3,2},{4,7},{5,4},{6,5},{7,6},{8,11},{9,8},{10,9... | collective-permute-start | bytes 3145736 | tf_op jit(solution)/shard_map/ppermute | solution.py:32
  141.4 4.1 %collective-permute-start.17 = (bf16[8,768]{1,0:T(8,128)(2,1)S(1)}, bf16[8,768]{1,0:T(8,128)(2,1)S(1)}, u32[]{:S(2)}, u32[]{:S(2)}) collective-permute-start(bf16[8,768]{1,0:T(8,128)(2,1)S(1)} %get-tuple-element.44), channel_id=1, source_target_pairs={{0,128},{64,192},{128,0},{192,64},{1,129},{65,193},{129,1},{193,65... | collective-permute-start | bytes 36872 | tf_op jit(solution)/shard_map/ppermute | solution.py:32
  142.1 4.2 %collective-permute-start.18 = (bf16[8,768]{1,0:T(8,128)(2,1)S(1)}, bf16[8,768]{1,0:T(8,128)(2,1)S(1)}, u32[]{:S(2)}, u32[]{:S(2)}) collective-permute-start(bf16[8,768]{1,0:T(8,128)(2,1)S(1)} %get-tuple-element.43), channel_id=1, source_target_pairs={{0,64},{64,128},{128,192},{192,0},{1,65},{65,129},{129,193},{193,1... | collective-permute-start | bytes 36872 | tf_op jit(solution)/shard_map/ppermute | solution.py:32
  149.0 37.5 %all-to-all-start.4 = ((f32[256,1,128]{2,1,0:T(1,128)}), f32[256,1,128]{2,1,0:T(1,128)S(1)}, u32[]{:S(2)}, u32[]{:S(2)}) async-start(f32[256,1,128]{2,1,0:T(1,128)} %get-tuple-element.24), calls=%async_computation.4 | async-start | bytes 262144 | tf_op jit(solution)/shard_map/all_to_all | solution.py:28
  163.7 3.0 %collective-permute-start.19 = (f32[4,4096]{1,0:T(4,128)S(1)}, f32[4,4096]{1,0:T(4,128)S(1)}, u32[]{:S(2)}, u32[]{:S(2)}) collective-permute-start(f32[4,4096]{1,0:T(4,128)S(1)} %get-tuple-element.41), channel_id=1, source_target_pairs={{0,4},{4,0},{1,5},{5,1},{2,6},{6,2},{3,7},{7,3},{8,12},{12,8},{9,1... | collective-permute-start | bytes 196616 | tf_op jit(solution)/shard_map/ppermute | solution.py:299
  (17 other events, 115.1 us)

commit v11 on v10

--- a/solution.py
+++ b/solution.py
@@ -49,19 +49,44 @@
 
 
 def score_kernel(
-    thin, a0_ref, a1_ref, a2_ref, a3_ref, b_ref, own_ref, mate_ref, head_ref, own_part_ref, mate_part_ref
+    thin, a0_ref, a1_ref, a2_ref, a3_ref, b_ref, tok_ref,
+    head_out_ref, own_part_ref, mate_part_ref, head_ref, held_ref, sems,
 ):
-    wide = a0_ref.shape[1]
-    y_rows = a0_ref.shape[0]
-    for s, a_ref in enumerate((a0_ref, a1_ref, a2_ref, a3_ref)):
-        head_ref[s * y_rows : (s + 1) * y_rows, :wide] = a_ref[...]
+    y_rows, wide = a0_ref.shape
+    rows = tok_ref.shape[0] // 2
+    blocks = [
+        pltpu.make_async_copy(
+            a_ref, head_ref.at[pl.ds(s * y_rows, y_rows), pl.ds(0, wide)], sems.at[s]
+        )
+        for s, a_ref in enumerate((a0_ref, a1_ref, a2_ref, a3_ref))
+    ]
+    mate_copy, own_copy = [
+        pltpu.make_async_copy(
+            tok_ref.at[pl.ds(at, rows)], held_ref.at[pl.ds(at, rows)], sems.at[sem]
+        )
+        for at, sem in ((rows, NY), (0, NY + 1))
+    ]
+    for copy in blocks:
+        copy.start()
+    mate_copy.start()
+    own_copy.start()
+    for s in range(NY):
         for z in range(NZ):
             at = s * y_rows + z * (y_rows // NZ)
             head_ref[at : at + y_rows // NZ, wide:] = b_ref[z, s, :, :thin]
-    for tok_ref, part_ref in ((mate_ref, mate_part_ref), (own_ref, own_part_ref)):
-        part_ref[...] = lax.dot_general(
-            head_ref[...], tok_ref[...], (((1,), (1,)), ((), ())), preferred_element_type=f32
-        )
+    for copy in blocks:
+        copy.wait()
+    out_copy = pltpu.make_async_copy(head_ref, head_out_ref, sems.at[NY + 2])
+    out_copy.start()
+    mate_copy.wait()
+    mate_part_ref[...] = lax.dot_general(
+        head_ref[...], held_ref[rows:], (((1,), (1,)), ((), ())), preferred_element_type=f32
+    )
+    own_copy.wait()
+    own_part_ref[...] = lax.dot_general(
+        head_ref[...], held_ref[:rows], (((1,), (1,)), ((), ())), preferred_element_type=f32
+    )
+    out_copy.wait()
 
 
 def final_kernel(
@@ -156,6 +181,7 @@
 
 
 VMEM = pl.BlockSpec(memory_space=pltpu.VMEM)
+ANY = pl.BlockSpec(memory_space=pl.ANY)
 SMEM = pl.BlockSpec(memory_space=pltpu.SMEM)
 
 
@@ -216,7 +242,7 @@
         hidden_states, (0, (1 - core) * half), (tok_rows, half), allow_negative_indices=False
     )
     mate_half = lax.ppermute(far_half, "core", SWAP)
-    tokens = jnp.concatenate([own_half, mate_half], 0)
+    tokens = lax.optimization_barrier(jnp.concatenate([own_half, mate_half], 0))
 
     head, own_part, mate_part = pl.pallas_call(
         functools.partial(score_kernel, thin),
@@ -225,10 +251,15 @@
             jax.ShapeDtypeStruct((group_rows, tok_rows), f32),
             jax.ShapeDtypeStruct((group_rows, tok_rows), f32),
         ),
-        in_specs=[VMEM] * (NY + 3),
-        out_specs=(VMEM, VMEM, VMEM),
+        in_specs=[ANY] * NY + [VMEM, ANY],
+        out_specs=(ANY, VMEM, VMEM),
+        scratch_shapes=[
+            pltpu.VMEM((group_rows, half), bf16),
+            pltpu.VMEM((NC * tok_rows, half), bf16),
+            pltpu.SemaphoreType.DMA((NY + 3,)),
+        ],
         name="score",
-    )(*parts_a, part_b, own_half, mate_half)
+    )(*parts_a, part_b, tokens)
     mate_part = lax.ppermute(mate_part, "core", SWAP)
     mate_head = lax.ppermute(head, "core", SWAP)
     logits, stats, rows = pl.pallas_call(

time: 196 us -> 194 us (0.990)
  local copies, waits for them, and re-layouts: 17.2 us -> 12.9 us
  waiting for transfers between devices: 71.7 us -> 67.6 us
  other arithmetic: 15.1 us -> 19 us
    all_to_all x5, waiting for transfers between devices: 39.8 us -> 34.7 us  [exchange(): return lax.all_to_all(x, axes, 0, 0, tiled=True)]
    concatenate x0 -> x1, other arithmetic: none -> 4.01 us  [step(): tokens = lax.optimization_barrier(jnp.concatenate([own_half, mate_half], 0))]
    unnamed x40 -> x36, local copies, waits for them, and re-layouts: 4.95 us -> 2.21 us
  transfers between devices with their start and end apart: 29 -> 29, of which waited for: 15 -> 15; matrix products, arithmetic and copies ran while one was open for 14% -> 16% of each run, Pallas kernels for 2% -> 2%
where the time goes in v11:
time: 194 us; the launch traced here: 193 us
  starting transfers between devices  67.6 us (35%)
  waiting for transfers between devices  67.6 us (35%)
  other arithmetic  19 us (10%)
  local copies, waits for them, and re-layouts  12.9 us (7%)
  Pallas kernels  12.9 us (7%)
  matrix products  12 us (6%)
    all_to_all x5, starting transfers between devices, exchange(): return lax.all_to_all(x, axes, 0, 0, tiled=True)  35.3 us
    all_to_all x5, waiting for transfers between devices, exchange(): return lax.all_to_all(x, axes, 0, 0, tiled=True)  34.7 us
    ppermute x18, waiting for transfers between devices, shift(): lax.ppermute(x, axis, [(i, (i + step) % count) for i in range(count)])  30.3 us
    ppermute x18, starting transfers between devices, shift(): lax.ppermute(x, axis, [(i, (i + step) % count) for i in range(count)])  24.1 us
    dot_general x4, matrix products, step(): lax.dot_general(dlogits, side, (((0,), (0,)), ((), ())), preferred_elemen...  8.53 us
    pallas_call x1, Pallas kernels, step(): pl.pallas_call(functools.partial(score_kernel, thin), out_shape=(jax.Shap...  6.71 us
    concatenate x1, other arithmetic, step(): tokens = lax.optimization_barrier(jnp.concatenate([own_half, mate_half], 0))  4.01 us
    dynamic_slice x1, local copies, waits for them, and re-layouts, step(): lax.dynamic_slice(hidden_states, (0, core * half), (tok_rows, half), allo...  3.97 us
  transfers between devices with their start and end apart: 29, of which 15 were waited for; matrix products, arithmetic and copies ran while one was open for 16% of the time, Pallas kernels for 2%

profile of v11, /device:TPU:1, one launch (start us, length us, event | category | flops | bytes accessed | tf_op | source)
XLA Modules:
  0.0 193.0 jit_solution(13777458257557067938)
XLA Ops:
  0.7 4.0 %constant_dynamic-slice_fusion.3 = (bf16[256,4096]{1,0:T(8,128)(2,1)S(1)}, bf16[256,4096]{1,0:T(8,128)(2,1)}) fusion(bf16[256,8192]{1,0:T(8,128)(2,1)} %param.9, s32[]{:T(128)S(6)} %mul.62, s32[]{:T(128)S(6)} %mul.63), kind=kLoop, calls=%fused_computation.61 | loop fusion | bytes 8388616 | tf_op jit(solution)/shard_map/dynamic_slice | solution.py:238
  4.6 3.3 %collective-permute-start.7 = (bf16[256,4096]{1,0:T(8,128)(2,1)}, bf16[256,4096]{1,0:T(8,128)(2,1)}, u32[]{:S(2)}, u32[]{:S(2)}) collective-permute-start(bf16[256,4096]{1,0:T(8,128)(2,1)} %get-tuple-element.37), channel_id=1, source_target_pairs={{0,4},{4,0},{1,5},{5,1},{2,6},{6,2},{3,7},{7,3},{8,12},{12,8},{9,1... | collective-permute-start | bytes 6291464 | tf_op jit(solution)/shard_map/ppermute | solution.py:244
  9.0 6.9 %all-to-all-start.1 = ((bf16[16,4,3840]{2,1,0:T(4,128)(2,1)}), bf16[16,4,3840]{2,1,0:T(4,128)(2,1)S(1)}, u32[]{:S(2)}, u32[]{:S(2)}) async-start(bf16[16,4,3840]{2,1,0:T(4,128)(2,1)} %bitcast.9), calls=%async_computation.1 | async-start | bytes 983040 | tf_op jit(solution)/shard_map/all_to_all | solution.py:28
  17.5 2.8 %collective-permute-start.3 = (bf16[8,768]{1,0:T(8,128)(2,1)S(1)}, bf16[8,768]{1,0:T(8,128)(2,1)S(1)}, u32[]{:S(2)}, u32[]{:S(2)}) collective-permute-start(bf16[8,768]{1,0:T(8,128)(2,1)S(1)} %maximum_select_fusion.1), channel_id=1, source_target_pairs={{0,192},{64,0},{128,64},{192,128},{1,193},{65,1},{129,65},{193,129... | collective-permute-start | bytes 36872 | tf_op jit(solution)/shard_map/ppermute | solution.py:32
  21.3 3.3 %collective-permute-done.2 = bf16[8,768]{1,0:T(8,128)(2,1)S(1)} collective-permute-done((bf16[8,768]{1,0:T(8,128)(2,1)S(1)}, bf16[8,768]{1,0:T(8,128)(2,1)S(1)}, u32[]{:S(2)}, u32[]{:S(2)}) %collective-permute-start.2) | collective-permute-done | bytes 12320 | tf_op jit(solution)/shard_map/ppermute | solution.py:32
  24.8 7.7 %all-to-all-done.1 = bf16[16,4,3840]{2,1,0:T(4,128)(2,1)S(1)} async-done(((bf16[16,4,3840]{2,1,0:T(4,128)(2,1)}), bf16[16,4,3840]{2,1,0:T(4,128)(2,1)S(1)}, u32[]{:S(2)}, u32[]{:S(2)}) %all-to-all-start.1) | async-done | bytes 491552 | tf_op jit(solution)/shard_map/all_to_all | solution.py:28
  33.2 3.5 %all-to-all-start = ((bf16[8,4,8,768]{3,2,1,0:T(8,128)(2,1)}), bf16[8,4,8,768]{3,2,1,0:T(8,128)(2,1)S(1)}, u32[]{:S(2)}, u32[]{:S(2)}) async-start(bf16[8,4,8,768]{3,2,1,0:T(8,128)(2,1)} %broadcast_in_dim.51), calls=%async_computation | async-start | bytes 786432 | tf_op jit(solution)/shard_map/all_to_all | solution.py:28
  38.2 2.6 %collective-permute-start.5 = (bf16[64,3840]{1,0:T(8,128)(2,1)S(1)}, bf16[64,3840]{1,0:T(8,128)(2,1)}, u32[]{:S(2)}, u32[]{:S(2)}) collective-permute-start(bf16[64,3840]{1,0:T(8,128)(2,1)S(1)} %reshape.95.a0_ref), channel_id=1, source_target_pairs={{0,128},{64,192},{128,0},{192,64},{1,129},{65,193},{129,1},{193,65... | collective-permute-start | bytes 1474568 | tf_op jit(solution)/shard_map/ppermute | solution.py:32
  41.9 4.0 %pad_maximum_fusion.tok_ref = bf16[512,4096]{1,0:T(8,128)(2,1)} fusion(bf16[256,4096]{1,0:T(8,128)(2,1)} %collective-permute-done.7, bf16[256,4096]{1,0:T(8,128)(2,1)S(1)} %get-tuple-element.36), kind=kLoop, calls=%fused_computation.1 | loop fusion | flops 8388608 | bytes 8388608 | tf_op jit(solution)/shard_map/concatenate | solution.py:245
  45.9 6.0 %all-to-all-done.b_ref = bf16[8,4,8,768]{3,2,1,0:T(8,128)(2,1)S(1)} async-done(((bf16[8,4,8,768]{3,2,1,0:T(8,128)(2,1)}), bf16[8,4,8,768]{3,2,1,0:T(8,128)(2,1)S(1)}, u32[]{:S(2)}, u32[]{:S(2)}) %all-to-all-start) | async-done | bytes 393248 | tf_op jit(solution)/shard_map/all_to_all | solution.py:28
  51.9 11.2 %collective-permute-done.5.a2_ref = bf16[64,3840]{1,0:T(8,128)(2,1)} collective-permute-done((bf16[64,3840]{1,0:T(8,128)(2,1)S(1)}, bf16[64,3840]{1,0:T(8,128)(2,1)}, u32[]{:S(2)}, u32[]{:S(2)}) %collective-permute-start.5) | collective-permute-done | bytes 491552 | tf_op jit(solution)/shard_map/ppermute | solution.py:32
  63.1 6.7 %score.1 = (bf16[256,4096]{1,0:T(8,128)(2,1)}, f32[256,256]{1,0:T(8,128)}, f32[256,256]{1,0:T(8,128)}) custom-call(bf16[64,3840]{1,0:T(8,128)(2,1)} %copy-done.3, bf16[64,3840]{1,0:T(8,128)(2,1)} %copy-done.7, bf16[64,3840]{1,0:T(8,128)(2,1)} %collective-permute-done.5.a2_ref, bf16[64,3840]{1,0:T(8,128)(2,1)} %collective-permute-done.6.a3_ref, ...), custom_call_target="tpu_custom_call" | custom-call | tf_op jit(solution)/shard_map/score/pallas_call | solution.py:247
  73.4 1.9 %front.1 = (f32[256,256]{1,0:T(8,128)}, f32[8,256]{1,0:T(8,128)}, f32[8,256]{1,0:T(8,128)}) custom-call(s32[128]{0:T(128)} %span_ref.1, s32[8]{0:T(128)} %compare_select_fusion.6.place_ref, bf16[8,4,8,768]{3,2,1,0:T(8,128)(2,1)} %copy-done.1, f32[256,256]{1,0:T(8,128)} %get-tuple-element.19.own_ref, f32[256,256]{1,0:T(8,128)} %copy-done.8), custom_call_target="tpu_custom_call" | custom-call | tf_op jit(solution)/shard_map/front/pallas_call | solution.py:265
  75.4 2.5 %collective-permute-start.9 = (f32[8,256]{1,0:T(8,128)}, f32[8,256]{1,0:T(8,128)S(1)}, u32[]{:S(2)}, u32[]{:S(2)}) collective-permute-start(f32[8,256]{1,0:T(8,128)} %get-tuple-element.23), channel_id=1, source_target_pairs={{0,3},{1,0},{2,1},{3,2},{4,7},{5,4},{6,5},{7,6},{8,11},{9,8},{10,9... | collective-permute-start | bytes 24584 | tf_op jit(solution)/shard_map/ppermute | solution.py:32
  79.7 2.4 %collective-permute-done.10 = f32[8,256]{1,0:T(8,128)S(1)} collective-permute-done((f32[8,256]{1,0:T(8,128)}, f32[8,256]{1,0:T(8,128)S(1)}, u32[]{:S(2)}, u32[]{:S(2)}) %collective-permute-start.10) | collective-permute-done | bytes 8224 | tf_op jit(solution)/shard_map/ppermute | solution.py:32
  88.6 3.4 %convolution_convert_fusion = bf16[256,4096]{1,0:T(8,128)(2,1)S(1)} fusion(bf16[512,4096]{1,0:T(8,128)(2,1)} %pad_maximum_fusion.tok_ref, bf16[256,256]{1,0:T(8,128)(2,1)S(1)} %collective-permute-done.12, bf16[256,256]{1,0:T(8,128)(2,1)S(1)} %multiply_convert_fusion), kind=kOutput, calls=%fused_computation | convolution fusion | flops 1075314688 | bytes 6553600 | tf_op jit(solution)/shard_map/dot_general | solution.py:304
  94.0 2.2 %collective-permute-start.14 = (bf16[64,3328]{1,0:T(8,128)(2,1)S(1)}, bf16[64,3328]{1,0:T(8,128)(2,1)}, u32[]{:S(2)}, u32[]{:S(2)}) collective-permute-start(bf16[64,3328]{1,0:T(8,128)(2,1)S(1)} %get-tuple-element.40), channel_id=1, source_target_pairs={{0,128},{64,192},{128,0},{192,64},{1,129},{65,193},{129,1},{193,65... | collective-permute-start | bytes 1277960 | tf_op jit(solution)/shard_map/ppermute | solution.py:32
  99.0 6.7 %all-to-all-start.3 = ((bf16[8,4,8,768]{3,2,1,0:T(8,128)(2,1)}), bf16[8,4,8,768]{3,2,1,0:T(8,128)(2,1)S(1)}, u32[]{:S(2)}, u32[]{:S(2)}) async-start(bf16[8,4,8,768]{3,2,1,0:T(8,128)(2,1)} %bitcast.66), calls=%async_computation.3 | async-start | bytes 786432 | tf_op jit(solution)/shard_map/all_to_all | solution.py:28
  105.7 9.5 %collective-permute-done.14 = bf16[64,3328]{1,0:T(8,128)(2,1)} collective-permute-done((bf16[64,3328]{1,0:T(8,128)(2,1)S(1)}, bf16[64,3328]{1,0:T(8,128)(2,1)}, u32[]{:S(2)}, u32[]{:S(2)}) %collective-permute-start.14) | collective-permute-done | bytes 426016 | tf_op jit(solution)/shard_map/ppermute | solution.py:32
  115.2 2.4 %fusion.12 = bf16[8,8,3328]{2,1,0:T(8,128)(2,1)} fusion(bf16[64,3328]{1,0:T(8,128)(2,1)} %collective-permute-done.15, bf16[64,3328]{1,0:T(8,128)(2,1)} %collective-permute-done.14, bf16[64,3328]{1,0:T(8,128)(2,1)} %collective-permute-done.13, bf16[256,4096]{1,0:T(8,128)(2,1)} %copy-done.2), kind=kLoop, calls=%fused_computation.21 | loop fusion | flops 1703936 | bytes 2129920 | tf_op jit(solution)/shard_map/reshape | solution.py:309
  118.9 5.3 %all-to-all-start.2 = ((bf16[8,8,3328]{2,1,0:T(8,128)(2,1)}), bf16[8,8,3328]{2,1,0:T(8,128)(2,1)S(1)}, u32[]{:S(2)}, u32[]{:S(2)}) async-start(bf16[8,8,3328]{2,1,0:T(8,128)(2,1)} %fusion.12), calls=%async_computation.2 | async-start | bytes 851968 | tf_op jit(solution)/shard_map/all_to_all | solution.py:28
  124.8 3.1 %collective-permute-start.16 = (bf16[8,768]{1,0:T(8,128)(2,1)S(1)}, bf16[8,768]{1,0:T(8,128)(2,1)S(1)}, u32[]{:S(2)}, u32[]{:S(2)}) collective-permute-start(bf16[8,768]{1,0:T(8,128)(2,1)S(1)} %get-tuple-element.45), channel_id=1, source_target_pairs={{0,192},{64,0},{128,64},{192,128},{1,193},{65,1},{129,65},{193,129... | collective-permute-start | bytes 36872 | tf_op jit(solution)/shard_map/ppermute | solution.py:32
  127.9 2.7 %convolution_convert_fusion.2 = bf16[256,2048]{1,0:T(8,128)(2,1)} fusion(bf16[256,256]{1,0:T(8,128)(2,1)S(1)} %multiply_convert_fusion, bf16[256,4096]{1,0:T(8,128)(2,1)} %collective-permute-done.20, s32[]{:T(128)S(6)} %mul.76, bf16[256,4096]{1,0:T(8,128)(2,1)S(1)} %copy-done, pred[]{:T(512)S(6)} %eq.129), kind=kOutput, calls=%fused_computation.3 | convolution fusion | flops 269484032 | bytes 3276805 | tf_op jit(solution)/shard_map/dot_general | solution.py:347
  134.9 2.7 %convolution_convert_fusion.4 = bf16[256,2048]{1,0:T(8,128)(2,1)} fusion(bf16[256,256]{1,0:T(8,128)(2,1)S(1)} %multiply_convert_fusion, bf16[256,4096]{1,0:T(8,128)(2,1)} %collective-permute-done.20, s32[]{:T(128)S(6)} %mul.74, bf16[256,4096]{1,0:T(8,128)(2,1)S(1)} %copy-done, pred[]{:T(512)S(6)} %eq.127), kind=kOutput, calls=%fused_computation.5 | convolution fusion | flops 269484032 | bytes 3276805 | tf_op jit(solution)/shard_map/dot_general | solution.py:347
  137.6 2.1 %collective-permute-start.21 = (bf16[256,2048]{1,0:T(8,128)(2,1)}, bf16[256,2048]{1,0:T(8,128)(2,1)}, u32[]{:S(2)}, u32[]{:S(2)}) collective-permute-start(bf16[256,2048]{1,0:T(8,128)(2,1)} %convolution_convert_fusion.4), channel_id=1, source_target_pairs={{0,3},{1,0},{2,1},{3,2},{4,7},{5,4},{6,5},{7,6},{8,11},{9,8},{10,9... | collective-permute-start | bytes 3145736 | tf_op jit(solution)/shard_map/ppermute | solution.py:32
  141.0 2.8 %collective-permute-done.17.b2_ref = bf16[8,768]{1,0:T(8,128)(2,1)S(1)} collective-permute-done((bf16[8,768]{1,0:T(8,128)(2,1)S(1)}, bf16[8,768]{1,0:T(8,128)(2,1)S(1)}, u32[]{:S(2)}, u32[]{:S(2)}) %collective-permute-start.17) | collective-permute-done | bytes 12320 | tf_op jit(solution)/shard_map/ppermute | solution.py:32
  145.4 1.9 %square.1 = (f32[8,4096]{1,0:T(8,128)}, f32[256,1,128]{2,1,0:T(1,128)}) custom-call(bf16[8,8,3328]{2,1,0:T(8,128)(2,1)} %copy-done.4, bf16[8,768]{1,0:T(8,128)(2,1)} %get-tuple-element.46.b0_ref, bf16[8,768]{1,0:T(8,128)(2,1)} %copy-done.10, bf16[8,768]{1,0:T(8,128)(2,1)} %copy-done.11, bf16[8,768]{1,0:T(8,128)(2,1)} %copy-done.12, ...), custom_call_target="tpu_custom_call" | custom-call | tf_op jit(solution)/shard_map/square/pallas_call | solution.py:317
  147.3 13.0 %all-to-all-start.4 = ((f32[256,1,128]{2,1,0:T(1,128)}), f32[256,1,128]{2,1,0:T(1,128)S(1)}, u32[]{:S(2)}, u32[]{:S(2)}) async-start(f32[256,1,128]{2,1,0:T(1,128)} %get-tuple-element.24), calls=%async_computation.4 | async-start | bytes 262144 | tf_op jit(solution)/shard_map/all_to_all | solution.py:28
  161.9 2.1 %collective-permute-start.19 = (f32[4,4096]{1,0:T(4,128)S(1)}, f32[4,4096]{1,0:T(4,128)S(1)}, u32[]{:S(2)}, u32[]{:S(2)}) collective-permute-start(f32[4,4096]{1,0:T(4,128)S(1)} %get-tuple-element.41), channel_id=1, source_target_pairs={{0,4},{4,0},{1,5},{5,1},{2,6},{6,2},{3,7},{7,3},{8,12},{12,8},{9,1... | collective-permute-start | bytes 196616 | tf_op jit(solution)/shard_map/ppermute | solution.py:330
  165.0 19.8 %all-to-all-done.4.report_ref = f32[256,1,128]{2,1,0:T(1,128)S(1)} async-done(((f32[256,1,128]{2,1,0:T(1,128)}), f32[256,1,128]{2,1,0:T(1,128)S(1)}, u32[]{:S(2)}, u32[]{:S(2)}) %all-to-all-start.4) | async-done | bytes 131104 | tf_op jit(solution)/shard_map/all_to_all | solution.py:28
  185.4 2.3 %final.1 = (f32[2,128]{1,0:T(2,128)}, f32[1,1]{1,0:T(1,128)}, f32[4,8192]{1,0:T(4,128)}, f32[4,8192]{1,0:T(4,128)}, f32[4,8192]{1,0:T(4,128)}) custom-call(s32[8]{0:T(128)} %compare_select_fusion.6.place_ref, f32[256,1,128]{2,1,0:T(1,128)} %copy-done.6, f32[8,256]{1,0:T(8,128)} %get-tuple-element.21.row_ref, f32[4,4096]{1,0:T(4,128)} %get-tuple-element.42.near_ref, ...), custom_call_target="tpu_custom_call" | custom-call | tf_op jit(solution)/shard_map/final/pallas_call | solution.py:358
  189.5 3.5 %add_convert_fusion = bf16[256,2048]{1,0:T(8,128)(2,1)} fusion(bf16[256,2048]{1,0:T(8,128)(2,1)S(1)} %convolution_convert_fusion.1, bf16[256,2048]{1,0:T(8,128)(2,1)} %collective-permute-done.23, bf16[256,2048]{1,0:T(8,128)(2,1)} %collective-permute-done.22, bf16[256,2048]{1,0:T(8,128)(2,1)} %collective-permute-done.21), kind=kLoop, calls=%fused_computation.6 | loop fusion | flops 4194304 | bytes 5242880 | tf_op jit(solution)/shard_map/convert_element_type | solution.py:355
  (120 shorter events, 37.9 us)
Async XLA Ops:
  4.6 37.3 %collective-permute-start.7 = (bf16[256,4096]{1,0:T(8,128)(2,1)}, bf16[256,4096]{1,0:T(8,128)(2,1)}, u32[]{:S(2)}, u32[]{:S(2)}) collective-permute-start(bf16[256,4096]{1,0:T(8,128)(2,1)} %get-tuple-element.37), channel_id=1, source_target_pairs={{0,4},{4,0},{1,5},{5,1},{2,6},{6,2},{3,7},{7,3},{8,12},{12,8},{9,1... | collective-permute-start | bytes 6291464 | tf_op jit(solution)/shard_map/ppermute | solution.py:244
  9.0 23.4 %all-to-all-start.1 = ((bf16[16,4,3840]{2,1,0:T(4,128)(2,1)}), bf16[16,4,3840]{2,1,0:T(4,128)(2,1)S(1)}, u32[]{:S(2)}, u32[]{:S(2)}) async-start(bf16[16,4,3840]{2,1,0:T(4,128)(2,1)} %bitcast.9), calls=%async_computation.1 | async-start | bytes 983040 | tf_op jit(solution)/shard_map/all_to_all | solution.py:28
  16.2 1.3 collective-permute-start
  17.5 3.9 %collective-permute-start.3 = (bf16[8,768]{1,0:T(8,128)(2,1)S(1)}, bf16[8,768]{1,0:T(8,128)(2,1)S(1)}, u32[]{:S(2)}, u32[]{:S(2)}) collective-permute-start(bf16[8,768]{1,0:T(8,128)(2,1)S(1)} %maximum_select_fusion.1), channel_id=1, source_target_pairs={{0,192},{64,0},{128,64},{192,128},{1,193},{65,1},{129,65},{193,129... | collective-permute-start | bytes 36872 | tf_op jit(solution)/shard_map/ppermute | solution.py:32
  20.3 4.3 %collective-permute-start.2 = (bf16[8,768]{1,0:T(8,128)(2,1)S(1)}, bf16[8,768]{1,0:T(8,128)(2,1)S(1)}, u32[]{:S(2)}, u32[]{:S(2)}) collective-permute-start(bf16[8,768]{1,0:T(8,128)(2,1)S(1)} %maximum_select_fusion.1), channel_id=1, source_target_pairs={{0,128},{64,192},{128,0},{192,64},{1,129},{65,193},{129,1},{193,65... | collective-permute-start | bytes 36872 | tf_op jit(solution)/shard_map/ppermute | solution.py:32
  20.6 4.1 %collective-permute-start.1 = (bf16[8,768]{1,0:T(8,128)(2,1)S(1)}, bf16[8,768]{1,0:T(8,128)(2,1)S(1)}, u32[]{:S(2)}, u32[]{:S(2)}) collective-permute-start(bf16[8,768]{1,0:T(8,128)(2,1)S(1)} %maximum_select_fusion.1), channel_id=1, source_target_pairs={{0,64},{64,128},{128,192},{192,0},{1,65},{65,129},{129,193},{193,1... | collective-permute-start | bytes 36872 | tf_op jit(solution)/shard_map/ppermute | solution.py:32
  33.2 18.7 %all-to-all-start = ((bf16[8,4,8,768]{3,2,1,0:T(8,128)(2,1)}), bf16[8,4,8,768]{3,2,1,0:T(8,128)(2,1)S(1)}, u32[]{:S(2)}, u32[]{:S(2)}) async-start(bf16[8,4,8,768]{3,2,1,0:T(8,128)(2,1)} %broadcast_in_dim.51), calls=%async_computation | async-start | bytes 786432 | tf_op jit(solution)/shard_map/all_to_all | solution.py:28
  36.8 15.1 %collective-permute-start.4 = (bf16[64,3840]{1,0:T(8,128)(2,1)S(1)}, bf16[64,3840]{1,0:T(8,128)(2,1)S(1)}, u32[]{:S(2)}, u32[]{:S(2)}) collective-permute-start(bf16[64,3840]{1,0:T(8,128)(2,1)S(1)} %reshape.95.a0_ref), channel_id=1, source_target_pairs={{0,64},{64,128},{128,192},{192,0},{1,65},{65,129},{129,193},{193,1... | collective-permute-start | bytes 1474568 | tf_op jit(solution)/shard_map/ppermute | solution.py:32
  38.2 24.9 %collective-permute-start.5 = (bf16[64,3840]{1,0:T(8,128)(2,1)S(1)}, bf16[64,3840]{1,0:T(8,128)(2,1)}, u32[]{:S(2)}, u32[]{:S(2)}) collective-permute-start(bf16[64,3840]{1,0:T(8,128)(2,1)S(1)} %reshape.95.a0_ref), channel_id=1, source_target_pairs={{0,128},{64,192},{128,0},{192,64},{1,129},{65,193},{129,1},{193,65... | collective-permute-start | bytes 1474568 | tf_op jit(solution)/shard_map/ppermute | solution.py:32
  40.8 22.3 %collective-permute-start.6 = (bf16[64,3840]{1,0:T(8,128)(2,1)S(1)}, bf16[64,3840]{1,0:T(8,128)(2,1)}, u32[]{:S(2)}, u32[]{:S(2)}) collective-permute-start(bf16[64,3840]{1,0:T(8,128)(2,1)S(1)} %reshape.95.a0_ref), channel_id=1, source_target_pairs={{0,192},{64,0},{128,64},{192,128},{1,193},{65,1},{129,65},{193,129... | collective-permute-start | bytes 1474568 | tf_op jit(solution)/shard_map/ppermute | solution.py:32
  45.9 24.4 %copy-start.13 = (s32[128]{0:T(128)S(1)}, s32[128]{0:T(128)}, u32[]{:S(2)}) copy-start(s32[128]{0:T(128)} %span_ref.1) | copy-start | bytes 1540
  69.8 2.9 %collective-permute-start.8 = (f32[256,256]{1,0:T(8,128)}, f32[256,256]{1,0:T(8,128)S(1)}, u32[]{:S(2)}, u32[]{:S(2)}) collective-permute-start(f32[256,256]{1,0:T(8,128)} %get-tuple-element.20), channel_id=1, source_target_pairs={{0,4},{4,0},{1,5},{5,1},{2,6},{6,2},{3,7},{7,3},{8,12},{12,8},{9,1... | collective-permute-start | bytes 786440 | tf_op jit(solution)/shard_map/ppermute | solution.py:263
  75.4 4.3 %collective-permute-start.9 = (f32[8,256]{1,0:T(8,128)}, f32[8,256]{1,0:T(8,128)S(1)}, u32[]{:S(2)}, u32[]{:S(2)}) collective-permute-start(f32[8,256]{1,0:T(8,128)} %get-tuple-element.23), channel_id=1, source_target_pairs={{0,3},{1,0},{2,1},{3,2},{4,7},{5,4},{6,5},{7,6},{8,11},{9,8},{10,9... | collective-permute-start | bytes 24584 | tf_op jit(solution)/shard_map/ppermute | solution.py:32
  77.9 4.2 %collective-permute-start.10 = (f32[8,256]{1,0:T(8,128)}, f32[8,256]{1,0:T(8,128)S(1)}, u32[]{:S(2)}, u32[]{:S(2)}) collective-permute-start(f32[8,256]{1,0:T(8,128)} %get-tuple-element.23), channel_id=1, source_target_pairs={{0,2},{1,3},{2,0},{3,1},{4,6},{5,7},{6,4},{7,5},{8,10},{9,11},{10,... | collective-permute-start | bytes 24584 | tf_op jit(solution)/shard_map/ppermute | solution.py:32
  78.4 3.9 %collective-permute-start.11 = (f32[8,256]{1,0:T(8,128)}, f32[8,256]{1,0:T(8,128)S(1)}, u32[]{:S(2)}, u32[]{:S(2)}) collective-permute-start(f32[8,256]{1,0:T(8,128)} %get-tuple-element.23), channel_id=1, source_target_pairs={{0,1},{1,2},{2,3},{3,0},{4,5},{5,6},{6,7},{7,4},{8,9},{9,10},{10,1... | collective-permute-start | bytes 24584 | tf_op jit(solution)/shard_map/ppermute | solution.py:32
  85.7 2.9 %collective-permute-start.12 = (bf16[256,256]{1,0:T(8,128)(2,1)S(1)}, bf16[256,256]{1,0:T(8,128)(2,1)S(1)}, u32[]{:S(2)}, u32[]{:S(2)}) collective-permute-start(bf16[256,256]{1,0:T(8,128)(2,1)S(1)} %multiply_convert_fusion), channel_id=1, source_target_pairs={{0,4},{4,0},{1,5},{5,1},{2,6},{6,2},{3,7},{7,3},{8,12},{12,8},{9,1... | collective-permute-start | bytes 393224 | tf_op jit(solution)/shard_map/ppermute | solution.py:301
  87.6 40.3 %collective-permute-start.20 = (bf16[256,4096]{1,0:T(8,128)(2,1)}, bf16[256,4096]{1,0:T(8,128)(2,1)}, u32[]{:S(2)}, u32[]{:S(2)}) collective-permute-start(bf16[256,4096]{1,0:T(8,128)(2,1)} %get-tuple-element.28), channel_id=1, source_target_pairs={{0,4},{4,0},{1,5},{5,1},{2,6},{6,2},{3,7},{7,3},{8,12},{12,8},{9,1... | collective-permute-start | bytes 6291464 | tf_op jit(solution)/shard_map/ppermute | solution.py:264
  93.0 12.7 %collective-permute-start.15 = (bf16[64,3328]{1,0:T(8,128)(2,1)}, bf16[64,3328]{1,0:T(8,128)(2,1)}, u32[]{:S(2)}, u32[]{:S(2)}) collective-permute-start(bf16[64,3328]{1,0:T(8,128)(2,1)} %get-tuple-element.39), channel_id=1, source_target_pairs={{0,64},{64,128},{128,192},{192,0},{1,65},{65,129},{129,193},{193,1... | collective-permute-start | bytes 1277960 | tf_op jit(solution)/shard_map/ppermute | solution.py:32
  94.0 21.1 %collective-permute-start.14 = (bf16[64,3328]{1,0:T(8,128)(2,1)S(1)}, bf16[64,3328]{1,0:T(8,128)(2,1)}, u32[]{:S(2)}, u32[]{:S(2)}) collective-permute-start(bf16[64,3328]{1,0:T(8,128)(2,1)S(1)} %get-tuple-element.40), channel_id=1, source_target_pairs={{0,128},{64,192},{128,0},{192,64},{1,129},{65,193},{129,1},{193,65... | collective-permute-start | bytes 1277960 | tf_op jit(solution)/shard_map/ppermute | solution.py:32
  96.2 19.0 %collective-permute-start.13 = (bf16[64,3328]{1,0:T(8,128)(2,1)S(1)}, bf16[64,3328]{1,0:T(8,128)(2,1)}, u32[]{:S(2)}, u32[]{:S(2)}) collective-permute-start(bf16[64,3328]{1,0:T(8,128)(2,1)S(1)} %get-tuple-element.38), channel_id=1, source_target_pairs={{0,192},{64,0},{128,64},{192,128},{1,193},{65,1},{129,65},{193,129... | collective-permute-start | bytes 1277960 | tf_op jit(solution)/shard_map/ppermute | solution.py:32
  99.0 28.8 %copy-start = (bf16[256,4096]{1,0:T(8,128)(2,1)S(1)}, bf16[256,4096]{1,0:T(8,128)(2,1)}, u32[]{:S(2)}) copy-start(bf16[256,4096]{1,0:T(8,128)(2,1)} %get-tuple-element.28) | copy-start | bytes 6291460
  99.0 19.8 %all-to-all-start.3 = ((bf16[8,4,8,768]{3,2,1,0:T(8,128)(2,1)}), bf16[8,4,8,768]{3,2,1,0:T(8,128)(2,1)S(1)}, u32[]{:S(2)}, u32[]{:S(2)}) async-start(bf16[8,4,8,768]{3,2,1,0:T(8,128)(2,1)} %bitcast.66), calls=%async_computation.3 | async-start | bytes 786432 | tf_op jit(solution)/shard_map/all_to_all | solution.py:28
  118.9 25.7 %all-to-all-start.2 = ((bf16[8,8,3328]{2,1,0:T(8,128)(2,1)}), bf16[8,8,3328]{2,1,0:T(8,128)(2,1)S(1)}, u32[]{:S(2)}, u32[]{:S(2)}) async-start(bf16[8,8,3328]{2,1,0:T(8,128)(2,1)} %fusion.12), calls=%async_computation.2 | async-start | bytes 851968 | tf_op jit(solution)/shard_map/all_to_all | solution.py:28
  124.8 15.6 %collective-permute-start.16 = (bf16[8,768]{1,0:T(8,128)(2,1)S(1)}, bf16[8,768]{1,0:T(8,128)(2,1)S(1)}, u32[]{:S(2)}, u32[]{:S(2)}) collective-permute-start(bf16[8,768]{1,0:T(8,128)(2,1)S(1)} %get-tuple-element.45), channel_id=1, source_target_pairs={{0,192},{64,0},{128,64},{192,128},{1,193},{65,1},{129,65},{193,129... | collective-permute-start | bytes 36872 | tf_op jit(solution)/shard_map/ppermute | solution.py:32
  130.6 58.9 %collective-permute-start.23 = (bf16[256,2048]{1,0:T(8,128)(2,1)}, bf16[256,2048]{1,0:T(8,128)(2,1)}, u32[]{:S(2)}, u32[]{:S(2)}) collective-permute-start(bf16[256,2048]{1,0:T(8,128)(2,1)} %convolution_convert_fusion.2), channel_id=1, source_target_pairs={{0,1},{1,2},{2,3},{3,0},{4,5},{5,6},{6,7},{7,4},{8,9},{9,10},{10,1... | collective-permute-start | bytes 3145736 | tf_op jit(solution)/shard_map/ppermute | solution.py:32
  133.6 55.8 %collective-permute-start.22 = (bf16[256,2048]{1,0:T(8,128)(2,1)}, bf16[256,2048]{1,0:T(8,128)(2,1)}, u32[]{:S(2)}, u32[]{:S(2)}) collective-permute-start(bf16[256,2048]{1,0:T(8,128)(2,1)} %convolution_convert_fusion.3), channel_id=1, source_target_pairs={{0,2},{1,3},{2,0},{3,1},{4,6},{5,7},{6,4},{7,5},{8,10},{9,11},{10,... | collective-permute-start | bytes 3145736 | tf_op jit(solution)/shard_map/ppermute | solution.py:32
  137.6 51.9 %collective-permute-start.21 = (bf16[256,2048]{1,0:T(8,128)(2,1)}, bf16[256,2048]{1,0:T(8,128)(2,1)}, u32[]{:S(2)}, u32[]{:S(2)}) collective-permute-start(bf16[256,2048]{1,0:T(8,128)(2,1)} %convolution_convert_fusion.4), channel_id=1, source_target_pairs={{0,3},{1,0},{2,1},{3,2},{4,7},{5,4},{6,5},{7,6},{8,11},{9,8},{10,9... | collective-permute-start | bytes 3145736 | tf_op jit(solution)/shard_map/ppermute | solution.py:32
  139.6 4.1 %collective-permute-start.17 = (bf16[8,768]{1,0:T(8,128)(2,1)S(1)}, bf16[8,768]{1,0:T(8,128)(2,1)S(1)}, u32[]{:S(2)}, u32[]{:S(2)}) collective-permute-start(bf16[8,768]{1,0:T(8,128)(2,1)S(1)} %get-tuple-element.44), channel_id=1, source_target_pairs={{0,128},{64,192},{128,0},{192,64},{1,129},{65,193},{129,1},{193,65... | collective-permute-start | bytes 36872 | tf_op jit(solution)/shard_map/ppermute | solution.py:32
  140.4 4.2 %collective-permute-start.18 = (bf16[8,768]{1,0:T(8,128)(2,1)S(1)}, bf16[8,768]{1,0:T(8,128)(2,1)S(1)}, u32[]{:S(2)}, u32[]{:S(2)}) collective-permute-start(bf16[8,768]{1,0:T(8,128)(2,1)S(1)} %get-tuple-element.43), channel_id=1, source_target_pairs={{0,64},{64,128},{128,192},{192,0},{1,65},{65,129},{129,193},{193,1... | collective-permute-start | bytes 36872 | tf_op jit(solution)/shard_map/ppermute | solution.py:32
  147.3 37.5 %all-to-all-start.4 = ((f32[256,1,128]{2,1,0:T(1,128)}), f32[256,1,128]{2,1,0:T(1,128)S(1)}, u32[]{:S(2)}, u32[]{:S(2)}) async-start(f32[256,1,128]{2,1,0:T(1,128)} %get-tuple-element.24), calls=%async_computation.4 | async-start | bytes 262144 | tf_op jit(solution)/shard_map/all_to_all | solution.py:28
  161.9 3.0 %collective-permute-start.19 = (f32[4,4096]{1,0:T(4,128)S(1)}, f32[4,4096]{1,0:T(4,128)S(1)}, u32[]{:S(2)}, u32[]{:S(2)}) collective-permute-start(f32[4,4096]{1,0:T(4,128)S(1)} %get-tuple-element.41), channel_id=1, source_target_pairs={{0,4},{4,0},{1,5},{5,1},{2,6},{6,2},{3,7},{7,3},{8,12},{12,8},{9,1... | collective-permute-start | bytes 196616 | tf_op jit(solution)/shard_map/ppermute | solution.py:330
  165.0 19.8 %copy-start.9 = (f32[4,4096]{1,0:T(4,128)}, f32[4,4096]{1,0:T(4,128)S(1)}, u32[]{:S(2)}) copy-start(f32[4,4096]{1,0:T(4,128)S(1)} %collective-permute-done.19.mate_ref) | copy-start | bytes 196612
  (15 other events, 98.9 us)

commit v12 on v10

--- a/solution.py
+++ b/solution.py
@@ -49,7 +49,7 @@
 
 
 def score_kernel(
-    thin, a0_ref, a1_ref, a2_ref, a3_ref, b_ref, own_ref, mate_ref, head_ref, own_part_ref, mate_part_ref
+    thin, a0_ref, a1_ref, a2_ref, a3_ref, b_ref, tok_ref, head_ref, own_part_ref, mate_part_ref
 ):
     wide = a0_ref.shape[1]
     y_rows = a0_ref.shape[0]
@@ -58,9 +58,10 @@
         for z in range(NZ):
             at = s * y_rows + z * (y_rows // NZ)
             head_ref[at : at + y_rows // NZ, wide:] = b_ref[z, s, :, :thin]
-    for tok_ref, part_ref in ((mate_ref, mate_part_ref), (own_ref, own_part_ref)):
+    rows = tok_ref.shape[0] // 2
+    for at, part_ref in ((rows, mate_part_ref), (0, own_part_ref)):
         part_ref[...] = lax.dot_general(
-            head_ref[...], tok_ref[...], (((1,), (1,)), ((), ())), preferred_element_type=f32
+            head_ref[...], tok_ref[at : at + rows], (((1,), (1,)), ((), ())), preferred_element_type=f32
         )
 
 
@@ -182,8 +183,8 @@
     thin_g = half * 3 // 16
     wide_g = half - thin_g
     halves = master.astype(bf16).reshape(shard_rows, NC, half)
-    cut = halves[:, :, :wide].transpose(1, 0, 2)
-    cut = jnp.broadcast_to(cut[None], (NZ,) + cut.shape).reshape(NZ * NC, shard_rows, wide)
+    cut = master.astype(bf16)
+    cut = jnp.stack([cut[:, i * half : i * half + wide] for i in range(NC)] * NZ, 0)
     block = exchange(cut, ("z", "core")).reshape(y_rows, wide)
     digit = 256
     pieces = [targets // digit, targets % digit, loss_mask]
@@ -216,7 +217,7 @@
         hidden_states, (0, (1 - core) * half), (tok_rows, half), allow_negative_indices=False
     )
     mate_half = lax.ppermute(far_half, "core", SWAP)
-    tokens = jnp.concatenate([own_half, mate_half], 0)
+    tokens = lax.optimization_barrier(jnp.concatenate([own_half, mate_half], 0))
 
     head, own_part, mate_part = pl.pallas_call(
         functools.partial(score_kernel, thin),
@@ -225,10 +226,10 @@
             jax.ShapeDtypeStruct((group_rows, tok_rows), f32),
             jax.ShapeDtypeStruct((group_rows, tok_rows), f32),
         ),
-        in_specs=[VMEM] * (NY + 3),
+        in_specs=[VMEM] * (NY + 2),
         out_specs=(VMEM, VMEM, VMEM),
         name="score",
-    )(*parts_a, part_b, own_half, mate_half)
+    )(*parts_a, part_b, tokens)
     mate_part = lax.ppermute(mate_part, "core", SWAP)
     mate_head = lax.ppermute(head, "core", SWAP)
     logits, stats, rows = pl.pallas_call(

time: 196 us -> 202 us (1.031)
  local copies, waits for them, and re-layouts: 17.2 us -> 21.7 us
  waiting for transfers between devices: 71.7 us -> 67.6 us
  other arithmetic: 15.1 us -> 19 us
    unnamed x40 -> x51, local copies, waits for them, and re-layouts: 4.95 us -> 11.5 us
    all_to_all x5, waiting for transfers between devices: 39.8 us -> 34.7 us  [exchange(): return lax.all_to_all(x, axes, 0, 0, tiled=True)]
    concatenate x0 -> x1, other arithmetic: none -> 4.01 us  [step(): tokens = lax.optimization_barrier(jnp.concatenate([own_half, mate_half], 0))]
  transfers between devices with their start and end apart: 29 -> 29, of which waited for: 15 -> 15; matrix products, arithmetic and copies ran while one was open for 14% -> 20% of each run, Pallas kernels for 2% -> 2%
where the time goes in v12:
time: 202 us; the launch traced here: 201 us
  waiting for transfers between devices  67.6 us (33%)
  starting transfers between devices  67.5 us (33%)
  local copies, waits for them, and re-layouts  21.7 us (11%)
  other arithmetic  19 us (9%)
  matrix products  12 us (6%)
  Pallas kernels  11.7 us (6%)
    all_to_all x5, starting transfers between devices, exchange(): return lax.all_to_all(x, axes, 0, 0, tiled=True)  35.3 us
    all_to_all x5, waiting for transfers between devices, exchange(): return lax.all_to_all(x, axes, 0, 0, tiled=True)  34.7 us
    ppermute x18, waiting for transfers between devices, shift(): lax.ppermute(x, axis, [(i, (i + step) % count) for i in range(count)])  30.3 us
    ppermute x18, starting transfers between devices, shift(): lax.ppermute(x, axis, [(i, (i + step) % count) for i in range(count)])  24 us
    unnamed x51, local copies, waits for them, and re-layouts  11.5 us
    dot_general x4, matrix products, step(): lax.dot_general(dlogits, side, (((0,), (0,)), ((), ())), preferred_elemen...  8.51 us
    pallas_call x1, Pallas kernels, step(): pl.pallas_call(functools.partial(score_kernel, thin), out_shape=(jax.Shap...  5.54 us
  transfers between devices with their start and end apart: 29, of which 15 were waited for; matrix products, arithmetic and copies ran while one was open for 20% of the time, Pallas kernels for 2%

profile of v12, /device:TPU:1, one launch (start us, length us, event | category | flops | bytes accessed | tf_op | source)
XLA Modules:
  0.0 200.6 jit_solution(14451029339492383536)
XLA Ops:
  0.7 4.0 %constant_dynamic-slice_fusion.3 = (bf16[256,4096]{1,0:T(8,128)(2,1)S(1)}, bf16[256,4096]{1,0:T(8,128)(2,1)}) fusion(bf16[256,8192]{1,0:T(8,128)(2,1)} %param.9, s32[]{:T(128)S(6)} %mul.62, s32[]{:T(128)S(6)} %mul.63), kind=kLoop, calls=%fused_computation.78 | loop fusion | bytes 8388616 | tf_op jit(solution)/shard_map/dynamic_slice | solution.py:213
  4.6 3.3 %collective-permute-start.7 = (bf16[256,4096]{1,0:T(8,128)(2,1)}, bf16[256,4096]{1,0:T(8,128)(2,1)}, u32[]{:S(2)}, u32[]{:S(2)}) collective-permute-start(bf16[256,4096]{1,0:T(8,128)(2,1)} %get-tuple-element.37), channel_id=1, source_target_pairs={{0,4},{4,0},{1,5},{5,1},{2,6},{6,2},{3,7},{7,3},{8,12},{12,8},{9,1... | collective-permute-start | bytes 6291464 | tf_op jit(solution)/shard_map/ppermute | solution.py:219
  17.9 6.9 %all-to-all-start.1 = ((bf16[16,4,3840]{2,1,0:T(4,128)(2,1)}), bf16[16,4,3840]{2,1,0:T(4,128)(2,1)S(1)}, u32[]{:S(2)}, u32[]{:S(2)}) async-start(bf16[16,4,3840]{2,1,0:T(4,128)(2,1)} %constant_dynamic-update-slice_fusion), calls=%async_computation.1 | async-start | bytes 983040 | tf_op jit(solution)/shard_map/all_to_all | solution.py:28
  26.3 2.8 %collective-permute-start.3 = (bf16[8,768]{1,0:T(8,128)(2,1)S(1)}, bf16[8,768]{1,0:T(8,128)(2,1)S(1)}, u32[]{:S(2)}, u32[]{:S(2)}) collective-permute-start(bf16[8,768]{1,0:T(8,128)(2,1)S(1)} %maximum_select_fusion.1), channel_id=1, source_target_pairs={{0,192},{64,0},{128,64},{192,128},{1,193},{65,1},{129,65},{193,129... | collective-permute-start | bytes 36872 | tf_op jit(solution)/shard_map/ppermute | solution.py:32
  30.2 3.3 %collective-permute-done.2 = bf16[8,768]{1,0:T(8,128)(2,1)S(1)} collective-permute-done((bf16[8,768]{1,0:T(8,128)(2,1)S(1)}, bf16[8,768]{1,0:T(8,128)(2,1)S(1)}, u32[]{:S(2)}, u32[]{:S(2)}) %collective-permute-start.2) | collective-permute-done | bytes 12320 | tf_op jit(solution)/shard_map/ppermute | solution.py:32
  33.6 7.7 %all-to-all-done.1 = bf16[16,4,3840]{2,1,0:T(4,128)(2,1)S(1)} async-done(((bf16[16,4,3840]{2,1,0:T(4,128)(2,1)}), bf16[16,4,3840]{2,1,0:T(4,128)(2,1)S(1)}, u32[]{:S(2)}, u32[]{:S(2)}) %all-to-all-start.1) | async-done | bytes 491552 | tf_op jit(solution)/shard_map/all_to_all | solution.py:28
  42.1 3.5 %all-to-all-start = ((bf16[8,4,8,768]{3,2,1,0:T(8,128)(2,1)}), bf16[8,4,8,768]{3,2,1,0:T(8,128)(2,1)S(1)}, u32[]{:S(2)}, u32[]{:S(2)}) async-start(bf16[8,4,8,768]{3,2,1,0:T(8,128)(2,1)} %broadcast_in_dim.45), calls=%async_computation | async-start | bytes 786432 | tf_op jit(solution)/shard_map/all_to_all | solution.py:28
  47.1 2.6 %collective-permute-start.5 = (bf16[64,3840]{1,0:T(8,128)(2,1)S(1)}, bf16[64,3840]{1,0:T(8,128)(2,1)}, u32[]{:S(2)}, u32[]{:S(2)}) collective-permute-start(bf16[64,3840]{1,0:T(8,128)(2,1)S(1)} %reshape.90.a0_ref), channel_id=1, source_target_pairs={{0,128},{64,192},{128,0},{192,64},{1,129},{65,193},{129,1},{193,65... | collective-permute-start | bytes 1474568 | tf_op jit(solution)/shard_map/ppermute | solution.py:32
  50.8 4.0 %pad_maximum_fusion.tok_ref = bf16[512,4096]{1,0:T(8,128)(2,1)} fusion(bf16[256,4096]{1,0:T(8,128)(2,1)} %collective-permute-done.7, bf16[256,4096]{1,0:T(8,128)(2,1)S(1)} %get-tuple-element.36), kind=kLoop, calls=%fused_computation.1 | loop fusion | flops 8388608 | bytes 8388608 | tf_op jit(solution)/shard_map/concatenate | solution.py:220
  54.8 6.0 %all-to-all-done.b_ref = bf16[8,4,8,768]{3,2,1,0:T(8,128)(2,1)S(1)} async-done(((bf16[8,4,8,768]{3,2,1,0:T(8,128)(2,1)}), bf16[8,4,8,768]{3,2,1,0:T(8,128)(2,1)S(1)}, u32[]{:S(2)}, u32[]{:S(2)}) %all-to-all-start) | async-done | bytes 393248 | tf_op jit(solution)/shard_map/all_to_all | solution.py:28
  60.8 11.2 %collective-permute-done.5.a2_ref = bf16[64,3840]{1,0:T(8,128)(2,1)} collective-permute-done((bf16[64,3840]{1,0:T(8,128)(2,1)S(1)}, bf16[64,3840]{1,0:T(8,128)(2,1)}, u32[]{:S(2)}, u32[]{:S(2)}) %collective-permute-start.5) | collective-permute-done | bytes 491552 | tf_op jit(solution)/shard_map/ppermute | solution.py:32
  72.0 5.5 %score.1 = (bf16[256,4096]{1,0:T(8,128)(2,1)}, f32[256,256]{1,0:T(8,128)}, f32[256,256]{1,0:T(8,128)}) custom-call(bf16[64,3840]{1,0:T(8,128)(2,1)} %copy-done.3, bf16[64,3840]{1,0:T(8,128)(2,1)} %copy-done.7, bf16[64,3840]{1,0:T(8,128)(2,1)} %collective-permute-done.5.a2_ref, bf16[64,3840]{1,0:T(8,128)(2,1)} %collective-permute-done.6.a3_ref, ...), custom_call_target="tpu_custom_call" | custom-call | tf_op jit(solution)/shard_map/score/pallas_call | solution.py:222
  81.0 1.9 front.1
  83.0 2.5 %collective-permute-start.9 = (f32[8,256]{1,0:T(8,128)}, f32[8,256]{1,0:T(8,128)S(1)}, u32[]{:S(2)}, u32[]{:S(2)}) collective-permute-start(f32[8,256]{1,0:T(8,128)} %get-tuple-element.23), channel_id=1, source_target_pairs={{0,3},{1,0},{2,1},{3,2},{4,7},{5,4},{6,5},{7,6},{8,11},{9,8},{10,9... | collective-permute-start | bytes 24584 | tf_op jit(solution)/shard_map/ppermute | solution.py:32
  87.3 2.4 %collective-permute-done.10 = f32[8,256]{1,0:T(8,128)S(1)} collective-permute-done((f32[8,256]{1,0:T(8,128)}, f32[8,256]{1,0:T(8,128)S(1)}, u32[]{:S(2)}, u32[]{:S(2)}) %collective-permute-start.10) | collective-permute-done | bytes 8224 | tf_op jit(solution)/shard_map/ppermute | solution.py:32
  96.2 3.4 %convolution_convert_fusion = bf16[256,4096]{1,0:T(8,128)(2,1)S(1)} fusion(bf16[512,4096]{1,0:T(8,128)(2,1)} %pad_maximum_fusion.tok_ref, bf16[256,256]{1,0:T(8,128)(2,1)S(1)} %collective-permute-done.12, bf16[256,256]{1,0:T(8,128)(2,1)S(1)} %multiply_convert_fusion), kind=kOutput, calls=%fused_computation | convolution fusion | flops 1075314688 | bytes 6553600 | tf_op jit(solution)/shard_map/dot_general | solution.py:274
  101.6 2.2 %collective-permute-start.14 = (bf16[64,3328]{1,0:T(8,128)(2,1)S(1)}, bf16[64,3328]{1,0:T(8,128)(2,1)}, u32[]{:S(2)}, u32[]{:S(2)}) collective-permute-start(bf16[64,3328]{1,0:T(8,128)(2,1)S(1)} %get-tuple-element.40), channel_id=1, source_target_pairs={{0,128},{64,192},{128,0},{192,64},{1,129},{65,193},{129,1},{193,65... | collective-permute-start | bytes 1277960 | tf_op jit(solution)/shard_map/ppermute | solution.py:32
  106.6 6.7 %all-to-all-start.3 = ((bf16[8,4,8,768]{3,2,1,0:T(8,128)(2,1)}), bf16[8,4,8,768]{3,2,1,0:T(8,128)(2,1)S(1)}, u32[]{:S(2)}, u32[]{:S(2)}) async-start(bf16[8,4,8,768]{3,2,1,0:T(8,128)(2,1)} %bitcast.99), calls=%async_computation.3 | async-start | bytes 786432 | tf_op jit(solution)/shard_map/all_to_all | solution.py:28
  113.3 9.5 %collective-permute-done.14 = bf16[64,3328]{1,0:T(8,128)(2,1)} collective-permute-done((bf16[64,3328]{1,0:T(8,128)(2,1)S(1)}, bf16[64,3328]{1,0:T(8,128)(2,1)}, u32[]{:S(2)}, u32[]{:S(2)}) %collective-permute-start.14) | collective-permute-done | bytes 426016 | tf_op jit(solution)/shard_map/ppermute | solution.py:32
  122.8 2.4 %fusion.12 = bf16[8,8,3328]{2,1,0:T(8,128)(2,1)} fusion(bf16[64,3328]{1,0:T(8,128)(2,1)} %collective-permute-done.15, bf16[64,3328]{1,0:T(8,128)(2,1)} %collective-permute-done.14, bf16[64,3328]{1,0:T(8,128)(2,1)} %collective-permute-done.13, bf16[256,4096]{1,0:T(8,128)(2,1)} %copy-done.2), kind=kLoop, calls=%fused_computation.21 | loop fusion | flops 1703936 | bytes 2129920 | tf_op jit(solution)/shard_map/reshape | solution.py:279
  126.4 5.3 %all-to-all-start.2 = ((bf16[8,8,3328]{2,1,0:T(8,128)(2,1)}), bf16[8,8,3328]{2,1,0:T(8,128)(2,1)S(1)}, u32[]{:S(2)}, u32[]{:S(2)}) async-start(bf16[8,8,3328]{2,1,0:T(8,128)(2,1)} %fusion.12), calls=%async_computation.2 | async-start | bytes 851968 | tf_op jit(solution)/shard_map/all_to_all | solution.py:28
  132.4 3.1 %collective-permute-start.16 = (bf16[8,768]{1,0:T(8,128)(2,1)S(1)}, bf16[8,768]{1,0:T(8,128)(2,1)S(1)}, u32[]{:S(2)}, u32[]{:S(2)}) collective-permute-start(bf16[8,768]{1,0:T(8,128)(2,1)S(1)} %get-tuple-element.45), channel_id=1, source_target_pairs={{0,192},{64,0},{128,64},{192,128},{1,193},{65,1},{129,65},{193,129... | collective-permute-start | bytes 36872 | tf_op jit(solution)/shard_map/ppermute | solution.py:32
  135.5 2.7 %convolution_convert_fusion.2 = bf16[256,2048]{1,0:T(8,128)(2,1)} fusion(bf16[256,256]{1,0:T(8,128)(2,1)S(1)} %multiply_convert_fusion, bf16[256,4096]{1,0:T(8,128)(2,1)} %collective-permute-done.20, s32[]{:T(128)S(6)} %mul.76, bf16[256,4096]{1,0:T(8,128)(2,1)S(1)} %copy-done, pred[]{:T(512)S(6)} %eq.129), kind=kOutput, calls=%fused_computation.3 | convolution fusion | flops 269484032 | bytes 3276805 | tf_op jit(solution)/shard_map/dot_general | solution.py:317
  142.5 2.7 %convolution_convert_fusion.4 = bf16[256,2048]{1,0:T(8,128)(2,1)} fusion(bf16[256,256]{1,0:T(8,128)(2,1)S(1)} %multiply_convert_fusion, bf16[256,4096]{1,0:T(8,128)(2,1)} %collective-permute-done.20, s32[]{:T(128)S(6)} %mul.74, bf16[256,4096]{1,0:T(8,128)(2,1)S(1)} %copy-done, pred[]{:T(512)S(6)} %eq.127), kind=kOutput, calls=%fused_computation.5 | convolution fusion | flops 269484032 | bytes 3276805 | tf_op jit(solution)/shard_map/dot_general | solution.py:317
  145.1 2.1 %collective-permute-start.21 = (bf16[256,2048]{1,0:T(8,128)(2,1)}, bf16[256,2048]{1,0:T(8,128)(2,1)}, u32[]{:S(2)}, u32[]{:S(2)}) collective-permute-start(bf16[256,2048]{1,0:T(8,128)(2,1)} %convolution_convert_fusion.4), channel_id=1, source_target_pairs={{0,3},{1,0},{2,1},{3,2},{4,7},{5,4},{6,5},{7,6},{8,11},{9,8},{10,9... | collective-permute-start | bytes 3145736 | tf_op jit(solution)/shard_map/ppermute | solution.py:32
  148.6 2.8 %collective-permute-done.17.b2_ref = bf16[8,768]{1,0:T(8,128)(2,1)S(1)} collective-permute-done((bf16[8,768]{1,0:T(8,128)(2,1)S(1)}, bf16[8,768]{1,0:T(8,128)(2,1)S(1)}, u32[]{:S(2)}, u32[]{:S(2)}) %collective-permute-start.17) | collective-permute-done | bytes 12320 | tf_op jit(solution)/shard_map/ppermute | solution.py:32
  152.9 1.9 square.1
  154.9 13.0 %all-to-all-start.4 = ((f32[256,1,128]{2,1,0:T(1,128)}), f32[256,1,128]{2,1,0:T(1,128)S(1)}, u32[]{:S(2)}, u32[]{:S(2)}) async-start(f32[256,1,128]{2,1,0:T(1,128)} %get-tuple-element.24), calls=%async_computation.4 | async-start | bytes 262144 | tf_op jit(solution)/shard_map/all_to_all | solution.py:28
  169.5 2.1 %collective-permute-start.19 = (f32[4,4096]{1,0:T(4,128)S(1)}, f32[4,4096]{1,0:T(4,128)S(1)}, u32[]{:S(2)}, u32[]{:S(2)}) collective-permute-start(f32[4,4096]{1,0:T(4,128)S(1)} %get-tuple-element.41), channel_id=1, source_target_pairs={{0,4},{4,0},{1,5},{5,1},{2,6},{6,2},{3,7},{7,3},{8,12},{12,8},{9,1... | collective-permute-start | bytes 196616 | tf_op jit(solution)/shard_map/ppermute | solution.py:300
  172.6 19.8 %all-to-all-done.4.report_ref = f32[256,1,128]{2,1,0:T(1,128)S(1)} async-done(((f32[256,1,128]{2,1,0:T(1,128)}), f32[256,1,128]{2,1,0:T(1,128)S(1)}, u32[]{:S(2)}, u32[]{:S(2)}) %all-to-all-start.4) | async-done | bytes 131104 | tf_op jit(solution)/shard_map/all_to_all | solution.py:28
  193.0 2.3 %final.1 = (f32[2,128]{1,0:T(2,128)}, f32[1,1]{1,0:T(1,128)}, f32[4,8192]{1,0:T(4,128)}, f32[4,8192]{1,0:T(4,128)}, f32[4,8192]{1,0:T(4,128)}) custom-call(s32[8]{0:T(128)} %compare_select_fusion.6.place_ref, f32[256,1,128]{2,1,0:T(1,128)} %copy-done.6, f32[8,256]{1,0:T(8,128)} %get-tuple-element.21.row_ref, f32[4,4096]{1,0:T(4,128)} %get-tuple-element.42.near_ref, ...), custom_call_target="tpu_custom_call" | custom-call | tf_op jit(solution)/shard_map/final/pallas_call | solution.py:328
  197.1 3.5 %add_convert_fusion = bf16[256,2048]{1,0:T(8,128)(2,1)} fusion(bf16[256,2048]{1,0:T(8,128)(2,1)S(1)} %convolution_convert_fusion.1, bf16[256,2048]{1,0:T(8,128)(2,1)} %collective-permute-done.23, bf16[256,2048]{1,0:T(8,128)(2,1)} %collective-permute-done.22, bf16[256,2048]{1,0:T(8,128)(2,1)} %collective-permute-done.21), kind=kLoop, calls=%fused_computation.6 | loop fusion | flops 4194304 | bytes 5242880 | tf_op jit(solution)/shard_map/convert_element_type | solution.py:325
  (132 shorter events, 46.6 us)
Async XLA Ops:
  4.6 20.3 %copy-start.16 = (f32[256]{0:T(256)S(1)}, f32[256]{0:T(256)}, u32[]{:S(2)}) copy-start(f32[256]{0:T(256)} %param.16) | copy-start | bytes 3076
  4.6 46.1 %collective-permute-start.7 = (bf16[256,4096]{1,0:T(8,128)(2,1)}, bf16[256,4096]{1,0:T(8,128)(2,1)}, u32[]{:S(2)}, u32[]{:S(2)}) collective-permute-start(bf16[256,4096]{1,0:T(8,128)(2,1)} %get-tuple-element.37), channel_id=1, source_target_pairs={{0,4},{4,0},{1,5},{5,1},{2,6},{6,2},{3,7},{7,3},{8,12},{12,8},{9,1... | collective-permute-start | bytes 6291464 | tf_op jit(solution)/shard_map/ppermute | solution.py:219
  17.9 23.4 %all-to-all-start.1 = ((bf16[16,4,3840]{2,1,0:T(4,128)(2,1)}), bf16[16,4,3840]{2,1,0:T(4,128)(2,1)S(1)}, u32[]{:S(2)}, u32[]{:S(2)}) async-start(bf16[16,4,3840]{2,1,0:T(4,128)(2,1)} %constant_dynamic-update-slice_fusion), calls=%async_computation.1 | async-start | bytes 983040 | tf_op jit(solution)/shard_map/all_to_all | solution.py:28
  25.0 1.3 collective-permute-start
  26.3 3.9 %collective-permute-start.3 = (bf16[8,768]{1,0:T(8,128)(2,1)S(1)}, bf16[8,768]{1,0:T(8,128)(2,1)S(1)}, u32[]{:S(2)}, u32[]{:S(2)}) collective-permute-start(bf16[8,768]{1,0:T(8,128)(2,1)S(1)} %maximum_select_fusion.1), channel_id=1, source_target_pairs={{0,192},{64,0},{128,64},{192,128},{1,193},{65,1},{129,65},{193,129... | collective-permute-start | bytes 36872 | tf_op jit(solution)/shard_map/ppermute | solution.py:32
  29.1 4.3 %collective-permute-start.2 = (bf16[8,768]{1,0:T(8,128)(2,1)S(1)}, bf16[8,768]{1,0:T(8,128)(2,1)S(1)}, u32[]{:S(2)}, u32[]{:S(2)}) collective-permute-start(bf16[8,768]{1,0:T(8,128)(2,1)S(1)} %maximum_select_fusion.1), channel_id=1, source_target_pairs={{0,128},{64,192},{128,0},{192,64},{1,129},{65,193},{129,1},{193,65... | collective-permute-start | bytes 36872 | tf_op jit(solution)/shard_map/ppermute | solution.py:32
  29.5 4.1 %collective-permute-start.1 = (bf16[8,768]{1,0:T(8,128)(2,1)S(1)}, bf16[8,768]{1,0:T(8,128)(2,1)S(1)}, u32[]{:S(2)}, u32[]{:S(2)}) collective-permute-start(bf16[8,768]{1,0:T(8,128)(2,1)S(1)} %maximum_select_fusion.1), channel_id=1, source_target_pairs={{0,64},{64,128},{128,192},{192,0},{1,65},{65,129},{129,193},{193,1... | collective-permute-start | bytes 36872 | tf_op jit(solution)/shard_map/ppermute | solution.py:32
  42.1 18.7 %all-to-all-start = ((bf16[8,4,8,768]{3,2,1,0:T(8,128)(2,1)}), bf16[8,4,8,768]{3,2,1,0:T(8,128)(2,1)S(1)}, u32[]{:S(2)}, u32[]{:S(2)}) async-start(bf16[8,4,8,768]{3,2,1,0:T(8,128)(2,1)} %broadcast_in_dim.45), calls=%async_computation | async-start | bytes 786432 | tf_op jit(solution)/shard_map/all_to_all | solution.py:28
  45.7 15.1 %collective-permute-start.4 = (bf16[64,3840]{1,0:T(8,128)(2,1)S(1)}, bf16[64,3840]{1,0:T(8,128)(2,1)S(1)}, u32[]{:S(2)}, u32[]{:S(2)}) collective-permute-start(bf16[64,3840]{1,0:T(8,128)(2,1)S(1)} %reshape.90.a0_ref), channel_id=1, source_target_pairs={{0,64},{64,128},{128,192},{192,0},{1,65},{65,129},{129,193},{193,1... | collective-permute-start | bytes 1474568 | tf_op jit(solution)/shard_map/ppermute | solution.py:32
  47.1 24.9 %collective-permute-start.5 = (bf16[64,3840]{1,0:T(8,128)(2,1)S(1)}, bf16[64,3840]{1,0:T(8,128)(2,1)}, u32[]{:S(2)}, u32[]{:S(2)}) collective-permute-start(bf16[64,3840]{1,0:T(8,128)(2,1)S(1)} %reshape.90.a0_ref), channel_id=1, source_target_pairs={{0,128},{64,192},{128,0},{192,64},{1,129},{65,193},{129,1},{193,65... | collective-permute-start | bytes 1474568 | tf_op jit(solution)/shard_map/ppermute | solution.py:32
  49.7 22.3 %collective-permute-start.6 = (bf16[64,3840]{1,0:T(8,128)(2,1)S(1)}, bf16[64,3840]{1,0:T(8,128)(2,1)}, u32[]{:S(2)}, u32[]{:S(2)}) collective-permute-start(bf16[64,3840]{1,0:T(8,128)(2,1)S(1)} %reshape.90.a0_ref), channel_id=1, source_target_pairs={{0,192},{64,0},{128,64},{192,128},{1,193},{65,1},{129,65},{193,129... | collective-permute-start | bytes 1474568 | tf_op jit(solution)/shard_map/ppermute | solution.py:32
  54.8 23.1 %copy-start.13 = (s32[128]{0:T(128)S(1)}, s32[128]{0:T(128)}, u32[]{:S(2)}) copy-start(s32[128]{0:T(128)} %span_ref.1) | copy-start | bytes 1540
  77.5 2.8 %collective-permute-start.8 = (f32[256,256]{1,0:T(8,128)}, f32[256,256]{1,0:T(8,128)S(1)}, u32[]{:S(2)}, u32[]{:S(2)}) collective-permute-start(f32[256,256]{1,0:T(8,128)} %get-tuple-element.20), channel_id=1, source_target_pairs={{0,4},{4,0},{1,5},{5,1},{2,6},{6,2},{3,7},{7,3},{8,12},{12,8},{9,1... | collective-permute-start | bytes 786440 | tf_op jit(solution)/shard_map/ppermute | solution.py:233
  83.0 4.3 %collective-permute-start.9 = (f32[8,256]{1,0:T(8,128)}, f32[8,256]{1,0:T(8,128)S(1)}, u32[]{:S(2)}, u32[]{:S(2)}) collective-permute-start(f32[8,256]{1,0:T(8,128)} %get-tuple-element.23), channel_id=1, source_target_pairs={{0,3},{1,0},{2,1},{3,2},{4,7},{5,4},{6,5},{7,6},{8,11},{9,8},{10,9... | collective-permute-start | bytes 24584 | tf_op jit(solution)/shard_map/ppermute | solution.py:32
  85.5 4.2 %collective-permute-start.10 = (f32[8,256]{1,0:T(8,128)}, f32[8,256]{1,0:T(8,128)S(1)}, u32[]{:S(2)}, u32[]{:S(2)}) collective-permute-start(f32[8,256]{1,0:T(8,128)} %get-tuple-element.23), channel_id=1, source_target_pairs={{0,2},{1,3},{2,0},{3,1},{4,6},{5,7},{6,4},{7,5},{8,10},{9,11},{10,... | collective-permute-start | bytes 24584 | tf_op jit(solution)/shard_map/ppermute | solution.py:32
  86.0 3.9 %collective-permute-start.11 = (f32[8,256]{1,0:T(8,128)}, f32[8,256]{1,0:T(8,128)S(1)}, u32[]{:S(2)}, u32[]{:S(2)}) collective-permute-start(f32[8,256]{1,0:T(8,128)} %get-tuple-element.23), channel_id=1, source_target_pairs={{0,1},{1,2},{2,3},{3,0},{4,5},{5,6},{6,7},{7,4},{8,9},{9,10},{10,1... | collective-permute-start | bytes 24584 | tf_op jit(solution)/shard_map/ppermute | solution.py:32
  93.3 2.9 %collective-permute-start.12 = (bf16[256,256]{1,0:T(8,128)(2,1)S(1)}, bf16[256,256]{1,0:T(8,128)(2,1)S(1)}, u32[]{:S(2)}, u32[]{:S(2)}) collective-permute-start(bf16[256,256]{1,0:T(8,128)(2,1)S(1)} %multiply_convert_fusion), channel_id=1, source_target_pairs={{0,4},{4,0},{1,5},{5,1},{2,6},{6,2},{3,7},{7,3},{8,12},{12,8},{9,1... | collective-permute-start | bytes 393224 | tf_op jit(solution)/shard_map/ppermute | solution.py:271
  95.2 40.3 %collective-permute-start.20 = (bf16[256,4096]{1,0:T(8,128)(2,1)}, bf16[256,4096]{1,0:T(8,128)(2,1)}, u32[]{:S(2)}, u32[]{:S(2)}) collective-permute-start(bf16[256,4096]{1,0:T(8,128)(2,1)} %get-tuple-element.28), channel_id=1, source_target_pairs={{0,4},{4,0},{1,5},{5,1},{2,6},{6,2},{3,7},{7,3},{8,12},{12,8},{9,1... | collective-permute-start | bytes 6291464 | tf_op jit(solution)/shard_map/ppermute | solution.py:234
  100.6 12.7 %collective-permute-start.15 = (bf16[64,3328]{1,0:T(8,128)(2,1)}, bf16[64,3328]{1,0:T(8,128)(2,1)}, u32[]{:S(2)}, u32[]{:S(2)}) collective-permute-start(bf16[64,3328]{1,0:T(8,128)(2,1)} %get-tuple-element.39), channel_id=1, source_target_pairs={{0,64},{64,128},{128,192},{192,0},{1,65},{65,129},{129,193},{193,1... | collective-permute-start | bytes 1277960 | tf_op jit(solution)/shard_map/ppermute | solution.py:32
  101.6 21.2 %collective-permute-start.14 = (bf16[64,3328]{1,0:T(8,128)(2,1)S(1)}, bf16[64,3328]{1,0:T(8,128)(2,1)}, u32[]{:S(2)}, u32[]{:S(2)}) collective-permute-start(bf16[64,3328]{1,0:T(8,128)(2,1)S(1)} %get-tuple-element.40), channel_id=1, source_target_pairs={{0,128},{64,192},{128,0},{192,64},{1,129},{65,193},{129,1},{193,65... | collective-permute-start | bytes 1277960 | tf_op jit(solution)/shard_map/ppermute | solution.py:32
  103.8 19.0 %collective-permute-start.13 = (bf16[64,3328]{1,0:T(8,128)(2,1)S(1)}, bf16[64,3328]{1,0:T(8,128)(2,1)}, u32[]{:S(2)}, u32[]{:S(2)}) collective-permute-start(bf16[64,3328]{1,0:T(8,128)(2,1)S(1)} %get-tuple-element.38), channel_id=1, source_target_pairs={{0,192},{64,0},{128,64},{192,128},{1,193},{65,1},{129,65},{193,129... | collective-permute-start | bytes 1277960 | tf_op jit(solution)/shard_map/ppermute | solution.py:32
  106.6 28.8 %copy-start = (bf16[256,4096]{1,0:T(8,128)(2,1)S(1)}, bf16[256,4096]{1,0:T(8,128)(2,1)}, u32[]{:S(2)}) copy-start(bf16[256,4096]{1,0:T(8,128)(2,1)} %get-tuple-element.28) | copy-start | bytes 6291460
  106.6 19.8 %all-to-all-start.3 = ((bf16[8,4,8,768]{3,2,1,0:T(8,128)(2,1)}), bf16[8,4,8,768]{3,2,1,0:T(8,128)(2,1)S(1)}, u32[]{:S(2)}, u32[]{:S(2)}) async-start(bf16[8,4,8,768]{3,2,1,0:T(8,128)(2,1)} %bitcast.99), calls=%async_computation.3 | async-start | bytes 786432 | tf_op jit(solution)/shard_map/all_to_all | solution.py:28
  126.4 25.7 %all-to-all-start.2 = ((bf16[8,8,3328]{2,1,0:T(8,128)(2,1)}), bf16[8,8,3328]{2,1,0:T(8,128)(2,1)S(1)}, u32[]{:S(2)}, u32[]{:S(2)}) async-start(bf16[8,8,3328]{2,1,0:T(8,128)(2,1)} %fusion.12), calls=%async_computation.2 | async-start | bytes 851968 | tf_op jit(solution)/shard_map/all_to_all | solution.py:28
  132.4 15.6 %collective-permute-start.16 = (bf16[8,768]{1,0:T(8,128)(2,1)S(1)}, bf16[8,768]{1,0:T(8,128)(2,1)S(1)}, u32[]{:S(2)}, u32[]{:S(2)}) collective-permute-start(bf16[8,768]{1,0:T(8,128)(2,1)S(1)} %get-tuple-element.45), channel_id=1, source_target_pairs={{0,192},{64,0},{128,64},{192,128},{1,193},{65,1},{129,65},{193,129... | collective-permute-start | bytes 36872 | tf_op jit(solution)/shard_map/ppermute | solution.py:32
  138.1 58.9 %collective-permute-start.23 = (bf16[256,2048]{1,0:T(8,128)(2,1)}, bf16[256,2048]{1,0:T(8,128)(2,1)}, u32[]{:S(2)}, u32[]{:S(2)}) collective-permute-start(bf16[256,2048]{1,0:T(8,128)(2,1)} %convolution_convert_fusion.2), channel_id=1, source_target_pairs={{0,1},{1,2},{2,3},{3,0},{4,5},{5,6},{6,7},{7,4},{8,9},{9,10},{10,1... | collective-permute-start | bytes 3145736 | tf_op jit(solution)/shard_map/ppermute | solution.py:32
  141.2 55.8 %collective-permute-start.22 = (bf16[256,2048]{1,0:T(8,128)(2,1)}, bf16[256,2048]{1,0:T(8,128)(2,1)}, u32[]{:S(2)}, u32[]{:S(2)}) collective-permute-start(bf16[256,2048]{1,0:T(8,128)(2,1)} %convolution_convert_fusion.3), channel_id=1, source_target_pairs={{0,2},{1,3},{2,0},{3,1},{4,6},{5,7},{6,4},{7,5},{8,10},{9,11},{10,... | collective-permute-start | bytes 3145736 | tf_op jit(solution)/shard_map/ppermute | solution.py:32
  145.1 51.9 %collective-permute-start.21 = (bf16[256,2048]{1,0:T(8,128)(2,1)}, bf16[256,2048]{1,0:T(8,128)(2,1)}, u32[]{:S(2)}, u32[]{:S(2)}) collective-permute-start(bf16[256,2048]{1,0:T(8,128)(2,1)} %convolution_convert_fusion.4), channel_id=1, source_target_pairs={{0,3},{1,0},{2,1},{3,2},{4,7},{5,4},{6,5},{7,6},{8,11},{9,8},{10,9... | collective-permute-start | bytes 3145736 | tf_op jit(solution)/shard_map/ppermute | solution.py:32
  147.2 4.1 %collective-permute-start.17 = (bf16[8,768]{1,0:T(8,128)(2,1)S(1)}, bf16[8,768]{1,0:T(8,128)(2,1)S(1)}, u32[]{:S(2)}, u32[]{:S(2)}) collective-permute-start(bf16[8,768]{1,0:T(8,128)(2,1)S(1)} %get-tuple-element.44), channel_id=1, source_target_pairs={{0,128},{64,192},{128,0},{192,64},{1,129},{65,193},{129,1},{193,65... | collective-permute-start | bytes 36872 | tf_op jit(solution)/shard_map/ppermute | solution.py:32
  148.0 4.2 %collective-permute-start.18 = (bf16[8,768]{1,0:T(8,128)(2,1)S(1)}, bf16[8,768]{1,0:T(8,128)(2,1)S(1)}, u32[]{:S(2)}, u32[]{:S(2)}) collective-permute-start(bf16[8,768]{1,0:T(8,128)(2,1)S(1)} %get-tuple-element.43), channel_id=1, source_target_pairs={{0,64},{64,128},{128,192},{192,0},{1,65},{65,129},{129,193},{193,1... | collective-permute-start | bytes 36872 | tf_op jit(solution)/shard_map/ppermute | solution.py:32
  154.9 37.5 %all-to-all-start.4 = ((f32[256,1,128]{2,1,0:T(1,128)}), f32[256,1,128]{2,1,0:T(1,128)S(1)}, u32[]{:S(2)}, u32[]{:S(2)}) async-start(f32[256,1,128]{2,1,0:T(1,128)} %get-tuple-element.24), calls=%async_computation.4 | async-start | bytes 262144 | tf_op jit(solution)/shard_map/all_to_all | solution.py:28
  169.5 3.0 %collective-permute-start.19 = (f32[4,4096]{1,0:T(4,128)S(1)}, f32[4,4096]{1,0:T(4,128)S(1)}, u32[]{:S(2)}, u32[]{:S(2)}) collective-permute-start(f32[4,4096]{1,0:T(4,128)S(1)} %get-tuple-element.41), channel_id=1, source_target_pairs={{0,4},{4,0},{1,5},{5,1},{2,6},{6,2},{3,7},{7,3},{8,12},{12,8},{9,1... | collective-permute-start | bytes 196616 | tf_op jit(solution)/shard_map/ppermute | solution.py:300
  (15 other events, 133.9 us)
